TPU v7x, 256 devices: a whole 4x4x8 slice. The times are simulated.
256 devices in a mesh: frame: 16 (over z, core), mp: 8 (over x, y_hi), dp: 2 (over y_lo).
Axes of the slice: x: 4, y: 4 (y_hi: 2, y_lo: 2; y = y_hi * 2 + y_lo), z: 8, core: 2. Of those that a mesh axis runs over, the one named last changes fastest.
Arguments:
- tokens: bfloat16 [4, 16, 160, 5120], P('dp', 'frame', None, 'mp'), may hold values from -30 to 30
- token_mask: int32 [4, 16, 160], P('dp', 'frame'), may hold values 0 or 1
- mask_embed: bfloat16 [5120], P('mp'), may hold values from -6 to 6
- w_qkv: bfloat16 [5120, 3, 3072], P('frame', None, 'mp'), may hold values from -0.078125 to 0.078125
- w_out: bfloat16 [3072, 5120], P('mp'), may hold values from -0.109375 to 0.109375
- action_idx: int32 [4, 16], P('dp', 'frame'), may hold values from 0 to 7
- codebook: float32 [8, 32], replicated, may hold values from -6 to 6
- act_proj: float32 [32, 5120], P(None, 'mp'), may hold values from -1 to 1
- cotangent: bfloat16 [4, 16, 160, 5120], P('dp', 'frame', None, 'mp'), may hold values from -6 to 6
Outputs:
- next_state: bfloat16 [4, 16, 160, 5120], P('dp', 'frame', None, 'mp')
- grad_proj: float32 [32, 5120], P(None, 'mp')
All inputs are finite; a program needn't handle non-finite values. No bound on the sum of `token_mask` on one device may be relied on, other than what follows from the above.
Results may differ from a plain program's by a relative error of at most 0.0098.
Values may be sent and summed in bfloat16 or wider, within the bound.
No kernel may reach another device: no remote copies, remote signals or barrier semaphores. Data moves between devices by JAX's collectives and lax.ppermute only.
A program may use at most 128 MiB of HBM per device.

v0:
```python
import math

import jax
import jax.numpy as jnp
from jax import lax
from jax.sharding import Mesh
from jax.sharding import PartitionSpec as P

HS = 128
MP = ("mp_0", "mp_1")


floor_score = -1e30


def gathered_by_axis(x, axes, dim):
    for axis in reversed(axes):
        x = lax.all_gather(x, axis, axis=dim, tiled=True)
    return x


def in_one_piece(arrays, axis, dim, along):
    ends, at = ([], 0)
    for a in arrays[:-1]:
        at += a.shape[along]
        ends.append(at)
    both = jnp.concatenate(arrays, axis=along)
    return tuple(jnp.split(lax.all_gather(both, axis, axis=dim, tiled=True), ends, axis=along))


def laid_out(pieces, dim):
    pieces = jnp.moveaxis(pieces, 0, dim)
    shape = pieces.shape
    return pieces.reshape(*shape[:dim], shape[dim] * shape[dim + 1], *shape[dim + 2 :])


def from_everyone(x, axis):
    copies = jnp.broadcast_to(x, (lax.axis_size(axis), *x.shape))
    return lax.all_to_all(copies, axis, split_axis=0, concat_axis=0, tiled=True)


def gather_directly(x, axis, dim):
    return laid_out(from_everyone(x, axis), dim)


def of_everyone(x, axis):
    return from_everyone(x, axis).sum(axis=0)


def block_stats(query, past_keys, past_values, valid):
    scale = 1.0 / math.sqrt(HS)
    scores = (
        jnp.einsum("cphd,cnphd->cphn", query, past_keys, preferred_element_type=jnp.float32) * scale
    )
    scores = jnp.where(valid[None, None, None, :], scores, floor_score)
    peak = jnp.max(scores, axis=-1)
    weights = jnp.where(valid[None, None, None, :], jnp.exp(scores - peak[..., None]), 0.0)
    total = jnp.sum(weights, axis=-1)
    accum = jnp.einsum(
        "cphn,cnphd->cphd",
        weights,
        past_values.astype(jnp.float32),
        precision=lax.Precision.HIGHEST,
    )
    return (peak, total, accum)


def merge_stats(first, second):
    peak = jnp.maximum(first[0], second[0])
    right = jnp.exp(second[0] - peak)
    total = second[1] * right
    accum = second[2] * right[..., None]
    return (peak, total, accum)


def body(tokens, token_mask, mask_embed, w_qkv, w_out, action_idx, codebook, act_proj, cotangent):
    clip_count, _, spot_count, width_local = tokens.shape
    heads_width = w_qkv.shape[2]
    head_count = heads_width // HS
    xin = jnp.where(token_mask[..., None] == 1, mask_embed, tokens)
    row_block = xin.reshape(clip_count * spot_count, width_local)
    features = gathered_by_axis(row_block, MP, 1)
    piece = lax.all_gather(w_qkv, "frame", axis=0, tiled=True)
    count = piece.shape[0]
    qkv = jnp.dot(
        features, piece.reshape(count, 3 * heads_width), preferred_element_type=jnp.float32
    ).astype(jnp.bfloat16)
    query = qkv[:, :heads_width].reshape(clip_count, spot_count, head_count, HS)
    own_keys = qkv[:, heads_width : 2 * heads_width].reshape(clip_count, 1, spot_count, heads_width)
    own_values = qkv[:, 2 * heads_width :].reshape(clip_count, 1, spot_count, heads_width)
    own_frame = lax.axis_index("frame")
    start_carry = (
        jnp.full((clip_count, spot_count, head_count), floor_score, jnp.float32),
        jnp.zeros((clip_count, spot_count, head_count), jnp.float32),
        jnp.zeros((clip_count, spot_count, head_count, HS), jnp.float32),
    )
    piece_keys, piece_values = in_one_piece((own_keys, own_values), "frame", 1, 0)
    count = piece_keys.shape[1]
    frame_ids = jnp.arange(count)
    stats = block_stats(
        query,
        piece_keys.reshape(clip_count, count, spot_count, head_count, HS),
        piece_values.reshape(clip_count, count, spot_count, head_count, HS),
        frame_ids <= own_frame,
    )
    peak, total, accum = merge_stats(start_carry, stats)
    attn = (
        (accum / total[..., None])
        .astype(jnp.bfloat16)
        .reshape(clip_count * spot_count, heads_width)
    )
    all_heads = gather_directly(attn, MP, 1)
    out_block = lax.all_to_all(w_out, MP, split_axis=1, concat_axis=0, tiled=True)
    mixed_rows = jnp.dot(all_heads, out_block, preferred_element_type=jnp.float32)
    mixed = mixed_rows.reshape(clip_count, 1, spot_count, width_local)
    onehot = (
        action_idx.reshape(clip_count)[:, None] == jnp.arange(codebook.shape[0])[None, :]
    ).astype(jnp.float32)
    codevec = jnp.dot(onehot, codebook, precision=lax.Precision.HIGHEST)
    gate = jnp.dot(codevec, act_proj, precision=lax.Precision.HIGHEST)
    next_state = (xin.astype(jnp.float32) + gate[:, None, None, :] * mixed).astype(jnp.bfloat16)
    dgate = jnp.sum(cotangent.astype(jnp.float32) * mixed, axis=2).reshape(clip_count, width_local)
    grad_terms = jnp.dot(codevec.T, dgate, precision=lax.Precision.HIGHEST)
    grad_proj = of_everyone(grad_terms, ("frame", "dp"))
    return (next_state, grad_proj)


def solution(mesh):
    split = Mesh(
        mesh.devices.reshape(mesh.shape["frame"], 4, 2, mesh.shape["dp"]),
        ("frame", "mp_0", "mp_1", "dp"),
    )
    return jax.shard_map(
        body,
        mesh=split,
        in_specs=(
            P("dp", "frame", None, MP),
            P("dp", "frame", None),
            P(MP),
            P("frame", None, MP),
            P(MP, None),
            P("dp", "frame"),
            P(),
            P(None, MP),
            P("dp", "frame", None, MP),
        ),
        out_specs=(P("dp", "frame", None, MP), P(None, MP)),
        check_vma=False,
    )
```

profile of v0, /device:TPU:1, one launch (start us, length us, event | category | flops | bytes accessed | tf_op | source)
XLA Modules:
  0.0 355.9 jit_solution(12527661570367683001)
XLA Ops:
  7.2 0.7 all-gather.6.cloned.1.call-update
  8.0 0.7 broadcast_compare_fusion
  8.7 1.1 broadcast_select_fusion
  9.8 12.6 %all_gather.12 = bf16[320,1280]{1,0:T(8,128)(2,1)} all-gather(bf16[320,640]{1,0:T(8,128)(2,1)S(1)} %bitcast.65), channel_id=1, replica_groups=mesh['frame'=16,'mp_0'=4,'mp_1'=2,'dp'=2] {'mp_1'}, dimensions={1}, use_global_device_ids=true | all-gather | bytes 1228800 | tf_op jit(solution)/shard_map/all_gather | solution.py:18
  22.4 63.6 %all-gather.6.cloned.1.call-done = bf16[5120,3,384]{2,0,1:T(8,128)(2,1)} async-done(((bf16[320,3,384]{2,0,1:T(8,128)(2,1)}), bf16[5120,3,384]{2,0,1:T(8,128)(2,1)}) %all-gather.6.cloned.1.call-update) | async-done | bytes 11796496 | tf_op jit(solution)/shard_map/all_gather | solution.py:83
  86.1 15.2 %copy.27 = bf16[5120,3,384]{0,2,1:T(8,128)(2,1)} copy(bf16[5120,3,384]{2,0,1:T(8,128)(2,1)} %all-gather.6.cloned.1.call-done) | data formatting | bytes 23592960 | tf_op jit(solution)/shard_map/all_gather | solution.py:83
  101.3 27.9 %all-gather.4.cloned.1.call-done = bf16[320,5120]{1,0:T(8,128)(2,1)} async-done(((bf16[320,1280]{1,0:T(8,128)(2,1)}), bf16[320,5120]{1,0:T(8,128)(2,1)}) %all-gather.4.cloned.1.call-update) | async-done | bytes 3276816 | tf_op jit(solution)/shard_map/all_gather | solution.py:18
  129.2 9.8 %convolution_convert_fusion = bf16[320,1152]{1,0:T(8,128)(2,1)S(1)} fusion(bf16[320,5120]{1,0:T(8,128)(2,1)} %all-gather.4.cloned.1.call-done, bf16[5120,1152]{0,1:T(8,128)(2,1)} %bitcast.64), kind=kOutput, calls=%fused_computation.6 | convolution fusion | flops 3775242240 | bytes 15810560 | tf_op jit(solution)/shard_map/dot_general | solution.py:85
  139.0 0.8 pad_maximum_fusion
  139.9 6.1 %copy.32 = bf16[384,5120]{0,1:T(8,128)(2,1)} copy(bf16[384,5120]{1,0:T(8,128)(2,1)} %param.13) | data formatting | bytes 7864320 | tf_op args[4]
  146.0 6.3 %copy.33 = bf16[384,8,640]{2,0,1:T(8,128)(2,1)} copy(bf16[384,8,640]{0,2,1:T(8,128)(2,1)} %bitcast.63) | data formatting | bytes 7864320 | tf_op jit(solution)/shard_map/all_to_all | solution.py:113
  152.3 5.4 %all-to-all-start.1 = ((bf16[384,8,640]{2,0,1:T(8,128)(2,1)}), bf16[384,8,640]{2,0,1:T(8,128)(2,1)}, u32[]{:S(2)}, u32[]{:S(2)}) async-start(bf16[384,8,640]{2,0,1:T(8,128)(2,1)} %copy.33), calls=%async_computation.1 | async-start | bytes 7864320 | tf_op jit(solution)/shard_map/all_to_all | solution.py:113
  157.8 36.3 %all-gather.8.cloned.1.call-done = bf16[4,16,160,384]{3,2,1,0:T(8,128)(2,1)} async-done(((bf16[4,1,160,384]{3,2,1,0:T(8,128)(2,1)}), bf16[4,16,160,384]{3,2,1,0:T(8,128)(2,1)}) %all-gather.8.cloned.1.call-update) | async-done | bytes 7864336 | tf_op jit(solution)/shard_map/all_gather | solution.py:28
  194.2 5.8 %fusion.19 = (bf16[2,16,160,384]{3,2,1,0:T(8,128)(2,1)}, bf16[2,16,160,384]{3,2,1,0:T(8,128)(2,1)}) fusion(bf16[4,16,160,384]{3,2,1,0:T(8,128)(2,1)} %all-gather.8.cloned.1.call-done), kind=kLoop, calls=%fused_computation.32 | loop fusion | bytes 15728640 | tf_op jit(solution)/shard_map/split | solution.py:28
  200.0 10.8 %reshape.85 = bf16[2,16,160,3,128]{4,3,2,1,0:T(4,128)(2,1)} reshape(bf16[2,16,160,384]{3,2,1,0:T(8,128)(2,1)} %get-tuple-element.2) | data formatting | bytes 7864320 | tf_op jit(solution)/shard_map/reshape | solution.py:103
  210.8 10.9 %reshape.84 = bf16[2,16,160,3,128]{4,3,2,1,0:T(4,128)(2,1)} reshape(bf16[2,16,160,384]{3,2,1,0:T(8,128)(2,1)} %get-tuple-element.3) | data formatting | bytes 7864320 | tf_op jit(solution)/shard_map/reshape | solution.py:102
  221.7 5.8 %fusion.4 = f32[2,160,3,1,16]{4,3,2,1,0:T(1,128)S(1)} fusion(bf16[2,160,3,128,1]{3,4,2,1,0:T(2,128)(2,1)S(1)} %reshape.94, bf16[2,16,160,3,128]{4,3,2,1,0:T(4,128)(2,1)} %reshape.84), kind=kOutput, calls=%fused_computation.4 | convolution fusion | flops 3932160 | bytes 4239360 | tf_op jit(solution)/shard_map/cphd,cnphd->cphn/dot_general | solution.py:53
  227.6 0.3 copy.38
  228.4 0.4 copy.39
  228.8 8.4 %fusion.2 = f32[2,160,3,1,128]{4,3,2,1,0:T(1,128)S(1)} fusion(f32[2,160,3,16,1]{3,4,2,1,0:T(1,128)S(1)} %copy.39, bf16[2,16,160,3,128]{4,3,2,1,0:T(4,128)(2,1)} %reshape.85), kind=kOutput, calls=%fused_computation.2 | convolution fusion | flops 23592960 | bytes 4485120 | tf_op jit(solution)/shard_map/cphn,cnphd->cphd/dot_general | solution.py:59
  237.2 0.9 fusion.8
  238.1 1.5 broadcast_in_dim.53
  239.6 6.4 %all-to-all-start = ((bf16[8,320,384]{2,1,0:T(8,128)(2,1)}), bf16[8,320,384]{2,1,0:T(8,128)(2,1)S(1)}, u32[]{:S(2)}, u32[]{:S(2)}) async-start(bf16[8,320,384]{2,1,0:T(8,128)(2,1)} %broadcast_in_dim.53), calls=%async_computation | async-start | bytes 3932160 | tf_op jit(solution)/shard_map/all_to_all | solution.py:39
  246.0 0.2 fusion.14
  246.2 0.2 fusion.21
  246.4 28.8 %all-to-all-done = bf16[8,320,384]{2,1,0:T(8,128)(2,1)S(1)} async-done(((bf16[8,320,384]{2,1,0:T(8,128)(2,1)}), bf16[8,320,384]{2,1,0:T(8,128)(2,1)S(1)}, u32[]{:S(2)}, u32[]{:S(2)}) %all-to-all-start) | async-done | bytes 1966112 | tf_op jit(solution)/shard_map/all_to_all | solution.py:39
  275.2 3.8 %fusion = f32[320,640,1]{1,0,2:T(8,128)S(1)} fusion(bf16[384,8,640]{2,0,1:T(8,128)(2,1)} %all-to-all-done.1, bf16[8,320,384]{2,1,0:T(8,128)(2,1)S(1)} %all-to-all-done), kind=kOutput, calls=%fused_computation | convolution fusion | flops 1258291200 | bytes 6717440 | tf_op jit(solution)/shard_map/dot_general | solution.py:114
  279.0 1.0 multiply_reduce_fusion
  280.0 0.3 fusion.22
  280.3 0.3 broadcast_in_dim.54
  280.6 68.0 %all_to_all.26 = f32[32,32,640]{2,1,0:T(8,128)S(1)} all-to-all(f32[32,32,640]{2,1,0:T(8,128)S(1)} %broadcast_in_dim.54), channel_id=1, replica_groups=mesh['frame'=16,'mp_0'=4,'mp_1'=2,'dp'=2] {'frame','dp'}, dimensions={0} | all-to-all | bytes 5242880 | tf_op jit(solution)/shard_map/all_to_all | solution.py:39
  348.6 0.8 reduce_sum.29
  (28 shorter events, 1.0 us)
Async XLA Ops:
  7.2 239.0 %copy-start = (f32[32,640]{1,0:T(8,128)S(1)}, f32[32,640]{1,0:T(8,128)}, u32[]{:S(2)}) copy-start(f32[32,640]{1,0:T(8,128)} %param.16) | copy-start | bytes 245764
  7.2 78.9 %all-gather.6.cloned.1.call-start = ((), (), s32[]{:S(2)}) async-start(), calls=%async_computation.4 | async-start | bytes 12533760 | tf_op jit(solution)/shard_map/all_gather | solution.py:83
  7.9 121.2 %all-gather.4.cloned.1.call-start = ((), (), s32[]{:S(2)}) async-start(), calls=%async_computation.3 | async-start | bytes 4096000 | tf_op jit(solution)/shard_map/all_gather | solution.py:18
  22.4 171.8 %all-gather.8.cloned.1.call-start = ((), (), s32[]{:S(2)}) async-start(), calls=%async_computation.5 | async-start | bytes 8355840 | tf_op jit(solution)/shard_map/all_gather | solution.py:28
  152.3 85.9 %all-to-all-start.1 = ((bf16[384,8,640]{2,0,1:T(8,128)(2,1)}), bf16[384,8,640]{2,0,1:T(8,128)(2,1)}, u32[]{:S(2)}, u32[]{:S(2)}) async-start(bf16[384,8,640]{2,0,1:T(8,128)(2,1)} %copy.33), calls=%async_computation.1 | async-start | bytes 7864320 | tf_op jit(solution)/shard_map/all_to_all | solution.py:113
  237.2 8.8 %copy-start.4 = (f32[8,32]{1,0:T(8,128)S(1)}, f32[8,32]{1,0:T(8,128)}, u32[]{:S(2)}) copy-start(f32[8,32]{1,0:T(8,128)} %param.15) | copy-start | bytes 3076
  237.2 8.8 %copy-start.5 = (s32[2,1]{0,1:T(1,128)S(1)}, s32[2,1]{0,1:T(1,128)}, u32[]{:S(2)}) copy-start(s32[2,1]{0,1:T(1,128)} %param.14) | copy-start | bytes 28
  239.6 35.6 %all-to-all-start = ((bf16[8,320,384]{2,1,0:T(8,128)(2,1)}), bf16[8,320,384]{2,1,0:T(8,128)(2,1)S(1)}, u32[]{:S(2)}, u32[]{:S(2)}) async-start(bf16[8,320,384]{2,1,0:T(8,128)(2,1)} %broadcast_in_dim.53), calls=%async_computation | async-start | bytes 3932160 | tf_op jit(solution)/shard_map/all_to_all | solution.py:39
  246.4 32.6 %copy-start.1 = (bf16[2,1,160,640]{3,2,1,0:T(8,128)(2,1)S(1)}, bf16[2,1,160,640]{3,2,1,0:T(8,128)(2,1)}, u32[]{:S(2)}) copy-start(bf16[2,1,160,640]{3,2,1,0:T(8,128)(2,1)} %param.9) | copy-start | bytes 1228804
  246.4 32.6 %copy-start.2 = (bf16[2,1,160,640]{3,2,1,0:T(8,128)(2,1)S(1)}, bf16[2,1,160,640]{3,2,1,0:T(8,128)(2,1)}, u32[]{:S(2)}) copy-start(bf16[2,1,160,640]{3,2,1,0:T(8,128)(2,1)} %param.17) | copy-start | bytes 1228804
  246.4 32.6 %copy-start.3 = (bf16[640]{0:T(1024)(128)(2,1)S(1)}, bf16[640]{0:T(1024)(128)(2,1)}, u32[]{:S(2)}) copy-start(bf16[640]{0:T(1024)(128)(2,1)} %param.11) | copy-start | bytes 3844
Sparse Core Ops, SparseCore 0:
  9.9 76.1 all-gather.5
  87.9 41.2 all-gather.3
  140.0 54.1 all-gather.7
where the time goes:
time: 357 us; the launch traced here: 356 us
  waiting for transfers between devices  157 us (44%)
  blocking collectives  80.6 us (23%)
  local copies, waits for them, and re-layouts  58.2 us (16%)
  matrix products  28.4 us (8%)
  between operations  14 us (4%)
  starting transfers between devices  12 us (3%)
  other arithmetic  5.52 us (2%)
    all_to_all x1, blocking collectives, from_everyone(): return lax.all_to_all(copies, axis, split_axis=0, concat_axis=0, tiled=True)  68 us
    all_gather x1, waiting for transfers between devices, body(): piece = lax.all_gather(w_qkv, 'frame', axis=0, tiled=True)  63.6 us
    all_gather x1, waiting for transfers between devices, in_one_piece(): lax.all_gather(both, axis, axis=dim, tiled=True)  36.3 us
    all_to_all x1, waiting for transfers between devices, from_everyone(): return lax.all_to_all(copies, axis, split_axis=0, concat_axis=0, tiled=True)  28.8 us
    all_gather x1, waiting for transfers between devices, gathered_by_axis(): x = lax.all_gather(x, axis, axis=dim, tiled=True)  27.9 us
    all_gather x1, local copies, waits for them, and re-layouts, body(): piece = lax.all_gather(w_qkv, 'frame', axis=0, tiled=True)  15.2 us
    all_gather x1, blocking collectives, gathered_by_axis(): x = lax.all_gather(x, axis, axis=dim, tiled=True)  12.6 us
    reshape x1, local copies, waits for them, and re-layouts, body(): piece_keys.reshape(clip_count, count, spot_count, head_count, HS)  10.9 us
  transfers between devices with their start and end apart: 5, of which 4 were waited for; matrix products, arithmetic and copies ran while one was open for 21% of the time, Pallas kernels for 0%

commit v1 on v0

v1 whole, which is shorter than its diff:
```python
import math

import jax
import jax.numpy as jnp
from jax import lax
from jax.experimental import pallas as pl
from jax.experimental.pallas import tpu as pltpu
from jax.sharding import PartitionSpec as P

HS = 128
MASKED = -1e30


def exchange(x, axis):
    return lax.all_to_all(x, axis, split_axis=0, concat_axis=0, tiled=True)


def from_everyone(x, axis):
    return exchange(jnp.broadcast_to(x, (lax.axis_size(axis), *x.shape)), axis)


def attend(q, k, v, bias):
    s = lax.dot_general(q, k, (((1,), (1,)), ((), ())), preferred_element_type=jnp.float32)
    s = s * (1.0 / math.sqrt(HS)) + bias
    peak = jnp.max(s, axis=1, keepdims=True)
    w = jnp.exp(s - peak)
    total = jnp.sum(w, axis=1, keepdims=True)
    high = w.astype(jnp.bfloat16)
    low = (w - high.astype(jnp.float32)).astype(jnp.bfloat16)
    accum = jnp.dot(high, v, preferred_element_type=jnp.float32)
    accum += jnp.dot(low, v, preferred_element_type=jnp.float32)
    return (accum / total).astype(jnp.bfloat16)


def qkv_attention_kernel(x_ref, w_ref, bias_ref, out_ref, acc):
    step = pl.program_id(0)
    x = x_ref[0]
    for i in range(3):
        part = jnp.dot(x, w_ref[i], preferred_element_type=jnp.float32)

        @pl.when(step == 0)
        def _():
            acc[i] = part

        @pl.when(step > 0)
        def _():
            acc[i] += part

    @pl.when(step == pl.num_programs(0) - 1)
    def _():
        frames, spots, width = out_ref.shape
        bias = bias_ref[...]
        for h in range(width // HS):
            cols = slice(h * HS, (h + 1) * HS)
            q, k, v = (acc[i, :, cols].astype(jnp.bfloat16) for i in range(3))
            o = attend(q, k, v, bias)
            for t in range(frames):
                out_ref[t, :, cols] = o[t * spots : (t + 1) * spots]


def qkv_attention(x, w, frames):
    mp, rows, width = x.shape
    heads = w.shape[2]
    spots = rows // frames
    r = jnp.arange(rows)
    seen = (r[:, None] % spots == r[None, :] % spots) & (r[:, None] >= r[None, :])
    bias = jnp.where(seen, 0.0, MASKED).astype(jnp.float32)
    return pl.pallas_call(
        qkv_attention_kernel,
        grid=(mp,),
        in_specs=[
            pl.BlockSpec((1, rows, width), lambda m: (m, 0, 0)),
            pl.BlockSpec((3, width, heads), lambda m: (0, m, 0)),
            pl.BlockSpec((rows, rows), lambda m: (0, 0)),
        ],
        out_specs=pl.BlockSpec((frames, spots, heads), lambda m: (0, 0, 0)),
        out_shape=jax.ShapeDtypeStruct((frames, spots, heads), jnp.bfloat16),
        scratch_shapes=[pltpu.VMEM((3, rows, heads), jnp.float32)],
        compiler_params=pltpu.CompilerParams(vmem_limit_bytes=40 * 1024 * 1024),
    )(x, w, bias)


def body(tokens, token_mask, mask_embed, w_qkv, w_out, action_idx, codebook, act_proj, cotangent):
    clips, _, spots, width = tokens.shape
    rows = clips * spots
    frames = lax.axis_size("frame")
    mp = lax.axis_size("mp")
    heads = w_qkv.shape[2]
    weights = lax.all_gather(w_qkv, "frame", axis=0, tiled=True).transpose(1, 0, 2)
    xin = jnp.where(token_mask[..., None] == 1, mask_embed, tokens)
    mine = exchange(xin.reshape(frames, rows // frames, width), "frame").reshape(rows, width)
    features = from_everyone(mine, "mp")
    w_out, features = lax.optimization_barrier((w_out, features))
    out_block = lax.all_to_all(
        w_out.reshape(heads, mp, width).transpose(1, 0, 2), "mp", split_axis=0, concat_axis=0, tiled=True
    )
    attn = qkv_attention(features, weights, frames)
    attn = exchange(attn, "frame").reshape(rows, heads)
    all_heads = from_everyone(attn, "mp")
    mixed = lax.dot_general(
        all_heads, out_block, (((0, 2), (0, 1)), ((), ())), preferred_element_type=jnp.float32
    ).reshape(clips, spots, width)
    onehot = (action_idx.reshape(clips)[:, None] == jnp.arange(codebook.shape[0])[None, :]).astype(
        jnp.float32
    )
    codevec = jnp.dot(onehot, codebook, precision=lax.Precision.HIGHEST)
    gate = jnp.dot(codevec, act_proj, precision=lax.Precision.HIGHEST)
    xin = xin.reshape(clips, spots, width)
    next_state = (xin.astype(jnp.float32) + gate[:, None, :] * mixed).astype(jnp.bfloat16)
    dgate = jnp.sum(cotangent.reshape(clips, spots, width).astype(jnp.float32) * mixed, axis=1)
    terms = from_everyone(jnp.concatenate([dgate, codevec], axis=1), ("frame", "dp"))
    terms = terms.reshape(-1, terms.shape[-1])
    grad_proj = lax.dot_general(
        terms[:, width:],
        terms[:, :width],
        (((0,), (0,)), ((), ())),
        precision=lax.Precision.HIGHEST,
        preferred_element_type=jnp.float32,
    )
    return (next_state.reshape(tokens.shape), grad_proj)


def solution(mesh):
    return jax.shard_map(
        body,
        mesh=mesh,
        in_specs=(
            P("dp", "frame", None, "mp"),
            P("dp", "frame", None),
            P("mp"),
            P("frame", None, "mp"),
            P("mp", None),
            P("dp", "frame"),
            P(),
            P(None, "mp"),
            P("dp", "frame", None, "mp"),
        ),
        out_specs=(P("dp", "frame", None, "mp"), P(None, "mp")),
        check_vma=False,
    )
```

time: 357 us -> 255 us (0.71)
  blocking collectives: 80.6 us -> 28.7 us
  local copies, waits for them, and re-layouts: 58.2 us -> 18.9 us
  matrix products: 28.4 us -> 5.09 us
  starting transfers between devices: 12 us -> 30.8 us
  waiting for transfers between devices: 157 us -> 139 us
  Pallas kernels: 0 us -> 14.1 us
    all_gather x3 -> x1, waiting for transfers between devices: 128 us -> 0.01 us  [body(): lax.all_gather(w_qkv, 'frame', axis=0, tiled=True).transpose(1, 0, 2)]
    all_to_all x2 -> x5, waiting for transfers between devices: 28.8 us -> 138 us  [the longest x4 82.3 us: exchange(): return lax.all_to_all(x, axis, split_axis=0, concat_axis=0, tiled=True)]
    all_to_all x1, blocking collectives: 68 us -> 28.7 us  [exchange(): return lax.all_to_all(x, axis, split_axis=0, concat_axis=0, tiled=True)]
    dot_general x5 -> x2, matrix products: 28 us -> 4.75 us  [the longest x1 3.84 us: body(): lax.dot_general(all_heads, out_block, (((0, 2), (0, 1)), ((), ())), prefe...]
    all_to_all x2 -> x5, starting transfers between devices: 11.8 us -> 30.8 us  [the longest x4 25.5 us: exchange(): return lax.all_to_all(x, axis, split_axis=0, concat_axis=0, tiled=True)]
    all_gather x1 -> x0, local copies, waits for them, and re-layouts: 15.2 us -> none  [body(): piece = lax.all_gather(w_qkv, 'frame', axis=0, tiled=True)]
    reshape x3 -> x5, local copies, waits for them, and re-layouts: 21.9 us -> 6.67 us  [the longest x1 6.31 us: body(): w_out.reshape(heads, mp, width).transpose(1, 0, 2)]
    pallas_call x0 -> x1, Pallas kernels: none -> 14.1 us  [qkv_attention(): pl.pallas_call(qkv_attention_kernel, grid=(mp,), in_specs=[pl.BlockSpec((...]
  transfers between devices with their start and end apart: 5 -> 6, of which waited for: 4 -> 4; matrix products, arithmetic and copies ran while one was open for 21% -> 7% of each run, Pallas kernels for 0% -> 0%
where the time goes in v1:
time: 255 us; the launch traced here: 254 us
  waiting for transfers between devices  139 us (55%)
  starting transfers between devices  30.8 us (12%)
  blocking collectives  28.7 us (11%)
  local copies, waits for them, and re-layouts  18.9 us (7%)
  between operations  14.2 us (6%)
  Pallas kernels  14.1 us (6%)
  matrix products  5.09 us (2%)
  other arithmetic  3.79 us (1%)
    all_to_all x4, waiting for transfers between devices, exchange(): return lax.all_to_all(x, axis, split_axis=0, concat_axis=0, tiled=True)  82.3 us
    all_to_all x1, waiting for transfers between devices, body(): lax.all_to_all(w_out.reshape(heads, mp, width).transpose(1, 0, 2), 'mp',...  55.8 us
    all_to_all x1, blocking collectives, exchange(): return lax.all_to_all(x, axis, split_axis=0, concat_axis=0, tiled=True)  28.7 us
    all_to_all x4, starting transfers between devices, exchange(): return lax.all_to_all(x, axis, split_axis=0, concat_axis=0, tiled=True)  25.5 us
    pallas_call x1, Pallas kernels, qkv_attention(): pl.pallas_call(qkv_attention_kernel, grid=(mp,), in_specs=[pl.BlockSpec((...  14.1 us
    reshape x1, local copies, waits for them, and re-layouts, body(): w_out.reshape(heads, mp, width).transpose(1, 0, 2)  6.31 us
    optimization_barrier x1, local copies, waits for them, and re-layouts, body(): w_out, features = lax.optimization_barrier((w_out, features))  6.28 us
    all_to_all x1, starting transfers between devices, body(): lax.all_to_all(w_out.reshape(heads, mp, width).transpose(1, 0, 2), 'mp',...  5.27 us
  transfers between devices with their start and end apart: 6, of which 4 were waited for; matrix products, arithmetic and copies ran while one was open for 7% of the time, Pallas kernels for 0%

profile of v1, /device:TPU:1, one launch (start us, length us, event | category | flops | bytes accessed | tf_op | source)
XLA Modules:
  0.0 254.3 jit_solution(5409109433611140821)
XLA Ops:
  7.2 0.7 all-gather.2.cloned.1.call-update
  7.9 0.7 broadcast_compare_fusion
  8.6 1.1 broadcast_select_fusion
  9.7 0.1 reshape.81
  9.8 28.7 %all_to_all.30 = bf16[16,20,640]{2,1,0:T(8,128)(2,1)S(1)} all-to-all(bf16[16,20,640]{2,1,0:T(8,128)(2,1)S(1)} %reshape.81), channel_id=1, replica_groups=mesh['frame'=16,'mp'=8,'dp'=2] {'frame'}, dimensions={0} | all-to-all | bytes 819200 | tf_op jit(solution)/shard_map/all_to_all | solution.py:15
  38.5 0.1 reshape.82
  38.6 2.0 broadcast_in_dim.38
  40.6 6.8 %all-to-all-start.1 = ((bf16[8,320,640]{2,1,0:T(8,128)(2,1)}), bf16[8,320,640]{2,1,0:T(8,128)(2,1)S(1)}, u32[]{:S(2)}, u32[]{:S(2)}) async-start(bf16[8,320,640]{2,1,0:T(8,128)(2,1)} %broadcast_in_dim.38), calls=%async_computation.1 | async-start | bytes 6553600 | tf_op jit(solution)/shard_map/all_to_all | solution.py:15
  47.4 0.9 fusion.2.bias_ref
  48.3 45.5 %all-to-all-done.1.x_ref = bf16[8,320,640]{2,1,0:T(8,128)(2,1)S(1)} async-done(((bf16[8,320,640]{2,1,0:T(8,128)(2,1)}), bf16[8,320,640]{2,1,0:T(8,128)(2,1)S(1)}, u32[]{:S(2)}, u32[]{:S(2)}) %all-to-all-start.1) | async-done | bytes 3276832 | tf_op jit(solution)/shard_map/all_to_all | solution.py:15
  93.8 1.0 copy-done.1
  94.8 14.1 %shard_map.104 = bf16[16,20,384]{2,1,0:T(8,128)(2,1)S(1)} custom-call(bf16[8,320,640]{2,1,0:T(8,128)(2,1)S(1)} %all-to-all-done.1.x_ref, bf16[3,5120,384]{2,1,0:T(8,128)(2,1)} %bitcast.26, f32[320,320]{1,0:T(8,128)S(1)} %copy-done.1), custom_call_target="tpu_custom_call" | custom-call | tf_op jit(solution)/shard_map/pallas_call | solution.py:68
  108.9 0.7 copy-done.2
  109.6 5.1 %all-to-all-start.2 = ((bf16[16,20,384]{2,1,0:T(8,128)(2,1)}), bf16[16,20,384]{2,1,0:T(8,128)(2,1)S(1)}, u32[]{:S(2)}, u32[]{:S(2)}) async-start(bf16[16,20,384]{2,1,0:T(8,128)(2,1)} %copy-done.2), calls=%async_computation.2 | async-start | bytes 589824 | tf_op jit(solution)/shard_map/all_to_all | solution.py:15
  114.7 6.3 %copy.12 = bf16[384,5120]{0,1:T(8,128)(2,1)} copy(bf16[384,5120]{1,0:T(8,128)(2,1)} %param.13) | data formatting | bytes 7864320 | tf_op jit(solution)/shard_map/optimization_barrier | solution.py:93
  121.0 6.3 %copy.13 = bf16[384,8,640]{2,0,1:T(8,128)(2,1)} copy(bf16[384,8,640]{0,2,1:T(8,128)(2,1)} %bitcast.25) | data formatting | bytes 7864320 | tf_op jit(solution)/shard_map/reshape | solution.py:95
  127.3 5.3 %all-to-all-start.4 = ((bf16[8,384,640]{2,1,0:T(8,128)(2,1)}), bf16[8,384,640]{2,1,0:T(8,128)(2,1)}, u32[]{:S(2)}, u32[]{:S(2)}) async-start(bf16[8,384,640]{2,1,0:T(8,128)(2,1)} %bitcast.24), calls=%async_computation.4 | async-start | bytes 7864320 | tf_op jit(solution)/shard_map/all_to_all | solution.py:94
  132.6 0.1 reshape.83
  132.7 55.8 %all-to-all-done.4 = bf16[8,384,640]{2,1,0:T(8,128)(2,1)} async-done(((bf16[8,384,640]{2,1,0:T(8,128)(2,1)}), bf16[8,384,640]{2,1,0:T(8,128)(2,1)}, u32[]{:S(2)}, u32[]{:S(2)}) %all-to-all-start.4) | async-done | bytes 3932192 | tf_op jit(solution)/shard_map/all_to_all | solution.py:94
  188.4 1.5 broadcast_in_dim.41
  189.9 5.1 %all-to-all-start.3 = ((bf16[8,320,384]{2,1,0:T(8,128)(2,1)}), bf16[8,320,384]{2,1,0:T(8,128)(2,1)S(1)}, u32[]{:S(2)}, u32[]{:S(2)}) async-start(bf16[8,320,384]{2,1,0:T(8,128)(2,1)} %broadcast_in_dim.41), calls=%async_computation.3 | async-start | bytes 3932160 | tf_op jit(solution)/shard_map/all_to_all | solution.py:15
  195.0 0.2 fusion.9
  195.2 27.7 %all-to-all-done.3 = bf16[8,320,384]{2,1,0:T(8,128)(2,1)S(1)} async-done(((bf16[8,320,384]{2,1,0:T(8,128)(2,1)}), bf16[8,320,384]{2,1,0:T(8,128)(2,1)S(1)}, u32[]{:S(2)}, u32[]{:S(2)}) %all-to-all-start.3) | async-done | bytes 1966112 | tf_op jit(solution)/shard_map/all_to_all | solution.py:15
  223.0 3.8 %fusion.14 = f32[320,640,1]{1,0,2:T(8,128)S(1)} fusion(bf16[8,320,384]{2,1,0:T(8,128)(2,1)S(1)} %all-to-all-done.3, bf16[8,384,640]{2,1,0:T(8,128)(2,1)} %all-to-all-done.4), kind=kOutput, calls=%fused_computation.23 | convolution fusion | flops 1258291200 | bytes 6717440 | tf_op jit(solution)/shard_map/dot_general | solution.py:100
  226.8 0.1 fusion
  226.9 0.7 broadcast_in_dim.42
  227.7 8.5 %all-to-all-start.5 = ((f32[32,2,672]{2,1,0:T(2,128)}), f32[32,2,672]{2,1,0:T(2,128)S(1)}, u32[]{:S(2)}, u32[]{:S(2)}) async-start(f32[32,2,672]{2,1,0:T(2,128)} %broadcast_in_dim.42), calls=%async_computation.5 | async-start | bytes 393216 | tf_op jit(solution)/shard_map/all_to_all | solution.py:15
  236.2 0.2 fusion.13
  236.4 0.9 add_convert_fusion
  237.3 9.1 %all-to-all-done.5 = f32[32,2,672]{2,1,0:T(2,128)S(1)} async-done(((f32[32,2,672]{2,1,0:T(2,128)}), f32[32,2,672]{2,1,0:T(2,128)S(1)}, u32[]{:S(2)}, u32[]{:S(2)}) %all-to-all-start.5) | async-done | bytes 172064 | tf_op jit(solution)/shard_map/all_to_all | solution.py:15
  246.4 0.1 reshape.87
  246.6 0.9 fusion.3
  (20 shorter events, 0.1 us)
Async XLA Ops:
  7.2 229.0 %copy-start = (f32[32,640]{1,0:T(8,128)S(1)}, f32[32,640]{1,0:T(8,128)}, u32[]{:S(2)}) copy-start(f32[32,640]{1,0:T(8,128)} %param.16) | copy-start | bytes 245764
  7.2 86.6 %all-gather.2.cloned.1.call-start = ((), (), s32[]{:S(2)}) async-start(), calls=%async_computation.6 | async-start | bytes 12533760 | tf_op jit(solution)/shard_map/all_gather | solution.py:89
  40.6 53.1 %all-to-all-start.1 = ((bf16[8,320,640]{2,1,0:T(8,128)(2,1)}), bf16[8,320,640]{2,1,0:T(8,128)(2,1)S(1)}, u32[]{:S(2)}, u32[]{:S(2)}) async-start(bf16[8,320,640]{2,1,0:T(8,128)(2,1)} %broadcast_in_dim.38), calls=%async_computation.1 | async-start | bytes 6553600 | tf_op jit(solution)/shard_map/all_to_all | solution.py:15
  93.8 1.0 copy-start.1
  108.9 0.7 copy-start.2
  109.6 17.7 %all-to-all-start.2 = ((bf16[16,20,384]{2,1,0:T(8,128)(2,1)}), bf16[16,20,384]{2,1,0:T(8,128)(2,1)S(1)}, u32[]{:S(2)}, u32[]{:S(2)}) async-start(bf16[16,20,384]{2,1,0:T(8,128)(2,1)} %copy-done.2), calls=%async_computation.2 | async-start | bytes 589824 | tf_op jit(solution)/shard_map/all_to_all | solution.py:15
  127.3 61.1 %all-to-all-start.4 = ((bf16[8,384,640]{2,1,0:T(8,128)(2,1)}), bf16[8,384,640]{2,1,0:T(8,128)(2,1)}, u32[]{:S(2)}, u32[]{:S(2)}) async-start(bf16[8,384,640]{2,1,0:T(8,128)(2,1)} %bitcast.24), calls=%async_computation.4 | async-start | bytes 7864320 | tf_op jit(solution)/shard_map/all_to_all | solution.py:94
  132.6 62.4 %copy-start.6 = (f32[8,32]{1,0:T(8,128)S(1)}, f32[8,32]{1,0:T(8,128)}, u32[]{:S(2)}) copy-start(f32[8,32]{1,0:T(8,128)} %param.15) | copy-start | bytes 3076
  132.6 62.4 %copy-start.7 = (s32[2,1]{0,1:T(1,128)S(1)}, s32[2,1]{0,1:T(1,128)}, u32[]{:S(2)}) copy-start(s32[2,1]{0,1:T(1,128)} %param.14) | copy-start | bytes 28
  189.9 33.0 %all-to-all-start.3 = ((bf16[8,320,384]{2,1,0:T(8,128)(2,1)}), bf16[8,320,384]{2,1,0:T(8,128)(2,1)S(1)}, u32[]{:S(2)}, u32[]{:S(2)}) async-start(bf16[8,320,384]{2,1,0:T(8,128)(2,1)} %broadcast_in_dim.41), calls=%async_computation.3 | async-start | bytes 3932160 | tf_op jit(solution)/shard_map/all_to_all | solution.py:15
  195.2 41.2 %copy-start.3 = (bf16[2,1,160,640]{3,2,1,0:T(8,128)(2,1)S(1)}, bf16[2,1,160,640]{3,2,1,0:T(8,128)(2,1)}, u32[]{:S(2)}) copy-start(bf16[2,1,160,640]{3,2,1,0:T(8,128)(2,1)} %param.9) | copy-start | bytes 1228804
  195.2 41.2 %copy-start.5 = (bf16[640]{0:T(1024)(128)(2,1)S(1)}, bf16[640]{0:T(1024)(128)(2,1)}, u32[]{:S(2)}) copy-start(bf16[640]{0:T(1024)(128)(2,1)} %param.11) | copy-start | bytes 3844
  223.0 3.9 %copy-start.4 = (bf16[2,1,160,640]{3,2,1,0:T(8,128)(2,1)S(1)}, bf16[2,1,160,640]{3,2,1,0:T(8,128)(2,1)}, u32[]{:S(2)}) copy-start(bf16[2,1,160,640]{3,2,1,0:T(8,128)(2,1)} %param.17) | copy-start | bytes 1228804
  227.7 18.8 %all-to-all-start.5 = ((f32[32,2,672]{2,1,0:T(2,128)}), f32[32,2,672]{2,1,0:T(2,128)S(1)}, u32[]{:S(2)}, u32[]{:S(2)}) async-start(f32[32,2,672]{2,1,0:T(2,128)} %broadcast_in_dim.42), calls=%async_computation.5 | async-start | bytes 393216 | tf_op jit(solution)/shard_map/all_to_all | solution.py:15
Sparse Core Ops, SparseCore 0:
  9.9 81.5 all-gather.1

commit v2 on v1

v2 whole, which is shorter than its diff:
```python
import math

import jax
import jax.numpy as jnp
from jax import lax
from jax.experimental import pallas as pl
from jax.experimental.pallas import tpu as pltpu
from jax.sharding import Mesh
from jax.sharding import PartitionSpec as P

HS = 128
MASKED = -1e30
FRAME = ("z", "core")
MP = ("x", "yhi")
VMEM = pltpu.CompilerParams(vmem_limit_bytes=50 * 1024 * 1024)


def exchange(x, axis):
    return lax.all_to_all(x, axis, split_axis=0, concat_axis=0, tiled=True)


def from_everyone(x, axis):
    return exchange(jnp.broadcast_to(x, (lax.axis_size(axis), *x.shape)), axis)


def shift(x, axis, by):
    n = lax.axis_size(axis)
    return lax.ppermute(x, axis, [(i, (i + by) % n) for i in range(n)])


def accumulate_kernel(counts, first, last, slots, core, x_ref, *refs):
    n = sum(counts)
    w_refs, rest = refs[:n], refs[n:]
    acc_in = None if first else rest[0]
    rest = rest if first else rest[1:]
    parts = [[None if first else acc_in[s, i] for i in range(3)] for s in range(2)]
    at = 0
    for j, count in enumerate(counts):
        x = x_ref[slots[j]]
        half = x.shape[1] // 2
        xs = (x[:, :half], x[:, half:])
        for i in range(3):
            pieces = [w_refs[at + c][i] for c in range(count)]
            w = pieces[0] if count == 1 else jnp.concatenate(pieces, axis=0)
            for s in range(2):
                d = jnp.dot(xs[s], w, preferred_element_type=jnp.float32)
                parts[s][i] = d if parts[s][i] is None else parts[s][i] + d
        at += count
    for i in range(3):
        if last:
            mine = core[0] == 0
            rest[0][i] = jnp.where(mine, parts[0][i], parts[1][i])
            rest[1][i] = jnp.where(mine, parts[1][i], parts[0][i]).astype(jnp.bfloat16)
        else:
            for s in range(2):
                rest[0][s, i] = parts[s][i]


def accumulate(x, shards, slots, core, acc=None, last=False):
    counts = [len(s) for s in shards]
    flat = [w for s in shards for w in s]
    rows, heads = x.shape[1], flat[0].shape[2]
    if last:
        out_shape = (
            jax.ShapeDtypeStruct((3, rows, heads), jnp.float32),
            jax.ShapeDtypeStruct((3, rows, heads), jnp.bfloat16),
        )
    else:
        out_shape = jax.ShapeDtypeStruct((2, 3, rows, heads), jnp.float32)

    def kernel(*refs):
        accumulate_kernel(counts, acc is None, last, *refs)

    smem = pl.BlockSpec(memory_space=pltpu.SMEM)
    vmem = pl.BlockSpec(memory_space=pltpu.VMEM)
    operands = [x, *flat] + ([] if acc is None else [acc])
    return pl.pallas_call(
        kernel,
        in_specs=[smem, smem] + [vmem] * len(operands),
        out_specs=(vmem, vmem) if last else vmem,
        out_shape=out_shape,
        compiler_params=VMEM,
    )(slots, core, *operands)


def attend(q, k, v, bias):
    s = lax.dot_general(q, k, (((1,), (1,)), ((), ())), preferred_element_type=jnp.float32)
    s = s * (1.0 / math.sqrt(HS)) + bias
    peak = jnp.max(s, axis=1, keepdims=True)
    w = jnp.exp(s - peak)
    total = jnp.sum(w, axis=1, keepdims=True)
    high = w.astype(jnp.bfloat16)
    low = (w - high.astype(jnp.float32)).astype(jnp.bfloat16)
    accum = jnp.dot(high, v, preferred_element_type=jnp.float32)
    accum += jnp.dot(low, v, preferred_element_type=jnp.float32)
    return (accum / total).astype(jnp.bfloat16)


def attention_kernel(own_ref, other_ref, bias_ref, out_ref):
    frames, spots, width = out_ref.shape
    bias = bias_ref[...]
    for h in range(width // HS):
        cols = slice(h * HS, (h + 1) * HS)
        q, k, v = (
            (own_ref[i, :, cols] + other_ref[i, :, cols].astype(jnp.float32)).astype(jnp.bfloat16)
            for i in range(3)
        )
        o = attend(q, k, v, bias)
        for t in range(frames):
            out_ref[t, :, cols] = o[t * spots : (t + 1) * spots]


def attention(own, other, frames):
    _, rows, heads = own.shape
    spots = rows // frames
    r = jnp.arange(rows)
    seen = (r[:, None] % spots == r[None, :] % spots) & (r[:, None] >= r[None, :])
    bias = jnp.where(seen, 0.0, MASKED).astype(jnp.float32)
    return pl.pallas_call(
        attention_kernel,
        out_shape=jax.ShapeDtypeStruct((frames, spots, heads), jnp.bfloat16),
        compiler_params=VMEM,
    )(own, other, bias)


def blocks_kernel(core, w_ref, out_ref):
    out_ref[0] = w_ref[...]


def column_blocks(w, core, width):
    heads, full = w.shape
    half, n = heads // 2, full // width
    return pl.pallas_call(
        blocks_kernel,
        grid_spec=pltpu.PrefetchScalarGridSpec(
            num_scalar_prefetch=1,
            grid=(n,),
            in_specs=[pl.BlockSpec((half, width), lambda m, core: (core[0], m))],
            out_specs=pl.BlockSpec((1, half, width), lambda m, core: (m, 0, 0)),
        ),
        out_shape=jax.ShapeDtypeStruct((n, half, width), w.dtype),
        compiler_params=VMEM,
    )(core, w)


def gather_features(mine):
    both = jnp.stack([mine, shift(mine, "yhi", 1)])
    half = mine.shape[0] // 2
    left, right = shift(both, "x", 1), shift(both, "x", -1)
    far = jnp.concatenate([shift(left[:, :half], "x", 1), shift(right[:, half:], "x", -1)], axis=1)
    return jnp.concatenate([both, right, far, left])


def body(tokens, token_mask, mask_embed, w_qkv, w_out, action_idx, codebook, act_proj, cotangent):
    clips, _, spots, width = tokens.shape
    rows = clips * spots
    zs, cores = lax.axis_size("z"), lax.axis_size("core")
    frames, mp = zs * cores, lax.axis_size(MP)
    depth, heads = w_qkv.shape[0], w_qkv.shape[2]
    z, core = lax.axis_index("z"), lax.axis_index("core")
    core1 = core.reshape(1).astype(jnp.int32)
    xin = jnp.where(token_mask[..., None] == 1, mask_embed, tokens).reshape(rows, width)
    mine = xin.reshape(zs, 2, rows // frames, cores, depth).transpose(0, 3, 2, 1, 4)
    mine = exchange(mine.reshape(frames, rows // frames, 2 * depth), FRAME).reshape(rows, 2 * depth)

    own = w_qkv.transpose(1, 0, 2)
    up1, down1 = shift(own, "z", 1), shift(own, "z", -1)
    features = gather_features(mine)
    up2, down2 = shift(up1, "z", 1), shift(down1, "z", -1)
    up3, down3 = shift(up2, "z", 1), shift(down2, "z", -1)
    up4 = shift(up3[:, : depth // 2], "z", 1)
    down4 = shift(down3[:, depth // 2 :], "z", -1)

    w_out, features = lax.optimization_barrier((w_out, features))
    half = exchange(column_blocks(w_out, core1, width), MP)
    other_half = shift(half, "core", 1)
    out_block = jnp.concatenate(
        [jnp.where(core == 0, half, other_half), jnp.where(core == 0, other_half, half)], axis=1
    )

    x, yhi = lax.axis_index("x"), lax.axis_index("yhi")

    def slots(*shifts):
        shard = (z + jnp.array(shifts, jnp.int32)) % zs
        return (2 * ((shard // 2 - x) % (mp // 2)) + (shard % 2) ^ yhi).astype(jnp.int32)

    acc = accumulate(
        features, [(own,), (up1,), (down1,), (up2,), (down2,)], slots(0, -1, 1, -2, 2), core1
    )
    acc = accumulate(features, [(up3,), (down3,)], slots(-3, 3), core1, acc)
    kept, sent = accumulate(features, [(up4, down4)], slots(-4), core1, acc, last=True)
    attn = attention(kept, shift(sent, "core", 1), frames)
    attn = exchange(attn, FRAME).reshape(rows, heads)
    all_heads = from_everyone(attn, MP)
    mixed = lax.dot_general(
        all_heads, out_block, (((0, 2), (0, 1)), ((), ())), preferred_element_type=jnp.float32
    ).reshape(clips, spots, width)
    onehot = (action_idx.reshape(clips)[:, None] == jnp.arange(codebook.shape[0])[None, :]).astype(
        jnp.float32
    )
    codevec = jnp.dot(onehot, codebook, precision=lax.Precision.HIGHEST)
    gate = jnp.dot(codevec, act_proj, precision=lax.Precision.HIGHEST)
    xin = xin.reshape(clips, spots, width)
    next_state = (xin.astype(jnp.float32) + gate[:, None, :] * mixed).astype(jnp.bfloat16)
    dgate = jnp.sum(cotangent.reshape(clips, spots, width).astype(jnp.float32) * mixed, axis=1)
    terms = from_everyone(jnp.concatenate([dgate, codevec], axis=1), FRAME + ("dp",))
    terms = terms.reshape(-1, terms.shape[-1])
    grad_proj = lax.dot_general(
        terms[:, width:],
        terms[:, :width],
        (((0,), (0,)), ((), ())),
        precision=lax.Precision.HIGHEST,
        preferred_element_type=jnp.float32,
    )
    return (next_state.reshape(tokens.shape), grad_proj)


def solution(mesh):
    split = Mesh(
        mesh.devices.reshape(mesh.shape["frame"] // 2, 2, mesh.shape["mp"] // 2, 2, mesh.shape["dp"]),
        ("z", "core", "x", "yhi", "dp"),
    )
    return jax.shard_map(
        body,
        mesh=split,
        in_specs=(
            P("dp", FRAME, None, MP),
            P("dp", FRAME, None),
            P(MP),
            P(FRAME, None, MP),
            P(MP, None),
            P("dp", FRAME),
            P(),
            P(None, MP),
            P("dp", FRAME, None, MP),
        ),
        out_specs=(P("dp", FRAME, None, MP), P(None, MP)),
        check_vma=False,
    )
```

time: 255 us -> 216 us (0.85)
  waiting for transfers between devices: 139 us -> 79.3 us
  blocking collectives: 28.7 us -> 43.4 us
  between operations: 14.2 us -> 0.93 us
  Pallas kernels: 14.1 us -> 26 us
  starting transfers between devices: 30.8 us -> 40.4 us
  local copies, waits for them, and re-layouts: 18.9 us -> 11.7 us
  other arithmetic: 3.79 us -> 8.63 us
    all_to_all x1 -> x0, waiting for transfers between devices: 55.8 us -> none  [body(): lax.all_to_all(w_out.reshape(heads, mp, width).transpose(1, 0, 2), 'mp',...]
    all_to_all x4 -> x3, waiting for transfers between devices: 82.3 us -> 34.5 us  [exchange(): return lax.all_to_all(x, axis, split_axis=0, concat_axis=0, tiled=True)]
    ppermute x0 -> x15, waiting for transfers between devices: none -> 44.8 us  [shift(): return lax.ppermute(x, axis, [(i, (i + by) % n) for i in range(n)])]
    ppermute x0 -> x15, starting transfers between devices: none -> 22.1 us  [shift(): return lax.ppermute(x, axis, [(i, (i + by) % n) for i in range(n)])]
    all_to_all x1 -> x2, blocking collectives: 28.7 us -> 43.4 us  [exchange(): return lax.all_to_all(x, axis, split_axis=0, concat_axis=0, tiled=True)]
    pallas_call x1 -> x5, Pallas kernels: 14.1 us -> 26 us  [the longest x3 19 us: accumulate(): pl.pallas_call(kernel, in_specs=[smem, smem] + [vmem] * len(operands), ou...]
    all_to_all x4 -> x3, starting transfers between devices: 25.5 us -> 18.3 us  [exchange(): return lax.all_to_all(x, axis, split_axis=0, concat_axis=0, tiled=True)]
    optimization_barrier x1 -> x0, local copies, waits for them, and re-layouts: 6.28 us -> none  [body(): w_out, features = lax.optimization_barrier((w_out, features))]
  transfers between devices with their start and end apart: 6 -> 18, of which waited for: 4 -> 7; matrix products, arithmetic and copies ran while one was open for 7% -> 6% of each run, Pallas kernels for 0% -> 12%
where the time goes in v2:
time: 216 us
  waiting for transfers between devices  79.3 us (37%)
  blocking collectives  43.4 us (20%)
  starting transfers between devices  40.4 us (19%)
  Pallas kernels  26 us (12%)
  local copies, waits for them, and re-layouts  11.7 us (5%)
  other arithmetic  8.63 us (4%)
  matrix products  5.14 us (2%)
    ppermute x15, waiting for transfers between devices, shift(): return lax.ppermute(x, axis, [(i, (i + by) % n) for i in range(n)])  44.8 us
    all_to_all x2, blocking collectives, exchange(): return lax.all_to_all(x, axis, split_axis=0, concat_axis=0, tiled=True)  43.4 us
    all_to_all x3, waiting for transfers between devices, exchange(): return lax.all_to_all(x, axis, split_axis=0, concat_axis=0, tiled=True)  34.5 us
    ppermute x15, starting transfers between devices, shift(): return lax.ppermute(x, axis, [(i, (i + by) % n) for i in range(n)])  22.1 us
    pallas_call x3, Pallas kernels, accumulate(): pl.pallas_call(kernel, in_specs=[smem, smem] + [vmem] * len(operands), ou...  19 us
    all_to_all x3, starting transfers between devices, exchange(): return lax.all_to_all(x, axis, split_axis=0, concat_axis=0, tiled=True)  18.3 us
    pallas_call x1, Pallas kernels, column_blocks(): pl.pallas_call(blocks_kernel, grid_spec=pltpu.PrefetchScalarGridSpec(num_...  5.63 us
    select_n x1, other arithmetic, body(): jnp.where(core == 0, half, other_half)  4.39 us
  transfers between devices with their start and end apart: 18, of which 7 were waited for; matrix products, arithmetic and copies ran while one was open for 6% of the time, Pallas kernels for 12%

profile of v2, /device:TPU:1, one launch (start us, length us, event | category | flops | bytes accessed | tf_op | source)
XLA Modules:
  0.0 215.6 jit_solution(7269654156056130627)
XLA Ops:
  3.9 26.4 %all_to_all.25 = bf16[16,20,640]{2,1,0:T(8,128)(2,1)S(1)} all-to-all(bf16[16,20,640]{2,1,0:T(8,128)(2,1)S(1)} %copy.21), channel_id=1, replica_groups=mesh['z'=8,'core'=2,'x'=4,'yhi'=2,'dp'=2] {'z','core'}, dimensions={0} | all-to-all | bytes 819200 | tf_op jit(solution)/shard_map/all_to_all | solution.py:19
  30.3 3.0 %collective-permute-start = (bf16[320,640]{1,0:T(8,128)(2,1)S(1)}, bf16[320,640]{1,0:T(8,128)(2,1)S(1)}, u32[]{:S(2)}, u32[]{:S(2)}) collective-permute-start(bf16[320,640]{1,0:T(8,128)(2,1)S(1)} %reshape.90), channel_id=1, source_target_pairs={{0,2},{2,0},{1,3},{3,1},{4,6},{6,4},{5,7},{7,5},{8,10},{10,8},{9,1... | collective-permute-start | bytes 1228808 | tf_op jit(solution)/shard_map/ppermute | solution.py:28
  33.4 9.1 %collective-permute-done = bf16[320,640]{1,0:T(8,128)(2,1)S(1)} collective-permute-done((bf16[320,640]{1,0:T(8,128)(2,1)S(1)}, bf16[320,640]{1,0:T(8,128)(2,1)S(1)}, u32[]{:S(2)}, u32[]{:S(2)}) %collective-permute-start) | collective-permute-done | bytes 409632 | tf_op jit(solution)/shard_map/ppermute | solution.py:28
  44.7 1.5 collective-permute-start.1
  46.2 1.5 collective-permute-start.5
  47.7 16.0 %collective-permute-done.9.refs_5_ = bf16[3,320,384]{2,1,0:T(8,128)(2,1)S(1)} collective-permute-done((bf16[3,320,384]{2,1,0:T(8,128)(2,1)S(1)}, bf16[3,320,384]{2,1,0:T(8,128)(2,1)S(1)}, u32[]{:S(2)}, u32[]{:S(2)}) %collective-permute-start.9) | collective-permute-done | bytes 737312 | tf_op jit(solution)/shard_map/ppermute | solution.py:28
  63.6 1.4 collective-permute-start.10
  65.1 1.3 slice.24
  67.5 2.7 %collective-permute-start.4 = (bf16[2,160,640]{2,1,0:T(8,128)(2,1)S(1)}, bf16[2,160,640]{2,1,0:T(8,128)(2,1)S(1)}, u32[]{:S(2)}, u32[]{:S(2)}) collective-permute-start(bf16[2,160,640]{2,1,0:T(8,128)(2,1)S(1)} %slice.25), channel_id=1, source_target_pairs={{0,12},{4,0},{8,4},{12,8},{1,13},{5,1},{9,5},{13,9},{2,14},{6,2},{... | collective-permute-start | bytes 1228808 | tf_op jit(solution)/shard_map/ppermute | solution.py:28
  70.4 1.3 constant_dynamic-update-slice_fusion.1
  71.6 5.3 %collective-permute-done.3 = bf16[2,160,640]{2,1,0:T(8,128)(2,1)S(1)} collective-permute-done((bf16[2,160,640]{2,1,0:T(8,128)(2,1)S(1)}, bf16[2,160,640]{2,1,0:T(8,128)(2,1)S(1)}, u32[]{:S(2)}, u32[]{:S(2)}) %collective-permute-start.3) | collective-permute-done | bytes 409632 | tf_op jit(solution)/shard_map/ppermute | solution.py:28
  77.1 1.3 constant_dynamic-update-slice_fusion.refs_2_
  78.4 1.7 copy-done.4
  80.0 5.6 %shard_map.135 = bf16[8,192,640]{2,1,0:T(8,128)(2,1)} custom-call(s32[1]{0:T(128)} %bitcast.4.refs_1_.core, bf16[384,5120]{1,0:T(8,128)(2,1)} %w_ref), custom_call_target="tpu_custom_call" | custom-call | tf_op jit(solution)/shard_map/pallas_call | solution.py:133
  85.7 7.6 %all-to-all-start.3 = ((bf16[8,192,640]{2,1,0:T(8,128)(2,1)}), bf16[8,192,640]{2,1,0:T(8,128)(2,1)}, u32[]{:S(2)}, u32[]{:S(2)}) async-start(bf16[8,192,640]{2,1,0:T(8,128)(2,1)} %shard_map.135), calls=%async_computation.3 | async-start | bytes 3932160 | tf_op jit(solution)/shard_map/all_to_all | solution.py:19
  93.2 2.4 %collective-permute-start.11 = (bf16[3,320,384]{2,1,0:T(8,128)(2,1)}, bf16[3,320,384]{2,1,0:T(8,128)(2,1)S(1)}, u32[]{:S(2)}, u32[]{:S(2)}) collective-permute-start(bf16[3,320,384]{2,1,0:T(8,128)(2,1)} %collective-permute-done.10.refs_7_), channel_id=1, source_target_pairs={{0,224},{32,0},{64,32},{96,64},{128,96},{160,128},{192,160},{224,1... | collective-permute-start | bytes 2211848 | tf_op jit(solution)/shard_map/ppermute | solution.py:28
  95.7 12.9 %collective-permute-done.11.refs_4_ = bf16[3,320,384]{2,1,0:T(8,128)(2,1)S(1)} collective-permute-done((bf16[3,320,384]{2,1,0:T(8,128)(2,1)}, bf16[3,320,384]{2,1,0:T(8,128)(2,1)S(1)}, u32[]{:S(2)}, u32[]{:S(2)}) %collective-permute-start.11) | collective-permute-done | bytes 737312 | tf_op jit(solution)/shard_map/ppermute | solution.py:28
  108.6 3.5 %collective-permute-start.12 = (bf16[3,160,384]{2,1,0:T(8,128)(2,1)S(1)}, bf16[3,160,384]{2,1,0:T(8,128)(2,1)S(1)}, u32[]{:S(2)}, u32[]{:S(2)}) collective-permute-start(bf16[3,160,384]{2,1,0:T(8,128)(2,1)S(1)} %slice.27), channel_id=1, source_target_pairs={{0,224},{32,0},{64,32},{96,64},{128,96},{160,128},{192,160},{224,1... | collective-permute-start | bytes 1105928 | tf_op jit(solution)/shard_map/ppermute | solution.py:28
  113.6 8.6 %shard_map.131.refs_5_ = f32[2,3,320,384]{3,2,1,0:T(8,128)} custom-call(s32[5]{0:T(128)S(1)} %fusion.24.refs_0_, s32[1]{0:T(128)} %bitcast.4.refs_1_.core, bf16[8,320,640]{2,1,0:T(8,128)(2,1)} %copy-done.4, bf16[3,320,384]{2,1,0:T(8,128)(2,1)S(1)} %bitcast.34, bf16[3,320,384]{2,1,0:T(8,128)(2,1)S(1)} %copy-done.3, ...), custom_call_target="tpu_custom_call" | custom-call | tf_op jit(solution)/shard_map/pallas_call | solution.py:77
  122.2 6.4 %shard_map.132.refs_5_ = f32[2,3,320,384]{3,2,1,0:T(8,128)} custom-call(s32[2]{0:T(128)S(1)} %fusion.25.refs_0_, s32[1]{0:T(128)} %bitcast.4.refs_1_.core, bf16[8,320,640]{2,1,0:T(8,128)(2,1)} %copy-done.4, bf16[3,320,384]{2,1,0:T(8,128)(2,1)S(1)} %collective-permute-done.7.refs_3_, bf16[3,320,384]{2,1,0:T(8,128)(2,1)S(1)} %collective-permute-done.11.refs_4_, ...), custom_call_target="tpu_custom_call" | custom-call | tf_op jit(solution)/shard_map/pallas_call | solution.py:77
  128.6 4.0 %shard_map.133 = (f32[3,320,384]{2,1,0:T(8,128)S(1)}, bf16[3,320,384]{2,1,0:T(8,128)(2,1)S(1)}) custom-call(s32[1]{0:T(128)S(6)} %xor.19.refs_0_, s32[1]{0:T(128)} %bitcast.4.refs_1_.core, bf16[8,320,640]{2,1,0:T(8,128)(2,1)} %copy-done.4, bf16[3,160,384]{2,1,0:T(8,128)(2,1)S(1)} %collective-permute-done.8.refs_3_, ...), custom_call_target="tpu_custom_call" | custom-call | tf_op jit(solution)/shard_map/pallas_call | solution.py:77
  132.6 4.4 %collective-permute-start.13 = (bf16[3,320,384]{2,1,0:T(8,128)(2,1)S(1)}, bf16[3,320,384]{2,1,0:T(8,128)(2,1)S(1)}, u32[]{:S(2)}, u32[]{:S(2)}) collective-permute-start(bf16[3,320,384]{2,1,0:T(8,128)(2,1)S(1)} %get-tuple-element.8), channel_id=1, source_target_pairs={{0,16},{16,0},{1,17},{17,1},{2,18},{18,2},{3,19},{19,3},{4,20},{20... | collective-permute-start | bytes 2211848 | tf_op jit(solution)/shard_map/ppermute | solution.py:28
  137.3 1.6 collective-permute-done.13.other_ref
  138.9 1.4 shard_map.134
  140.2 17.0 %all_to_all.26 = bf16[16,20,384]{2,1,0:T(8,128)(2,1)S(1)} all-to-all(bf16[16,20,384]{2,1,0:T(8,128)(2,1)S(1)} %shard_map.134), channel_id=1, replica_groups=mesh['z'=8,'core'=2,'x'=4,'yhi'=2,'dp'=2] {'z','core'}, dimensions={0} | all-to-all | bytes 491520 | tf_op jit(solution)/shard_map/all_to_all | solution.py:19
  157.3 1.5 broadcast_in_dim.37
  158.8 6.6 %all-to-all-start.2 = ((bf16[8,320,384]{2,1,0:T(8,128)(2,1)}), bf16[8,320,384]{2,1,0:T(8,128)(2,1)S(1)}, u32[]{:S(2)}, u32[]{:S(2)}) async-start(bf16[8,320,384]{2,1,0:T(8,128)(2,1)} %broadcast_in_dim.37), calls=%async_computation.2 | async-start | bytes 3932160 | tf_op jit(solution)/shard_map/all_to_all | solution.py:19
  165.6 4.4 %broadcast_select_fusion.1 = (bf16[8,192,640]{2,1,0:T(8,128)(2,1)}, bf16[8,192,640]{2,1,0:T(8,128)(2,1)}) fusion(bf16[8,192,640]{2,1,0:T(8,128)(2,1)} %all-to-all-done.3, bf16[8,192,640]{2,1,0:T(8,128)(2,1)} %collective-permute-done.14, pred[]{:T(512)S(6)} %eq.72), kind=kLoop, calls=%fused_computation.5 | loop fusion | flops 1966080 | bytes 7864321 | tf_op jit(solution)/shard_map/jit(_where)/select_n | solution.py:178
  170.0 25.3 %all-to-all-done.2 = bf16[8,320,384]{2,1,0:T(8,128)(2,1)S(1)} async-done(((bf16[8,320,384]{2,1,0:T(8,128)(2,1)}), bf16[8,320,384]{2,1,0:T(8,128)(2,1)S(1)}, u32[]{:S(2)}, u32[]{:S(2)}) %all-to-all-start.2) | async-done | bytes 1966112 | tf_op jit(solution)/shard_map/all_to_all | solution.py:19
  195.3 3.9 %fusion = f32[320,640,1]{1,0,2:T(8,128)S(1)} fusion(bf16[8,320,384]{2,1,0:T(8,128)(2,1)S(1)} %all-to-all-done.2, bf16[8,192,640]{2,1,0:T(8,128)(2,1)} %get-tuple-element.11, bf16[8,192,640]{2,1,0:T(8,128)(2,1)} %get-tuple-element.10), kind=kOutput, calls=%fused_computation | convolution fusion | flops 1266155520 | bytes 6717440 | tf_op jit(solution)/shard_map/dot_general | solution.py:195
  200.1 4.2 %all-to-all-start.4 = ((f32[32,2,672]{2,1,0:T(2,128)}), f32[32,2,672]{2,1,0:T(2,128)S(1)}, u32[]{:S(2)}, u32[]{:S(2)}) async-start(f32[32,2,672]{2,1,0:T(2,128)} %broadcast_in_dim.38), calls=%async_computation.4 | async-start | bytes 393216 | tf_op jit(solution)/shard_map/all_to_all | solution.py:19
  205.4 9.1 %all-to-all-done.4 = f32[32,2,672]{2,1,0:T(2,128)S(1)} async-done(((f32[32,2,672]{2,1,0:T(2,128)}), f32[32,2,672]{2,1,0:T(2,128)S(1)}, u32[]{:S(2)}, u32[]{:S(2)}) %all-to-all-start.4) | async-done | bytes 172064 | tf_op jit(solution)/shard_map/all_to_all | solution.py:19
  (70 shorter events, 12.0 us)
Async XLA Ops:
  0.6 203.7 %copy-start = (f32[32,640]{1,0:T(8,128)S(1)}, f32[32,640]{1,0:T(8,128)}, u32[]{:S(2)}) copy-start(f32[32,640]{1,0:T(8,128)} %param.19) | copy-start | bytes 245764
  3.4 42.8 %copy-start.1 = (bf16[320,3,384]{2,0,1:T(8,128)(2,1)S(1)}, bf16[320,3,384]{2,0,1:T(8,128)(2,1)}, u32[]{:S(2)}) copy-start(bf16[320,3,384]{2,0,1:T(8,128)(2,1)} %param.15) | copy-start | bytes 2211844
  30.3 12.2 %collective-permute-start = (bf16[320,640]{1,0:T(8,128)(2,1)S(1)}, bf16[320,640]{1,0:T(8,128)(2,1)S(1)}, u32[]{:S(2)}, u32[]{:S(2)}) collective-permute-start(bf16[320,640]{1,0:T(8,128)(2,1)S(1)} %reshape.90), channel_id=1, source_target_pairs={{0,2},{2,0},{1,3},{3,1},{4,6},{6,4},{5,7},{7,5},{8,10},{10,8},{9,1... | collective-permute-start | bytes 1228808 | tf_op jit(solution)/shard_map/ppermute | solution.py:28
  43.5 21.6 %collective-permute-start.2 = (bf16[2,320,640]{2,1,0:T(8,128)(2,1)}, bf16[2,320,640]{2,1,0:T(8,128)(2,1)}, u32[]{:S(2)}, u32[]{:S(2)}) collective-permute-start(bf16[2,320,640]{2,1,0:T(8,128)(2,1)} %pad_maximum_fusion), channel_id=1, source_target_pairs={{0,4},{4,8},{8,12},{12,0},{1,5},{5,9},{9,13},{13,1},{2,6},{6,10},{... | collective-permute-start | bytes 2457608 | tf_op jit(solution)/shard_map/ppermute | solution.py:28
  44.7 21.7 %collective-permute-start.1 = (bf16[2,320,640]{2,1,0:T(8,128)(2,1)}, bf16[2,320,640]{2,1,0:T(8,128)(2,1)}, u32[]{:S(2)}, u32[]{:S(2)}) collective-permute-start(bf16[2,320,640]{2,1,0:T(8,128)(2,1)} %pad_maximum_fusion), channel_id=1, source_target_pairs={{0,12},{4,0},{8,4},{12,8},{1,13},{5,1},{9,5},{13,9},{2,14},{6,2},{... | collective-permute-start | bytes 2457608 | tf_op jit(solution)/shard_map/ppermute | solution.py:28
  46.2 17.4 %collective-permute-start.9 = (bf16[3,320,384]{2,1,0:T(8,128)(2,1)S(1)}, bf16[3,320,384]{2,1,0:T(8,128)(2,1)S(1)}, u32[]{:S(2)}, u32[]{:S(2)}) collective-permute-start(bf16[3,320,384]{2,1,0:T(8,128)(2,1)S(1)} %bitcast.32), channel_id=1, source_target_pairs={{0,224},{32,0},{64,32},{96,64},{128,96},{160,128},{192,160},{224,1... | collective-permute-start | bytes 2211848 | tf_op jit(solution)/shard_map/ppermute | solution.py:28
  46.2 18.9 %collective-permute-start.5 = (bf16[3,320,384]{2,1,0:T(8,128)(2,1)S(1)}, bf16[3,320,384]{2,1,0:T(8,128)(2,1)S(1)}, u32[]{:S(2)}, u32[]{:S(2)}) collective-permute-start(bf16[3,320,384]{2,1,0:T(8,128)(2,1)S(1)} %bitcast.33), channel_id=1, source_target_pairs={{0,32},{32,64},{64,96},{96,128},{128,160},{160,192},{192,224},{224... | collective-permute-start | bytes 2211848 | tf_op jit(solution)/shard_map/ppermute | solution.py:28
  63.6 29.6 %collective-permute-start.10 = (bf16[3,320,384]{2,1,0:T(8,128)(2,1)S(1)}, bf16[3,320,384]{2,1,0:T(8,128)(2,1)}, u32[]{:S(2)}, u32[]{:S(2)}) collective-permute-start(bf16[3,320,384]{2,1,0:T(8,128)(2,1)S(1)} %collective-permute-done.9.refs_5_), channel_id=1, source_target_pairs={{0,224},{32,0},{64,32},{96,64},{128,96},{160,128},{192,160},{224,1... | collective-permute-start | bytes 2211848 | tf_op jit(solution)/shard_map/ppermute | solution.py:28
  65.1 12.0 %copy-start.2 = (bf16[3,320,384]{2,1,0:T(8,128)(2,1)}, bf16[3,320,384]{2,1,0:T(8,128)(2,1)S(1)}, u32[]{:S(2)}) copy-start(bf16[3,320,384]{2,1,0:T(8,128)(2,1)S(1)} %collective-permute-done.5.refs_4_) | copy-start | bytes 2211844
  65.1 30.6 %collective-permute-start.6 = (bf16[3,320,384]{2,1,0:T(8,128)(2,1)S(1)}, bf16[3,320,384]{2,1,0:T(8,128)(2,1)}, u32[]{:S(2)}, u32[]{:S(2)}) collective-permute-start(bf16[3,320,384]{2,1,0:T(8,128)(2,1)S(1)} %collective-permute-done.5.refs_4_), channel_id=1, source_target_pairs={{0,32},{32,64},{64,96},{96,128},{128,160},{160,192},{192,224},{224... | collective-permute-start | bytes 2211848 | tf_op jit(solution)/shard_map/ppermute | solution.py:28
  66.4 10.6 %collective-permute-start.3 = (bf16[2,160,640]{2,1,0:T(8,128)(2,1)S(1)}, bf16[2,160,640]{2,1,0:T(8,128)(2,1)S(1)}, u32[]{:S(2)}, u32[]{:S(2)}) collective-permute-start(bf16[2,160,640]{2,1,0:T(8,128)(2,1)S(1)} %slice.24), channel_id=1, source_target_pairs={{0,4},{4,8},{8,12},{12,0},{1,5},{5,9},{9,13},{13,1},{2,6},{6,10},{... | collective-permute-start | bytes 1228808 | tf_op jit(solution)/shard_map/ppermute | solution.py:28
  67.5 9.4 %collective-permute-start.4 = (bf16[2,160,640]{2,1,0:T(8,128)(2,1)S(1)}, bf16[2,160,640]{2,1,0:T(8,128)(2,1)S(1)}, u32[]{:S(2)}, u32[]{:S(2)}) collective-permute-start(bf16[2,160,640]{2,1,0:T(8,128)(2,1)S(1)} %slice.25), channel_id=1, source_target_pairs={{0,12},{4,0},{8,4},{12,8},{1,13},{5,1},{9,5},{13,9},{2,14},{6,2},{... | collective-permute-start | bytes 1228808 | tf_op jit(solution)/shard_map/ppermute | solution.py:28
  78.4 1.7 copy-start.4
  85.7 26.8 %copy-start.9 = (s32[5]{0:T(128)S(1)}, s32[5]{0:T(128)}, u32[]{:S(2)}) copy-start(s32[5]{0:T(128)} %constant.175.clone) | copy-start | bytes 64
  85.7 26.8 %copy-start.8 = (s32[2]{0:T(128)S(1)}, s32[2]{0:T(128)}, u32[]{:S(2)}) copy-start(s32[2]{0:T(128)} %constant.176.clone) | copy-start | bytes 28
  85.7 51.4 %all-to-all-start.3 = ((bf16[8,192,640]{2,1,0:T(8,128)(2,1)}), bf16[8,192,640]{2,1,0:T(8,128)(2,1)}, u32[]{:S(2)}, u32[]{:S(2)}) async-start(bf16[8,192,640]{2,1,0:T(8,128)(2,1)} %shard_map.135), calls=%async_computation.3 | async-start | bytes 3932160 | tf_op jit(solution)/shard_map/all_to_all | solution.py:19
  93.2 15.3 %collective-permute-start.11 = (bf16[3,320,384]{2,1,0:T(8,128)(2,1)}, bf16[3,320,384]{2,1,0:T(8,128)(2,1)S(1)}, u32[]{:S(2)}, u32[]{:S(2)}) collective-permute-start(bf16[3,320,384]{2,1,0:T(8,128)(2,1)} %collective-permute-done.10.refs_7_), channel_id=1, source_target_pairs={{0,224},{32,0},{64,32},{96,64},{128,96},{160,128},{192,160},{224,1... | collective-permute-start | bytes 2211848 | tf_op jit(solution)/shard_map/ppermute | solution.py:28
  95.7 16.4 %collective-permute-start.7 = (bf16[3,320,384]{2,1,0:T(8,128)(2,1)}, bf16[3,320,384]{2,1,0:T(8,128)(2,1)S(1)}, u32[]{:S(2)}, u32[]{:S(2)}) collective-permute-start(bf16[3,320,384]{2,1,0:T(8,128)(2,1)} %collective-permute-done.6.refs_6_), channel_id=1, source_target_pairs={{0,32},{32,64},{64,96},{96,128},{128,160},{160,192},{192,224},{224... | collective-permute-start | bytes 2211848 | tf_op jit(solution)/shard_map/ppermute | solution.py:28
  108.6 20.0 %collective-permute-start.12 = (bf16[3,160,384]{2,1,0:T(8,128)(2,1)S(1)}, bf16[3,160,384]{2,1,0:T(8,128)(2,1)S(1)}, u32[]{:S(2)}, u32[]{:S(2)}) collective-permute-start(bf16[3,160,384]{2,1,0:T(8,128)(2,1)S(1)} %slice.27), channel_id=1, source_target_pairs={{0,224},{32,0},{64,32},{96,64},{128,96},{160,128},{192,160},{224,1... | collective-permute-start | bytes 1105928 | tf_op jit(solution)/shard_map/ppermute | solution.py:28
  112.1 16.5 %collective-permute-start.8 = (bf16[3,160,384]{2,1,0:T(8,128)(2,1)S(1)}, bf16[3,160,384]{2,1,0:T(8,128)(2,1)S(1)}, u32[]{:S(2)}, u32[]{:S(2)}) collective-permute-start(bf16[3,160,384]{2,1,0:T(8,128)(2,1)S(1)} %slice.26), channel_id=1, source_target_pairs={{0,32},{32,64},{64,96},{96,128},{128,160},{160,192},{192,224},{224... | collective-permute-start | bytes 1105928 | tf_op jit(solution)/shard_map/ppermute | solution.py:28
  112.5 1.1 copy-start.3
  132.6 6.2 %collective-permute-start.13 = (bf16[3,320,384]{2,1,0:T(8,128)(2,1)S(1)}, bf16[3,320,384]{2,1,0:T(8,128)(2,1)S(1)}, u32[]{:S(2)}, u32[]{:S(2)}) collective-permute-start(bf16[3,320,384]{2,1,0:T(8,128)(2,1)S(1)} %get-tuple-element.8), channel_id=1, source_target_pairs={{0,16},{16,0},{1,17},{17,1},{2,18},{18,2},{3,19},{19,3},{4,20},{20... | collective-permute-start | bytes 2211848 | tf_op jit(solution)/shard_map/ppermute | solution.py:28
  137.0 28.6 %collective-permute-start.14 = (bf16[8,192,640]{2,1,0:T(8,128)(2,1)}, bf16[8,192,640]{2,1,0:T(8,128)(2,1)}, u32[]{:S(2)}, u32[]{:S(2)}) collective-permute-start(bf16[8,192,640]{2,1,0:T(8,128)(2,1)} %all-to-all-done.3), channel_id=1, source_target_pairs={{0,16},{16,0},{1,17},{17,1},{2,18},{18,2},{3,19},{19,3},{4,20},{20... | collective-permute-start | bytes 5898248 | tf_op jit(solution)/shard_map/ppermute | solution.py:28
  157.3 8.1 %copy-start.10 = (f32[8,32]{1,0:T(8,128)S(1)}, f32[8,32]{1,0:T(8,128)}, u32[]{:S(2)}) copy-start(f32[8,32]{1,0:T(8,128)} %param.18) | copy-start | bytes 3076
  157.3 8.1 %copy-start.11 = (s32[2,1]{0,1:T(1,128)S(1)}, s32[2,1]{0,1:T(1,128)}, u32[]{:S(2)}) copy-start(s32[2,1]{0,1:T(1,128)} %param.17) | copy-start | bytes 28
  158.8 36.5 %all-to-all-start.2 = ((bf16[8,320,384]{2,1,0:T(8,128)(2,1)}), bf16[8,320,384]{2,1,0:T(8,128)(2,1)S(1)}, u32[]{:S(2)}, u32[]{:S(2)}) async-start(bf16[8,320,384]{2,1,0:T(8,128)(2,1)} %broadcast_in_dim.37), calls=%async_computation.2 | async-start | bytes 3932160 | tf_op jit(solution)/shard_map/all_to_all | solution.py:19
  195.3 3.9 %copy-start.6 = (bf16[2,1,160,640]{3,2,1,0:T(8,128)(2,1)S(1)}, bf16[2,1,160,640]{3,2,1,0:T(8,128)(2,1)}, u32[]{:S(2)}) copy-start(bf16[2,1,160,640]{3,2,1,0:T(8,128)(2,1)} %param.20) | copy-start | bytes 1228804
  195.3 9.1 %copy-start.5 = (bf16[2,1,160,640]{3,2,1,0:T(8,128)(2,1)S(1)}, bf16[2,1,160,640]{3,2,1,0:T(8,128)(2,1)}, u32[]{:S(2)}) copy-start(bf16[2,1,160,640]{3,2,1,0:T(8,128)(2,1)} %param.12) | copy-start | bytes 1228804
  195.3 9.1 %copy-start.7 = (bf16[640]{0:T(1024)(128)(2,1)S(1)}, bf16[640]{0:T(1024)(128)(2,1)}, u32[]{:S(2)}) copy-start(bf16[640]{0:T(1024)(128)(2,1)} %param.14) | copy-start | bytes 3844
  200.1 14.5 %all-to-all-start.4 = ((f32[32,2,672]{2,1,0:T(2,128)}), f32[32,2,672]{2,1,0:T(2,128)S(1)}, u32[]{:S(2)}, u32[]{:S(2)}) async-start(f32[32,2,672]{2,1,0:T(2,128)} %broadcast_in_dim.38), calls=%async_computation.4 | async-start | bytes 393216 | tf_op jit(solution)/shard_map/all_to_all | solution.py:19

commit v3 on v2

--- a/solution.py
+++ b/solution.py
@@ -12,7 +12,7 @@
 MASKED = -1e30
 FRAME = ("z", "core")
 MP = ("x", "yhi")
-VMEM = pltpu.CompilerParams(vmem_limit_bytes=50 * 1024 * 1024)
+SMALL = pltpu.CompilerParams(vmem_limit_bytes=16 * 1024 * 1024)
 
 
 def exchange(x, axis):
@@ -28,59 +28,66 @@
     return lax.ppermute(x, axis, [(i, (i + by) % n) for i in range(n)])
 
 
-def accumulate_kernel(counts, first, last, slots, core, x_ref, *refs):
-    n = sum(counts)
-    w_refs, rest = refs[:n], refs[n:]
-    acc_in = None if first else rest[0]
-    rest = rest if first else rest[1:]
-    parts = [[None if first else acc_in[s, i] for i in range(3)] for s in range(2)]
-    at = 0
-    for j, count in enumerate(counts):
-        x = x_ref[slots[j]]
-        half = x.shape[1] // 2
-        xs = (x[:, :half], x[:, half:])
-        for i in range(3):
-            pieces = [w_refs[at + c][i] for c in range(count)]
-            w = pieces[0] if count == 1 else jnp.concatenate(pieces, axis=0)
-            for s in range(2):
-                d = jnp.dot(xs[s], w, preferred_element_type=jnp.float32)
-                parts[s][i] = d if parts[s][i] is None else parts[s][i] + d
-        at += count
-    for i in range(3):
-        if last:
-            mine = core[0] == 0
-            rest[0][i] = jnp.where(mine, parts[0][i], parts[1][i])
-            rest[1][i] = jnp.where(mine, parts[1][i], parts[0][i]).astype(jnp.bfloat16)
+def qkv_kernel(slots, core, x_any, *refs):
+    n = len(refs) - 7
+    shards, (kept, sent, x_ref, w_ref, acc, x_sem, w_sem) = refs[:n], refs[n:]
+    copies, at = [], 0
+    for j in range(x_ref.shape[0]):
+        copies.append([pltpu.make_async_copy(x_any.at[slots[j]], x_ref.at[j], x_sem.at[j])])
+        full = x_ref.shape[2] // 2
+        row = 0
+        while row < full:
+            depth = shards[at].shape[1]
+            target = w_ref.at[:, pl.ds(j * full + row, depth)]
+            copies[j].append(pltpu.make_async_copy(shards[at], target, w_sem.at[at]))
+            row += depth
+            at += 1
+    for group in copies:
+        for copy in group:
+            copy.start()
+    rows, half = x_ref.shape[1], x_ref.shape[2] // 2
+    for j in range(0, x_ref.shape[0], 2):
+        for copy in copies[j] + copies[j + 1]:
+            copy.wait()
+        a, b = x_ref[j], x_ref[j + 1]
+        low = jnp.concatenate([a[:, :half], b[:, :half]], axis=1)
+        high = jnp.concatenate([a[:, half:], b[:, half:]], axis=1)
+        x = jnp.concatenate([low, high], axis=0)
+        depth = pl.ds(j * half, 2 * half)
+        w = jnp.concatenate([w_ref[i, depth] for i in range(3)], axis=1)
+        part = jnp.dot(x, w, preferred_element_type=jnp.float32)
+        if j == 0:
+            acc[...] = part
         else:
-            for s in range(2):
-                rest[0][s, i] = parts[s][i]
-
-
-def accumulate(x, shards, slots, core, acc=None, last=False):
-    counts = [len(s) for s in shards]
-    flat = [w for s in shards for w in s]
-    rows, heads = x.shape[1], flat[0].shape[2]
-    if last:
-        out_shape = (
-            jax.ShapeDtypeStruct((3, rows, heads), jnp.float32),
-            jax.ShapeDtypeStruct((3, rows, heads), jnp.bfloat16),
-        )
-    else:
-        out_shape = jax.ShapeDtypeStruct((2, 3, rows, heads), jnp.float32)
-
-    def kernel(*refs):
-        accumulate_kernel(counts, acc is None, last, *refs)
-
+            acc[...] += part
+    me = core[0]
+    kept[...] = acc[pl.ds(me * rows, rows)]
+    sent[...] = acc[pl.ds((1 - me) * rows, rows)].astype(jnp.bfloat16)
+
+
+def project(x, shards, slots, core):
+    n, rows, width = x.shape
+    heads = 3 * shards[0].shape[2]
     smem = pl.BlockSpec(memory_space=pltpu.SMEM)
     vmem = pl.BlockSpec(memory_space=pltpu.VMEM)
-    operands = [x, *flat] + ([] if acc is None else [acc])
+    hbm = pl.BlockSpec(memory_space=pl.ANY)
     return pl.pallas_call(
-        kernel,
-        in_specs=[smem, smem] + [vmem] * len(operands),
-        out_specs=(vmem, vmem) if last else vmem,
-        out_shape=out_shape,
-        compiler_params=VMEM,
-    )(slots, core, *operands)
+        qkv_kernel,
+        in_specs=[smem, smem] + [hbm] * (1 + len(shards)),
+        out_specs=(vmem, vmem),
+        out_shape=(
+            jax.ShapeDtypeStruct((rows, heads), jnp.float32),
+            jax.ShapeDtypeStruct((rows, heads), jnp.bfloat16),
+        ),
+        scratch_shapes=[
+            pltpu.VMEM((n, rows, width), jnp.bfloat16),
+            pltpu.VMEM((3, n * width // 2, heads // 3), jnp.bfloat16),
+            pltpu.VMEM((2 * rows, heads), jnp.float32),
+            pltpu.SemaphoreType.DMA((n,)),
+            pltpu.SemaphoreType.DMA((len(shards),)),
+        ],
+        compiler_params=pltpu.CompilerParams(vmem_limit_bytes=28 * 1024 * 1024),
+    )(slots, core, x, *shards)
 
 
 def attend(q, k, v, bias):
@@ -100,18 +107,17 @@
     frames, spots, width = out_ref.shape
     bias = bias_ref[...]
     for h in range(width // HS):
-        cols = slice(h * HS, (h + 1) * HS)
         q, k, v = (
-            (own_ref[i, :, cols] + other_ref[i, :, cols].astype(jnp.float32)).astype(jnp.bfloat16)
-            for i in range(3)
+            (own_ref[:, cols] + other_ref[:, cols].astype(jnp.float32)).astype(jnp.bfloat16)
+            for cols in (slice(i * width + h * HS, i * width + (h + 1) * HS) for i in range(3))
         )
         o = attend(q, k, v, bias)
         for t in range(frames):
-            out_ref[t, :, cols] = o[t * spots : (t + 1) * spots]
+            out_ref[t, :, h * HS : (h + 1) * HS] = o[t * spots : (t + 1) * spots]
 
 
 def attention(own, other, frames):
-    _, rows, heads = own.shape
+    rows, heads = own.shape[0], own.shape[1] // 3
     spots = rows // frames
     r = jnp.arange(rows)
     seen = (r[:, None] % spots == r[None, :] % spots) & (r[:, None] >= r[None, :])
@@ -119,7 +125,7 @@
     return pl.pallas_call(
         attention_kernel,
         out_shape=jax.ShapeDtypeStruct((frames, spots, heads), jnp.bfloat16),
-        compiler_params=VMEM,
+        compiler_params=SMALL,
     )(own, other, bias)
 
 
@@ -139,16 +145,8 @@
             out_specs=pl.BlockSpec((1, half, width), lambda m, core: (m, 0, 0)),
         ),
         out_shape=jax.ShapeDtypeStruct((n, half, width), w.dtype),
-        compiler_params=VMEM,
+        compiler_params=SMALL,
     )(core, w)
-
-
-def gather_features(mine):
-    both = jnp.stack([mine, shift(mine, "yhi", 1)])
-    half = mine.shape[0] // 2
-    left, right = shift(both, "x", 1), shift(both, "x", -1)
-    far = jnp.concatenate([shift(left[:, :half], "x", 1), shift(right[:, half:], "x", -1)], axis=1)
-    return jnp.concatenate([both, right, far, left])
 
 
 def body(tokens, token_mask, mask_embed, w_qkv, w_out, action_idx, codebook, act_proj, cotangent):
@@ -165,30 +163,32 @@
 
     own = w_qkv.transpose(1, 0, 2)
     up1, down1 = shift(own, "z", 1), shift(own, "z", -1)
-    features = gather_features(mine)
+    mine, up1, down1 = lax.optimization_barrier((mine, up1, down1))
     up2, down2 = shift(up1, "z", 1), shift(down1, "z", -1)
+    both = jnp.stack([mine, shift(mine, "yhi", 1)])
+    both, w_out = lax.optimization_barrier((both, w_out))
+    left, right = shift(both, "x", 1), shift(both, "x", -1)
+    blocks = column_blocks(w_out, core1, width)
+    left, right, up2, down2, blocks = lax.optimization_barrier((left, right, up2, down2, blocks))
     up3, down3 = shift(up2, "z", 1), shift(down2, "z", -1)
+    middle = rows // 2
+    far = (shift(left[:, :middle], "x", 1), shift(right[:, middle:], "x", -1))
+    up3, down3, far, blocks = lax.optimization_barrier((up3, down3, far, blocks))
     up4 = shift(up3[:, : depth // 2], "z", 1)
     down4 = shift(down3[:, depth // 2 :], "z", -1)
-
-    w_out, features = lax.optimization_barrier((w_out, features))
-    half = exchange(column_blocks(w_out, core1, width), MP)
+    features = jnp.concatenate([both, right, jnp.concatenate(far, axis=1), left])
+
+    half = exchange(blocks, MP)
     other_half = shift(half, "core", 1)
     out_block = jnp.concatenate(
         [jnp.where(core == 0, half, other_half), jnp.where(core == 0, other_half, half)], axis=1
     )
 
     x, yhi = lax.axis_index("x"), lax.axis_index("yhi")
-
-    def slots(*shifts):
-        shard = (z + jnp.array(shifts, jnp.int32)) % zs
-        return (2 * ((shard // 2 - x) % (mp // 2)) + (shard % 2) ^ yhi).astype(jnp.int32)
-
-    acc = accumulate(
-        features, [(own,), (up1,), (down1,), (up2,), (down2,)], slots(0, -1, 1, -2, 2), core1
-    )
-    acc = accumulate(features, [(up3,), (down3,)], slots(-3, 3), core1, acc)
-    kept, sent = accumulate(features, [(up4, down4)], slots(-4), core1, acc, last=True)
+    shard = (z + jnp.array([0, zs - 1, 1, zs - 2, 2, zs - 3, 3, zs - 4], jnp.int32)) & (zs - 1)
+    slots = (2 * (((shard >> 1) - x) & (mp // 2 - 1)) + ((shard & 1) ^ yhi)).astype(jnp.int32)
+    shards = [own, up1, down1, up2, down2, up3, down3, up4, down4]
+    kept, sent = project(features, shards, slots, core1)
     attn = attention(kept, shift(sent, "core", 1), frames)
     attn = exchange(attn, FRAME).reshape(rows, heads)
     all_heads = from_everyone(attn, MP)

time: 216 us -> 204 us (0.944)
  blocking collectives: 43.4 us -> 18.4 us
  waiting for transfers between devices: 79.3 us -> 92.3 us
  starting transfers between devices: 40.4 us -> 52 us
  Pallas kernels: 26 us -> 14.8 us
  other arithmetic: 8.63 us -> 11.5 us
  local copies, waits for them, and re-layouts: 11.7 us -> 8.89 us
    all_to_all x2 -> x1, blocking collectives: 43.4 us -> 18.4 us  [exchange(): return lax.all_to_all(x, axis, split_axis=0, concat_axis=0, tiled=True)]
    all_to_all x3 -> x4, waiting for transfers between devices: 34.5 us -> 48.4 us  [exchange(): return lax.all_to_all(x, axis, split_axis=0, concat_axis=0, tiled=True)]
    pallas_call x3 -> x1, Pallas kernels: 19 us -> 10.3 us  [project(): pl.pallas_call(qkv_kernel, in_specs=[smem, smem] + [hbm] * (1 + len(shard...]
    ppermute x15, starting transfers between devices: 22.1 us -> 28 us  [shift(): return lax.ppermute(x, axis, [(i, (i + by) % n) for i in range(n)])]
    all_to_all x3 -> x4, starting transfers between devices: 18.3 us -> 24 us  [exchange(): return lax.all_to_all(x, axis, split_axis=0, concat_axis=0, tiled=True)]
    concatenate x0 -> x1, other arithmetic: none -> 2.94 us  [body(): jnp.concatenate([both, right, jnp.concatenate(far, axis=1), left])]
    pallas_call x1, Pallas kernels: 5.63 us -> 3.11 us  [column_blocks(): pl.pallas_call(blocks_kernel, grid_spec=pltpu.PrefetchScalarGridSpec(num_...]
  transfers between devices with their start and end apart: 18 -> 19, of which waited for: 7 -> 13; matrix products, arithmetic and copies ran while one was open for 6% -> 6% of each run, Pallas kernels for 12% -> 7%
where the time goes in v3:
time: 204 us
  waiting for transfers between devices  92.3 us (45%)
  starting transfers between devices  52 us (25%)
  blocking collectives  18.4 us (9%)
  Pallas kernels  14.8 us (7%)
  other arithmetic  11.5 us (6%)
  local copies, waits for them, and re-layouts  8.89 us (4%)
  matrix products  5.14 us (3%)
    all_to_all x4, waiting for transfers between devices, exchange(): return lax.all_to_all(x, axis, split_axis=0, concat_axis=0, tiled=True)  48.4 us
    ppermute x15, waiting for transfers between devices, shift(): return lax.ppermute(x, axis, [(i, (i + by) % n) for i in range(n)])  43.9 us
    ppermute x15, starting transfers between devices, shift(): return lax.ppermute(x, axis, [(i, (i + by) % n) for i in range(n)])  28 us
    all_to_all x4, starting transfers between devices, exchange(): return lax.all_to_all(x, axis, split_axis=0, concat_axis=0, tiled=True)  24 us
    all_to_all x1, blocking collectives, exchange(): return lax.all_to_all(x, axis, split_axis=0, concat_axis=0, tiled=True)  18.4 us
    pallas_call x1, Pallas kernels, project(): pl.pallas_call(qkv_kernel, in_specs=[smem, smem] + [hbm] * (1 + len(shard...  10.3 us
    select_n x1, other arithmetic, body(): jnp.where(core == 0, half, other_half)  4.47 us
  transfers between devices with their start and end apart: 19, of which 13 were waited for; matrix products, arithmetic and copies ran while one was open for 6% of the time, Pallas kernels for 7%

profile of v3, /device:TPU:1, one launch (start us, length us, event | category | flops | bytes accessed | tf_op | source)
XLA Modules:
  0.0 203.8 jit_solution(5576645696934342304)
XLA Ops:
  4.7 10.0 %all-to-all-start = ((bf16[16,20,640]{2,1,0:T(8,128)(2,1)}), bf16[16,20,640]{2,1,0:T(8,128)(2,1)S(1)}, u32[]{:S(2)}, u32[]{:S(2)}) async-start(bf16[16,20,640]{2,1,0:T(8,128)(2,1)} %copy.18), calls=%async_computation | async-start | bytes 983040 | tf_op jit(solution)/shard_map/all_to_all | solution.py:19
  14.7 1.5 collective-permute-start
  17.4 13.8 %all-to-all-done = bf16[16,20,640]{2,1,0:T(8,128)(2,1)S(1)} async-done(((bf16[16,20,640]{2,1,0:T(8,128)(2,1)}), bf16[16,20,640]{2,1,0:T(8,128)(2,1)S(1)}, u32[]{:S(2)}, u32[]{:S(2)}) %all-to-all-start) | async-done | bytes 409632 | tf_op jit(solution)/shard_map/all_to_all | solution.py:19
  31.4 13.2 %collective-permute-done.refs_1_ = bf16[3,320,384]{2,1,0:T(8,128)(2,1)S(1)} collective-permute-done((bf16[3,320,384]{2,1,0:T(8,128)(2,1)S(1)}, bf16[3,320,384]{2,1,0:T(8,128)(2,1)S(1)}, u32[]{:S(2)}, u32[]{:S(2)}) %collective-permute-start) | collective-permute-done | bytes 737312 | tf_op jit(solution)/shard_map/ppermute | solution.py:28
  44.6 3.0 %collective-permute-start.2 = (bf16[320,640]{1,0:T(8,128)(2,1)S(1)}, bf16[320,640]{1,0:T(8,128)(2,1)S(1)}, u32[]{:S(2)}, u32[]{:S(2)}) collective-permute-start(bf16[320,640]{1,0:T(8,128)(2,1)S(1)} %reshape.82), channel_id=1, source_target_pairs={{0,2},{2,0},{1,3},{3,1},{4,6},{6,4},{5,7},{7,5},{8,10},{10,8},{9,1... | collective-permute-start | bytes 1228808 | tf_op jit(solution)/shard_map/ppermute | solution.py:28
  47.6 8.7 %collective-permute-done.2 = bf16[320,640]{1,0:T(8,128)(2,1)S(1)} collective-permute-done((bf16[320,640]{1,0:T(8,128)(2,1)S(1)}, bf16[320,640]{1,0:T(8,128)(2,1)S(1)}, u32[]{:S(2)}, u32[]{:S(2)}) %collective-permute-start.2) | collective-permute-done | bytes 409632 | tf_op jit(solution)/shard_map/ppermute | solution.py:28
  58.4 1.5 collective-permute-start.4
  59.9 2.7 %collective-permute-start.6 = (bf16[3,320,384]{2,1,0:T(8,128)(2,1)S(1)}, bf16[3,320,384]{2,1,0:T(8,128)(2,1)}, u32[]{:S(2)}, u32[]{:S(2)}) collective-permute-start(bf16[3,320,384]{2,1,0:T(8,128)(2,1)S(1)} %collective-permute-done.1.refs_2_), channel_id=1, source_target_pairs={{0,224},{32,0},{64,32},{96,64},{128,96},{160,128},{192,160},{224,1... | collective-permute-start | bytes 2211848 | tf_op jit(solution)/shard_map/ppermute | solution.py:28
  62.6 2.1 %copy-done.1 = bf16[384,5120]{1,0:T(8,128)(2,1)S(1)} copy-done((bf16[384,5120]{1,0:T(8,128)(2,1)S(1)}, bf16[384,5120]{1,0:T(8,128)(2,1)}, u32[]{:S(2)}) %copy-start.1) | copy-done | bytes 3932184
  64.7 3.1 %shard_map.113 = bf16[8,192,640]{2,1,0:T(8,128)(2,1)} custom-call(s32[1]{0:T(128)} %bitcast.1.core, bf16[384,5120]{1,0:T(8,128)(2,1)S(1)} %copy-done.1), custom_call_target="tpu_custom_call" | custom-call | tf_op jit(solution)/shard_map/pallas_call | solution.py:139
  67.8 9.1 %collective-permute-done.5.refs_3_ = bf16[3,320,384]{2,1,0:T(8,128)(2,1)S(1)} collective-permute-done((bf16[3,320,384]{2,1,0:T(8,128)(2,1)S(1)}, bf16[3,320,384]{2,1,0:T(8,128)(2,1)S(1)}, u32[]{:S(2)}, u32[]{:S(2)}) %collective-permute-start.5) | collective-permute-done | bytes 737312 | tf_op jit(solution)/shard_map/ppermute | solution.py:28
  76.9 2.0 collective-permute-start.7
  82.5 2.1 %collective-permute-start.10 = (bf16[2,160,640]{2,1,0:T(8,128)(2,1)S(1)}, bf16[2,160,640]{2,1,0:T(8,128)(2,1)S(1)}, u32[]{:S(2)}, u32[]{:S(2)}) collective-permute-start(bf16[2,160,640]{2,1,0:T(8,128)(2,1)S(1)} %slice.19), channel_id=1, source_target_pairs={{0,12},{4,0},{8,4},{12,8},{1,13},{5,1},{9,5},{13,9},{2,14},{6,2},{... | collective-permute-start | bytes 1228808 | tf_op jit(solution)/shard_map/ppermute | solution.py:28
  84.6 4.7 %collective-permute-done.9 = bf16[2,160,640]{2,1,0:T(8,128)(2,1)S(1)} collective-permute-done((bf16[2,160,640]{2,1,0:T(8,128)(2,1)S(1)}, bf16[2,160,640]{2,1,0:T(8,128)(2,1)S(1)}, u32[]{:S(2)}, u32[]{:S(2)}) %collective-permute-start.9) | collective-permute-done | bytes 409632 | tf_op jit(solution)/shard_map/ppermute | solution.py:28
  89.7 3.3 %collective-permute-done.7.refs_5_ = bf16[3,320,384]{2,1,0:T(8,128)(2,1)S(1)} collective-permute-done((bf16[3,320,384]{2,1,0:T(8,128)(2,1)S(1)}, bf16[3,320,384]{2,1,0:T(8,128)(2,1)S(1)}, u32[]{:S(2)}, u32[]{:S(2)}) %collective-permute-start.7) | collective-permute-done | bytes 737312 | tf_op jit(solution)/shard_map/ppermute | solution.py:28
  94.0 5.4 %all-to-all-start.3 = ((bf16[8,192,640]{2,1,0:T(8,128)(2,1)}), bf16[8,192,640]{2,1,0:T(8,128)(2,1)}, u32[]{:S(2)}, u32[]{:S(2)}) async-start(bf16[8,192,640]{2,1,0:T(8,128)(2,1)} %shard_map.113), calls=%async_computation.3 | async-start | bytes 3932160 | tf_op jit(solution)/shard_map/all_to_all | solution.py:19
  99.5 2.5 %collective-permute-start.11 = (bf16[3,160,384]{2,1,0:T(8,128)(2,1)S(1)}, bf16[3,160,384]{2,1,0:T(8,128)(2,1)S(1)}, u32[]{:S(2)}, u32[]{:S(2)}) collective-permute-start(bf16[3,160,384]{2,1,0:T(8,128)(2,1)S(1)} %slice.20), channel_id=1, source_target_pairs={{0,32},{32,64},{64,96},{96,128},{128,160},{160,192},{192,224},{224... | collective-permute-start | bytes 1105928 | tf_op jit(solution)/shard_map/ppermute | solution.py:28
  102.6 2.9 %pad_maximum_fusion.x_any = bf16[8,320,640]{2,1,0:T(8,128)(2,1)S(1)} fusion(bf16[2,320,640]{2,1,0:T(8,128)(2,1)} %collective-permute-done.3, bf16[2,160,640]{2,1,0:T(8,128)(2,1)S(1)} %collective-permute-done.10, bf16[2,160,640]{2,1,0:T(8,128)(2,1)S(1)} %collective-permute-done.9, bf16[2,320,640]{2,1,0:T(8,128)(2,1)} %collective-permute-done.4, ...), kind=kLoop, calls=%fused_computation.4 | loop fusion | flops 16384000 | bytes 6553600 | tf_op jit(solution)/shard_map/concatenate | solution.py:179
  105.5 1.6 collective-permute-done.11.refs_7_
  107.1 1.9 collective-permute-done.12.refs_8_
  109.1 10.3 %shard_map.114 = (f32[320,1152]{1,0:T(8,128)S(1)}, bf16[320,1152]{1,0:T(8,128)(2,1)}) custom-call(s32[8]{0:T(128)S(1)} %xor_add_fusion.slots, s32[1]{0:T(128)} %bitcast.1.core, bf16[8,320,640]{2,1,0:T(8,128)(2,1)S(1)} %pad_maximum_fusion.x_any, bf16[3,320,384]{2,1,0:T(8,128)(2,1)S(1)} %bitcast.31, bf16[3,320,384]{2,1,0:T(8,128)(2,1)S(1)} %copy-done.5, ...), custom_call_target="tpu_custom_call" | custom-call | tf_op jit(solution)/shard_map/pallas_call | solution.py:74
  119.4 5.0 %collective-permute-start.13 = (bf16[320,1152]{1,0:T(8,128)(2,1)}, bf16[320,1152]{1,0:T(8,128)(2,1)S(1)}, u32[]{:S(2)}, u32[]{:S(2)}) collective-permute-start(bf16[320,1152]{1,0:T(8,128)(2,1)} %get-tuple-element.34), channel_id=1, source_target_pairs={{0,16},{16,0},{1,17},{17,1},{2,18},{18,2},{3,19},{19,3},{4,20},{20... | collective-permute-start | bytes 2211848 | tf_op jit(solution)/shard_map/ppermute | solution.py:28
  124.5 3.3 %collective-permute-start.14 = (bf16[8,192,640]{2,1,0:T(8,128)(2,1)}, bf16[8,192,640]{2,1,0:T(8,128)(2,1)}, u32[]{:S(2)}, u32[]{:S(2)}) collective-permute-start(bf16[8,192,640]{2,1,0:T(8,128)(2,1)} %all-to-all-done.3), channel_id=1, source_target_pairs={{0,16},{16,0},{1,17},{17,1},{2,18},{18,2},{3,19},{19,3},{4,20},{20... | collective-permute-start | bytes 5898248 | tf_op jit(solution)/shard_map/ppermute | solution.py:28
  127.9 1.4 shard_map.115
  129.3 18.4 %all_to_all.25 = bf16[16,20,384]{2,1,0:T(8,128)(2,1)S(1)} all-to-all(bf16[16,20,384]{2,1,0:T(8,128)(2,1)S(1)} %shard_map.115), channel_id=1, replica_groups=mesh['z'=8,'core'=2,'x'=4,'yhi'=2,'dp'=2] {'z','core'}, dimensions={0} | all-to-all | bytes 491520 | tf_op jit(solution)/shard_map/all_to_all | solution.py:19
  147.8 1.5 broadcast_in_dim.37
  149.2 4.4 %all-to-all-start.2 = ((bf16[8,320,384]{2,1,0:T(8,128)(2,1)}), bf16[8,320,384]{2,1,0:T(8,128)(2,1)S(1)}, u32[]{:S(2)}, u32[]{:S(2)}) async-start(bf16[8,320,384]{2,1,0:T(8,128)(2,1)} %broadcast_in_dim.37), calls=%async_computation.2 | async-start | bytes 3932160 | tf_op jit(solution)/shard_map/all_to_all | solution.py:19
  153.8 4.5 %broadcast_select_fusion.1 = (bf16[8,192,640]{2,1,0:T(8,128)(2,1)}, bf16[8,192,640]{2,1,0:T(8,128)(2,1)}) fusion(bf16[8,192,640]{2,1,0:T(8,128)(2,1)} %all-to-all-done.3, bf16[8,192,640]{2,1,0:T(8,128)(2,1)} %collective-permute-done.14, pred[]{:T(512)S(6)} %eq.60), kind=kLoop, calls=%fused_computation.6 | loop fusion | flops 1966080 | bytes 7864321 | tf_op jit(solution)/shard_map/jit(_where)/select_n | solution.py:184
  158.3 25.3 %all-to-all-done.2 = bf16[8,320,384]{2,1,0:T(8,128)(2,1)S(1)} async-done(((bf16[8,320,384]{2,1,0:T(8,128)(2,1)}), bf16[8,320,384]{2,1,0:T(8,128)(2,1)S(1)}, u32[]{:S(2)}, u32[]{:S(2)}) %all-to-all-start.2) | async-done | bytes 1966112 | tf_op jit(solution)/shard_map/all_to_all | solution.py:19
  183.5 3.9 %fusion = f32[320,640,1]{1,0,2:T(8,128)S(1)} fusion(bf16[8,320,384]{2,1,0:T(8,128)(2,1)S(1)} %all-to-all-done.2, bf16[8,192,640]{2,1,0:T(8,128)(2,1)} %get-tuple-element.37, bf16[8,192,640]{2,1,0:T(8,128)(2,1)} %get-tuple-element.36), kind=kOutput, calls=%fused_computation | convolution fusion | flops 1266155520 | bytes 6717440 | tf_op jit(solution)/shard_map/dot_general | solution.py:195
  188.3 4.2 %all-to-all-start.4 = ((f32[32,2,672]{2,1,0:T(2,128)}), f32[32,2,672]{2,1,0:T(2,128)S(1)}, u32[]{:S(2)}, u32[]{:S(2)}) async-start(f32[32,2,672]{2,1,0:T(2,128)} %broadcast_in_dim.38), calls=%async_computation.4 | async-start | bytes 393216 | tf_op jit(solution)/shard_map/all_to_all | solution.py:19
  193.6 9.1 %all-to-all-done.4 = f32[32,2,672]{2,1,0:T(2,128)S(1)} async-done(((f32[32,2,672]{2,1,0:T(2,128)}), f32[32,2,672]{2,1,0:T(2,128)S(1)}, u32[]{:S(2)}, u32[]{:S(2)}) %all-to-all-start.4) | async-done | bytes 172064 | tf_op jit(solution)/shard_map/all_to_all | solution.py:19
  (71 shorter events, 16.7 us)
Async XLA Ops:
  0.6 191.9 %copy-start = (f32[32,640]{1,0:T(8,128)S(1)}, f32[32,640]{1,0:T(8,128)}, u32[]{:S(2)}) copy-start(f32[32,640]{1,0:T(8,128)} %param.17) | copy-start | bytes 245764
  0.6 14.0 %copy-start.2 = (bf16[320,3,384]{2,0,1:T(8,128)(2,1)S(1)}, bf16[320,3,384]{2,0,1:T(8,128)(2,1)}, u32[]{:S(2)}) copy-start(bf16[320,3,384]{2,0,1:T(8,128)(2,1)} %param.13) | copy-start | bytes 2211844
  4.7 26.6 %all-to-all-start = ((bf16[16,20,640]{2,1,0:T(8,128)(2,1)}), bf16[16,20,640]{2,1,0:T(8,128)(2,1)S(1)}, u32[]{:S(2)}, u32[]{:S(2)}) async-start(bf16[16,20,640]{2,1,0:T(8,128)(2,1)} %copy.18), calls=%async_computation | async-start | bytes 983040 | tf_op jit(solution)/shard_map/all_to_all | solution.py:19
  14.7 29.9 %collective-permute-start = (bf16[3,320,384]{2,1,0:T(8,128)(2,1)S(1)}, bf16[3,320,384]{2,1,0:T(8,128)(2,1)S(1)}, u32[]{:S(2)}, u32[]{:S(2)}) collective-permute-start(bf16[3,320,384]{2,1,0:T(8,128)(2,1)S(1)} %bitcast.29), channel_id=1, source_target_pairs={{0,32},{32,64},{64,96},{96,128},{128,160},{160,192},{192,224},{224... | collective-permute-start | bytes 2211848 | tf_op jit(solution)/shard_map/ppermute | solution.py:28
  16.1 28.4 %collective-permute-start.1 = (bf16[3,320,384]{2,1,0:T(8,128)(2,1)S(1)}, bf16[3,320,384]{2,1,0:T(8,128)(2,1)S(1)}, u32[]{:S(2)}, u32[]{:S(2)}) collective-permute-start(bf16[3,320,384]{2,1,0:T(8,128)(2,1)S(1)} %bitcast.30), channel_id=1, source_target_pairs={{0,224},{32,0},{64,32},{96,64},{128,96},{160,128},{192,160},{224,1... | collective-permute-start | bytes 2211848 | tf_op jit(solution)/shard_map/ppermute | solution.py:28
  44.6 23.2 %copy-start.4 = (bf16[3,320,384]{2,1,0:T(8,128)(2,1)}, bf16[3,320,384]{2,1,0:T(8,128)(2,1)S(1)}, u32[]{:S(2)}) copy-start(bf16[3,320,384]{2,1,0:T(8,128)(2,1)S(1)} %collective-permute-done.refs_1_) | copy-start | bytes 2211844
  44.6 23.2 %copy-start.6 = (bf16[3,320,384]{2,1,0:T(8,128)(2,1)}, bf16[3,320,384]{2,1,0:T(8,128)(2,1)S(1)}, u32[]{:S(2)}) copy-start(bf16[3,320,384]{2,1,0:T(8,128)(2,1)S(1)} %collective-permute-done.1.refs_2_) | copy-start | bytes 2211844
  44.6 11.7 %collective-permute-start.2 = (bf16[320,640]{1,0:T(8,128)(2,1)S(1)}, bf16[320,640]{1,0:T(8,128)(2,1)S(1)}, u32[]{:S(2)}, u32[]{:S(2)}) collective-permute-start(bf16[320,640]{1,0:T(8,128)(2,1)S(1)} %reshape.82), channel_id=1, source_target_pairs={{0,2},{2,0},{1,3},{3,1},{4,6},{6,4},{5,7},{7,5},{8,10},{10,8},{9,1... | collective-permute-start | bytes 1228808 | tf_op jit(solution)/shard_map/ppermute | solution.py:28
  57.2 19.7 %collective-permute-start.3 = (bf16[2,320,640]{2,1,0:T(8,128)(2,1)}, bf16[2,320,640]{2,1,0:T(8,128)(2,1)}, u32[]{:S(2)}, u32[]{:S(2)}) collective-permute-start(bf16[2,320,640]{2,1,0:T(8,128)(2,1)} %pad_maximum_fusion.1), channel_id=1, source_target_pairs={{0,4},{4,8},{8,12},{12,0},{1,5},{5,9},{9,13},{13,1},{2,6},{6,10},{... | collective-permute-start | bytes 2457608 | tf_op jit(solution)/shard_map/ppermute | solution.py:28
  58.4 18.4 %collective-permute-start.4 = (bf16[2,320,640]{2,1,0:T(8,128)(2,1)}, bf16[2,320,640]{2,1,0:T(8,128)(2,1)}, u32[]{:S(2)}, u32[]{:S(2)}) collective-permute-start(bf16[2,320,640]{2,1,0:T(8,128)(2,1)} %pad_maximum_fusion.1), channel_id=1, source_target_pairs={{0,12},{4,0},{8,4},{12,8},{1,13},{5,1},{9,5},{13,9},{2,14},{6,2},{... | collective-permute-start | bytes 2457608 | tf_op jit(solution)/shard_map/ppermute | solution.py:28
  59.9 17.0 %collective-permute-start.5 = (bf16[3,320,384]{2,1,0:T(8,128)(2,1)S(1)}, bf16[3,320,384]{2,1,0:T(8,128)(2,1)S(1)}, u32[]{:S(2)}, u32[]{:S(2)}) collective-permute-start(bf16[3,320,384]{2,1,0:T(8,128)(2,1)S(1)} %collective-permute-done.refs_1_), channel_id=1, source_target_pairs={{0,32},{32,64},{64,96},{96,128},{128,160},{160,192},{192,224},{224... | collective-permute-start | bytes 2211848 | tf_op jit(solution)/shard_map/ppermute | solution.py:28
  59.9 17.0 %collective-permute-start.6 = (bf16[3,320,384]{2,1,0:T(8,128)(2,1)S(1)}, bf16[3,320,384]{2,1,0:T(8,128)(2,1)}, u32[]{:S(2)}, u32[]{:S(2)}) collective-permute-start(bf16[3,320,384]{2,1,0:T(8,128)(2,1)S(1)} %collective-permute-done.1.refs_2_), channel_id=1, source_target_pairs={{0,224},{32,0},{64,32},{96,64},{128,96},{160,128},{192,160},{224,1... | collective-permute-start | bytes 2211848 | tf_op jit(solution)/shard_map/ppermute | solution.py:28
  67.8 31.6 %copy-start.13 = (s32[8]{0:T(128)S(1)}, s32[8]{0:T(128)}, u32[]{:S(2)}) copy-start(s32[8]{0:T(128)} %constant.53.clone) | copy-start | bytes 100
  76.9 25.2 %copy-start.8 = (bf16[3,320,384]{2,1,0:T(8,128)(2,1)}, bf16[3,320,384]{2,1,0:T(8,128)(2,1)S(1)}, u32[]{:S(2)}) copy-start(bf16[3,320,384]{2,1,0:T(8,128)(2,1)S(1)} %collective-permute-done.5.refs_3_) | copy-start | bytes 2211844
  76.9 16.1 %collective-permute-start.7 = (bf16[3,320,384]{2,1,0:T(8,128)(2,1)S(1)}, bf16[3,320,384]{2,1,0:T(8,128)(2,1)S(1)}, u32[]{:S(2)}, u32[]{:S(2)}) collective-permute-start(bf16[3,320,384]{2,1,0:T(8,128)(2,1)S(1)} %collective-permute-done.5.refs_3_), channel_id=1, source_target_pairs={{0,32},{32,64},{64,96},{96,128},{128,160},{160,192},{192,224},{224... | collective-permute-start | bytes 2211848 | tf_op jit(solution)/shard_map/ppermute | solution.py:28
  78.9 15.1 %collective-permute-start.8 = (bf16[3,320,384]{2,1,0:T(8,128)(2,1)}, bf16[3,320,384]{2,1,0:T(8,128)(2,1)S(1)}, u32[]{:S(2)}, u32[]{:S(2)}) collective-permute-start(bf16[3,320,384]{2,1,0:T(8,128)(2,1)} %collective-permute-done.6.refs_4_), channel_id=1, source_target_pairs={{0,224},{32,0},{64,32},{96,64},{128,96},{160,128},{192,160},{224,1... | collective-permute-start | bytes 2211848 | tf_op jit(solution)/shard_map/ppermute | solution.py:28
  80.7 8.5 %collective-permute-start.9 = (bf16[2,160,640]{2,1,0:T(8,128)(2,1)S(1)}, bf16[2,160,640]{2,1,0:T(8,128)(2,1)S(1)}, u32[]{:S(2)}, u32[]{:S(2)}) collective-permute-start(bf16[2,160,640]{2,1,0:T(8,128)(2,1)S(1)} %slice.18), channel_id=1, source_target_pairs={{0,4},{4,8},{8,12},{12,0},{1,5},{5,9},{9,13},{13,1},{2,6},{6,10},{... | collective-permute-start | bytes 1228808 | tf_op jit(solution)/shard_map/ppermute | solution.py:28
  82.5 7.2 %collective-permute-start.10 = (bf16[2,160,640]{2,1,0:T(8,128)(2,1)S(1)}, bf16[2,160,640]{2,1,0:T(8,128)(2,1)S(1)}, u32[]{:S(2)}, u32[]{:S(2)}) collective-permute-start(bf16[2,160,640]{2,1,0:T(8,128)(2,1)S(1)} %slice.19), channel_id=1, source_target_pairs={{0,12},{4,0},{8,4},{12,8},{1,13},{5,1},{9,5},{13,9},{2,14},{6,2},{... | collective-permute-start | bytes 1228808 | tf_op jit(solution)/shard_map/ppermute | solution.py:28
  94.0 30.5 %all-to-all-start.3 = ((bf16[8,192,640]{2,1,0:T(8,128)(2,1)}), bf16[8,192,640]{2,1,0:T(8,128)(2,1)}, u32[]{:S(2)}, u32[]{:S(2)}) async-start(bf16[8,192,640]{2,1,0:T(8,128)(2,1)} %shard_map.113), calls=%async_computation.3 | async-start | bytes 3932160 | tf_op jit(solution)/shard_map/all_to_all | solution.py:19
  99.5 7.7 %collective-permute-start.11 = (bf16[3,160,384]{2,1,0:T(8,128)(2,1)S(1)}, bf16[3,160,384]{2,1,0:T(8,128)(2,1)S(1)}, u32[]{:S(2)}, u32[]{:S(2)}) collective-permute-start(bf16[3,160,384]{2,1,0:T(8,128)(2,1)S(1)} %slice.20), channel_id=1, source_target_pairs={{0,32},{32,64},{64,96},{96,128},{128,160},{160,192},{192,224},{224... | collective-permute-start | bytes 1105928 | tf_op jit(solution)/shard_map/ppermute | solution.py:28
  102.1 7.0 %copy-start.3 = (bf16[320,3,384]{2,0,1:T(8,128)(2,1)S(1)}, bf16[320,3,384]{2,0,1:T(8,128)(2,1)}, u32[]{:S(2)}) copy-start(bf16[320,3,384]{2,0,1:T(8,128)(2,1)} %param.13) | copy-start | bytes 2211844
  102.1 6.9 %copy-start.5 = (bf16[3,320,384]{2,1,0:T(8,128)(2,1)S(1)}, bf16[3,320,384]{2,1,0:T(8,128)(2,1)}, u32[]{:S(2)}) copy-start(bf16[3,320,384]{2,1,0:T(8,128)(2,1)} %copy-done.4) | copy-start | bytes 2211844
  102.1 6.9 %copy-start.7 = (bf16[3,320,384]{2,1,0:T(8,128)(2,1)S(1)}, bf16[3,320,384]{2,1,0:T(8,128)(2,1)}, u32[]{:S(2)}) copy-start(bf16[3,320,384]{2,1,0:T(8,128)(2,1)} %copy-done.6) | copy-start | bytes 2211844
  102.1 6.9 %collective-permute-start.12 = (bf16[3,160,384]{2,1,0:T(8,128)(2,1)S(1)}, bf16[3,160,384]{2,1,0:T(8,128)(2,1)S(1)}, u32[]{:S(2)}, u32[]{:S(2)}) collective-permute-start(bf16[3,160,384]{2,1,0:T(8,128)(2,1)S(1)} %slice.21), channel_id=1, source_target_pairs={{0,224},{32,0},{64,32},{96,64},{128,96},{160,128},{192,160},{224,1... | collective-permute-start | bytes 1105928 | tf_op jit(solution)/shard_map/ppermute | solution.py:28
  102.6 6.5 %copy-start.9 = (bf16[3,320,384]{2,1,0:T(8,128)(2,1)S(1)}, bf16[3,320,384]{2,1,0:T(8,128)(2,1)}, u32[]{:S(2)}) copy-start(bf16[3,320,384]{2,1,0:T(8,128)(2,1)} %copy-done.8) | copy-start | bytes 2211844
  119.4 8.5 %collective-permute-start.13 = (bf16[320,1152]{1,0:T(8,128)(2,1)}, bf16[320,1152]{1,0:T(8,128)(2,1)S(1)}, u32[]{:S(2)}, u32[]{:S(2)}) collective-permute-start(bf16[320,1152]{1,0:T(8,128)(2,1)} %get-tuple-element.34), channel_id=1, source_target_pairs={{0,16},{16,0},{1,17},{17,1},{2,18},{18,2},{3,19},{19,3},{4,20},{20... | collective-permute-start | bytes 2211848 | tf_op jit(solution)/shard_map/ppermute | solution.py:28
  124.5 29.3 %collective-permute-start.14 = (bf16[8,192,640]{2,1,0:T(8,128)(2,1)}, bf16[8,192,640]{2,1,0:T(8,128)(2,1)}, u32[]{:S(2)}, u32[]{:S(2)}) collective-permute-start(bf16[8,192,640]{2,1,0:T(8,128)(2,1)} %all-to-all-done.3), channel_id=1, source_target_pairs={{0,16},{16,0},{1,17},{17,1},{2,18},{18,2},{3,19},{19,3},{4,20},{20... | collective-permute-start | bytes 5898248 | tf_op jit(solution)/shard_map/ppermute | solution.py:28
  147.7 5.9 %copy-start.15 = (s32[2,1]{0,1:T(1,128)S(1)}, s32[2,1]{0,1:T(1,128)}, u32[]{:S(2)}) copy-start(s32[2,1]{0,1:T(1,128)} %param.15) | copy-start | bytes 28
  149.2 34.3 %all-to-all-start.2 = ((bf16[8,320,384]{2,1,0:T(8,128)(2,1)}), bf16[8,320,384]{2,1,0:T(8,128)(2,1)S(1)}, u32[]{:S(2)}, u32[]{:S(2)}) async-start(bf16[8,320,384]{2,1,0:T(8,128)(2,1)} %broadcast_in_dim.37), calls=%async_computation.2 | async-start | bytes 3932160 | tf_op jit(solution)/shard_map/all_to_all | solution.py:19
  183.5 9.1 %copy-start.10 = (bf16[2,1,160,640]{3,2,1,0:T(8,128)(2,1)S(1)}, bf16[2,1,160,640]{3,2,1,0:T(8,128)(2,1)}, u32[]{:S(2)}) copy-start(bf16[2,1,160,640]{3,2,1,0:T(8,128)(2,1)} %param.10) | copy-start | bytes 1228804
  183.5 9.1 %copy-start.12 = (bf16[640]{0:T(1024)(128)(2,1)S(1)}, bf16[640]{0:T(1024)(128)(2,1)}, u32[]{:S(2)}) copy-start(bf16[640]{0:T(1024)(128)(2,1)} %param.12) | copy-start | bytes 3844
  188.3 14.5 %all-to-all-start.4 = ((f32[32,2,672]{2,1,0:T(2,128)}), f32[32,2,672]{2,1,0:T(2,128)S(1)}, u32[]{:S(2)}, u32[]{:S(2)}) async-start(f32[32,2,672]{2,1,0:T(2,128)} %broadcast_in_dim.38), calls=%async_computation.4 | async-start | bytes 393216 | tf_op jit(solution)/shard_map/all_to_all | solution.py:19
  (3 other events, 11.9 us)

commit v4 on v3

--- a/solution.py
+++ b/solution.py
@@ -10,6 +10,7 @@
 
 HS = 128
 MASKED = -1e30
+LENT = 2
 FRAME = ("z", "core")
 MP = ("x", "yhi")
 SMALL = pltpu.CompilerParams(vmem_limit_bytes=16 * 1024 * 1024)
@@ -28,33 +29,46 @@
     return lax.ppermute(x, axis, [(i, (i + by) % n) for i in range(n)])
 
 
-def qkv_kernel(slots, core, x_any, *refs):
-    n = len(refs) - 7
-    shards, (kept, sent, x_ref, w_ref, acc, x_sem, w_sem) = refs[:n], refs[n:]
+def qkv_kernel(places, slots, core, *refs):
+    n_x, n_w = 5, len(refs) - 12
+    (both, right, top, low, left), shards = refs[:n_x], refs[n_x : n_x + n_w]
+    kept, sent, x_ref, w_ref, acc, x_sem, w_sem = refs[n_x + n_w :]
+    rows, full = x_ref.shape[1], x_ref.shape[2] // 2
     copies, at = [], 0
-    for j in range(x_ref.shape[0]):
-        copies.append([pltpu.make_async_copy(x_any.at[slots[j]], x_ref.at[j], x_sem.at[j])])
-        full = x_ref.shape[2] // 2
-        row = 0
-        while row < full:
-            depth = shards[at].shape[1]
-            target = w_ref.at[:, pl.ds(j * full + row, depth)]
-            copies[j].append(pltpu.make_async_copy(shards[at], target, w_sem.at[at]))
+    for j, pieces in enumerate(places):
+        far, own = slots[j] >> 1, slots[j] & 1
+        for k, source in ((0, both), (1, right), (3, left)):
+
+            @pl.when(far == k)
+            def _():
+                pltpu.make_async_copy(source.at[own], x_ref.at[j], x_sem.at[j]).start()
+
+        @pl.when(far == 2)
+        def _():
+            half = rows // 2
+            pltpu.make_async_copy(top.at[own], x_ref.at[j, pl.ds(0, half)], x_sem.at[j]).start()
+            pltpu.make_async_copy(low.at[own], x_ref.at[j, pl.ds(half, half)], x_sem.at[j]).start()
+
+        copies.append([])
+        row = j * full
+        for index, part in pieces:
+            source = shards[index] if part is None else shards[index].at[part]
+            depth = source.shape[1]
+            copy = pltpu.make_async_copy(source, w_ref.at[:, pl.ds(row, depth)], w_sem.at[at])
+            copy.start()
+            copies[j].append(copy)
             row += depth
             at += 1
-    for group in copies:
-        for copy in group:
-            copy.start()
-    rows, half = x_ref.shape[1], x_ref.shape[2] // 2
-    for j in range(0, x_ref.shape[0], 2):
-        for copy in copies[j] + copies[j + 1]:
-            copy.wait()
+    for j in range(0, len(places), 2):
+        for i in (j, j + 1):
+            pltpu.make_async_copy(both.at[0], x_ref.at[i], x_sem.at[i]).wait()
+            for copy in copies[i]:
+                copy.wait()
         a, b = x_ref[j], x_ref[j + 1]
-        low = jnp.concatenate([a[:, :half], b[:, :half]], axis=1)
-        high = jnp.concatenate([a[:, half:], b[:, half:]], axis=1)
-        x = jnp.concatenate([low, high], axis=0)
-        depth = pl.ds(j * half, 2 * half)
-        w = jnp.concatenate([w_ref[i, depth] for i in range(3)], axis=1)
+        first = jnp.concatenate([a[:, :full], b[:, :full]], axis=1)
+        second = jnp.concatenate([a[:, full:], b[:, full:]], axis=1)
+        x = jnp.concatenate([first, second], axis=0)
+        w = jnp.concatenate([w_ref[i, pl.ds(j * full, 2 * full)] for i in range(3)], axis=1)
         part = jnp.dot(x, w, preferred_element_type=jnp.float32)
         if j == 0:
             acc[...] = part
@@ -65,29 +79,33 @@
     sent[...] = acc[pl.ds((1 - me) * rows, rows)].astype(jnp.bfloat16)
 
 
-def project(x, shards, slots, core):
-    n, rows, width = x.shape
-    heads = 3 * shards[0].shape[2]
+def project(features, shards, places, slots, core):
+    _, rows, width = features[0].shape
+    n, heads = len(places), shards[0].shape[-1]
     smem = pl.BlockSpec(memory_space=pltpu.SMEM)
     vmem = pl.BlockSpec(memory_space=pltpu.VMEM)
     hbm = pl.BlockSpec(memory_space=pl.ANY)
+
+    def kernel(*refs):
+        qkv_kernel(places, *refs)
+
     return pl.pallas_call(
-        qkv_kernel,
-        in_specs=[smem, smem] + [hbm] * (1 + len(shards)),
+        kernel,
+        in_specs=[smem, smem] + [hbm] * (len(features) + len(shards)),
         out_specs=(vmem, vmem),
         out_shape=(
-            jax.ShapeDtypeStruct((rows, heads), jnp.float32),
-            jax.ShapeDtypeStruct((rows, heads), jnp.bfloat16),
+            jax.ShapeDtypeStruct((rows, 3 * heads), jnp.float32),
+            jax.ShapeDtypeStruct((rows, 3 * heads), jnp.bfloat16),
         ),
         scratch_shapes=[
             pltpu.VMEM((n, rows, width), jnp.bfloat16),
-            pltpu.VMEM((3, n * width // 2, heads // 3), jnp.bfloat16),
-            pltpu.VMEM((2 * rows, heads), jnp.float32),
+            pltpu.VMEM((3, n * width // 2, heads), jnp.bfloat16),
+            pltpu.VMEM((2 * rows, 3 * heads), jnp.float32),
             pltpu.SemaphoreType.DMA((n,)),
-            pltpu.SemaphoreType.DMA((len(shards),)),
+            pltpu.SemaphoreType.DMA((sum(len(p) for p in places),)),
         ],
         compiler_params=pltpu.CompilerParams(vmem_limit_bytes=28 * 1024 * 1024),
-    )(slots, core, x, *shards)
+    )(slots, core, *features, *shards)
 
 
 def attend(q, k, v, bias):
@@ -158,25 +176,47 @@
     z, core = lax.axis_index("z"), lax.axis_index("core")
     core1 = core.reshape(1).astype(jnp.int32)
     xin = jnp.where(token_mask[..., None] == 1, mask_embed, tokens).reshape(rows, width)
-    mine = xin.reshape(zs, 2, rows // frames, cores, depth).transpose(0, 3, 2, 1, 4)
+    lent = LENT * depth // 10
+    kept_rows = depth - lent
+    dp = lax.axis_index("dp")
+    rolled = xin.reshape(rows, cores, depth)
+    rolled = jnp.concatenate([rolled[..., lent:], rolled[..., :lent]], axis=2)
+    mine = jnp.where(dp == 0, xin, rolled.reshape(rows, width))
+    mine = mine.reshape(zs, 2, rows // frames, cores, depth).transpose(0, 3, 2, 1, 4)
     mine = exchange(mine.reshape(frames, rows // frames, 2 * depth), FRAME).reshape(rows, 2 * depth)
 
-    own = w_qkv.transpose(1, 0, 2)
+    def lend(*pieces):
+        start = dp * (kept_rows - lent)
+        cut = [lax.dynamic_slice_in_dim(p, start, lent, 1) for p in pieces]
+        return shift(jnp.stack(cut), "dp", 1)
+
+    whole = w_qkv.transpose(1, 0, 2)
+    own = lax.dynamic_slice_in_dim(whole, dp * lent, kept_rows, 1)
+    rest = lax.dynamic_slice_in_dim(whole, (1 - dp) * kept_rows, lent, 1)
     up1, down1 = shift(own, "z", 1), shift(own, "z", -1)
     mine, up1, down1 = lax.optimization_barrier((mine, up1, down1))
     up2, down2 = shift(up1, "z", 1), shift(down1, "z", -1)
     both = jnp.stack([mine, shift(mine, "yhi", 1)])
-    both, w_out = lax.optimization_barrier((both, w_out))
+    both, w_out, up2, down2, up1, down1 = lax.optimization_barrier(
+        (both, w_out, up2, down2, up1, down1)
+    )
     left, right = shift(both, "x", 1), shift(both, "x", -1)
+    up3, down3 = shift(up2, "z", 1), shift(down2, "z", -1)
+    lent1, lent2 = lend(up1, down1), lend(up2, down2)
     blocks = column_blocks(w_out, core1, width)
-    left, right, up2, down2, blocks = lax.optimization_barrier((left, right, up2, down2, blocks))
-    up3, down3 = shift(up2, "z", 1), shift(down2, "z", -1)
+    left, right, up3, down3, lent1, lent2, blocks = lax.optimization_barrier(
+        (left, right, up3, down3, lent1, lent2, blocks)
+    )
     middle = rows // 2
-    far = (shift(left[:, :middle], "x", 1), shift(right[:, middle:], "x", -1))
-    up3, down3, far, blocks = lax.optimization_barrier((up3, down3, far, blocks))
-    up4 = shift(up3[:, : depth // 2], "z", 1)
-    down4 = shift(down3[:, depth // 2 :], "z", -1)
-    features = jnp.concatenate([both, right, jnp.concatenate(far, axis=1), left])
+    top, low = shift(left[:, :middle], "x", 1), shift(right[:, middle:], "x", -1)
+    up4 = shift(up3[:, : kept_rows // 2], "z", 1)
+    down4 = shift(down3[:, kept_rows // 2 :], "z", -1)
+    lent3 = lend(up3, down3)
+    top, low, up4, down4, lent3, blocks = lax.optimization_barrier(
+        (top, low, up4, down4, lent3, blocks)
+    )
+    cut = jnp.where(dp == 0, up4[:, :lent], down4[:, kept_rows // 2 - lent :])
+    lent4 = shift(cut, "dp", 1)
 
     half = exchange(blocks, MP)
     other_half = shift(half, "core", 1)
@@ -187,8 +227,12 @@
     x, yhi = lax.axis_index("x"), lax.axis_index("yhi")
     shard = (z + jnp.array([0, zs - 1, 1, zs - 2, 2, zs - 3, 3, zs - 4], jnp.int32)) & (zs - 1)
     slots = (2 * (((shard >> 1) - x) & (mp // 2 - 1)) + ((shard & 1) ^ yhi)).astype(jnp.int32)
-    shards = [own, up1, down1, up2, down2, up3, down3, up4, down4]
-    kept, sent = project(features, shards, slots, core1)
+    shards = [own, rest, up1, down1, lent1, up2, down2, lent2, up3, down3, lent3, up4, down4, lent4]
+    places = [[(0, None), (1, None)]]
+    for k in (2, 5, 8):
+        places += [[(k, None), (k + 2, 0)], [(k + 1, None), (k + 2, 1)]]
+    places.append([(11, None), (12, None), (13, None)])
+    kept, sent = project((both, right, top, low, left), shards, places, slots, core1)
     attn = attention(kept, shift(sent, "core", 1), frames)
     attn = exchange(attn, FRAME).reshape(rows, heads)
     all_heads = from_everyone(attn, MP)

time: 204 us -> 229 us (1.12)
  local copies, waits for them, and re-layouts: 8.89 us -> 27 us
  starting transfers between devices: 52 us -> 54.6 us
    unnamed x33 -> x51, local copies, waits for them, and re-layouts: 2.19 us -> 15.6 us
    all_to_all x4, starting transfers between devices: 24 us -> 26.8 us  [exchange(): return lax.all_to_all(x, axis, split_axis=0, concat_axis=0, tiled=True)]
    another operation x2 -> x5, local copies, waits for them, and re-layouts: 0.89 us -> 3.32 us  [the longest x4 2.91 us: lend(): return shift(jnp.stack(cut), 'dp', 1)]
    concatenate x1, other arithmetic: 2.94 us -> 0.54 us  [body(): rolled = jnp.concatenate([rolled[..., lent:], rolled[..., :lent]], axis=2)]
    ppermute x15 -> x19, waiting for transfers between devices: 43.9 us -> 45.4 us  [shift(): return lax.ppermute(x, axis, [(i, (i + by) % n) for i in range(n)])]
    ppermute x15 -> x19, starting transfers between devices: 28 us -> 27.8 us  [shift(): return lax.ppermute(x, axis, [(i, (i + by) % n) for i in range(n)])]
  transfers between devices with their start and end apart: 19 -> 23, of which waited for: 13 -> 13; matrix products, arithmetic and copies ran while one was open for 6% -> 7% of each run, Pallas kernels for 7% -> 7%
where the time goes in v4:
time: 229 us; the launch traced here: 228 us
  waiting for transfers between devices  92.7 us (40%)
  starting transfers between devices  54.6 us (24%)
  local copies, waits for them, and re-layouts  27 us (12%)
  blocking collectives  18.3 us (8%)
  Pallas kernels  15 us (7%)
  other arithmetic  13.5 us (6%)
  matrix products  6 us (3%)
    all_to_all x4, waiting for transfers between devices, exchange(): return lax.all_to_all(x, axis, split_axis=0, concat_axis=0, tiled=True)  47.3 us
    ppermute x19, waiting for transfers between devices, shift(): return lax.ppermute(x, axis, [(i, (i + by) % n) for i in range(n)])  45.4 us
    ppermute x19, starting transfers between devices, shift(): return lax.ppermute(x, axis, [(i, (i + by) % n) for i in range(n)])  27.8 us
    all_to_all x4, starting transfers between devices, exchange(): return lax.all_to_all(x, axis, split_axis=0, concat_axis=0, tiled=True)  26.8 us
    all_to_all x1, blocking collectives, exchange(): return lax.all_to_all(x, axis, split_axis=0, concat_axis=0, tiled=True)  18.3 us
    unnamed x51, local copies, waits for them, and re-layouts  15.6 us
    pallas_call x1, Pallas kernels, project(): pl.pallas_call(kernel, in_specs=[smem, smem] + [hbm] * (len(features) + l...  10.6 us
  transfers between devices with their start and end apart: 23, of which 13 were waited for; matrix products, arithmetic and copies ran while one was open for 7% of the time, Pallas kernels for 7%

profile of v4, /device:TPU:1, one launch (start us, length us, event | category | flops | bytes accessed | tf_op | source)
XLA Modules:
  0.0 228.1 jit_solution(11273193523462962610)
XLA Ops:
  7.3 10.0 %all-to-all-start = ((bf16[16,20,640]{2,1,0:T(8,128)(2,1)}), bf16[16,20,640]{2,1,0:T(8,128)(2,1)S(1)}, u32[]{:S(2)}, u32[]{:S(2)}) async-start(bf16[16,20,640]{2,1,0:T(8,128)(2,1)} %reshape.100), calls=%async_computation | async-start | bytes 983040 | tf_op jit(solution)/shard_map/all_to_all | solution.py:20
  17.3 1.5 collective-permute-start
  20.1 13.8 %all-to-all-done = bf16[16,20,640]{2,1,0:T(8,128)(2,1)S(1)} async-done(((bf16[16,20,640]{2,1,0:T(8,128)(2,1)}), bf16[16,20,640]{2,1,0:T(8,128)(2,1)S(1)}, u32[]{:S(2)}, u32[]{:S(2)}) %all-to-all-start) | async-done | bytes 409632 | tf_op jit(solution)/shard_map/all_to_all | solution.py:20
  34.7 9.3 %collective-permute-done.refs_9_ = bf16[3,256,384]{2,1,0:T(8,128)(2,1)S(1)} collective-permute-done((bf16[3,256,384]{2,1,0:T(8,128)(2,1)S(1)}, bf16[3,256,384]{2,1,0:T(8,128)(2,1)S(1)}, u32[]{:S(2)}, u32[]{:S(2)}) %collective-permute-start) | collective-permute-done | bytes 589856 | tf_op jit(solution)/shard_map/ppermute | solution.py:29
  44.1 2.7 %collective-permute-start.4 = (bf16[3,256,384]{2,1,0:T(8,128)(2,1)S(1)}, bf16[3,256,384]{2,1,0:T(8,128)(2,1)}, u32[]{:S(2)}, u32[]{:S(2)}) collective-permute-start(bf16[3,256,384]{2,1,0:T(8,128)(2,1)S(1)} %collective-permute-done.1.refs_10_), channel_id=1, source_target_pairs={{0,224},{32,0},{64,32},{96,64},{128,96},{160,128},{192,160},{224,1... | collective-permute-start | bytes 1769480 | tf_op jit(solution)/shard_map/ppermute | solution.py:29
  46.8 2.9 %collective-permute-start.2 = (bf16[320,640]{1,0:T(8,128)(2,1)}, bf16[320,640]{1,0:T(8,128)(2,1)S(1)}, u32[]{:S(2)}, u32[]{:S(2)}) collective-permute-start(bf16[320,640]{1,0:T(8,128)(2,1)} %reshape.93), channel_id=1, source_target_pairs={{0,2},{2,0},{1,3},{3,1},{4,6},{6,4},{5,7},{7,5},{8,10},{10,8},{9,1... | collective-permute-start | bytes 1228808 | tf_op jit(solution)/shard_map/ppermute | solution.py:29
  49.7 8.3 %collective-permute-done.2 = bf16[320,640]{1,0:T(8,128)(2,1)S(1)} collective-permute-done((bf16[320,640]{1,0:T(8,128)(2,1)}, bf16[320,640]{1,0:T(8,128)(2,1)S(1)}, u32[]{:S(2)}, u32[]{:S(2)}) %collective-permute-start.2) | collective-permute-done | bytes 409632 | tf_op jit(solution)/shard_map/ppermute | solution.py:29
  61.3 1.5 collective-permute-start.6
  63.7 1.5 collective-permute-start.9
  66.0 1.9 collective-permute-start.8
  70.5 1.4 collective-permute-start.10
  71.9 2.1 copy-done.1
  74.0 3.1 %shard_map.113 = bf16[8,192,640]{2,1,0:T(8,128)(2,1)} custom-call(s32[1]{0:T(128)} %bitcast.1.core.refs_1_, bf16[384,5120]{1,0:T(8,128)(2,1)S(1)} %copy-done.1), custom_call_target="tpu_custom_call" | custom-call | tf_op jit(solution)/shard_map/pallas_call | solution.py:157
  82.9 1.7 collective-permute-start.12
  84.6 1.9 collective-permute-start.13
  87.3 1.6 collective-permute-start.15
  88.9 2.8 %collective-permute-done.13.refs_18_ = bf16[3,128,384]{2,1,0:T(8,128)(2,1)} collective-permute-done((bf16[3,128,384]{2,1,0:T(8,128)(2,1)S(1)}, bf16[3,128,384]{2,1,0:T(8,128)(2,1)}, u32[]{:S(2)}, u32[]{:S(2)}) %collective-permute-start.13) | collective-permute-done | bytes 294944 | tf_op jit(solution)/shard_map/ppermute | solution.py:29
  95.7 5.4 %all-to-all-start.3 = ((bf16[8,192,640]{2,1,0:T(8,128)(2,1)}), bf16[8,192,640]{2,1,0:T(8,128)(2,1)}, u32[]{:S(2)}, u32[]{:S(2)}) async-start(bf16[8,192,640]{2,1,0:T(8,128)(2,1)} %shard_map.113), calls=%async_computation.3 | async-start | bytes 3932160 | tf_op jit(solution)/shard_map/all_to_all | solution.py:20
  101.0 1.7 slice_select_fusion
  104.4 19.8 %collective-permute-done.16.refs_20_ = bf16[3,64,384]{2,1,0:T(8,128)(2,1)} collective-permute-done((bf16[3,64,384]{2,1,0:T(8,128)(2,1)}, bf16[3,64,384]{2,1,0:T(8,128)(2,1)}, u32[]{:S(2)}, u32[]{:S(2)}) %collective-permute-start.16) | collective-permute-done | bytes 147488 | tf_op jit(solution)/shard_map/ppermute | solution.py:29
  130.9 10.6 %shard_map.114 = (f32[320,1152]{1,0:T(8,128)S(1)}, bf16[320,1152]{1,0:T(8,128)(2,1)}) custom-call(s32[8]{0:T(128)S(1)} %copy-done.16, s32[1]{0:T(128)} %bitcast.1.core.refs_1_, bf16[2,320,640]{2,1,0:T(8,128)(2,1)S(1)} %pad_maximum_fusion.refs_2_, bf16[2,320,640]{2,1,0:T(8,128)(2,1)} %collective-permute-done.6.refs_3_, bf16[2,160,640]{2,1,0:T(8,128)(2,1)S(1)} %copy-done.9, ...), custom_call_target="tpu_custom_call" | custom-call | tf_op jit(solution)/shard_map/pallas_call | solution.py:92
  142.6 3.4 %collective-permute-start.17 = (bf16[320,1152]{1,0:T(8,128)(2,1)}, bf16[320,1152]{1,0:T(8,128)(2,1)S(1)}, u32[]{:S(2)}, u32[]{:S(2)}) collective-permute-start(bf16[320,1152]{1,0:T(8,128)(2,1)} %get-tuple-element.48), channel_id=1, source_target_pairs={{0,16},{16,0},{1,17},{17,1},{2,18},{18,2},{3,19},{19,3},{4,20},{20... | collective-permute-start | bytes 2211848 | tf_op jit(solution)/shard_map/ppermute | solution.py:29
  146.2 1.8 collective-permute-done.17.other_ref
  148.0 1.4 copy-done.3
  150.8 18.3 %all_to_all.25 = bf16[16,20,384]{2,1,0:T(8,128)(2,1)S(1)} all-to-all(bf16[16,20,384]{2,1,0:T(8,128)(2,1)S(1)} %shard_map.115), channel_id=1, replica_groups=mesh['z'=8,'core'=2,'x'=4,'yhi'=2,'dp'=2] {'z','core'}, dimensions={0} | all-to-all | bytes 491520 | tf_op jit(solution)/shard_map/all_to_all | solution.py:20
  169.1 1.5 broadcast_in_dim.37
  170.6 7.3 %all-to-all-start.2 = ((bf16[8,320,384]{2,1,0:T(8,128)(2,1)}), bf16[8,320,384]{2,1,0:T(8,128)(2,1)S(1)}, u32[]{:S(2)}, u32[]{:S(2)}) async-start(bf16[8,320,384]{2,1,0:T(8,128)(2,1)} %broadcast_in_dim.37), calls=%async_computation.2 | async-start | bytes 3932160 | tf_op jit(solution)/shard_map/all_to_all | solution.py:20
  178.1 4.5 %broadcast_select_fusion.1 = (bf16[8,192,640]{2,1,0:T(8,128)(2,1)}, bf16[8,192,640]{2,1,0:T(8,128)(2,1)}) fusion(bf16[8,192,640]{2,1,0:T(8,128)(2,1)} %all-to-all-done.3, bf16[8,192,640]{2,1,0:T(8,128)(2,1)} %collective-permute-done.18, pred[]{:T(512)S(6)} %eq.65), kind=kLoop, calls=%fused_computation.5 | loop fusion | flops 1966080 | bytes 7864321 | tf_op jit(solution)/shard_map/jit(_where)/select_n | solution.py:224
  182.5 25.3 %all-to-all-done.2 = bf16[8,320,384]{2,1,0:T(8,128)(2,1)S(1)} async-done(((bf16[8,320,384]{2,1,0:T(8,128)(2,1)}), bf16[8,320,384]{2,1,0:T(8,128)(2,1)S(1)}, u32[]{:S(2)}, u32[]{:S(2)}) %all-to-all-start.2) | async-done | bytes 1966112 | tf_op jit(solution)/shard_map/all_to_all | solution.py:20
  207.8 3.9 %fusion = f32[320,640,1]{1,0,2:T(8,128)S(1)} fusion(bf16[8,320,384]{2,1,0:T(8,128)(2,1)S(1)} %all-to-all-done.2, bf16[8,192,640]{2,1,0:T(8,128)(2,1)} %get-tuple-element.51, bf16[8,192,640]{2,1,0:T(8,128)(2,1)} %get-tuple-element.50), kind=kOutput, calls=%fused_computation | convolution fusion | flops 1266155520 | bytes 6717440 | tf_op jit(solution)/shard_map/dot_general | solution.py:239
  212.6 4.2 %all-to-all-start.4 = ((f32[32,2,672]{2,1,0:T(2,128)}), f32[32,2,672]{2,1,0:T(2,128)S(1)}, u32[]{:S(2)}, u32[]{:S(2)}) async-start(f32[32,2,672]{2,1,0:T(2,128)} %broadcast_in_dim.38), calls=%async_computation.4 | async-start | bytes 393216 | tf_op jit(solution)/shard_map/all_to_all | solution.py:20
  218.8 8.3 %all-to-all-done.4 = f32[32,2,672]{2,1,0:T(2,128)S(1)} async-done(((f32[32,2,672]{2,1,0:T(2,128)}), f32[32,2,672]{2,1,0:T(2,128)S(1)}, u32[]{:S(2)}, u32[]{:S(2)}) %all-to-all-start.4) | async-done | bytes 172064 | tf_op jit(solution)/shard_map/all_to_all | solution.py:20
  (110 shorter events, 42.1 us)
Async XLA Ops:
  0.6 16.6 %copy-start = (bf16[320,3,384]{2,0,1:T(8,128)(2,1)S(1)}, bf16[320,3,384]{2,0,1:T(8,128)(2,1)}, u32[]{:S(2)}) copy-start(bf16[320,3,384]{2,0,1:T(8,128)(2,1)} %param.13) | copy-start | bytes 2211844
  7.3 26.6 %all-to-all-start = ((bf16[16,20,640]{2,1,0:T(8,128)(2,1)}), bf16[16,20,640]{2,1,0:T(8,128)(2,1)S(1)}, u32[]{:S(2)}, u32[]{:S(2)}) async-start(bf16[16,20,640]{2,1,0:T(8,128)(2,1)} %reshape.100), calls=%async_computation | async-start | bytes 983040 | tf_op jit(solution)/shard_map/all_to_all | solution.py:20
  17.3 26.7 %collective-permute-start = (bf16[3,256,384]{2,1,0:T(8,128)(2,1)S(1)}, bf16[3,256,384]{2,1,0:T(8,128)(2,1)S(1)}, u32[]{:S(2)}, u32[]{:S(2)}) collective-permute-start(bf16[3,256,384]{2,1,0:T(8,128)(2,1)S(1)} %dynamic-slice_bitcast_fusion.refs_7_), channel_id=1, source_target_pairs={{0,32},{32,64},{64,96},{96,128},{128,160},{160,192},{192,224},{224... | collective-permute-start | bytes 1769480 | tf_op jit(solution)/shard_map/ppermute | solution.py:29
  18.8 25.2 %collective-permute-start.1 = (bf16[3,256,384]{2,1,0:T(8,128)(2,1)S(1)}, bf16[3,256,384]{2,1,0:T(8,128)(2,1)S(1)}, u32[]{:S(2)}, u32[]{:S(2)}) collective-permute-start(bf16[3,256,384]{2,1,0:T(8,128)(2,1)S(1)} %dynamic-slice_bitcast_fusion.refs_7_), channel_id=1, source_target_pairs={{0,224},{32,0},{64,32},{96,64},{128,96},{160,128},{192,160},{224,1... | collective-permute-start | bytes 1769480 | tf_op jit(solution)/shard_map/ppermute | solution.py:29
  44.0 19.7 %copy-start.4 = (bf16[3,256,384]{2,1,0:T(8,128)(2,1)}, bf16[3,256,384]{2,1,0:T(8,128)(2,1)S(1)}, u32[]{:S(2)}) copy-start(bf16[3,256,384]{2,1,0:T(8,128)(2,1)S(1)} %collective-permute-done.refs_9_) | copy-start | bytes 1769476
  44.0 16.0 %copy-start.6 = (bf16[3,256,384]{2,1,0:T(8,128)(2,1)}, bf16[3,256,384]{2,1,0:T(8,128)(2,1)S(1)}, u32[]{:S(2)}) copy-start(bf16[3,256,384]{2,1,0:T(8,128)(2,1)S(1)} %collective-permute-done.1.refs_10_) | copy-start | bytes 1769476
  44.0 16.0 %collective-permute-start.3 = (bf16[3,256,384]{2,1,0:T(8,128)(2,1)S(1)}, bf16[3,256,384]{2,1,0:T(8,128)(2,1)}, u32[]{:S(2)}, u32[]{:S(2)}) collective-permute-start(bf16[3,256,384]{2,1,0:T(8,128)(2,1)S(1)} %collective-permute-done.refs_9_), channel_id=1, source_target_pairs={{0,32},{32,64},{64,96},{96,128},{128,160},{160,192},{192,224},{224... | collective-permute-start | bytes 1769480 | tf_op jit(solution)/shard_map/ppermute | solution.py:29
  44.1 15.9 %collective-permute-start.4 = (bf16[3,256,384]{2,1,0:T(8,128)(2,1)S(1)}, bf16[3,256,384]{2,1,0:T(8,128)(2,1)}, u32[]{:S(2)}, u32[]{:S(2)}) collective-permute-start(bf16[3,256,384]{2,1,0:T(8,128)(2,1)S(1)} %collective-permute-done.1.refs_10_), channel_id=1, source_target_pairs={{0,224},{32,0},{64,32},{96,64},{128,96},{160,128},{192,160},{224,1... | collective-permute-start | bytes 1769480 | tf_op jit(solution)/shard_map/ppermute | solution.py:29
  46.8 11.2 %collective-permute-start.2 = (bf16[320,640]{1,0:T(8,128)(2,1)}, bf16[320,640]{1,0:T(8,128)(2,1)S(1)}, u32[]{:S(2)}, u32[]{:S(2)}) collective-permute-start(bf16[320,640]{1,0:T(8,128)(2,1)} %reshape.93), channel_id=1, source_target_pairs={{0,2},{2,0},{1,3},{3,1},{4,6},{6,4},{5,7},{7,5},{8,10},{10,8},{9,1... | collective-permute-start | bytes 1228808 | tf_op jit(solution)/shard_map/ppermute | solution.py:29
  60.0 18.7 %collective-permute-start.5 = (bf16[2,320,640]{2,1,0:T(8,128)(2,1)S(1)}, bf16[2,320,640]{2,1,0:T(8,128)(2,1)S(1)}, u32[]{:S(2)}, u32[]{:S(2)}) collective-permute-start(bf16[2,320,640]{2,1,0:T(8,128)(2,1)S(1)} %pad_maximum_fusion.refs_2_), channel_id=1, source_target_pairs={{0,4},{4,8},{8,12},{12,0},{1,5},{5,9},{9,13},{13,1},{2,6},{6,10},{... | collective-permute-start | bytes 2457608 | tf_op jit(solution)/shard_map/ppermute | solution.py:29
  61.3 17.4 %collective-permute-start.6 = (bf16[2,320,640]{2,1,0:T(8,128)(2,1)S(1)}, bf16[2,320,640]{2,1,0:T(8,128)(2,1)}, u32[]{:S(2)}, u32[]{:S(2)}) collective-permute-start(bf16[2,320,640]{2,1,0:T(8,128)(2,1)S(1)} %pad_maximum_fusion.refs_2_), channel_id=1, source_target_pairs={{0,12},{4,0},{8,4},{12,8},{1,13},{5,1},{9,5},{13,9},{2,14},{6,2},{... | collective-permute-start | bytes 2457608 | tf_op jit(solution)/shard_map/ppermute | solution.py:29
  63.7 6.1 %collective-permute-start.9 = (bf16[2,3,64,384]{3,2,1,0:T(8,128)(2,1)S(1)}, bf16[2,3,64,384]{3,2,1,0:T(8,128)(2,1)S(1)}, u32[]{:S(2)}, u32[]{:S(2)}) collective-permute-start(bf16[2,3,64,384]{3,2,1,0:T(8,128)(2,1)S(1)} %pad_maximum_fusion.2), channel_id=1, source_target_pairs={{0,1},{1,0},{2,3},{3,2},{4,5},{5,4},{6,7},{7,6},{8,9},{9,8},{10,11... | collective-permute-start | bytes 884744 | tf_op jit(solution)/shard_map/ppermute | solution.py:29
  65.2 13.2 %collective-permute-start.7 = (bf16[3,256,384]{2,1,0:T(8,128)(2,1)}, bf16[3,256,384]{2,1,0:T(8,128)(2,1)S(1)}, u32[]{:S(2)}, u32[]{:S(2)}) collective-permute-start(bf16[3,256,384]{2,1,0:T(8,128)(2,1)} %collective-permute-done.3.refs_12_), channel_id=1, source_target_pairs={{0,32},{32,64},{64,96},{96,128},{128,160},{160,192},{192,224},{224... | collective-permute-start | bytes 1769480 | tf_op jit(solution)/shard_map/ppermute | solution.py:29
  66.0 12.7 %collective-permute-start.8 = (bf16[3,256,384]{2,1,0:T(8,128)(2,1)}, bf16[3,256,384]{2,1,0:T(8,128)(2,1)}, u32[]{:S(2)}, u32[]{:S(2)}) collective-permute-start(bf16[3,256,384]{2,1,0:T(8,128)(2,1)} %collective-permute-done.4.refs_13_), channel_id=1, source_target_pairs={{0,224},{32,0},{64,32},{96,64},{128,96},{160,128},{192,160},{224,1... | collective-permute-start | bytes 1769480 | tf_op jit(solution)/shard_map/ppermute | solution.py:29
  70.5 6.6 %collective-permute-start.10 = (bf16[2,3,64,384]{3,2,1,0:T(8,128)(2,1)}, bf16[2,3,64,384]{3,2,1,0:T(8,128)(2,1)}, u32[]{:S(2)}, u32[]{:S(2)}) collective-permute-start(bf16[2,3,64,384]{3,2,1,0:T(8,128)(2,1)} %pad_maximum_fusion.3), channel_id=1, source_target_pairs={{0,1},{1,0},{2,3},{3,2},{4,5},{5,4},{6,7},{7,6},{8,9},{9,8},{10,11... | collective-permute-start | bytes 884744 | tf_op jit(solution)/shard_map/ppermute | solution.py:29
  80.7 13.4 %collective-permute-start.11 = (bf16[2,160,640]{2,1,0:T(8,128)(2,1)S(1)}, bf16[2,160,640]{2,1,0:T(8,128)(2,1)S(1)}, u32[]{:S(2)}, u32[]{:S(2)}) collective-permute-start(bf16[2,160,640]{2,1,0:T(8,128)(2,1)S(1)} %slice.32), channel_id=1, source_target_pairs={{0,4},{4,8},{8,12},{12,0},{1,5},{5,9},{9,13},{13,1},{2,6},{6,10},{... | collective-permute-start | bytes 1228808 | tf_op jit(solution)/shard_map/ppermute | solution.py:29
  82.9 12.0 %collective-permute-start.12 = (bf16[2,160,640]{2,1,0:T(8,128)(2,1)S(1)}, bf16[2,160,640]{2,1,0:T(8,128)(2,1)S(1)}, u32[]{:S(2)}, u32[]{:S(2)}) collective-permute-start(bf16[2,160,640]{2,1,0:T(8,128)(2,1)S(1)} %slice.33), channel_id=1, source_target_pairs={{0,12},{4,0},{8,4},{12,8},{1,13},{5,1},{9,5},{13,9},{2,14},{6,2},{... | collective-permute-start | bytes 1228808 | tf_op jit(solution)/shard_map/ppermute | solution.py:29
  84.6 7.1 %collective-permute-start.13 = (bf16[3,128,384]{2,1,0:T(8,128)(2,1)S(1)}, bf16[3,128,384]{2,1,0:T(8,128)(2,1)}, u32[]{:S(2)}, u32[]{:S(2)}) collective-permute-start(bf16[3,128,384]{2,1,0:T(8,128)(2,1)S(1)} %slice.34), channel_id=1, source_target_pairs={{0,32},{32,64},{64,96},{96,128},{128,160},{160,192},{192,224},{224... | collective-permute-start | bytes 884744 | tf_op jit(solution)/shard_map/ppermute | solution.py:29
  86.5 5.9 %collective-permute-start.14 = (bf16[3,128,384]{2,1,0:T(8,128)(2,1)S(1)}, bf16[3,128,384]{2,1,0:T(8,128)(2,1)}, u32[]{:S(2)}, u32[]{:S(2)}) collective-permute-start(bf16[3,128,384]{2,1,0:T(8,128)(2,1)S(1)} %slice.35), channel_id=1, source_target_pairs={{0,224},{32,0},{64,32},{96,64},{128,96},{160,128},{192,160},{224,1... | collective-permute-start | bytes 884744 | tf_op jit(solution)/shard_map/ppermute | solution.py:29
  87.3 6.1 %collective-permute-start.15 = (bf16[2,3,64,384]{3,2,1,0:T(8,128)(2,1)S(1)}, bf16[2,3,64,384]{3,2,1,0:T(8,128)(2,1)S(1)}, u32[]{:S(2)}, u32[]{:S(2)}) collective-permute-start(bf16[2,3,64,384]{3,2,1,0:T(8,128)(2,1)S(1)} %pad_maximum_fusion.4), channel_id=1, source_target_pairs={{0,1},{1,0},{2,3},{3,2},{4,5},{5,4},{6,7},{7,6},{8,9},{9,8},{10,11... | collective-permute-start | bytes 884744 | tf_op jit(solution)/shard_map/ppermute | solution.py:29
  95.7 50.3 %all-to-all-start.3 = ((bf16[8,192,640]{2,1,0:T(8,128)(2,1)}), bf16[8,192,640]{2,1,0:T(8,128)(2,1)}, u32[]{:S(2)}, u32[]{:S(2)}) async-start(bf16[8,192,640]{2,1,0:T(8,128)(2,1)} %shard_map.113), calls=%async_computation.3 | async-start | bytes 3932160 | tf_op jit(solution)/shard_map/all_to_all | solution.py:20
  102.7 21.5 %collective-permute-start.16 = (bf16[3,64,384]{2,1,0:T(8,128)(2,1)}, bf16[3,64,384]{2,1,0:T(8,128)(2,1)}, u32[]{:S(2)}, u32[]{:S(2)}) collective-permute-start(bf16[3,64,384]{2,1,0:T(8,128)(2,1)} %slice_select_fusion), channel_id=1, source_target_pairs={{0,1},{1,0},{2,3},{3,2},{4,5},{5,4},{6,7},{7,6},{8,9},{9,8},{10,11... | collective-permute-start | bytes 442376 | tf_op jit(solution)/shard_map/ppermute | solution.py:29
  142.6 5.5 %collective-permute-start.17 = (bf16[320,1152]{1,0:T(8,128)(2,1)}, bf16[320,1152]{1,0:T(8,128)(2,1)S(1)}, u32[]{:S(2)}, u32[]{:S(2)}) collective-permute-start(bf16[320,1152]{1,0:T(8,128)(2,1)} %get-tuple-element.48), channel_id=1, source_target_pairs={{0,16},{16,0},{1,17},{17,1},{2,18},{18,2},{3,19},{19,3},{4,20},{20... | collective-permute-start | bytes 2211848 | tf_op jit(solution)/shard_map/ppermute | solution.py:29
  146.0 32.1 %collective-permute-start.18 = (bf16[8,192,640]{2,1,0:T(8,128)(2,1)}, bf16[8,192,640]{2,1,0:T(8,128)(2,1)}, u32[]{:S(2)}, u32[]{:S(2)}) collective-permute-start(bf16[8,192,640]{2,1,0:T(8,128)(2,1)} %all-to-all-done.3), channel_id=1, source_target_pairs={{0,16},{16,0},{1,17},{17,1},{2,18},{18,2},{3,19},{19,3},{4,20},{20... | collective-permute-start | bytes 5898248 | tf_op jit(solution)/shard_map/ppermute | solution.py:29
  170.6 7.3 %copy-start.23 = (f32[8,32]{1,0:T(8,128)S(1)}, f32[8,32]{1,0:T(8,128)}, u32[]{:S(2)}) copy-start(f32[8,32]{1,0:T(8,128)} %param.16) | copy-start | bytes 3076
  170.6 7.3 %copy-start.24 = (s32[2,1]{0,1:T(1,128)S(1)}, s32[2,1]{0,1:T(1,128)}, u32[]{:S(2)}) copy-start(s32[2,1]{0,1:T(1,128)} %param.15) | copy-start | bytes 28
  170.6 37.2 %all-to-all-start.2 = ((bf16[8,320,384]{2,1,0:T(8,128)(2,1)}), bf16[8,320,384]{2,1,0:T(8,128)(2,1)S(1)}, u32[]{:S(2)}, u32[]{:S(2)}) async-start(bf16[8,320,384]{2,1,0:T(8,128)(2,1)} %broadcast_in_dim.37), calls=%async_computation.2 | async-start | bytes 3932160 | tf_op jit(solution)/shard_map/all_to_all | solution.py:20
  207.8 3.9 %copy-start.19 = (bf16[2,1,160,640]{3,2,1,0:T(8,128)(2,1)S(1)}, bf16[2,1,160,640]{3,2,1,0:T(8,128)(2,1)}, u32[]{:S(2)}) copy-start(bf16[2,1,160,640]{3,2,1,0:T(8,128)(2,1)} %param.18) | copy-start | bytes 1228804
  207.8 10.0 %copy-start.21 = (pred[2,1,160]{2,0,1:T(4,128)(4,1)S(1)}, pred[2,1,160]{2,0,1:T(4,128)(4,1)}, u32[]{:S(2)}) copy-start(pred[2,1,160]{2,0,1:T(4,128)(4,1)} %copy-done.20) | copy-start | bytes 964
  207.8 10.0 %copy-start.22 = (bf16[640]{0:T(1024)(128)(2,1)S(1)}, bf16[640]{0:T(1024)(128)(2,1)}, u32[]{:S(2)}) copy-start(bf16[640]{0:T(1024)(128)(2,1)} %param.12) | copy-start | bytes 3844
  211.7 6.1 %copy-start.17 = (bf16[2,1,160,640]{3,2,1,0:T(8,128)(2,1)S(1)}, bf16[2,1,160,640]{3,2,1,0:T(8,128)(2,1)}, u32[]{:S(2)}) copy-start(bf16[2,1,160,640]{3,2,1,0:T(8,128)(2,1)} %param.10) | copy-start | bytes 1228804
  212.6 14.5 %all-to-all-start.4 = ((f32[32,2,672]{2,1,0:T(2,128)}), f32[32,2,672]{2,1,0:T(2,128)S(1)}, u32[]{:S(2)}, u32[]{:S(2)}) async-start(f32[32,2,672]{2,1,0:T(2,128)} %broadcast_in_dim.38), calls=%async_computation.4 | async-start | bytes 393216 | tf_op jit(solution)/shard_map/all_to_all | solution.py:20
  (16 other events, 15.5 us)

commit v5 on v4

--- a/solution.py
+++ b/solution.py
@@ -84,7 +84,7 @@
     n, heads = len(places), shards[0].shape[-1]
     smem = pl.BlockSpec(memory_space=pltpu.SMEM)
     vmem = pl.BlockSpec(memory_space=pltpu.VMEM)
-    hbm = pl.BlockSpec(memory_space=pl.ANY)
+    hbm = pl.BlockSpec(memory_space=pltpu.HBM)
 
     def kernel(*refs):
         qkv_kernel(places, *refs)
@@ -194,29 +194,26 @@
     own = lax.dynamic_slice_in_dim(whole, dp * lent, kept_rows, 1)
     rest = lax.dynamic_slice_in_dim(whole, (1 - dp) * kept_rows, lent, 1)
     up1, down1 = shift(own, "z", 1), shift(own, "z", -1)
-    mine, up1, down1 = lax.optimization_barrier((mine, up1, down1))
+    both = jnp.stack([mine, shift(mine, "yhi", 1)])
+    both, w_out, up1, down1 = lax.optimization_barrier((both, w_out, up1, down1))
+    left, right = shift(both, "x", 1), shift(both, "x", -1)
     up2, down2 = shift(up1, "z", 1), shift(down1, "z", -1)
-    both = jnp.stack([mine, shift(mine, "yhi", 1)])
-    both, w_out, up2, down2, up1, down1 = lax.optimization_barrier(
-        (both, w_out, up2, down2, up1, down1)
-    )
-    left, right = shift(both, "x", 1), shift(both, "x", -1)
-    up3, down3 = shift(up2, "z", 1), shift(down2, "z", -1)
-    lent1, lent2 = lend(up1, down1), lend(up2, down2)
+    lent1 = lend(up1, down1)
     blocks = column_blocks(w_out, core1, width)
-    left, right, up3, down3, lent1, lent2, blocks = lax.optimization_barrier(
-        (left, right, up3, down3, lent1, lent2, blocks)
+    left, right, up2, down2, lent1, blocks = lax.optimization_barrier(
+        (left, right, up2, down2, lent1, blocks)
     )
     middle = rows // 2
     top, low = shift(left[:, :middle], "x", 1), shift(right[:, middle:], "x", -1)
+    up3, down3 = shift(up2, "z", 1), shift(down2, "z", -1)
+    lent2 = lend(up2, down2)
+    up3, down3, top, low, lent2 = lax.optimization_barrier((up3, down3, top, low, lent2))
     up4 = shift(up3[:, : kept_rows // 2], "z", 1)
     down4 = shift(down3[:, kept_rows // 2 :], "z", -1)
     lent3 = lend(up3, down3)
-    top, low, up4, down4, lent3, blocks = lax.optimization_barrier(
-        (top, low, up4, down4, lent3, blocks)
-    )
     cut = jnp.where(dp == 0, up4[:, :lent], down4[:, kept_rows // 2 - lent :])
     lent4 = shift(cut, "dp", 1)
+    lent3, lent4, blocks = lax.optimization_barrier((lent3, lent4, blocks))
 
     half = exchange(blocks, MP)
     other_half = shift(half, "core", 1)

time: 229 us -> 212 us (0.926)
  waiting for transfers between devices: 92.7 us -> 75.8 us
  starting transfers between devices: 54.6 us -> 58.2 us
  blocking collectives: 18.3 us -> 15.5 us
  other arithmetic: 13.5 us -> 11.2 us
    ppermute x19, waiting for transfers between devices: 45.4 us -> 28.5 us  [shift(): return lax.ppermute(x, axis, [(i, (i + by) % n) for i in range(n)])]
    ppermute x19, starting transfers between devices: 27.8 us -> 30.9 us  [shift(): return lax.ppermute(x, axis, [(i, (i + by) % n) for i in range(n)])]
    all_to_all x1, blocking collectives: 18.3 us -> 15.5 us  [exchange(): return lax.all_to_all(x, axis, split_axis=0, concat_axis=0, tiled=True)]
    unnamed x51 -> x59, local copies, waits for them, and re-layouts: 15.6 us -> 18.4 us
  transfers between devices with their start and end apart: 23 -> 23, of which waited for: 13 -> 12; matrix products, arithmetic and copies ran while one was open for 7% -> 7% of each run, Pallas kernels for 7% -> 7%
where the time goes in v5:
time: 212 us; the launch traced here: 211 us
  waiting for transfers between devices  75.8 us (36%)
  starting transfers between devices  58.2 us (27%)
  local copies, waits for them, and re-layouts  28.1 us (13%)
  blocking collectives  15.5 us (7%)
  Pallas kernels  15.1 us (7%)
  other arithmetic  11.2 us (5%)
  matrix products  6 us (3%)
    all_to_all x4, waiting for transfers between devices, exchange(): return lax.all_to_all(x, axis, split_axis=0, concat_axis=0, tiled=True)  47.3 us
    ppermute x19, starting transfers between devices, shift(): return lax.ppermute(x, axis, [(i, (i + by) % n) for i in range(n)])  30.9 us
    ppermute x19, waiting for transfers between devices, shift(): return lax.ppermute(x, axis, [(i, (i + by) % n) for i in range(n)])  28.5 us
    all_to_all x4, starting transfers between devices, exchange(): return lax.all_to_all(x, axis, split_axis=0, concat_axis=0, tiled=True)  27.2 us
    unnamed x59, local copies, waits for them, and re-layouts  18.4 us
    all_to_all x1, blocking collectives, exchange(): return lax.all_to_all(x, axis, split_axis=0, concat_axis=0, tiled=True)  15.5 us
    pallas_call x1, Pallas kernels, project(): pl.pallas_call(kernel, in_specs=[smem, smem] + [hbm] * (len(features) + l...  10.6 us
    select_n x1, other arithmetic, body(): jnp.where(core == 0, half, other_half)  4.45 us
  transfers between devices with their start and end apart: 23, of which 12 were waited for; matrix products, arithmetic and copies ran while one was open for 7% of the time, Pallas kernels for 7%

profile of v5, /device:TPU:1, one launch (start us, length us, event | category | flops | bytes accessed | tf_op | source)
XLA Modules:
  0.0 210.9 jit_solution(16871613454567145480)
XLA Ops:
  7.3 10.0 %all-to-all-start = ((bf16[16,20,640]{2,1,0:T(8,128)(2,1)}), bf16[16,20,640]{2,1,0:T(8,128)(2,1)S(1)}, u32[]{:S(2)}, u32[]{:S(2)}) async-start(bf16[16,20,640]{2,1,0:T(8,128)(2,1)} %reshape.100), calls=%async_computation | async-start | bytes 983040 | tf_op jit(solution)/shard_map/all_to_all | solution.py:20
  17.3 1.5 collective-permute-start.1
  20.1 13.8 %all-to-all-done = bf16[16,20,640]{2,1,0:T(8,128)(2,1)S(1)} async-done(((bf16[16,20,640]{2,1,0:T(8,128)(2,1)}), bf16[16,20,640]{2,1,0:T(8,128)(2,1)S(1)}, u32[]{:S(2)}, u32[]{:S(2)}) %all-to-all-start) | async-done | bytes 409632 | tf_op jit(solution)/shard_map/all_to_all | solution.py:20
  34.0 3.0 %collective-permute-start = (bf16[320,640]{1,0:T(8,128)(2,1)S(1)}, bf16[320,640]{1,0:T(8,128)(2,1)}, u32[]{:S(2)}, u32[]{:S(2)}) collective-permute-start(bf16[320,640]{1,0:T(8,128)(2,1)S(1)} %reshape.93), channel_id=1, source_target_pairs={{0,2},{2,0},{1,3},{3,1},{4,6},{6,4},{5,7},{7,5},{8,10},{10,8},{9,1... | collective-permute-start | bytes 1228808 | tf_op jit(solution)/shard_map/ppermute | solution.py:29
  37.1 9.2 %collective-permute-done = bf16[320,640]{1,0:T(8,128)(2,1)} collective-permute-done((bf16[320,640]{1,0:T(8,128)(2,1)S(1)}, bf16[320,640]{1,0:T(8,128)(2,1)}, u32[]{:S(2)}, u32[]{:S(2)}) %collective-permute-start) | collective-permute-done | bytes 409632 | tf_op jit(solution)/shard_map/ppermute | solution.py:29
  48.7 1.5 collective-permute-start.4
  50.1 2.7 %collective-permute-start.6 = (bf16[3,256,384]{2,1,0:T(8,128)(2,1)}, bf16[3,256,384]{2,1,0:T(8,128)(2,1)}, u32[]{:S(2)}, u32[]{:S(2)}) collective-permute-start(bf16[3,256,384]{2,1,0:T(8,128)(2,1)} %collective-permute-done.2.refs_10_), channel_id=1, source_target_pairs={{0,224},{32,0},{64,32},{96,64},{128,96},{160,128},{192,160},{224,1... | collective-permute-start | bytes 1769480 | tf_op jit(solution)/shard_map/ppermute | solution.py:29
  55.8 2.1 %copy-done.1 = bf16[384,5120]{1,0:T(8,128)(2,1)S(1)} copy-done((bf16[384,5120]{1,0:T(8,128)(2,1)S(1)}, bf16[384,5120]{1,0:T(8,128)(2,1)}, u32[]{:S(2)}) %copy-start.1) | copy-done | bytes 3932184
  57.9 3.1 %shard_map.113 = bf16[8,192,640]{2,1,0:T(8,128)(2,1)} custom-call(s32[1]{0:T(128)} %bitcast.1.core.refs_1_, bf16[384,5120]{1,0:T(8,128)(2,1)S(1)} %copy-done.1), custom_call_target="tpu_custom_call" | custom-call | tf_op jit(solution)/shard_map/pallas_call | solution.py:157
  62.1 3.5 %collective-permute-done.5.refs_12_ = bf16[3,256,384]{2,1,0:T(8,128)(2,1)} collective-permute-done((bf16[3,256,384]{2,1,0:T(8,128)(2,1)S(1)}, bf16[3,256,384]{2,1,0:T(8,128)(2,1)}, u32[]{:S(2)}, u32[]{:S(2)}) %collective-permute-start.5) | collective-permute-done | bytes 589856 | tf_op jit(solution)/shard_map/ppermute | solution.py:29
  65.6 2.8 %collective-permute-done.3.refs_6_ = bf16[2,320,640]{2,1,0:T(8,128)(2,1)S(1)} collective-permute-done((bf16[2,320,640]{2,1,0:T(8,128)(2,1)S(1)}, bf16[2,320,640]{2,1,0:T(8,128)(2,1)S(1)}, u32[]{:S(2)}, u32[]{:S(2)}) %collective-permute-start.3) | collective-permute-done | bytes 819232 | tf_op jit(solution)/shard_map/ppermute | solution.py:29
  68.4 2.7 %collective-permute-start.9 = (bf16[3,256,384]{2,1,0:T(8,128)(2,1)}, bf16[3,256,384]{2,1,0:T(8,128)(2,1)S(1)}, u32[]{:S(2)}, u32[]{:S(2)}) collective-permute-start(bf16[3,256,384]{2,1,0:T(8,128)(2,1)} %collective-permute-done.6.refs_13_), channel_id=1, source_target_pairs={{0,224},{32,0},{64,32},{96,64},{128,96},{160,128},{192,160},{224,1... | collective-permute-start | bytes 1769480 | tf_op jit(solution)/shard_map/ppermute | solution.py:29
  73.4 1.8 collective-permute-start.11
  77.1 1.4 collective-permute-start.12
  78.4 5.0 %collective-permute-done.12.refs_14_ = bf16[2,3,64,384]{3,2,1,0:T(8,128)(2,1)S(1)} collective-permute-done((bf16[2,3,64,384]{3,2,1,0:T(8,128)(2,1)S(1)}, bf16[2,3,64,384]{3,2,1,0:T(8,128)(2,1)S(1)}, u32[]{:S(2)}, u32[]{:S(2)}) %collective-permute-start.12) | collective-permute-done | bytes 294944 | tf_op jit(solution)/shard_map/ppermute | solution.py:29
  86.8 1.4 collective-permute-start.13
  88.1 2.5 %collective-permute-done.15.refs_19_ = bf16[3,128,384]{2,1,0:T(8,128)(2,1)S(1)} collective-permute-done((bf16[3,128,384]{2,1,0:T(8,128)(2,1)S(1)}, bf16[3,128,384]{2,1,0:T(8,128)(2,1)S(1)}, u32[]{:S(2)}, u32[]{:S(2)}) %collective-permute-start.15) | collective-permute-done | bytes 294944 | tf_op jit(solution)/shard_map/ppermute | solution.py:29
  90.7 2.3 %collective-permute-done.14.refs_18_ = bf16[3,128,384]{2,1,0:T(8,128)(2,1)S(1)} collective-permute-done((bf16[3,128,384]{2,1,0:T(8,128)(2,1)S(1)}, bf16[3,128,384]{2,1,0:T(8,128)(2,1)S(1)}, u32[]{:S(2)}, u32[]{:S(2)}) %collective-permute-start.14) | collective-permute-done | bytes 294944 | tf_op jit(solution)/shard_map/ppermute | solution.py:29
  96.4 2.0 collective-permute-done.16.refs_20_
  99.1 6.2 %all-to-all-start.3 = ((bf16[8,192,640]{2,1,0:T(8,128)(2,1)}), bf16[8,192,640]{2,1,0:T(8,128)(2,1)}, u32[]{:S(2)}, u32[]{:S(2)}) async-start(bf16[8,192,640]{2,1,0:T(8,128)(2,1)} %shard_map.113), calls=%async_computation.3 | async-start | bytes 3932160 | tf_op jit(solution)/shard_map/all_to_all | solution.py:20
  114.8 10.6 %shard_map.114 = (f32[320,1152]{1,0:T(8,128)S(1)}, bf16[320,1152]{1,0:T(8,128)(2,1)}) custom-call(s32[8]{0:T(128)S(1)} %xor_add_fusion.refs_0_, s32[1]{0:T(128)} %bitcast.1.core.refs_1_, bf16[2,320,640]{2,1,0:T(8,128)(2,1)S(1)} %pad_maximum_fusion.refs_2_, bf16[2,320,640]{2,1,0:T(8,128)(2,1)} %collective-permute-done.4.refs_3_, ...), custom_call_target="tpu_custom_call" | custom-call | tf_op jit(solution)/shard_map/pallas_call | solution.py:92
  126.6 5.3 %collective-permute-start.17 = (bf16[320,1152]{1,0:T(8,128)(2,1)}, bf16[320,1152]{1,0:T(8,128)(2,1)S(1)}, u32[]{:S(2)}, u32[]{:S(2)}) collective-permute-start(bf16[320,1152]{1,0:T(8,128)(2,1)} %get-tuple-element.40), channel_id=1, source_target_pairs={{0,16},{16,0},{1,17},{17,1},{2,18},{18,2},{3,19},{19,3},{4,20},{20... | collective-permute-start | bytes 2211848 | tf_op jit(solution)/shard_map/ppermute | solution.py:29
  131.9 1.7 collective-permute-start.18
  133.9 1.4 copy-done.5
  136.7 15.5 %all_to_all.25 = bf16[16,20,384]{2,1,0:T(8,128)(2,1)S(1)} all-to-all(bf16[16,20,384]{2,1,0:T(8,128)(2,1)S(1)} %shard_map.115), channel_id=1, replica_groups=mesh['z'=8,'core'=2,'x'=4,'yhi'=2,'dp'=2] {'z','core'}, dimensions={0} | all-to-all | bytes 491520 | tf_op jit(solution)/shard_map/all_to_all | solution.py:20
  152.2 1.5 broadcast_in_dim.37
  153.7 7.1 %all-to-all-start.2 = ((bf16[8,320,384]{2,1,0:T(8,128)(2,1)}), bf16[8,320,384]{2,1,0:T(8,128)(2,1)S(1)}, u32[]{:S(2)}, u32[]{:S(2)}) async-start(bf16[8,320,384]{2,1,0:T(8,128)(2,1)} %broadcast_in_dim.37), calls=%async_computation.2 | async-start | bytes 3932160 | tf_op jit(solution)/shard_map/all_to_all | solution.py:20
  161.0 4.5 %broadcast_select_fusion.1 = (bf16[8,192,640]{2,1,0:T(8,128)(2,1)}, bf16[8,192,640]{2,1,0:T(8,128)(2,1)}) fusion(bf16[8,192,640]{2,1,0:T(8,128)(2,1)} %all-to-all-done.3, bf16[8,192,640]{2,1,0:T(8,128)(2,1)} %collective-permute-done.18, pred[]{:T(512)S(6)} %eq.65), kind=kLoop, calls=%fused_computation.5 | loop fusion | flops 1966080 | bytes 7864321 | tf_op jit(solution)/shard_map/jit(_where)/select_n | solution.py:221
  165.4 25.3 %all-to-all-done.2 = bf16[8,320,384]{2,1,0:T(8,128)(2,1)S(1)} async-done(((bf16[8,320,384]{2,1,0:T(8,128)(2,1)}), bf16[8,320,384]{2,1,0:T(8,128)(2,1)S(1)}, u32[]{:S(2)}, u32[]{:S(2)}) %all-to-all-start.2) | async-done | bytes 1966112 | tf_op jit(solution)/shard_map/all_to_all | solution.py:20
  190.7 3.9 %fusion = f32[320,640,1]{1,0,2:T(8,128)S(1)} fusion(bf16[8,320,384]{2,1,0:T(8,128)(2,1)S(1)} %all-to-all-done.2, bf16[8,192,640]{2,1,0:T(8,128)(2,1)} %get-tuple-element.43, bf16[8,192,640]{2,1,0:T(8,128)(2,1)} %get-tuple-element.42), kind=kOutput, calls=%fused_computation | convolution fusion | flops 1266155520 | bytes 6717440 | tf_op jit(solution)/shard_map/dot_general | solution.py:236
  195.5 4.1 %all-to-all-start.4 = ((f32[32,2,672]{2,1,0:T(2,128)}), f32[32,2,672]{2,1,0:T(2,128)S(1)}, u32[]{:S(2)}, u32[]{:S(2)}) async-start(f32[32,2,672]{2,1,0:T(2,128)} %broadcast_in_dim.38), calls=%async_computation.4 | async-start | bytes 393216 | tf_op jit(solution)/shard_map/all_to_all | solution.py:20
  201.6 8.3 %all-to-all-done.4 = f32[32,2,672]{2,1,0:T(2,128)S(1)} async-done(((f32[32,2,672]{2,1,0:T(2,128)}), f32[32,2,672]{2,1,0:T(2,128)S(1)}, u32[]{:S(2)}, u32[]{:S(2)}) %all-to-all-start.4) | async-done | bytes 172064 | tf_op jit(solution)/shard_map/all_to_all | solution.py:20
  (120 shorter events, 42.6 us)
Async XLA Ops:
  0.6 16.6 %copy-start = (bf16[320,3,384]{2,0,1:T(8,128)(2,1)S(1)}, bf16[320,3,384]{2,0,1:T(8,128)(2,1)}, u32[]{:S(2)}) copy-start(bf16[320,3,384]{2,0,1:T(8,128)(2,1)} %param.13) | copy-start | bytes 2211844
  7.3 26.6 %all-to-all-start = ((bf16[16,20,640]{2,1,0:T(8,128)(2,1)}), bf16[16,20,640]{2,1,0:T(8,128)(2,1)S(1)}, u32[]{:S(2)}, u32[]{:S(2)}) async-start(bf16[16,20,640]{2,1,0:T(8,128)(2,1)} %reshape.100), calls=%async_computation | async-start | bytes 983040 | tf_op jit(solution)/shard_map/all_to_all | solution.py:20
  17.3 30.0 %collective-permute-start.1 = (bf16[3,256,384]{2,1,0:T(8,128)(2,1)S(1)}, bf16[3,256,384]{2,1,0:T(8,128)(2,1)S(1)}, u32[]{:S(2)}, u32[]{:S(2)}) collective-permute-start(bf16[3,256,384]{2,1,0:T(8,128)(2,1)S(1)} %dynamic-slice_bitcast_fusion.refs_7_), channel_id=1, source_target_pairs={{0,32},{32,64},{64,96},{96,128},{128,160},{160,192},{192,224},{224... | collective-permute-start | bytes 1769480 | tf_op jit(solution)/shard_map/ppermute | solution.py:29
  18.8 28.6 %collective-permute-start.2 = (bf16[3,256,384]{2,1,0:T(8,128)(2,1)S(1)}, bf16[3,256,384]{2,1,0:T(8,128)(2,1)}, u32[]{:S(2)}, u32[]{:S(2)}) collective-permute-start(bf16[3,256,384]{2,1,0:T(8,128)(2,1)S(1)} %dynamic-slice_bitcast_fusion.refs_7_), channel_id=1, source_target_pairs={{0,224},{32,0},{64,32},{96,64},{128,96},{160,128},{192,160},{224,1... | collective-permute-start | bytes 1769480 | tf_op jit(solution)/shard_map/ppermute | solution.py:29
  34.0 12.3 %collective-permute-start = (bf16[320,640]{1,0:T(8,128)(2,1)S(1)}, bf16[320,640]{1,0:T(8,128)(2,1)}, u32[]{:S(2)}, u32[]{:S(2)}) collective-permute-start(bf16[320,640]{1,0:T(8,128)(2,1)S(1)} %reshape.93), channel_id=1, source_target_pairs={{0,2},{2,0},{1,3},{3,1},{4,6},{6,4},{5,7},{7,5},{8,10},{10,8},{9,1... | collective-permute-start | bytes 1228808 | tf_op jit(solution)/shard_map/ppermute | solution.py:29
  47.3 13.7 %copy-start.6 = (bf16[3,256,384]{2,1,0:T(8,128)(2,1)}, bf16[3,256,384]{2,1,0:T(8,128)(2,1)S(1)}, u32[]{:S(2)}) copy-start(bf16[3,256,384]{2,1,0:T(8,128)(2,1)S(1)} %collective-permute-done.1.refs_9_) | copy-start | bytes 1769476
  47.4 21.0 %collective-permute-start.3 = (bf16[2,320,640]{2,1,0:T(8,128)(2,1)S(1)}, bf16[2,320,640]{2,1,0:T(8,128)(2,1)S(1)}, u32[]{:S(2)}, u32[]{:S(2)}) collective-permute-start(bf16[2,320,640]{2,1,0:T(8,128)(2,1)S(1)} %pad_maximum_fusion.refs_2_), channel_id=1, source_target_pairs={{0,4},{4,8},{8,12},{12,0},{1,5},{5,9},{9,13},{13,1},{2,6},{6,10},{... | collective-permute-start | bytes 2457608 | tf_op jit(solution)/shard_map/ppermute | solution.py:29
  48.7 19.7 %collective-permute-start.4 = (bf16[2,320,640]{2,1,0:T(8,128)(2,1)S(1)}, bf16[2,320,640]{2,1,0:T(8,128)(2,1)}, u32[]{:S(2)}, u32[]{:S(2)}) collective-permute-start(bf16[2,320,640]{2,1,0:T(8,128)(2,1)S(1)} %pad_maximum_fusion.refs_2_), channel_id=1, source_target_pairs={{0,12},{4,0},{8,4},{12,8},{1,13},{5,1},{9,5},{13,9},{2,14},{6,2},{... | collective-permute-start | bytes 2457608 | tf_op jit(solution)/shard_map/ppermute | solution.py:29
  50.1 15.5 %collective-permute-start.5 = (bf16[3,256,384]{2,1,0:T(8,128)(2,1)S(1)}, bf16[3,256,384]{2,1,0:T(8,128)(2,1)}, u32[]{:S(2)}, u32[]{:S(2)}) collective-permute-start(bf16[3,256,384]{2,1,0:T(8,128)(2,1)S(1)} %collective-permute-done.1.refs_9_), channel_id=1, source_target_pairs={{0,32},{32,64},{64,96},{96,128},{128,160},{160,192},{192,224},{224... | collective-permute-start | bytes 1769480 | tf_op jit(solution)/shard_map/ppermute | solution.py:29
  50.1 15.5 %collective-permute-start.6 = (bf16[3,256,384]{2,1,0:T(8,128)(2,1)}, bf16[3,256,384]{2,1,0:T(8,128)(2,1)}, u32[]{:S(2)}, u32[]{:S(2)}) collective-permute-start(bf16[3,256,384]{2,1,0:T(8,128)(2,1)} %collective-permute-done.2.refs_10_), channel_id=1, source_target_pairs={{0,224},{32,0},{64,32},{96,64},{128,96},{160,128},{192,160},{224,1... | collective-permute-start | bytes 1769480 | tf_op jit(solution)/shard_map/ppermute | solution.py:29
  54.5 7.5 %collective-permute-start.7 = (bf16[2,3,64,384]{3,2,1,0:T(8,128)(2,1)}, bf16[2,3,64,384]{3,2,1,0:T(8,128)(2,1)}, u32[]{:S(2)}, u32[]{:S(2)}) collective-permute-start(bf16[2,3,64,384]{3,2,1,0:T(8,128)(2,1)} %pad_maximum_fusion.2), channel_id=1, source_target_pairs={{0,1},{1,0},{2,3},{3,2},{4,5},{5,4},{6,7},{7,6},{8,9},{9,8},{10,11... | collective-permute-start | bytes 884744 | tf_op jit(solution)/shard_map/ppermute | solution.py:29
  55.8 2.1 %copy-start.1 = (bf16[384,5120]{1,0:T(8,128)(2,1)S(1)}, bf16[384,5120]{1,0:T(8,128)(2,1)}, u32[]{:S(2)}) copy-start(bf16[384,5120]{1,0:T(8,128)(2,1)} %w_ref) | copy-start | bytes 11796484
  68.4 16.6 %collective-permute-start.8 = (bf16[3,256,384]{2,1,0:T(8,128)(2,1)}, bf16[3,256,384]{2,1,0:T(8,128)(2,1)S(1)}, u32[]{:S(2)}, u32[]{:S(2)}) collective-permute-start(bf16[3,256,384]{2,1,0:T(8,128)(2,1)} %collective-permute-done.5.refs_12_), channel_id=1, source_target_pairs={{0,32},{32,64},{64,96},{96,128},{128,160},{160,192},{192,224},{224... | collective-permute-start | bytes 1769480 | tf_op jit(solution)/shard_map/ppermute | solution.py:29
  68.4 16.6 %collective-permute-start.9 = (bf16[3,256,384]{2,1,0:T(8,128)(2,1)}, bf16[3,256,384]{2,1,0:T(8,128)(2,1)S(1)}, u32[]{:S(2)}, u32[]{:S(2)}) collective-permute-start(bf16[3,256,384]{2,1,0:T(8,128)(2,1)} %collective-permute-done.6.refs_13_), channel_id=1, source_target_pairs={{0,224},{32,0},{64,32},{96,64},{128,96},{160,128},{192,160},{224,1... | collective-permute-start | bytes 1769480 | tf_op jit(solution)/shard_map/ppermute | solution.py:29
  71.1 13.1 %collective-permute-start.10 = (bf16[2,160,640]{2,1,0:T(8,128)(2,1)S(1)}, bf16[2,160,640]{2,1,0:T(8,128)(2,1)S(1)}, u32[]{:S(2)}, u32[]{:S(2)}) collective-permute-start(bf16[2,160,640]{2,1,0:T(8,128)(2,1)S(1)} %slice.32), channel_id=1, source_target_pairs={{0,4},{4,8},{8,12},{12,0},{1,5},{5,9},{9,13},{13,1},{2,6},{6,10},{... | collective-permute-start | bytes 1228808 | tf_op jit(solution)/shard_map/ppermute | solution.py:29
  73.4 11.6 %collective-permute-start.11 = (bf16[2,160,640]{2,1,0:T(8,128)(2,1)S(1)}, bf16[2,160,640]{2,1,0:T(8,128)(2,1)S(1)}, u32[]{:S(2)}, u32[]{:S(2)}) collective-permute-start(bf16[2,160,640]{2,1,0:T(8,128)(2,1)S(1)} %slice.33), channel_id=1, source_target_pairs={{0,12},{4,0},{8,4},{12,8},{1,13},{5,1},{9,5},{13,9},{2,14},{6,2},{... | collective-permute-start | bytes 1228808 | tf_op jit(solution)/shard_map/ppermute | solution.py:29
  77.1 6.4 %collective-permute-start.12 = (bf16[2,3,64,384]{3,2,1,0:T(8,128)(2,1)S(1)}, bf16[2,3,64,384]{3,2,1,0:T(8,128)(2,1)S(1)}, u32[]{:S(2)}, u32[]{:S(2)}) collective-permute-start(bf16[2,3,64,384]{3,2,1,0:T(8,128)(2,1)S(1)} %pad_maximum_fusion.3), channel_id=1, source_target_pairs={{0,1},{1,0},{2,3},{3,2},{4,5},{5,4},{6,7},{7,6},{8,9},{9,8},{10,11... | collective-permute-start | bytes 884744 | tf_op jit(solution)/shard_map/ppermute | solution.py:29
  85.0 5.7 %collective-permute-start.15 = (bf16[3,128,384]{2,1,0:T(8,128)(2,1)S(1)}, bf16[3,128,384]{2,1,0:T(8,128)(2,1)S(1)}, u32[]{:S(2)}, u32[]{:S(2)}) collective-permute-start(bf16[3,128,384]{2,1,0:T(8,128)(2,1)S(1)} %slice.36), channel_id=1, source_target_pairs={{0,224},{32,0},{64,32},{96,64},{128,96},{160,128},{192,160},{224,1... | collective-permute-start | bytes 884744 | tf_op jit(solution)/shard_map/ppermute | solution.py:29
  86.1 6.9 %collective-permute-start.14 = (bf16[3,128,384]{2,1,0:T(8,128)(2,1)S(1)}, bf16[3,128,384]{2,1,0:T(8,128)(2,1)S(1)}, u32[]{:S(2)}, u32[]{:S(2)}) collective-permute-start(bf16[3,128,384]{2,1,0:T(8,128)(2,1)S(1)} %slice.34), channel_id=1, source_target_pairs={{0,32},{32,64},{64,96},{96,128},{128,160},{160,192},{192,224},{224... | collective-permute-start | bytes 884744 | tf_op jit(solution)/shard_map/ppermute | solution.py:29
  86.8 8.9 %collective-permute-start.13 = (bf16[2,3,64,384]{3,2,1,0:T(8,128)(2,1)S(1)}, bf16[2,3,64,384]{3,2,1,0:T(8,128)(2,1)S(1)}, u32[]{:S(2)}, u32[]{:S(2)}) collective-permute-start(bf16[2,3,64,384]{3,2,1,0:T(8,128)(2,1)S(1)} %pad_maximum_fusion.4), channel_id=1, source_target_pairs={{0,1},{1,0},{2,3},{3,2},{4,5},{5,4},{6,7},{7,6},{8,9},{9,8},{10,11... | collective-permute-start | bytes 884744 | tf_op jit(solution)/shard_map/ppermute | solution.py:29
  94.4 4.0 %collective-permute-start.16 = (bf16[3,64,384]{2,1,0:T(8,128)(2,1)S(1)}, bf16[3,64,384]{2,1,0:T(8,128)(2,1)S(1)}, u32[]{:S(2)}, u32[]{:S(2)}) collective-permute-start(bf16[3,64,384]{2,1,0:T(8,128)(2,1)S(1)} %slice_select_fusion), channel_id=1, source_target_pairs={{0,1},{1,0},{2,3},{3,2},{4,5},{5,4},{6,7},{7,6},{8,9},{9,8},{10,11... | collective-permute-start | bytes 442376 | tf_op jit(solution)/shard_map/ppermute | solution.py:29
  99.1 32.8 %all-to-all-start.3 = ((bf16[8,192,640]{2,1,0:T(8,128)(2,1)}), bf16[8,192,640]{2,1,0:T(8,128)(2,1)}, u32[]{:S(2)}, u32[]{:S(2)}) async-start(bf16[8,192,640]{2,1,0:T(8,128)(2,1)} %shard_map.113), calls=%async_computation.3 | async-start | bytes 3932160 | tf_op jit(solution)/shard_map/all_to_all | solution.py:20
  126.6 7.4 %collective-permute-start.17 = (bf16[320,1152]{1,0:T(8,128)(2,1)}, bf16[320,1152]{1,0:T(8,128)(2,1)S(1)}, u32[]{:S(2)}, u32[]{:S(2)}) collective-permute-start(bf16[320,1152]{1,0:T(8,128)(2,1)} %get-tuple-element.40), channel_id=1, source_target_pairs={{0,16},{16,0},{1,17},{17,1},{2,18},{18,2},{3,19},{19,3},{4,20},{20... | collective-permute-start | bytes 2211848 | tf_op jit(solution)/shard_map/ppermute | solution.py:29
  131.9 29.1 %collective-permute-start.18 = (bf16[8,192,640]{2,1,0:T(8,128)(2,1)}, bf16[8,192,640]{2,1,0:T(8,128)(2,1)}, u32[]{:S(2)}, u32[]{:S(2)}) collective-permute-start(bf16[8,192,640]{2,1,0:T(8,128)(2,1)} %all-to-all-done.3), channel_id=1, source_target_pairs={{0,16},{16,0},{1,17},{17,1},{2,18},{18,2},{3,19},{19,3},{4,20},{20... | collective-permute-start | bytes 5898248 | tf_op jit(solution)/shard_map/ppermute | solution.py:29
  153.7 7.1 %copy-start.27 = (f32[8,32]{1,0:T(8,128)S(1)}, f32[8,32]{1,0:T(8,128)}, u32[]{:S(2)}) copy-start(f32[8,32]{1,0:T(8,128)} %param.16) | copy-start | bytes 3076
  153.7 7.1 %copy-start.28 = (s32[2,1]{0,1:T(1,128)S(1)}, s32[2,1]{0,1:T(1,128)}, u32[]{:S(2)}) copy-start(s32[2,1]{0,1:T(1,128)} %param.15) | copy-start | bytes 28
  153.7 37.0 %all-to-all-start.2 = ((bf16[8,320,384]{2,1,0:T(8,128)(2,1)}), bf16[8,320,384]{2,1,0:T(8,128)(2,1)S(1)}, u32[]{:S(2)}, u32[]{:S(2)}) async-start(bf16[8,320,384]{2,1,0:T(8,128)(2,1)} %broadcast_in_dim.37), calls=%async_computation.2 | async-start | bytes 3932160 | tf_op jit(solution)/shard_map/all_to_all | solution.py:20
  190.7 3.9 %copy-start.23 = (bf16[2,1,160,640]{3,2,1,0:T(8,128)(2,1)S(1)}, bf16[2,1,160,640]{3,2,1,0:T(8,128)(2,1)}, u32[]{:S(2)}) copy-start(bf16[2,1,160,640]{3,2,1,0:T(8,128)(2,1)} %param.18) | copy-start | bytes 1228804
  190.7 9.9 %copy-start.25 = (pred[2,1,160]{2,0,1:T(4,128)(4,1)S(1)}, pred[2,1,160]{2,0,1:T(4,128)(4,1)}, u32[]{:S(2)}) copy-start(pred[2,1,160]{2,0,1:T(4,128)(4,1)} %copy-done.24) | copy-start | bytes 964
  190.7 9.9 %copy-start.26 = (bf16[640]{0:T(1024)(128)(2,1)S(1)}, bf16[640]{0:T(1024)(128)(2,1)}, u32[]{:S(2)}) copy-start(bf16[640]{0:T(1024)(128)(2,1)} %param.12) | copy-start | bytes 3844
  194.6 6.0 %copy-start.22 = (bf16[2,1,160,640]{3,2,1,0:T(8,128)(2,1)S(1)}, bf16[2,1,160,640]{3,2,1,0:T(8,128)(2,1)}, u32[]{:S(2)}) copy-start(bf16[2,1,160,640]{3,2,1,0:T(8,128)(2,1)} %param.10) | copy-start | bytes 1228804
  195.5 14.3 %all-to-all-start.4 = ((f32[32,2,672]{2,1,0:T(2,128)}), f32[32,2,672]{2,1,0:T(2,128)S(1)}, u32[]{:S(2)}, u32[]{:S(2)}) async-start(f32[32,2,672]{2,1,0:T(2,128)} %broadcast_in_dim.38), calls=%async_computation.4 | async-start | bytes 393216 | tf_op jit(solution)/shard_map/all_to_all | solution.py:20
  (20 other events, 19.1 us)

commit v6 on v3

--- a/solution.py
+++ b/solution.py
@@ -28,66 +28,82 @@
     return lax.ppermute(x, axis, [(i, (i + by) % n) for i in range(n)])
 
 
-def qkv_kernel(slots, core, x_any, *refs):
-    n = len(refs) - 7
-    shards, (kept, sent, x_ref, w_ref, acc, x_sem, w_sem) = refs[:n], refs[n:]
-    copies, at = [], 0
-    for j in range(x_ref.shape[0]):
-        copies.append([pltpu.make_async_copy(x_any.at[slots[j]], x_ref.at[j], x_sem.at[j])])
-        full = x_ref.shape[2] // 2
-        row = 0
-        while row < full:
-            depth = shards[at].shape[1]
-            target = w_ref.at[:, pl.ds(j * full + row, depth)]
-            copies[j].append(pltpu.make_async_copy(shards[at], target, w_sem.at[at]))
-            row += depth
-            at += 1
-    for group in copies:
-        for copy in group:
-            copy.start()
-    rows, half = x_ref.shape[1], x_ref.shape[2] // 2
-    for j in range(0, x_ref.shape[0], 2):
-        for copy in copies[j] + copies[j + 1]:
-            copy.wait()
-        a, b = x_ref[j], x_ref[j + 1]
-        low = jnp.concatenate([a[:, :half], b[:, :half]], axis=1)
-        high = jnp.concatenate([a[:, half:], b[:, half:]], axis=1)
-        x = jnp.concatenate([low, high], axis=0)
-        depth = pl.ds(j * half, 2 * half)
-        w = jnp.concatenate([w_ref[i, depth] for i in range(3)], axis=1)
+def qkv_kernel(groups, first, last, slots, core, both, right, top, low, left, *refs):
+    pieces = [w for group in groups for w in group]
+    count = sum(pieces)
+    shards, refs = refs[:count], refs[count:]
+    acc_in, refs = (None, refs) if first else (refs[0], refs[1:])
+    outs, x_ref = refs[:-1], refs[-1]
+    rows, full = x_ref.shape[1], x_ref.shape[2] // 2
+    for j in range(len(pieces)):
+        far, own = slots[j] >> 1, slots[j] & 1
+        for k, source in ((0, both), (1, right), (3, left)):
+
+            @pl.when(far == k)
+            def _():
+                x_ref[j] = source[own]
+
+        @pl.when(far == 2)
+        def _():
+            x_ref[j, : rows // 2] = top[own]
+            x_ref[j, rows // 2 :] = low[own]
+
+    at, j, acc = 0, 0, outs[0]
+    for number, group in enumerate(groups):
+        xs = [x_ref[j + i] for i in range(len(group))]
+        x = jnp.concatenate(
+            [
+                jnp.concatenate([x[:, :full] for x in xs], axis=1),
+                jnp.concatenate([x[:, full:] for x in xs], axis=1),
+            ],
+            axis=0,
+        )
+        use = shards[at : at + sum(group)]
+        w = jnp.concatenate(
+            [jnp.concatenate([u[i] for u in use], axis=0) for i in range(3)], axis=1
+        )
         part = jnp.dot(x, w, preferred_element_type=jnp.float32)
-        if j == 0:
+        if number:
+            acc[...] += part
+        elif first:
             acc[...] = part
         else:
-            acc[...] += part
-    me = core[0]
-    kept[...] = acc[pl.ds(me * rows, rows)]
-    sent[...] = acc[pl.ds((1 - me) * rows, rows)].astype(jnp.bfloat16)
-
-
-def project(x, shards, slots, core):
-    n, rows, width = x.shape
-    heads = 3 * shards[0].shape[2]
+            acc[...] = acc_in[...] + part
+        at += len(use)
+        j += len(group)
+    if last:
+        me = core[0]
+        outs[1][...] = acc[pl.ds(me * rows, rows)]
+        outs[2][...] = acc[pl.ds((1 - me) * rows, rows)].astype(jnp.bfloat16)
+
+
+def project(features, groups, slots, core, acc=None, last=False):
+    _, rows, width = features[0].shape
+    counts = [[len(s) for s in group] for group in groups]
+    shards = [w for group in groups for s in group for w in s]
+    heads = shards[0].shape[-1]
     smem = pl.BlockSpec(memory_space=pltpu.SMEM)
     vmem = pl.BlockSpec(memory_space=pltpu.VMEM)
-    hbm = pl.BlockSpec(memory_space=pl.ANY)
+    out_shape = [jax.ShapeDtypeStruct((2 * rows, 3 * heads), jnp.float32)]
+    if last:
+        out_shape += [
+            jax.ShapeDtypeStruct((rows, 3 * heads), jnp.float32),
+            jax.ShapeDtypeStruct((rows, 3 * heads), jnp.bfloat16),
+        ]
+    operands = [*features, *shards] + ([] if acc is None else [acc])
+
+    def kernel(*refs):
+        qkv_kernel(counts, acc is None, last, *refs)
+
     return pl.pallas_call(
-        qkv_kernel,
-        in_specs=[smem, smem] + [hbm] * (1 + len(shards)),
-        out_specs=(vmem, vmem),
-        out_shape=(
-            jax.ShapeDtypeStruct((rows, heads), jnp.float32),
-            jax.ShapeDtypeStruct((rows, heads), jnp.bfloat16),
-        ),
-        scratch_shapes=[
-            pltpu.VMEM((n, rows, width), jnp.bfloat16),
-            pltpu.VMEM((3, n * width // 2, heads // 3), jnp.bfloat16),
-            pltpu.VMEM((2 * rows, heads), jnp.float32),
-            pltpu.SemaphoreType.DMA((n,)),
-            pltpu.SemaphoreType.DMA((len(shards),)),
-        ],
-        compiler_params=pltpu.CompilerParams(vmem_limit_bytes=28 * 1024 * 1024),
-    )(slots, core, x, *shards)
+        kernel,
+        in_specs=[smem, smem] + [vmem] * len(operands),
+        out_specs=[vmem] * len(out_shape),
+        out_shape=out_shape,
+        input_output_aliases={} if acc is None else {len(operands) + 1: 0},
+        scratch_shapes=[pltpu.VMEM((sum(len(c) for c in counts), rows, width), jnp.bfloat16)],
+        compiler_params=pltpu.CompilerParams(vmem_limit_bytes=32 * 1024 * 1024),
+    )(slots, core, *operands)
 
 
 def attend(q, k, v, bias):
@@ -163,20 +179,18 @@
 
     own = w_qkv.transpose(1, 0, 2)
     up1, down1 = shift(own, "z", 1), shift(own, "z", -1)
-    mine, up1, down1 = lax.optimization_barrier((mine, up1, down1))
+    both = jnp.stack([mine, shift(mine, "yhi", 1)])
+    both, w_out, up1, down1 = lax.optimization_barrier((both, w_out, up1, down1))
+    left, right = shift(both, "x", 1), shift(both, "x", -1)
     up2, down2 = shift(up1, "z", 1), shift(down1, "z", -1)
-    both = jnp.stack([mine, shift(mine, "yhi", 1)])
-    both, w_out = lax.optimization_barrier((both, w_out))
-    left, right = shift(both, "x", 1), shift(both, "x", -1)
     blocks = column_blocks(w_out, core1, width)
     left, right, up2, down2, blocks = lax.optimization_barrier((left, right, up2, down2, blocks))
+    middle = rows // 2
+    top, low = shift(left[:, :middle], "x", 1), shift(right[:, middle:], "x", -1)
     up3, down3 = shift(up2, "z", 1), shift(down2, "z", -1)
-    middle = rows // 2
-    far = (shift(left[:, :middle], "x", 1), shift(right[:, middle:], "x", -1))
-    up3, down3, far, blocks = lax.optimization_barrier((up3, down3, far, blocks))
+    up3, down3, top, low, blocks = lax.optimization_barrier((up3, down3, top, low, blocks))
     up4 = shift(up3[:, : depth // 2], "z", 1)
     down4 = shift(down3[:, depth // 2 :], "z", -1)
-    features = jnp.concatenate([both, right, jnp.concatenate(far, axis=1), left])
 
     half = exchange(blocks, MP)
     other_half = shift(half, "core", 1)
@@ -187,8 +201,10 @@
     x, yhi = lax.axis_index("x"), lax.axis_index("yhi")
     shard = (z + jnp.array([0, zs - 1, 1, zs - 2, 2, zs - 3, 3, zs - 4], jnp.int32)) & (zs - 1)
     slots = (2 * (((shard >> 1) - x) & (mp // 2 - 1)) + ((shard & 1) ^ yhi)).astype(jnp.int32)
-    shards = [own, up1, down1, up2, down2, up3, down3, up4, down4]
-    kept, sent = project(features, shards, slots, core1)
+    features = (both, right, top, low, left)
+    early = [[(own,), (up1,)], [(down1,), (up2,)], [(down2,), (up3,)], [(down3,)]]
+    (acc,) = project(features, early, slots[:7], core1)
+    _, kept, sent = project(features, [[(up4, down4)]], slots[7:], core1, acc, last=True)
     attn = attention(kept, shift(sent, "core", 1), frames)
     attn = exchange(attn, FRAME).reshape(rows, heads)
     all_heads = from_everyone(attn, MP)

time: 204 us -> 195 us (0.956)
  waiting for transfers between devices: 92.3 us -> 80.1 us
  local copies, waits for them, and re-layouts: 8.89 us -> 18.4 us
  other arithmetic: 11.5 us -> 8.59 us
  blocking collectives: 18.4 us -> 16.2 us
    ppermute x15, waiting for transfers between devices: 43.9 us -> 29.6 us  [shift(): return lax.ppermute(x, axis, [(i, (i + by) % n) for i in range(n)])]
    unnamed x33 -> x39, local copies, waits for them, and re-layouts: 2.19 us -> 10.5 us
    concatenate x1 -> x0, other arithmetic: 2.94 us -> none  [body(): jnp.concatenate([both, right, jnp.concatenate(far, axis=1), left])]
    ppermute x15, starting transfers between devices: 28 us -> 25.1 us  [shift(): return lax.ppermute(x, axis, [(i, (i + by) % n) for i in range(n)])]
    all_to_all x1, blocking collectives: 18.4 us -> 16.2 us  [exchange(): return lax.all_to_all(x, axis, split_axis=0, concat_axis=0, tiled=True)]
    all_to_all x4, waiting for transfers between devices: 48.4 us -> 50.5 us  [exchange(): return lax.all_to_all(x, axis, split_axis=0, concat_axis=0, tiled=True)]
    pallas_call x1 -> x2, Pallas kernels: 10.3 us -> 9.99 us  [project(): pl.pallas_call(kernel, in_specs=[smem, smem] + [vmem] * len(operands), ou...]
  transfers between devices with their start and end apart: 19 -> 19, of which waited for: 13 -> 8; matrix products, arithmetic and copies ran while one was open for 6% -> 6% of each run, Pallas kernels for 7% -> 7%
where the time goes in v6:
time: 195 us
  waiting for transfers between devices  80.1 us (41%)
  starting transfers between devices  50.8 us (26%)
  local copies, waits for them, and re-layouts  18.4 us (9%)
  blocking collectives  16.2 us (8%)
  Pallas kernels  14.4 us (7%)
  other arithmetic  8.59 us (4%)
  matrix products  5.12 us (3%)
    all_to_all x4, waiting for transfers between devices, exchange(): return lax.all_to_all(x, axis, split_axis=0, concat_axis=0, tiled=True)  50.5 us
    ppermute x15, waiting for transfers between devices, shift(): return lax.ppermute(x, axis, [(i, (i + by) % n) for i in range(n)])  29.6 us
    all_to_all x4, starting transfers between devices, exchange(): return lax.all_to_all(x, axis, split_axis=0, concat_axis=0, tiled=True)  25.6 us
    ppermute x15, starting transfers between devices, shift(): return lax.ppermute(x, axis, [(i, (i + by) % n) for i in range(n)])  25.1 us
    all_to_all x1, blocking collectives, exchange(): return lax.all_to_all(x, axis, split_axis=0, concat_axis=0, tiled=True)  16.2 us
    unnamed x39, local copies, waits for them, and re-layouts  10.5 us
    pallas_call x2, Pallas kernels, project(): pl.pallas_call(kernel, in_specs=[smem, smem] + [vmem] * len(operands), ou...  9.99 us
    select_n x1, other arithmetic, body(): jnp.where(core == 0, half, other_half)  4.45 us
  transfers between devices with their start and end apart: 19, of which 8 were waited for; matrix products, arithmetic and copies ran while one was open for 6% of the time, Pallas kernels for 7%

profile of v6, /device:TPU:1, one launch (start us, length us, event | category | flops | bytes accessed | tf_op | source)
XLA Modules:
  0.0 194.6 jit_solution(4664127335291902668)
XLA Ops:
  4.6 10.0 %all-to-all-start = ((bf16[16,20,640]{2,1,0:T(8,128)(2,1)}), bf16[16,20,640]{2,1,0:T(8,128)(2,1)S(1)}, u32[]{:S(2)}, u32[]{:S(2)}) async-start(bf16[16,20,640]{2,1,0:T(8,128)(2,1)} %copy.20), calls=%async_computation | async-start | bytes 983040 | tf_op jit(solution)/shard_map/all_to_all | solution.py:19
  14.6 1.5 collective-permute-start.1
  17.4 13.8 %all-to-all-done = bf16[16,20,640]{2,1,0:T(8,128)(2,1)S(1)} async-done(((bf16[16,20,640]{2,1,0:T(8,128)(2,1)}), bf16[16,20,640]{2,1,0:T(8,128)(2,1)S(1)}, u32[]{:S(2)}, u32[]{:S(2)}) %all-to-all-start) | async-done | bytes 409632 | tf_op jit(solution)/shard_map/all_to_all | solution.py:19
  31.3 3.0 %collective-permute-start = (bf16[320,640]{1,0:T(8,128)(2,1)S(1)}, bf16[320,640]{1,0:T(8,128)(2,1)}, u32[]{:S(2)}, u32[]{:S(2)}) collective-permute-start(bf16[320,640]{1,0:T(8,128)(2,1)S(1)} %reshape.82), channel_id=1, source_target_pairs={{0,2},{2,0},{1,3},{3,1},{4,6},{6,4},{5,7},{7,5},{8,10},{10,8},{9,1... | collective-permute-start | bytes 1228808 | tf_op jit(solution)/shard_map/ppermute | solution.py:28
  34.4 9.2 %collective-permute-done = bf16[320,640]{1,0:T(8,128)(2,1)} collective-permute-done((bf16[320,640]{1,0:T(8,128)(2,1)S(1)}, bf16[320,640]{1,0:T(8,128)(2,1)}, u32[]{:S(2)}, u32[]{:S(2)}) %collective-permute-start) | collective-permute-done | bytes 409632 | tf_op jit(solution)/shard_map/ppermute | solution.py:28
  46.0 1.5 collective-permute-start.4
  47.5 2.7 %collective-permute-start.6 = (bf16[3,320,384]{2,1,0:T(8,128)(2,1)}, bf16[3,320,384]{2,1,0:T(8,128)(2,1)}, u32[]{:S(2)}, u32[]{:S(2)}) collective-permute-start(bf16[3,320,384]{2,1,0:T(8,128)(2,1)} %collective-permute-done.2.refs_9_), channel_id=1, source_target_pairs={{0,224},{32,0},{64,32},{96,64},{128,96},{160,128},{192,160},{224,1... | collective-permute-start | bytes 2211848 | tf_op jit(solution)/shard_map/ppermute | solution.py:28
  50.2 2.1 %copy-done.1 = bf16[384,5120]{1,0:T(8,128)(2,1)S(1)} copy-done((bf16[384,5120]{1,0:T(8,128)(2,1)S(1)}, bf16[384,5120]{1,0:T(8,128)(2,1)}, u32[]{:S(2)}) %copy-start.1) | copy-done | bytes 3932184
  52.3 3.1 %shard_map.113 = bf16[8,192,640]{2,1,0:T(8,128)(2,1)} custom-call(s32[1]{0:T(128)} %bitcast.1.core.refs_1_, bf16[384,5120]{1,0:T(8,128)(2,1)S(1)} %copy-done.1), custom_call_target="tpu_custom_call" | custom-call | tf_op jit(solution)/shard_map/pallas_call | solution.py:155
  55.4 10.2 %collective-permute-done.5.refs_10_ = bf16[3,320,384]{2,1,0:T(8,128)(2,1)} collective-permute-done((bf16[3,320,384]{2,1,0:T(8,128)(2,1)S(1)}, bf16[3,320,384]{2,1,0:T(8,128)(2,1)}, u32[]{:S(2)}, u32[]{:S(2)}) %collective-permute-start.5) | collective-permute-done | bytes 737312 | tf_op jit(solution)/shard_map/ppermute | solution.py:28
  65.6 1.4 collective-permute-start.7
  67.0 1.4 collective-permute-start.8
  69.1 2.3 %collective-permute-start.10 = (bf16[2,160,640]{2,1,0:T(8,128)(2,1)S(1)}, bf16[2,160,640]{2,1,0:T(8,128)(2,1)S(1)}, u32[]{:S(2)}, u32[]{:S(2)}) collective-permute-start(bf16[2,160,640]{2,1,0:T(8,128)(2,1)S(1)} %slice.26), channel_id=1, source_target_pairs={{0,12},{4,0},{8,4},{12,8},{1,13},{5,1},{9,5},{13,9},{2,14},{6,2},{... | collective-permute-start | bytes 1228808 | tf_op jit(solution)/shard_map/ppermute | solution.py:28
  71.3 6.7 %collective-permute-done.9.refs_4_ = bf16[2,160,640]{2,1,0:T(8,128)(2,1)S(1)} collective-permute-done((bf16[2,160,640]{2,1,0:T(8,128)(2,1)S(1)}, bf16[2,160,640]{2,1,0:T(8,128)(2,1)S(1)}, u32[]{:S(2)}, u32[]{:S(2)}) %collective-permute-start.9) | collective-permute-done | bytes 409632 | tf_op jit(solution)/shard_map/ppermute | solution.py:28
  79.6 3.4 %collective-permute-done.7.refs_12_ = bf16[3,320,384]{2,1,0:T(8,128)(2,1)S(1)} collective-permute-done((bf16[3,320,384]{2,1,0:T(8,128)(2,1)}, bf16[3,320,384]{2,1,0:T(8,128)(2,1)S(1)}, u32[]{:S(2)}, u32[]{:S(2)}) %collective-permute-start.7) | collective-permute-done | bytes 737312 | tf_op jit(solution)/shard_map/ppermute | solution.py:28
  83.0 6.9 %all-to-all-start.3 = ((bf16[8,192,640]{2,1,0:T(8,128)(2,1)}), bf16[8,192,640]{2,1,0:T(8,128)(2,1)}, u32[]{:S(2)}, u32[]{:S(2)}) async-start(bf16[8,192,640]{2,1,0:T(8,128)(2,1)} %shard_map.113), calls=%async_computation.3 | async-start | bytes 3932160 | tf_op jit(solution)/shard_map/all_to_all | solution.py:19
  91.1 1.8 slice.28
  92.9 2.3 %collective-permute-start.12 = (bf16[3,160,384]{2,1,0:T(8,128)(2,1)}, bf16[3,160,384]{2,1,0:T(8,128)(2,1)}, u32[]{:S(2)}, u32[]{:S(2)}) collective-permute-start(bf16[3,160,384]{2,1,0:T(8,128)(2,1)} %slice.28), channel_id=1, source_target_pairs={{0,224},{32,0},{64,32},{96,64},{128,96},{160,128},{192,160},{224,1... | collective-permute-start | bytes 1105928 | tf_op jit(solution)/shard_map/ppermute | solution.py:28
  100.0 6.9 %shard_map.114.refs_9_ = f32[640,1152]{1,0:T(8,128)S(1)} custom-call(s32[7]{0:T(128)S(1)} %bitcast.32, s32[1]{0:T(128)} %bitcast.1.core.refs_1_, bf16[2,320,640]{2,1,0:T(8,128)(2,1)S(1)} %pad_maximum_fusion.refs_2_, bf16[2,320,640]{2,1,0:T(8,128)(2,1)S(1)} %collective-permute-done.4.refs_3_, bf16[2,160,640]{2,1,0:T(8,128)(2,1)S(1)} %copy-done.3, ...), custom_call_target="tpu_custom_call" | custom-call | tf_op jit(solution)/shard_map/pallas_call | solution.py:98
  107.0 3.1 %shard_map.115 = (f32[640,1152]{1,0:T(8,128)S(1)}, f32[320,1152]{1,0:T(8,128)S(1)}, bf16[320,1152]{1,0:T(8,128)(2,1)S(1)}) custom-call(s32[1]{0:T(128)} %slice.24.refs_0_, s32[1]{0:T(128)} %bitcast.1.core.refs_1_, bf16[2,320,640]{2,1,0:T(8,128)(2,1)S(1)} %pad_maximum_fusion.refs_2_, ...), custom_call_target="tpu_custom_call", output_to_operand_aliasing={{0}: (9, {})} | custom-call | tf_op jit(solution)/shard_map/pallas_call | solution.py:98
  111.2 3.2 %collective-permute-start.13 = (bf16[320,1152]{1,0:T(8,128)(2,1)S(1)}, bf16[320,1152]{1,0:T(8,128)(2,1)S(1)}, u32[]{:S(2)}, u32[]{:S(2)}) collective-permute-start(bf16[320,1152]{1,0:T(8,128)(2,1)S(1)} %get-tuple-element.32), channel_id=1, source_target_pairs={{0,16},{16,0},{1,17},{17,1},{2,18},{18,2},{3,19},{19,3},{4,20},{20... | collective-permute-start | bytes 2211848 | tf_op jit(solution)/shard_map/ppermute | solution.py:28
  114.5 2.2 %all-to-all-done.3 = bf16[8,192,640]{2,1,0:T(8,128)(2,1)} async-done(((bf16[8,192,640]{2,1,0:T(8,128)(2,1)}), bf16[8,192,640]{2,1,0:T(8,128)(2,1)}, u32[]{:S(2)}, u32[]{:S(2)}) %all-to-all-start.3) | async-done | bytes 1966112 | tf_op jit(solution)/shard_map/all_to_all | solution.py:19
  116.7 2.4 %collective-permute-start.14 = (bf16[8,192,640]{2,1,0:T(8,128)(2,1)}, bf16[8,192,640]{2,1,0:T(8,128)(2,1)}, u32[]{:S(2)}, u32[]{:S(2)}) collective-permute-start(bf16[8,192,640]{2,1,0:T(8,128)(2,1)} %all-to-all-done.3), channel_id=1, source_target_pairs={{0,16},{16,0},{1,17},{17,1},{2,18},{18,2},{3,19},{19,3},{4,20},{20... | collective-permute-start | bytes 5898248 | tf_op jit(solution)/shard_map/ppermute | solution.py:28
  119.3 1.4 copy-done.8
  122.0 16.2 %all_to_all.25 = bf16[16,20,384]{2,1,0:T(8,128)(2,1)S(1)} all-to-all(bf16[16,20,384]{2,1,0:T(8,128)(2,1)S(1)} %shard_map.116), channel_id=1, replica_groups=mesh['z'=8,'core'=2,'x'=4,'yhi'=2,'dp'=2] {'z','core'}, dimensions={0} | all-to-all | bytes 491520 | tf_op jit(solution)/shard_map/all_to_all | solution.py:19
  138.3 1.5 broadcast_in_dim.37
  139.8 4.6 %all-to-all-start.2 = ((bf16[8,320,384]{2,1,0:T(8,128)(2,1)}), bf16[8,320,384]{2,1,0:T(8,128)(2,1)S(1)}, u32[]{:S(2)}, u32[]{:S(2)}) async-start(bf16[8,320,384]{2,1,0:T(8,128)(2,1)} %broadcast_in_dim.37), calls=%async_computation.2 | async-start | bytes 3932160 | tf_op jit(solution)/shard_map/all_to_all | solution.py:19
  144.5 4.5 %broadcast_select_fusion.1 = (bf16[8,192,640]{2,1,0:T(8,128)(2,1)}, bf16[8,192,640]{2,1,0:T(8,128)(2,1)}) fusion(bf16[8,192,640]{2,1,0:T(8,128)(2,1)} %all-to-all-done.3, bf16[8,192,640]{2,1,0:T(8,128)(2,1)} %collective-permute-done.14, pred[]{:T(512)S(6)} %eq.60), kind=kLoop, calls=%fused_computation.5 | loop fusion | flops 1966080 | bytes 7864321 | tf_op jit(solution)/shard_map/jit(_where)/select_n | solution.py:198
  149.0 25.3 %all-to-all-done.2 = bf16[8,320,384]{2,1,0:T(8,128)(2,1)S(1)} async-done(((bf16[8,320,384]{2,1,0:T(8,128)(2,1)}), bf16[8,320,384]{2,1,0:T(8,128)(2,1)S(1)}, u32[]{:S(2)}, u32[]{:S(2)}) %all-to-all-start.2) | async-done | bytes 1966112 | tf_op jit(solution)/shard_map/all_to_all | solution.py:19
  174.3 3.9 %fusion = f32[320,640,1]{1,0,2:T(8,128)S(1)} fusion(bf16[8,320,384]{2,1,0:T(8,128)(2,1)S(1)} %all-to-all-done.2, bf16[8,192,640]{2,1,0:T(8,128)(2,1)} %get-tuple-element.35, bf16[8,192,640]{2,1,0:T(8,128)(2,1)} %get-tuple-element.34), kind=kOutput, calls=%fused_computation | convolution fusion | flops 1266155520 | bytes 6717440 | tf_op jit(solution)/shard_map/dot_general | solution.py:211
  179.0 4.2 %all-to-all-start.4 = ((f32[32,2,672]{2,1,0:T(2,128)}), f32[32,2,672]{2,1,0:T(2,128)S(1)}, u32[]{:S(2)}, u32[]{:S(2)}) async-start(f32[32,2,672]{2,1,0:T(2,128)} %broadcast_in_dim.38), calls=%async_computation.4 | async-start | bytes 393216 | tf_op jit(solution)/shard_map/all_to_all | solution.py:19
  184.4 9.1 %all-to-all-done.4 = f32[32,2,672]{2,1,0:T(2,128)S(1)} async-done(((f32[32,2,672]{2,1,0:T(2,128)}), f32[32,2,672]{2,1,0:T(2,128)S(1)}, u32[]{:S(2)}, u32[]{:S(2)}) %all-to-all-start.4) | async-done | bytes 172064 | tf_op jit(solution)/shard_map/all_to_all | solution.py:19
  (79 shorter events, 22.0 us)
Async XLA Ops:
  0.6 182.6 %copy-start = (f32[32,640]{1,0:T(8,128)S(1)}, f32[32,640]{1,0:T(8,128)}, u32[]{:S(2)}) copy-start(f32[32,640]{1,0:T(8,128)} %param.17) | copy-start | bytes 245764
  2.9 11.7 %copy-start.9 = (bf16[320,3,384]{2,0,1:T(8,128)(2,1)S(1)}, bf16[320,3,384]{2,0,1:T(8,128)(2,1)}, u32[]{:S(2)}) copy-start(bf16[320,3,384]{2,0,1:T(8,128)(2,1)} %param.13) | copy-start | bytes 2211844
  4.6 26.6 %all-to-all-start = ((bf16[16,20,640]{2,1,0:T(8,128)(2,1)}), bf16[16,20,640]{2,1,0:T(8,128)(2,1)S(1)}, u32[]{:S(2)}, u32[]{:S(2)}) async-start(bf16[16,20,640]{2,1,0:T(8,128)(2,1)} %copy.20), calls=%async_computation | async-start | bytes 983040 | tf_op jit(solution)/shard_map/all_to_all | solution.py:19
  14.6 30.1 %collective-permute-start.1 = (bf16[3,320,384]{2,1,0:T(8,128)(2,1)S(1)}, bf16[3,320,384]{2,1,0:T(8,128)(2,1)S(1)}, u32[]{:S(2)}, u32[]{:S(2)}) collective-permute-start(bf16[3,320,384]{2,1,0:T(8,128)(2,1)S(1)} %bitcast.29), channel_id=1, source_target_pairs={{0,32},{32,64},{64,96},{96,128},{128,160},{160,192},{192,224},{224... | collective-permute-start | bytes 2211848 | tf_op jit(solution)/shard_map/ppermute | solution.py:28
  16.1 28.6 %collective-permute-start.2 = (bf16[3,320,384]{2,1,0:T(8,128)(2,1)S(1)}, bf16[3,320,384]{2,1,0:T(8,128)(2,1)}, u32[]{:S(2)}, u32[]{:S(2)}) collective-permute-start(bf16[3,320,384]{2,1,0:T(8,128)(2,1)S(1)} %bitcast.30), channel_id=1, source_target_pairs={{0,224},{32,0},{64,32},{96,64},{128,96},{160,128},{192,160},{224,1... | collective-permute-start | bytes 2211848 | tf_op jit(solution)/shard_map/ppermute | solution.py:28
  31.3 12.3 %collective-permute-start = (bf16[320,640]{1,0:T(8,128)(2,1)S(1)}, bf16[320,640]{1,0:T(8,128)(2,1)}, u32[]{:S(2)}, u32[]{:S(2)}) collective-permute-start(bf16[320,640]{1,0:T(8,128)(2,1)S(1)} %reshape.82), channel_id=1, source_target_pairs={{0,2},{2,0},{1,3},{3,1},{4,6},{6,4},{5,7},{7,5},{8,10},{10,8},{9,1... | collective-permute-start | bytes 1228808 | tf_op jit(solution)/shard_map/ppermute | solution.py:28
  44.7 10.7 %copy-start.11 = (bf16[3,320,384]{2,1,0:T(8,128)(2,1)}, bf16[3,320,384]{2,1,0:T(8,128)(2,1)S(1)}, u32[]{:S(2)}) copy-start(bf16[3,320,384]{2,1,0:T(8,128)(2,1)S(1)} %collective-permute-done.1.refs_8_) | copy-start | bytes 2211844
  44.7 20.9 %collective-permute-start.3 = (bf16[2,320,640]{2,1,0:T(8,128)(2,1)S(1)}, bf16[2,320,640]{2,1,0:T(8,128)(2,1)S(1)}, u32[]{:S(2)}, u32[]{:S(2)}) collective-permute-start(bf16[2,320,640]{2,1,0:T(8,128)(2,1)S(1)} %pad_maximum_fusion.refs_2_), channel_id=1, source_target_pairs={{0,4},{4,8},{8,12},{12,0},{1,5},{5,9},{9,13},{13,1},{2,6},{6,10},{... | collective-permute-start | bytes 2457608 | tf_op jit(solution)/shard_map/ppermute | solution.py:28
  46.0 19.6 %collective-permute-start.4 = (bf16[2,320,640]{2,1,0:T(8,128)(2,1)S(1)}, bf16[2,320,640]{2,1,0:T(8,128)(2,1)S(1)}, u32[]{:S(2)}, u32[]{:S(2)}) collective-permute-start(bf16[2,320,640]{2,1,0:T(8,128)(2,1)S(1)} %pad_maximum_fusion.refs_2_), channel_id=1, source_target_pairs={{0,12},{4,0},{8,4},{12,8},{1,13},{5,1},{9,5},{13,9},{2,14},{6,2},{... | collective-permute-start | bytes 2457608 | tf_op jit(solution)/shard_map/ppermute | solution.py:28
  47.5 18.1 %collective-permute-start.5 = (bf16[3,320,384]{2,1,0:T(8,128)(2,1)S(1)}, bf16[3,320,384]{2,1,0:T(8,128)(2,1)}, u32[]{:S(2)}, u32[]{:S(2)}) collective-permute-start(bf16[3,320,384]{2,1,0:T(8,128)(2,1)S(1)} %collective-permute-done.1.refs_8_), channel_id=1, source_target_pairs={{0,32},{32,64},{64,96},{96,128},{128,160},{160,192},{192,224},{224... | collective-permute-start | bytes 2211848 | tf_op jit(solution)/shard_map/ppermute | solution.py:28
  47.5 18.1 %collective-permute-start.6 = (bf16[3,320,384]{2,1,0:T(8,128)(2,1)}, bf16[3,320,384]{2,1,0:T(8,128)(2,1)}, u32[]{:S(2)}, u32[]{:S(2)}) collective-permute-start(bf16[3,320,384]{2,1,0:T(8,128)(2,1)} %collective-permute-done.2.refs_9_), channel_id=1, source_target_pairs={{0,224},{32,0},{64,32},{96,64},{128,96},{160,128},{192,160},{224,1... | collective-permute-start | bytes 2211848 | tf_op jit(solution)/shard_map/ppermute | solution.py:28
  50.2 2.1 %copy-start.1 = (bf16[384,5120]{1,0:T(8,128)(2,1)S(1)}, bf16[384,5120]{1,0:T(8,128)(2,1)}, u32[]{:S(2)}) copy-start(bf16[384,5120]{1,0:T(8,128)(2,1)} %w_ref) | copy-start | bytes 11796484
  65.6 17.4 %collective-permute-start.7 = (bf16[3,320,384]{2,1,0:T(8,128)(2,1)}, bf16[3,320,384]{2,1,0:T(8,128)(2,1)S(1)}, u32[]{:S(2)}, u32[]{:S(2)}) collective-permute-start(bf16[3,320,384]{2,1,0:T(8,128)(2,1)} %collective-permute-done.5.refs_10_), channel_id=1, source_target_pairs={{0,32},{32,64},{64,96},{96,128},{128,160},{160,192},{192,224},{224... | collective-permute-start | bytes 2211848 | tf_op jit(solution)/shard_map/ppermute | solution.py:28
  67.0 16.0 %collective-permute-start.8 = (bf16[3,320,384]{2,1,0:T(8,128)(2,1)}, bf16[3,320,384]{2,1,0:T(8,128)(2,1)}, u32[]{:S(2)}, u32[]{:S(2)}) collective-permute-start(bf16[3,320,384]{2,1,0:T(8,128)(2,1)} %collective-permute-done.6.refs_11_), channel_id=1, source_target_pairs={{0,224},{32,0},{64,32},{96,64},{128,96},{160,128},{192,160},{224,1... | collective-permute-start | bytes 2211848 | tf_op jit(solution)/shard_map/ppermute | solution.py:28
  68.4 9.6 %collective-permute-start.9 = (bf16[2,160,640]{2,1,0:T(8,128)(2,1)S(1)}, bf16[2,160,640]{2,1,0:T(8,128)(2,1)S(1)}, u32[]{:S(2)}, u32[]{:S(2)}) collective-permute-start(bf16[2,160,640]{2,1,0:T(8,128)(2,1)S(1)} %slice.25), channel_id=1, source_target_pairs={{0,4},{4,8},{8,12},{12,0},{1,5},{5,9},{9,13},{13,1},{2,6},{6,10},{... | collective-permute-start | bytes 1228808 | tf_op jit(solution)/shard_map/ppermute | solution.py:28
  69.0 26.2 %copy-start.16 = (s32[8]{0:T(128)S(1)}, s32[8]{0:T(128)}, u32[]{:S(2)}) copy-start(s32[8]{0:T(128)} %constant.53.clone) | copy-start | bytes 100
  69.1 9.7 %collective-permute-start.10 = (bf16[2,160,640]{2,1,0:T(8,128)(2,1)S(1)}, bf16[2,160,640]{2,1,0:T(8,128)(2,1)S(1)}, u32[]{:S(2)}, u32[]{:S(2)}) collective-permute-start(bf16[2,160,640]{2,1,0:T(8,128)(2,1)S(1)} %slice.26), channel_id=1, source_target_pairs={{0,12},{4,0},{8,4},{12,8},{1,13},{5,1},{9,5},{13,9},{2,14},{6,2},{... | collective-permute-start | bytes 1228808 | tf_op jit(solution)/shard_map/ppermute | solution.py:28
  83.0 33.7 %all-to-all-start.3 = ((bf16[8,192,640]{2,1,0:T(8,128)(2,1)}), bf16[8,192,640]{2,1,0:T(8,128)(2,1)}, u32[]{:S(2)}, u32[]{:S(2)}) async-start(bf16[8,192,640]{2,1,0:T(8,128)(2,1)} %shard_map.113), calls=%async_computation.3 | async-start | bytes 3932160 | tf_op jit(solution)/shard_map/all_to_all | solution.py:19
  90.8 16.2 %collective-permute-start.11 = (bf16[3,160,384]{2,1,0:T(8,128)(2,1)}, bf16[3,160,384]{2,1,0:T(8,128)(2,1)}, u32[]{:S(2)}, u32[]{:S(2)}) collective-permute-start(bf16[3,160,384]{2,1,0:T(8,128)(2,1)} %slice.27), channel_id=1, source_target_pairs={{0,32},{32,64},{64,96},{96,128},{128,160},{160,192},{192,224},{224... | collective-permute-start | bytes 1105928 | tf_op jit(solution)/shard_map/ppermute | solution.py:28
  92.9 14.0 %collective-permute-start.12 = (bf16[3,160,384]{2,1,0:T(8,128)(2,1)}, bf16[3,160,384]{2,1,0:T(8,128)(2,1)}, u32[]{:S(2)}, u32[]{:S(2)}) collective-permute-start(bf16[3,160,384]{2,1,0:T(8,128)(2,1)} %slice.28), channel_id=1, source_target_pairs={{0,224},{32,0},{64,32},{96,64},{128,96},{160,128},{192,160},{224,1... | collective-permute-start | bytes 1105928 | tf_op jit(solution)/shard_map/ppermute | solution.py:28
  100.0 6.9 %copy-start.4 = (bf16[2,160,640]{2,1,0:T(8,128)(2,1)S(1)}, bf16[2,160,640]{2,1,0:T(8,128)(2,1)}, u32[]{:S(2)}) copy-start(bf16[2,160,640]{2,1,0:T(8,128)(2,1)} %copy-done.2) | copy-start | bytes 1228804
  110.1 1.2 copy-start.7
  111.2 8.0 %collective-permute-start.13 = (bf16[320,1152]{1,0:T(8,128)(2,1)S(1)}, bf16[320,1152]{1,0:T(8,128)(2,1)S(1)}, u32[]{:S(2)}, u32[]{:S(2)}) collective-permute-start(bf16[320,1152]{1,0:T(8,128)(2,1)S(1)} %get-tuple-element.32), channel_id=1, source_target_pairs={{0,16},{16,0},{1,17},{17,1},{2,18},{18,2},{3,19},{19,3},{4,20},{20... | collective-permute-start | bytes 2211848 | tf_op jit(solution)/shard_map/ppermute | solution.py:28
  116.7 27.8 %collective-permute-start.14 = (bf16[8,192,640]{2,1,0:T(8,128)(2,1)}, bf16[8,192,640]{2,1,0:T(8,128)(2,1)}, u32[]{:S(2)}, u32[]{:S(2)}) collective-permute-start(bf16[8,192,640]{2,1,0:T(8,128)(2,1)} %all-to-all-done.3), channel_id=1, source_target_pairs={{0,16},{16,0},{1,17},{17,1},{2,18},{18,2},{3,19},{19,3},{4,20},{20... | collective-permute-start | bytes 5898248 | tf_op jit(solution)/shard_map/ppermute | solution.py:28
  119.3 1.4 copy-start.8
  139.8 4.6 %copy-start.17 = (f32[8,32]{1,0:T(8,128)S(1)}, f32[8,32]{1,0:T(8,128)}, u32[]{:S(2)}) copy-start(f32[8,32]{1,0:T(8,128)} %param.16) | copy-start | bytes 3076
  139.8 4.6 %copy-start.18 = (s32[2,1]{0,1:T(1,128)S(1)}, s32[2,1]{0,1:T(1,128)}, u32[]{:S(2)}) copy-start(s32[2,1]{0,1:T(1,128)} %param.15) | copy-start | bytes 28
  139.8 34.5 %all-to-all-start.2 = ((bf16[8,320,384]{2,1,0:T(8,128)(2,1)}), bf16[8,320,384]{2,1,0:T(8,128)(2,1)S(1)}, u32[]{:S(2)}, u32[]{:S(2)}) async-start(bf16[8,320,384]{2,1,0:T(8,128)(2,1)} %broadcast_in_dim.37), calls=%async_computation.2 | async-start | bytes 3932160 | tf_op jit(solution)/shard_map/all_to_all | solution.py:19
  174.3 3.9 %copy-start.14 = (bf16[2,1,160,640]{3,2,1,0:T(8,128)(2,1)S(1)}, bf16[2,1,160,640]{3,2,1,0:T(8,128)(2,1)}, u32[]{:S(2)}) copy-start(bf16[2,1,160,640]{3,2,1,0:T(8,128)(2,1)} %param.18) | copy-start | bytes 1228804
  174.3 9.1 %copy-start.15 = (bf16[640]{0:T(1024)(128)(2,1)S(1)}, bf16[640]{0:T(1024)(128)(2,1)}, u32[]{:S(2)}) copy-start(bf16[640]{0:T(1024)(128)(2,1)} %param.12) | copy-start | bytes 3844
  178.2 5.2 %copy-start.13 = (bf16[2,1,160,640]{3,2,1,0:T(8,128)(2,1)S(1)}, bf16[2,1,160,640]{3,2,1,0:T(8,128)(2,1)}, u32[]{:S(2)}) copy-start(bf16[2,1,160,640]{3,2,1,0:T(8,128)(2,1)} %param.10) | copy-start | bytes 1228804
  179.0 14.5 %all-to-all-start.4 = ((f32[32,2,672]{2,1,0:T(2,128)}), f32[32,2,672]{2,1,0:T(2,128)S(1)}, u32[]{:S(2)}, u32[]{:S(2)}) async-start(f32[32,2,672]{2,1,0:T(2,128)} %broadcast_in_dim.38), calls=%async_computation.4 | async-start | bytes 393216 | tf_op jit(solution)/shard_map/all_to_all | solution.py:19
  (6 other events, 5.8 us)

commit v7 on v6

--- a/solution.py
+++ b/solution.py
@@ -12,15 +12,11 @@
 MASKED = -1e30
 FRAME = ("z", "core")
 MP = ("x", "yhi")
-SMALL = pltpu.CompilerParams(vmem_limit_bytes=16 * 1024 * 1024)
+SMALL = pltpu.CompilerParams(vmem_limit_bytes=10 * 1024 * 1024)
 
 
 def exchange(x, axis):
     return lax.all_to_all(x, axis, split_axis=0, concat_axis=0, tiled=True)
-
-
-def from_everyone(x, axis):
-    return exchange(jnp.broadcast_to(x, (lax.axis_size(axis), *x.shape)), axis)
 
 
 def shift(x, axis, by):
@@ -102,7 +98,7 @@
         out_shape=out_shape,
         input_output_aliases={} if acc is None else {len(operands) + 1: 0},
         scratch_shapes=[pltpu.VMEM((sum(len(c) for c in counts), rows, width), jnp.bfloat16)],
-        compiler_params=pltpu.CompilerParams(vmem_limit_bytes=32 * 1024 * 1024),
+        compiler_params=pltpu.CompilerParams(vmem_limit_bytes=20 * 1024 * 1024),
     )(slots, core, *operands)
 
 
@@ -145,22 +141,95 @@
     )(own, other, bias)
 
 
-def blocks_kernel(core, w_ref, out_ref):
-    out_ref[0] = w_ref[...]
+def out_product(a, where, dx, half, other):
+    n = half.shape[0] // 2
+    block = 2 * ((where[1] + dx) & (n - 1))
+    w = []
+    for b in range(2):
+        m = block + (b ^ where[2])
+        mine, theirs = half[m], other[m]
+        first = where[0] == 0
+        w += [jnp.where(first, mine, theirs), jnp.where(first, theirs, mine)]
+    x = jnp.concatenate(a, axis=1)
+    return jnp.dot(x, jnp.concatenate(w, axis=0), preferred_element_type=jnp.float32)
+
+
+def near_kernel(where, both, right, left, half, other, acc):
+    acc[...] = out_product((both[0], both[1]), where, 0, half, other)
+    acc[...] += out_product((right[0], right[1]), where, 1, half, other)
+    acc[...] += out_product((left[0], left[1]), where, 3, half, other)
+
+
+def far_kernel(where, top, low, half, other, acc, xin, gate, cot, codevec, next_ref, terms):
+    far = tuple(jnp.concatenate([top[b], low[b]], axis=0) for b in range(2))
+    mixed = acc[...] + out_product(far, where, 2, half, other)
+    rows, width = mixed.shape
+    clips = gate.shape[0]
+    spots = rows // clips
+    sums = []
+    for c in range(clips):
+        at = slice(c * spots, (c + 1) * spots)
+        m = mixed[at]
+        moved = xin[at].astype(jnp.float32) + gate[c : c + 1] * m
+        next_ref[at] = moved.astype(jnp.bfloat16)
+        sums.append(jnp.sum(cot[at].astype(jnp.float32) * m, axis=0, keepdims=True))
+    dgate = jnp.concatenate(sums, axis=0)
+    for i in range(terms.shape[0]):
+        terms[i, :, :width] = dgate
+        terms[i, :, width:] = codevec[...]
+
+
+def near(where, *operands):
+    rows, width = operands[0].shape[1], operands[3].shape[2]
+    smem, vmem = pl.BlockSpec(memory_space=pltpu.SMEM), pl.BlockSpec(memory_space=pltpu.VMEM)
+    return pl.pallas_call(
+        near_kernel,
+        in_specs=[smem] + [vmem] * 5,
+        out_specs=vmem,
+        out_shape=jax.ShapeDtypeStruct((rows, width), jnp.float32),
+        compiler_params=SMALL,
+    )(where, *operands)
+
+
+def finish(where, peers, *operands):
+    rows, width = operands[4].shape
+    clips = operands[6].shape[0]
+    smem, vmem = pl.BlockSpec(memory_space=pltpu.SMEM), pl.BlockSpec(memory_space=pltpu.VMEM)
+    return pl.pallas_call(
+        far_kernel,
+        in_specs=[smem] + [vmem] * 9,
+        out_specs=[vmem, vmem],
+        out_shape=[
+            jax.ShapeDtypeStruct((rows, width), jnp.bfloat16),
+            jax.ShapeDtypeStruct((peers, clips, width + operands[8].shape[1]), jnp.float32),
+        ],
+        compiler_params=SMALL,
+    )(where, *operands)
+
+
+def blocks_kernel(core, w_ref, out_ref, sem):
+    n, half, width = out_ref.shape
+    rows = pl.ds(pl.multiple_of(core[0] * half, half), half)
+    copies = [
+        pltpu.make_async_copy(w_ref.at[rows, pl.ds(m * width, width)], out_ref.at[m], sem.at[m])
+        for m in range(n)
+    ]
+    for copy in copies:
+        copy.start()
+    for copy in copies:
+        copy.wait()
 
 
 def column_blocks(w, core, width):
     heads, full = w.shape
     half, n = heads // 2, full // width
+    hbm = pl.BlockSpec(memory_space=pltpu.HBM)
     return pl.pallas_call(
         blocks_kernel,
-        grid_spec=pltpu.PrefetchScalarGridSpec(
-            num_scalar_prefetch=1,
-            grid=(n,),
-            in_specs=[pl.BlockSpec((half, width), lambda m, core: (core[0], m))],
-            out_specs=pl.BlockSpec((1, half, width), lambda m, core: (m, 0, 0)),
-        ),
+        in_specs=[pl.BlockSpec(memory_space=pltpu.SMEM), hbm],
+        out_specs=hbm,
         out_shape=jax.ShapeDtypeStruct((n, half, width), w.dtype),
+        scratch_shapes=[pltpu.SemaphoreType.DMA((n,))],
         compiler_params=SMALL,
     )(core, w)
 
@@ -188,15 +257,12 @@
     middle = rows // 2
     top, low = shift(left[:, :middle], "x", 1), shift(right[:, middle:], "x", -1)
     up3, down3 = shift(up2, "z", 1), shift(down2, "z", -1)
-    up3, down3, top, low, blocks = lax.optimization_barrier((up3, down3, top, low, blocks))
+    top, low, blocks = lax.optimization_barrier((top, low, blocks))
+    up3, down3, top, low = lax.optimization_barrier((up3, down3, top, low))
     up4 = shift(up3[:, : depth // 2], "z", 1)
     down4 = shift(down3[:, depth // 2 :], "z", -1)
 
     half = exchange(blocks, MP)
-    other_half = shift(half, "core", 1)
-    out_block = jnp.concatenate(
-        [jnp.where(core == 0, half, other_half), jnp.where(core == 0, other_half, half)], axis=1
-    )
 
     x, yhi = lax.axis_index("x"), lax.axis_index("yhi")
     shard = (z + jnp.array([0, zs - 1, 1, zs - 2, 2, zs - 3, 3, zs - 4], jnp.int32)) & (zs - 1)
@@ -206,20 +272,26 @@
     (acc,) = project(features, early, slots[:7], core1)
     _, kept, sent = project(features, [[(up4, down4)]], slots[7:], core1, acc, last=True)
     attn = attention(kept, shift(sent, "core", 1), frames)
+    attn, half = lax.optimization_barrier((attn, half))
+    other_half = shift(half, "core", 1)
     attn = exchange(attn, FRAME).reshape(rows, heads)
-    all_heads = from_everyone(attn, MP)
-    mixed = lax.dot_general(
-        all_heads, out_block, (((0, 2), (0, 1)), ((), ())), preferred_element_type=jnp.float32
-    ).reshape(clips, spots, width)
+    attn_both = jnp.stack([attn, shift(attn, "yhi", 1)])
+    attn_left, attn_right = shift(attn_both, "x", 1), shift(attn_both, "x", -1)
+    attn_top = shift(attn_left[:, :middle], "x", 1)
+    attn_low = shift(attn_right[:, middle:], "x", -1)
+    where = jnp.stack([core, x, yhi]).astype(jnp.int32)
+    acc = near(where, attn_both, attn_right, attn_left, half, other_half)
     onehot = (action_idx.reshape(clips)[:, None] == jnp.arange(codebook.shape[0])[None, :]).astype(
         jnp.float32
     )
     codevec = jnp.dot(onehot, codebook, precision=lax.Precision.HIGHEST)
     gate = jnp.dot(codevec, act_proj, precision=lax.Precision.HIGHEST)
-    xin = xin.reshape(clips, spots, width)
-    next_state = (xin.astype(jnp.float32) + gate[:, None, :] * mixed).astype(jnp.bfloat16)
-    dgate = jnp.sum(cotangent.reshape(clips, spots, width).astype(jnp.float32) * mixed, axis=1)
-    terms = from_everyone(jnp.concatenate([dgate, codevec], axis=1), FRAME + ("dp",))
+    peers = frames * lax.axis_size("dp")
+    next_state, terms = finish(
+        where, peers, attn_top, attn_low, half, other_half, acc, xin, gate,
+        cotangent.reshape(rows, width), codevec,
+    )
+    terms = exchange(terms, FRAME + ("dp",))
     terms = terms.reshape(-1, terms.shape[-1])
     grad_proj = lax.dot_general(
         terms[:, width:],

time: 195 us -> 186 us (0.954)
  waiting for transfers between devices: 80.1 us -> 60.5 us
  blocking collectives: 16.2 us -> 31.5 us
  other arithmetic: 8.59 us -> 3.32 us
  matrix products: 5.12 us -> 1.25 us
  Pallas kernels: 14.4 us -> 18 us
  local copies, waits for them, and re-layouts: 18.4 us -> 20.8 us
    all_to_all x4 -> x2, waiting for transfers between devices: 50.5 us -> 13.9 us  [exchange(): return lax.all_to_all(x, axis, split_axis=0, concat_axis=0, tiled=True)]
    ppermute x15 -> x20, waiting for transfers between devices: 29.6 us -> 46.6 us  [shift(): return lax.ppermute(x, axis, [(i, (i + by) % n) for i in range(n)])]
    all_to_all x1 -> x2, blocking collectives: 16.2 us -> 31.5 us  [exchange(): return lax.all_to_all(x, axis, split_axis=0, concat_axis=0, tiled=True)]
    all_to_all x4 -> x2, starting transfers between devices: 25.6 us -> 16.8 us  [exchange(): return lax.all_to_all(x, axis, split_axis=0, concat_axis=0, tiled=True)]
    ppermute x15 -> x20, starting transfers between devices: 25.1 us -> 32.5 us  [shift(): return lax.ppermute(x, axis, [(i, (i + by) % n) for i in range(n)])]
    select_n x1 -> x0, other arithmetic: 4.45 us -> none  [body(): jnp.where(core == 0, half, other_half)]
    dot_general x1 -> x0, matrix products: 3.87 us -> none  [body(): lax.dot_general(all_heads, out_block, (((0, 2), (0, 1)), ((), ())), prefe...]
    pallas_call x1 -> x3, Pallas kernels: 3.11 us -> 6.29 us  [the longest x1 3 us: near(): pl.pallas_call(near_kernel, in_specs=[smem] + [vmem] * 5, out_specs=vmem,...]
  transfers between devices with their start and end apart: 19 -> 22, of which waited for: 8 -> 9; matrix products, arithmetic and copies ran while one was open for 6% -> 4% of each run, Pallas kernels for 7% -> 8%
where the time goes in v7:
time: 186 us
  waiting for transfers between devices  60.5 us (33%)
  starting transfers between devices  49.3 us (27%)
  blocking collectives  31.5 us (17%)
  local copies, waits for them, and re-layouts  20.8 us (11%)
  Pallas kernels  18 us (10%)
  other arithmetic  3.32 us (2%)
    ppermute x20, waiting for transfers between devices, shift(): return lax.ppermute(x, axis, [(i, (i + by) % n) for i in range(n)])  46.6 us
    ppermute x20, starting transfers between devices, shift(): return lax.ppermute(x, axis, [(i, (i + by) % n) for i in range(n)])  32.5 us
    all_to_all x2, blocking collectives, exchange(): return lax.all_to_all(x, axis, split_axis=0, concat_axis=0, tiled=True)  31.5 us
    all_to_all x2, starting transfers between devices, exchange(): return lax.all_to_all(x, axis, split_axis=0, concat_axis=0, tiled=True)  16.8 us
    all_to_all x2, waiting for transfers between devices, exchange(): return lax.all_to_all(x, axis, split_axis=0, concat_axis=0, tiled=True)  13.9 us
    unnamed x45, local copies, waits for them, and re-layouts  13.2 us
    pallas_call x2, Pallas kernels, project(): pl.pallas_call(kernel, in_specs=[smem, smem] + [vmem] * len(operands), ou...  10.3 us
  transfers between devices with their start and end apart: 22, of which 9 were waited for; matrix products, arithmetic and copies ran while one was open for 4% of the time, Pallas kernels for 8%

profile of v7, /device:TPU:1, one launch (start us, length us, event | category | flops | bytes accessed | tf_op | source)
XLA Modules:
  0.0 185.5 jit_solution(10001163234324229216)
XLA Ops:
  4.6 10.0 %all-to-all-start = ((bf16[16,20,640]{2,1,0:T(8,128)(2,1)}), bf16[16,20,640]{2,1,0:T(8,128)(2,1)S(1)}, u32[]{:S(2)}, u32[]{:S(2)}) async-start(bf16[16,20,640]{2,1,0:T(8,128)(2,1)} %copy.20), calls=%async_computation | async-start | bytes 983040 | tf_op jit(solution)/shard_map/all_to_all | solution.py:19
  14.6 1.5 collective-permute-start.1
  16.1 1.3 collective-permute-start.2
  17.4 13.8 %all-to-all-done = bf16[16,20,640]{2,1,0:T(8,128)(2,1)S(1)} async-done(((bf16[16,20,640]{2,1,0:T(8,128)(2,1)}), bf16[16,20,640]{2,1,0:T(8,128)(2,1)S(1)}, u32[]{:S(2)}, u32[]{:S(2)}) %all-to-all-start) | async-done | bytes 409632 | tf_op jit(solution)/shard_map/all_to_all | solution.py:19
  31.3 3.0 %collective-permute-start = (bf16[320,640]{1,0:T(8,128)(2,1)S(1)}, bf16[320,640]{1,0:T(8,128)(2,1)S(1)}, u32[]{:S(2)}, u32[]{:S(2)}) collective-permute-start(bf16[320,640]{1,0:T(8,128)(2,1)S(1)} %reshape.68), channel_id=1, source_target_pairs={{0,2},{2,0},{1,3},{3,1},{4,6},{6,4},{5,7},{7,5},{8,10},{10,8},{9,1... | collective-permute-start | bytes 1228808 | tf_op jit(solution)/shard_map/ppermute | solution.py:24
  35.2 8.3 %collective-permute-done = bf16[320,640]{1,0:T(8,128)(2,1)S(1)} collective-permute-done((bf16[320,640]{1,0:T(8,128)(2,1)S(1)}, bf16[320,640]{1,0:T(8,128)(2,1)S(1)}, u32[]{:S(2)}, u32[]{:S(2)}) %collective-permute-start) | collective-permute-done | bytes 409632 | tf_op jit(solution)/shard_map/ppermute | solution.py:24
  47.6 1.5 collective-permute-start.4
  49.0 2.7 %collective-permute-start.6 = (bf16[3,320,384]{2,1,0:T(8,128)(2,1)}, bf16[3,320,384]{2,1,0:T(8,128)(2,1)}, u32[]{:S(2)}, u32[]{:S(2)}) collective-permute-start(bf16[3,320,384]{2,1,0:T(8,128)(2,1)} %collective-permute-done.2.refs_9_), channel_id=1, source_target_pairs={{0,224},{32,0},{64,32},{96,64},{128,96},{160,128},{192,160},{224,1... | collective-permute-start | bytes 2211848 | tf_op jit(solution)/shard_map/ppermute | solution.py:24
  51.7 2.1 %copy-done.8 = bf16[384,5120]{1,0:T(8,128)(2,1)S(1)} copy-done((bf16[384,5120]{1,0:T(8,128)(2,1)S(1)}, bf16[384,5120]{1,0:T(8,128)(2,1)}, u32[]{:S(2)}) %copy-start.8) | copy-done | bytes 3932184
  54.2 1.3 copy-done.1
  55.5 12.4 %collective-permute-done.5.refs_10_ = bf16[3,320,384]{2,1,0:T(8,128)(2,1)} collective-permute-done((bf16[3,320,384]{2,1,0:T(8,128)(2,1)}, bf16[3,320,384]{2,1,0:T(8,128)(2,1)}, u32[]{:S(2)}, u32[]{:S(2)}) %collective-permute-start.5) | collective-permute-done | bytes 737312 | tf_op jit(solution)/shard_map/ppermute | solution.py:24
  68.5 2.4 %collective-permute-start.10 = (bf16[2,160,640]{2,1,0:T(8,128)(2,1)S(1)}, bf16[2,160,640]{2,1,0:T(8,128)(2,1)S(1)}, u32[]{:S(2)}, u32[]{:S(2)}) collective-permute-start(bf16[2,160,640]{2,1,0:T(8,128)(2,1)S(1)} %slice.32), channel_id=1, source_target_pairs={{0,12},{4,0},{8,4},{12,8},{1,13},{5,1},{9,5},{13,9},{2,14},{6,2},{... | collective-permute-start | bytes 1228808 | tf_op jit(solution)/shard_map/ppermute | solution.py:24
  70.9 2.7 %collective-permute-start.8 = (bf16[3,320,384]{2,1,0:T(8,128)(2,1)}, bf16[3,320,384]{2,1,0:T(8,128)(2,1)}, u32[]{:S(2)}, u32[]{:S(2)}) collective-permute-start(bf16[3,320,384]{2,1,0:T(8,128)(2,1)} %collective-permute-done.6.refs_11_), channel_id=1, source_target_pairs={{0,224},{32,0},{64,32},{96,64},{128,96},{160,128},{192,160},{224,1... | collective-permute-start | bytes 2211848 | tf_op jit(solution)/shard_map/ppermute | solution.py:24
  73.5 5.2 %collective-permute-done.9.refs_4_ = bf16[2,160,640]{2,1,0:T(8,128)(2,1)S(1)} collective-permute-done((bf16[2,160,640]{2,1,0:T(8,128)(2,1)S(1)}, bf16[2,160,640]{2,1,0:T(8,128)(2,1)S(1)}, u32[]{:S(2)}, u32[]{:S(2)}) %collective-permute-start.9) | collective-permute-done | bytes 409632 | tf_op jit(solution)/shard_map/ppermute | solution.py:24
  80.3 6.8 %all-to-all-start.1 = ((bf16[8,192,640]{2,1,0:T(8,128)(2,1)}), bf16[8,192,640]{2,1,0:T(8,128)(2,1)S(1)}, u32[]{:S(2)}, u32[]{:S(2)}) async-start(bf16[8,192,640]{2,1,0:T(8,128)(2,1)} %copy-done.1), calls=%async_computation.1 | async-start | bytes 3932160 | tf_op jit(solution)/shard_map/all_to_all | solution.py:19
  88.2 1.8 slice.33
  90.0 1.8 slice.34
  91.8 2.7 %collective-permute-start.12 = (bf16[3,160,384]{2,1,0:T(8,128)(2,1)}, bf16[3,160,384]{2,1,0:T(8,128)(2,1)}, u32[]{:S(2)}, u32[]{:S(2)}) collective-permute-start(bf16[3,160,384]{2,1,0:T(8,128)(2,1)} %slice.34), channel_id=1, source_target_pairs={{0,224},{32,0},{64,32},{96,64},{128,96},{160,128},{192,160},{224,1... | collective-permute-start | bytes 1105928 | tf_op jit(solution)/shard_map/ppermute | solution.py:24
  101.6 7.2 %shard_map.114.refs_9_ = f32[640,1152]{1,0:T(8,128)S(1)} custom-call(s32[7]{0:T(128)S(1)} %bitcast.31, s32[1]{0:T(128)} %bitcast.core.refs_1_, bf16[2,320,640]{2,1,0:T(8,128)(2,1)S(1)} %pad_maximum_fusion.refs_2_, bf16[2,320,640]{2,1,0:T(8,128)(2,1)S(1)} %copy-done.6, bf16[2,160,640]{2,1,0:T(8,128)(2,1)S(1)} %copy-done.10, ...), custom_call_target="tpu_custom_call" | custom-call | tf_op jit(solution)/shard_map/pallas_call | solution.py:94
  108.9 3.1 %shard_map.115 = (f32[640,1152]{1,0:T(8,128)S(1)}, f32[320,1152]{1,0:T(8,128)S(1)}, bf16[320,1152]{1,0:T(8,128)(2,1)S(1)}) custom-call(s32[1]{0:T(128)} %slice.30.refs_0_, s32[1]{0:T(128)} %bitcast.core.refs_1_, bf16[2,320,640]{2,1,0:T(8,128)(2,1)S(1)} %pad_maximum_fusion.refs_2_, ...), custom_call_target="tpu_custom_call", output_to_operand_aliasing={{0}: (9, {})} | custom-call | tf_op jit(solution)/shard_map/pallas_call | solution.py:94
  112.0 3.7 %collective-permute-start.13 = (bf16[320,1152]{1,0:T(8,128)(2,1)S(1)}, bf16[320,1152]{1,0:T(8,128)(2,1)S(1)}, u32[]{:S(2)}, u32[]{:S(2)}) collective-permute-start(bf16[320,1152]{1,0:T(8,128)(2,1)S(1)} %get-tuple-element.40), channel_id=1, source_target_pairs={{0,16},{16,0},{1,17},{17,1},{2,18},{18,2},{3,19},{19,3},{4,20},{20... | collective-permute-start | bytes 2211848 | tf_op jit(solution)/shard_map/ppermute | solution.py:24
  115.9 1.7 collective-permute-done.13.other_ref
  117.6 1.4 shard_map.116
  119.4 15.8 %all_to_all.20 = bf16[16,20,384]{2,1,0:T(8,128)(2,1)S(1)} all-to-all(bf16[16,20,384]{2,1,0:T(8,128)(2,1)S(1)} %shard_map.116), channel_id=1, replica_groups=mesh['z'=8,'core'=2,'x'=4,'yhi'=2,'dp'=2] {'z','core'}, dimensions={0} | all-to-all | bytes 491520 | tf_op jit(solution)/shard_map/all_to_all | solution.py:19
  135.3 3.3 %collective-permute-start.14 = (bf16[320,384]{1,0:T(8,128)(2,1)S(1)}, bf16[320,384]{1,0:T(8,128)(2,1)S(1)}, u32[]{:S(2)}, u32[]{:S(2)}) collective-permute-start(bf16[320,384]{1,0:T(8,128)(2,1)S(1)} %reshape.69), channel_id=1, source_target_pairs={{0,2},{2,0},{1,3},{3,1},{4,6},{6,4},{5,7},{7,5},{8,10},{10,8},{9,1... | collective-permute-start | bytes 737288 | tf_op jit(solution)/shard_map/ppermute | solution.py:24
  138.6 6.0 %collective-permute-done.14 = bf16[320,384]{1,0:T(8,128)(2,1)S(1)} collective-permute-done((bf16[320,384]{1,0:T(8,128)(2,1)S(1)}, bf16[320,384]{1,0:T(8,128)(2,1)S(1)}, u32[]{:S(2)}, u32[]{:S(2)}) %collective-permute-start.14) | collective-permute-done | bytes 245792 | tf_op jit(solution)/shard_map/ppermute | solution.py:24
  144.7 2.7 %collective-permute-start.17 = (bf16[2,320,384]{2,1,0:T(8,128)(2,1)S(1)}, bf16[2,320,384]{2,1,0:T(8,128)(2,1)S(1)}, u32[]{:S(2)}, u32[]{:S(2)}) collective-permute-start(bf16[2,320,384]{2,1,0:T(8,128)(2,1)S(1)} %pad_maximum_fusion.1.both), channel_id=1, source_target_pairs={{0,12},{4,0},{8,4},{12,8},{1,13},{5,1},{9,5},{13,9},{2,14},{6,2},{... | collective-permute-start | bytes 1474568 | tf_op jit(solution)/shard_map/ppermute | solution.py:24
  147.6 10.8 %collective-permute-done.15.left = bf16[2,320,384]{2,1,0:T(8,128)(2,1)S(1)} collective-permute-done((bf16[2,320,384]{2,1,0:T(8,128)(2,1)S(1)}, bf16[2,320,384]{2,1,0:T(8,128)(2,1)S(1)}, u32[]{:S(2)}, u32[]{:S(2)}) %collective-permute-start.15) | collective-permute-done | bytes 491552 | tf_op jit(solution)/shard_map/ppermute | solution.py:24
  158.5 2.9 %collective-permute-start.18 = (bf16[2,160,384]{2,1,0:T(8,128)(2,1)S(1)}, bf16[2,160,384]{2,1,0:T(8,128)(2,1)S(1)}, u32[]{:S(2)}, u32[]{:S(2)}) collective-permute-start(bf16[2,160,384]{2,1,0:T(8,128)(2,1)S(1)} %slice.41), channel_id=1, source_target_pairs={{0,12},{4,0},{8,4},{12,8},{1,13},{5,1},{9,5},{13,9},{2,14},{6,2},{... | collective-permute-start | bytes 737288 | tf_op jit(solution)/shard_map/ppermute | solution.py:24
  161.7 3.0 %shard_map.117.acc = f32[320,640]{1,0:T(8,128)S(1)} custom-call(s32[3]{0:T(128)S(1)} %pad_add_fusion.where, bf16[2,320,384]{2,1,0:T(8,128)(2,1)S(1)} %pad_maximum_fusion.1.both, bf16[2,320,384]{2,1,0:T(8,128)(2,1)S(1)} %collective-permute-done.17.right, bf16[2,320,384]{2,1,0:T(8,128)(2,1)S(1)} %collective-permute-done.15.left, ...), custom_call_target="tpu_custom_call" | custom-call | tf_op jit(solution)/shard_map/pallas_call | solution.py:185
  165.9 2.9 %shard_map.118 = (bf16[320,640]{1,0:T(8,128)(2,1)}, f32[32,2,672]{2,1,0:T(2,128)S(1)}) custom-call(s32[3]{0:T(128)S(1)} %pad_add_fusion.where, bf16[2,160,384]{2,1,0:T(8,128)(2,1)S(1)} %collective-permute-done.16.top, bf16[2,160,384]{2,1,0:T(8,128)(2,1)S(1)} %collective-permute-done.18.low, bf16[8,192,640]{2,1,0:T(8,128)(2,1)S(1)} %all-to-all-done.1.half, ...), custom_call_target="tpu_custom_call" | custom-call | tf_op jit(solution)/shard_map/pallas_call | solution.py:198
  168.8 15.7 %all_to_all.21 = f32[32,2,672]{2,1,0:T(2,128)S(1)} all-to-all(f32[32,2,672]{2,1,0:T(2,128)S(1)} %get-tuple-element.45), channel_id=1, replica_groups=mesh['z'=8,'core'=2,'x'=4,'yhi'=2,'dp'=2] {'z','core','dp'}, dimensions={0} | all-to-all | bytes 344064 | tf_op jit(solution)/shard_map/all_to_all | solution.py:19
  (92 shorter events, 23.3 us)
Async XLA Ops:
  0.6 160.9 %copy-start = (f32[32,640]{1,0:T(8,128)S(1)}, f32[32,640]{1,0:T(8,128)}, u32[]{:S(2)}) copy-start(f32[32,640]{1,0:T(8,128)} %param.17) | copy-start | bytes 245764
  2.9 11.7 %copy-start.13 = (bf16[320,3,384]{2,0,1:T(8,128)(2,1)S(1)}, bf16[320,3,384]{2,0,1:T(8,128)(2,1)}, u32[]{:S(2)}) copy-start(bf16[320,3,384]{2,0,1:T(8,128)(2,1)} %param.13) | copy-start | bytes 2211844
  4.6 26.6 %all-to-all-start = ((bf16[16,20,640]{2,1,0:T(8,128)(2,1)}), bf16[16,20,640]{2,1,0:T(8,128)(2,1)S(1)}, u32[]{:S(2)}, u32[]{:S(2)}) async-start(bf16[16,20,640]{2,1,0:T(8,128)(2,1)} %copy.20), calls=%async_computation | async-start | bytes 983040 | tf_op jit(solution)/shard_map/all_to_all | solution.py:19
  14.6 30.8 %collective-permute-start.1 = (bf16[3,320,384]{2,1,0:T(8,128)(2,1)S(1)}, bf16[3,320,384]{2,1,0:T(8,128)(2,1)S(1)}, u32[]{:S(2)}, u32[]{:S(2)}) collective-permute-start(bf16[3,320,384]{2,1,0:T(8,128)(2,1)S(1)} %bitcast.27), channel_id=1, source_target_pairs={{0,32},{32,64},{64,96},{96,128},{128,160},{160,192},{192,224},{224... | collective-permute-start | bytes 2211848 | tf_op jit(solution)/shard_map/ppermute | solution.py:24
  16.1 30.3 %collective-permute-start.2 = (bf16[3,320,384]{2,1,0:T(8,128)(2,1)S(1)}, bf16[3,320,384]{2,1,0:T(8,128)(2,1)}, u32[]{:S(2)}, u32[]{:S(2)}) collective-permute-start(bf16[3,320,384]{2,1,0:T(8,128)(2,1)S(1)} %bitcast.28), channel_id=1, source_target_pairs={{0,224},{32,0},{64,32},{96,64},{128,96},{160,128},{192,160},{224,1... | collective-permute-start | bytes 2211848 | tf_op jit(solution)/shard_map/ppermute | solution.py:24
  31.3 12.2 %collective-permute-start = (bf16[320,640]{1,0:T(8,128)(2,1)S(1)}, bf16[320,640]{1,0:T(8,128)(2,1)S(1)}, u32[]{:S(2)}, u32[]{:S(2)}) collective-permute-start(bf16[320,640]{1,0:T(8,128)(2,1)S(1)} %reshape.68), channel_id=1, source_target_pairs={{0,2},{2,0},{1,3},{3,1},{4,6},{6,4},{5,7},{7,5},{8,10},{10,8},{9,1... | collective-permute-start | bytes 1228808 | tf_op jit(solution)/shard_map/ppermute | solution.py:24
  46.4 21.5 %collective-permute-start.3 = (bf16[2,320,640]{2,1,0:T(8,128)(2,1)S(1)}, bf16[2,320,640]{2,1,0:T(8,128)(2,1)S(1)}, u32[]{:S(2)}, u32[]{:S(2)}) collective-permute-start(bf16[2,320,640]{2,1,0:T(8,128)(2,1)S(1)} %pad_maximum_fusion.refs_2_), channel_id=1, source_target_pairs={{0,4},{4,8},{8,12},{12,0},{1,5},{5,9},{9,13},{13,1},{2,6},{6,10},{... | collective-permute-start | bytes 2457608 | tf_op jit(solution)/shard_map/ppermute | solution.py:24
  47.6 20.3 %collective-permute-start.4 = (bf16[2,320,640]{2,1,0:T(8,128)(2,1)S(1)}, bf16[2,320,640]{2,1,0:T(8,128)(2,1)S(1)}, u32[]{:S(2)}, u32[]{:S(2)}) collective-permute-start(bf16[2,320,640]{2,1,0:T(8,128)(2,1)S(1)} %pad_maximum_fusion.refs_2_), channel_id=1, source_target_pairs={{0,12},{4,0},{8,4},{12,8},{1,13},{5,1},{9,5},{13,9},{2,14},{6,2},{... | collective-permute-start | bytes 2457608 | tf_op jit(solution)/shard_map/ppermute | solution.py:24
  49.0 18.8 %collective-permute-start.5 = (bf16[3,320,384]{2,1,0:T(8,128)(2,1)}, bf16[3,320,384]{2,1,0:T(8,128)(2,1)}, u32[]{:S(2)}, u32[]{:S(2)}) collective-permute-start(bf16[3,320,384]{2,1,0:T(8,128)(2,1)} %copy-done.15), channel_id=1, source_target_pairs={{0,32},{32,64},{64,96},{96,128},{128,160},{160,192},{192,224},{224... | collective-permute-start | bytes 2211848 | tf_op jit(solution)/shard_map/ppermute | solution.py:24
  49.0 18.8 %collective-permute-start.6 = (bf16[3,320,384]{2,1,0:T(8,128)(2,1)}, bf16[3,320,384]{2,1,0:T(8,128)(2,1)}, u32[]{:S(2)}, u32[]{:S(2)}) collective-permute-start(bf16[3,320,384]{2,1,0:T(8,128)(2,1)} %collective-permute-done.2.refs_9_), channel_id=1, source_target_pairs={{0,224},{32,0},{64,32},{96,64},{128,96},{160,128},{192,160},{224,1... | collective-permute-start | bytes 2211848 | tf_op jit(solution)/shard_map/ppermute | solution.py:24
  67.9 12.4 %copy-start.2 = (bf16[2,320,640]{2,1,0:T(8,128)(2,1)}, bf16[2,320,640]{2,1,0:T(8,128)(2,1)S(1)}, u32[]{:S(2)}) copy-start(bf16[2,320,640]{2,1,0:T(8,128)(2,1)S(1)} %collective-permute-done.3.refs_6_) | copy-start | bytes 2457604
  67.9 12.4 %copy-start.5 = (bf16[2,320,640]{2,1,0:T(8,128)(2,1)}, bf16[2,320,640]{2,1,0:T(8,128)(2,1)S(1)}, u32[]{:S(2)}) copy-start(bf16[2,320,640]{2,1,0:T(8,128)(2,1)S(1)} %collective-permute-done.4.refs_3_) | copy-start | bytes 2457604
  68.0 10.8 %collective-permute-start.9 = (bf16[2,160,640]{2,1,0:T(8,128)(2,1)S(1)}, bf16[2,160,640]{2,1,0:T(8,128)(2,1)S(1)}, u32[]{:S(2)}, u32[]{:S(2)}) collective-permute-start(bf16[2,160,640]{2,1,0:T(8,128)(2,1)S(1)} %slice.31), channel_id=1, source_target_pairs={{0,4},{4,8},{8,12},{12,0},{1,5},{5,9},{9,13},{13,1},{2,6},{6,10},{... | collective-permute-start | bytes 1228808 | tf_op jit(solution)/shard_map/ppermute | solution.py:24
  68.4 26.0 %copy-start.19 = (s32[8]{0:T(128)S(1)}, s32[8]{0:T(128)}, u32[]{:S(2)}) copy-start(s32[8]{0:T(128)} %constant.52.clone) | copy-start | bytes 100
  68.5 11.0 %collective-permute-start.10 = (bf16[2,160,640]{2,1,0:T(8,128)(2,1)S(1)}, bf16[2,160,640]{2,1,0:T(8,128)(2,1)S(1)}, u32[]{:S(2)}, u32[]{:S(2)}) collective-permute-start(bf16[2,160,640]{2,1,0:T(8,128)(2,1)S(1)} %slice.32), channel_id=1, source_target_pairs={{0,12},{4,0},{8,4},{12,8},{1,13},{5,1},{9,5},{13,9},{2,14},{6,2},{... | collective-permute-start | bytes 1228808 | tf_op jit(solution)/shard_map/ppermute | solution.py:24
  70.8 17.4 %collective-permute-start.7 = (bf16[3,320,384]{2,1,0:T(8,128)(2,1)}, bf16[3,320,384]{2,1,0:T(8,128)(2,1)}, u32[]{:S(2)}, u32[]{:S(2)}) collective-permute-start(bf16[3,320,384]{2,1,0:T(8,128)(2,1)} %collective-permute-done.5.refs_10_), channel_id=1, source_target_pairs={{0,32},{32,64},{64,96},{96,128},{128,160},{160,192},{192,224},{224... | collective-permute-start | bytes 2211848 | tf_op jit(solution)/shard_map/ppermute | solution.py:24
  70.9 17.4 %collective-permute-start.8 = (bf16[3,320,384]{2,1,0:T(8,128)(2,1)}, bf16[3,320,384]{2,1,0:T(8,128)(2,1)}, u32[]{:S(2)}, u32[]{:S(2)}) collective-permute-start(bf16[3,320,384]{2,1,0:T(8,128)(2,1)} %collective-permute-done.6.refs_11_), channel_id=1, source_target_pairs={{0,224},{32,0},{64,32},{96,64},{128,96},{160,128},{192,160},{224,1... | collective-permute-start | bytes 2211848 | tf_op jit(solution)/shard_map/ppermute | solution.py:24
  80.3 38.7 %all-to-all-start.1 = ((bf16[8,192,640]{2,1,0:T(8,128)(2,1)}), bf16[8,192,640]{2,1,0:T(8,128)(2,1)S(1)}, u32[]{:S(2)}, u32[]{:S(2)}) async-start(bf16[8,192,640]{2,1,0:T(8,128)(2,1)} %copy-done.1), calls=%async_computation.1 | async-start | bytes 3932160 | tf_op jit(solution)/shard_map/all_to_all | solution.py:19
  90.0 18.9 %collective-permute-start.11 = (bf16[3,160,384]{2,1,0:T(8,128)(2,1)}, bf16[3,160,384]{2,1,0:T(8,128)(2,1)}, u32[]{:S(2)}, u32[]{:S(2)}) collective-permute-start(bf16[3,160,384]{2,1,0:T(8,128)(2,1)} %slice.33), channel_id=1, source_target_pairs={{0,32},{32,64},{64,96},{96,128},{128,160},{160,192},{192,224},{224... | collective-permute-start | bytes 1105928 | tf_op jit(solution)/shard_map/ppermute | solution.py:24
  91.8 17.1 %collective-permute-start.12 = (bf16[3,160,384]{2,1,0:T(8,128)(2,1)}, bf16[3,160,384]{2,1,0:T(8,128)(2,1)}, u32[]{:S(2)}, u32[]{:S(2)}) collective-permute-start(bf16[3,160,384]{2,1,0:T(8,128)(2,1)} %slice.34), channel_id=1, source_target_pairs={{0,224},{32,0},{64,32},{96,64},{128,96},{160,128},{192,160},{224,1... | collective-permute-start | bytes 1105928 | tf_op jit(solution)/shard_map/ppermute | solution.py:24
  101.6 7.2 %copy-start.4 = (bf16[2,320,640]{2,1,0:T(8,128)(2,1)S(1)}, bf16[2,320,640]{2,1,0:T(8,128)(2,1)}, u32[]{:S(2)}) copy-start(bf16[2,320,640]{2,1,0:T(8,128)(2,1)} %copy-done.2) | copy-start | bytes 2457604
  101.6 7.2 %copy-start.7 = (bf16[2,320,640]{2,1,0:T(8,128)(2,1)S(1)}, bf16[2,320,640]{2,1,0:T(8,128)(2,1)}, u32[]{:S(2)}) copy-start(bf16[2,320,640]{2,1,0:T(8,128)(2,1)} %copy-done.5) | copy-start | bytes 2457604
  112.0 5.6 %collective-permute-start.13 = (bf16[320,1152]{1,0:T(8,128)(2,1)S(1)}, bf16[320,1152]{1,0:T(8,128)(2,1)S(1)}, u32[]{:S(2)}, u32[]{:S(2)}) collective-permute-start(bf16[320,1152]{1,0:T(8,128)(2,1)S(1)} %get-tuple-element.40), channel_id=1, source_target_pairs={{0,16},{16,0},{1,17},{17,1},{2,18},{18,2},{3,19},{19,3},{4,20},{20... | collective-permute-start | bytes 2211848 | tf_op jit(solution)/shard_map/ppermute | solution.py:24
  118.9 28.4 %copy-start.20 = (f32[8,32]{1,0:T(8,128)S(1)}, f32[8,32]{1,0:T(8,128)}, u32[]{:S(2)}) copy-start(f32[8,32]{1,0:T(8,128)} %param.16) | copy-start | bytes 3076
  119.0 28.4 %copy-start.21 = (s32[2,1]{0,1:T(1,128)S(1)}, s32[2,1]{0,1:T(1,128)}, u32[]{:S(2)}) copy-start(s32[2,1]{0,1:T(1,128)} %param.15) | copy-start | bytes 28
  119.0 42.7 %collective-permute-start.19 = (bf16[8,192,640]{2,1,0:T(8,128)(2,1)S(1)}, bf16[8,192,640]{2,1,0:T(8,128)(2,1)}, u32[]{:S(2)}, u32[]{:S(2)}) collective-permute-start(bf16[8,192,640]{2,1,0:T(8,128)(2,1)S(1)} %all-to-all-done.1.half), channel_id=1, source_target_pairs={{0,16},{16,0},{1,17},{17,1},{2,18},{18,2},{3,19},{19,3},{4,20},{20... | collective-permute-start | bytes 5898248 | tf_op jit(solution)/shard_map/ppermute | solution.py:24
  135.3 9.3 %collective-permute-start.14 = (bf16[320,384]{1,0:T(8,128)(2,1)S(1)}, bf16[320,384]{1,0:T(8,128)(2,1)S(1)}, u32[]{:S(2)}, u32[]{:S(2)}) collective-permute-start(bf16[320,384]{1,0:T(8,128)(2,1)S(1)} %reshape.69), channel_id=1, source_target_pairs={{0,2},{2,0},{1,3},{3,1},{4,6},{6,4},{5,7},{7,5},{8,10},{10,8},{9,1... | collective-permute-start | bytes 737288 | tf_op jit(solution)/shard_map/ppermute | solution.py:24
  144.6 13.7 %collective-permute-start.15 = (bf16[2,320,384]{2,1,0:T(8,128)(2,1)S(1)}, bf16[2,320,384]{2,1,0:T(8,128)(2,1)S(1)}, u32[]{:S(2)}, u32[]{:S(2)}) collective-permute-start(bf16[2,320,384]{2,1,0:T(8,128)(2,1)S(1)} %pad_maximum_fusion.1.both), channel_id=1, source_target_pairs={{0,4},{4,8},{8,12},{12,0},{1,5},{5,9},{9,13},{13,1},{2,6},{6,10},{... | collective-permute-start | bytes 1474568 | tf_op jit(solution)/shard_map/ppermute | solution.py:24
  144.7 13.7 %collective-permute-start.17 = (bf16[2,320,384]{2,1,0:T(8,128)(2,1)S(1)}, bf16[2,320,384]{2,1,0:T(8,128)(2,1)S(1)}, u32[]{:S(2)}, u32[]{:S(2)}) collective-permute-start(bf16[2,320,384]{2,1,0:T(8,128)(2,1)S(1)} %pad_maximum_fusion.1.both), channel_id=1, source_target_pairs={{0,12},{4,0},{8,4},{12,8},{1,13},{5,1},{9,5},{13,9},{2,14},{6,2},{... | collective-permute-start | bytes 1474568 | tf_op jit(solution)/shard_map/ppermute | solution.py:24
  158.3 7.5 %collective-permute-start.16 = (bf16[2,160,384]{2,1,0:T(8,128)(2,1)S(1)}, bf16[2,160,384]{2,1,0:T(8,128)(2,1)S(1)}, u32[]{:S(2)}, u32[]{:S(2)}) collective-permute-start(bf16[2,160,384]{2,1,0:T(8,128)(2,1)S(1)} %slice.40), channel_id=1, source_target_pairs={{0,4},{4,8},{8,12},{12,0},{1,5},{5,9},{9,13},{13,1},{2,6},{6,10},{... | collective-permute-start | bytes 737288 | tf_op jit(solution)/shard_map/ppermute | solution.py:24
  158.5 7.4 %collective-permute-start.18 = (bf16[2,160,384]{2,1,0:T(8,128)(2,1)S(1)}, bf16[2,160,384]{2,1,0:T(8,128)(2,1)S(1)}, u32[]{:S(2)}, u32[]{:S(2)}) collective-permute-start(bf16[2,160,384]{2,1,0:T(8,128)(2,1)S(1)} %slice.41), channel_id=1, source_target_pairs={{0,12},{4,0},{8,4},{12,8},{1,13},{5,1},{9,5},{13,9},{2,14},{6,2},{... | collective-permute-start | bytes 737288 | tf_op jit(solution)/shard_map/ppermute | solution.py:24
  161.7 4.2 %copy-start.17 = (bf16[2,1,160,640]{3,2,1,0:T(8,128)(2,1)S(1)}, bf16[2,1,160,640]{3,2,1,0:T(8,128)(2,1)}, u32[]{:S(2)}) copy-start(bf16[2,1,160,640]{3,2,1,0:T(8,128)(2,1)} %param.18) | copy-start | bytes 1228804
  (12 other events, 13.1 us)

commit v8 on v7

--- a/solution.py
+++ b/solution.py
@@ -10,6 +10,7 @@
 
 HS = 128
 MASKED = -1e30
+QKV_VMEM = 58
 FRAME = ("z", "core")
 MP = ("x", "yhi")
 SMALL = pltpu.CompilerParams(vmem_limit_bytes=10 * 1024 * 1024)
@@ -29,23 +30,40 @@
     count = sum(pieces)
     shards, refs = refs[:count], refs[count:]
     acc_in, refs = (None, refs) if first else (refs[0], refs[1:])
-    outs, x_ref = refs[:-1], refs[-1]
+    outs, (x_ref, w_ref, x_sem, w_sem) = refs[:-4], refs[-4:]
+    acc = outs[-1]
     rows, full = x_ref.shape[1], x_ref.shape[2] // 2
-    for j in range(len(pieces)):
+    copies, at = [], 0
+    for j, n in enumerate(pieces):
         far, own = slots[j] >> 1, slots[j] & 1
         for k, source in ((0, both), (1, right), (3, left)):
 
             @pl.when(far == k)
             def _():
-                x_ref[j] = source[own]
+                pltpu.make_async_copy(source.at[own], x_ref.at[j], x_sem.at[j]).start()
 
         @pl.when(far == 2)
         def _():
-            x_ref[j, : rows // 2] = top[own]
-            x_ref[j, rows // 2 :] = low[own]
-
-    at, j, acc = 0, 0, outs[0]
+            half = rows // 2
+            pltpu.make_async_copy(top.at[own], x_ref.at[j, pl.ds(0, half)], x_sem.at[j]).start()
+            pltpu.make_async_copy(low.at[own], x_ref.at[j, pl.ds(half, half)], x_sem.at[j]).start()
+
+        copies.append([])
+        row = j * full
+        for source in shards[at : at + n]:
+            depth = source.shape[1]
+            copy = pltpu.make_async_copy(source, w_ref.at[:, pl.ds(row, depth)], w_sem.at[at])
+            copy.start()
+            copies[j].append(copy)
+            row += depth
+            at += 1
+
+    j = 0
     for number, group in enumerate(groups):
+        for i in range(j, j + len(group)):
+            pltpu.make_async_copy(both.at[0], x_ref.at[i], x_sem.at[i]).wait()
+            for copy in copies[i]:
+                copy.wait()
         xs = [x_ref[j + i] for i in range(len(group))]
         x = jnp.concatenate(
             [
@@ -54,10 +72,8 @@
             ],
             axis=0,
         )
-        use = shards[at : at + sum(group)]
-        w = jnp.concatenate(
-            [jnp.concatenate([u[i] for u in use], axis=0) for i in range(3)], axis=1
-        )
+        span = pl.ds(j * full, len(group) * full)
+        w = jnp.concatenate([w_ref[i, span] for i in range(3)], axis=1)
         part = jnp.dot(x, w, preferred_element_type=jnp.float32)
         if number:
             acc[...] += part
@@ -65,12 +81,11 @@
             acc[...] = part
         else:
             acc[...] = acc_in[...] + part
-        at += len(use)
         j += len(group)
     if last:
         me = core[0]
-        outs[1][...] = acc[pl.ds(me * rows, rows)]
-        outs[2][...] = acc[pl.ds((1 - me) * rows, rows)].astype(jnp.bfloat16)
+        outs[0][...] = acc[pl.ds(me * rows, rows)]
+        outs[1][...] = acc[pl.ds((1 - me) * rows, rows)].astype(jnp.bfloat16)
 
 
 def project(features, groups, slots, core, acc=None, last=False):
@@ -80,25 +95,35 @@
     heads = shards[0].shape[-1]
     smem = pl.BlockSpec(memory_space=pltpu.SMEM)
     vmem = pl.BlockSpec(memory_space=pltpu.VMEM)
-    out_shape = [jax.ShapeDtypeStruct((2 * rows, 3 * heads), jnp.float32)]
+    anywhere = pl.BlockSpec(memory_space=pl.ANY)
+    total = (2 * rows, 3 * heads)
     if last:
-        out_shape += [
+        out_shape = [
             jax.ShapeDtypeStruct((rows, 3 * heads), jnp.float32),
             jax.ShapeDtypeStruct((rows, 3 * heads), jnp.bfloat16),
         ]
-    operands = [*features, *shards] + ([] if acc is None else [acc])
+    else:
+        out_shape = [jax.ShapeDtypeStruct(total, jnp.float32)]
+    pieces = [*features, *shards]
+    operands = pieces + ([] if acc is None else [acc])
+    n = sum(len(c) for c in counts)
 
     def kernel(*refs):
         qkv_kernel(counts, acc is None, last, *refs)
 
     return pl.pallas_call(
         kernel,
-        in_specs=[smem, smem] + [vmem] * len(operands),
+        in_specs=[smem, smem] + [anywhere] * len(pieces) + ([] if acc is None else [vmem]),
         out_specs=[vmem] * len(out_shape),
         out_shape=out_shape,
-        input_output_aliases={} if acc is None else {len(operands) + 1: 0},
-        scratch_shapes=[pltpu.VMEM((sum(len(c) for c in counts), rows, width), jnp.bfloat16)],
-        compiler_params=pltpu.CompilerParams(vmem_limit_bytes=20 * 1024 * 1024),
+        scratch_shapes=([pltpu.VMEM(total, jnp.float32)] if last else [])
+        + [
+            pltpu.VMEM((n, rows, width), jnp.bfloat16),
+            pltpu.VMEM((3, n * width // 2, heads), jnp.bfloat16),
+            pltpu.SemaphoreType.DMA((n,)),
+            pltpu.SemaphoreType.DMA((len(shards),)),
+        ],
+        compiler_params=pltpu.CompilerParams(vmem_limit_bytes=QKV_VMEM << 20),
     )(slots, core, *operands)
 
 
@@ -270,7 +295,7 @@
     features = (both, right, top, low, left)
     early = [[(own,), (up1,)], [(down1,), (up2,)], [(down2,), (up3,)], [(down3,)]]
     (acc,) = project(features, early, slots[:7], core1)
-    _, kept, sent = project(features, [[(up4, down4)]], slots[7:], core1, acc, last=True)
+    kept, sent = project(features, [[(up4, down4)]], slots[7:], core1, acc, last=True)
     attn = attention(kept, shift(sent, "core", 1), frames)
     attn, half = lax.optimization_barrier((attn, half))
     other_half = shift(half, "core", 1)

time: 186 us -> 185 us (level)
  local copies, waits for them, and re-layouts: 20.8 us -> 10.8 us
  Pallas kernels: 18 us -> 24.1 us
  waiting for transfers between devices: 60.5 us -> 65.9 us
  starting transfers between devices: 49.3 us -> 46.1 us
    unnamed x45 -> x29, local copies, waits for them, and re-layouts: 13.2 us -> 4.85 us
    pallas_call x2, Pallas kernels: 10.3 us -> 16.4 us  [project(): pl.pallas_call(kernel, in_specs=[smem, smem] + [anywhere] * len(pieces) +...]
    ppermute x20, waiting for transfers between devices: 46.6 us -> 52 us  [shift(): return lax.ppermute(x, axis, [(i, (i + by) % n) for i in range(n)])]
    all_to_all x2, starting transfers between devices: 16.8 us -> 14.2 us  [exchange(): return lax.all_to_all(x, axis, split_axis=0, concat_axis=0, tiled=True)]
  transfers between devices with their start and end apart: 22 -> 22, of which waited for: 9 -> 11; matrix products, arithmetic and copies ran while one was open for 4% -> 2% of each run, Pallas kernels for 8% -> 12%
where the time goes in v8:
time: 185 us; the launch traced here: 184 us
  waiting for transfers between devices  65.9 us (36%)
  starting transfers between devices  46.1 us (25%)
  blocking collectives  32.7 us (18%)
  Pallas kernels  24.1 us (13%)
  local copies, waits for them, and re-layouts  10.8 us (6%)
  other arithmetic  2.2 us (1%)
    ppermute x20, waiting for transfers between devices, shift(): return lax.ppermute(x, axis, [(i, (i + by) % n) for i in range(n)])  52 us
    all_to_all x2, blocking collectives, exchange(): return lax.all_to_all(x, axis, split_axis=0, concat_axis=0, tiled=True)  32.7 us
    ppermute x20, starting transfers between devices, shift(): return lax.ppermute(x, axis, [(i, (i + by) % n) for i in range(n)])  31.9 us
    pallas_call x2, Pallas kernels, project(): pl.pallas_call(kernel, in_specs=[smem, smem] + [anywhere] * len(pieces) +...  16.4 us
    all_to_all x2, starting transfers between devices, exchange(): return lax.all_to_all(x, axis, split_axis=0, concat_axis=0, tiled=True)  14.2 us
    all_to_all x2, waiting for transfers between devices, exchange(): return lax.all_to_all(x, axis, split_axis=0, concat_axis=0, tiled=True)  13.9 us
    unnamed x29, local copies, waits for them, and re-layouts  4.85 us
  transfers between devices with their start and end apart: 22, of which 11 were waited for; matrix products, arithmetic and copies ran while one was open for 2% of the time, Pallas kernels for 12%

profile of v8, /device:TPU:1, one launch (start us, length us, event | category | flops | bytes accessed | tf_op | source)
XLA Modules:
  0.0 183.9 jit_solution(16309422774848229795)
XLA Ops:
  4.6 10.0 %all-to-all-start = ((bf16[16,20,640]{2,1,0:T(8,128)(2,1)}), bf16[16,20,640]{2,1,0:T(8,128)(2,1)S(1)}, u32[]{:S(2)}, u32[]{:S(2)}) async-start(bf16[16,20,640]{2,1,0:T(8,128)(2,1)} %copy.19), calls=%async_computation | async-start | bytes 983040 | tf_op jit(solution)/shard_map/all_to_all | solution.py:20
  14.6 1.5 collective-permute-start.1
  17.4 13.8 %all-to-all-done = bf16[16,20,640]{2,1,0:T(8,128)(2,1)S(1)} async-done(((bf16[16,20,640]{2,1,0:T(8,128)(2,1)}), bf16[16,20,640]{2,1,0:T(8,128)(2,1)S(1)}, u32[]{:S(2)}, u32[]{:S(2)}) %all-to-all-start) | async-done | bytes 409632 | tf_op jit(solution)/shard_map/all_to_all | solution.py:20
  31.3 3.0 %collective-permute-start = (bf16[320,640]{1,0:T(8,128)(2,1)S(1)}, bf16[320,640]{1,0:T(8,128)(2,1)S(1)}, u32[]{:S(2)}, u32[]{:S(2)}) collective-permute-start(bf16[320,640]{1,0:T(8,128)(2,1)S(1)} %reshape.68), channel_id=1, source_target_pairs={{0,2},{2,0},{1,3},{3,1},{4,6},{6,4},{5,7},{7,5},{8,10},{10,8},{9,1... | collective-permute-start | bytes 1228808 | tf_op jit(solution)/shard_map/ppermute | solution.py:25
  34.4 9.1 %collective-permute-done = bf16[320,640]{1,0:T(8,128)(2,1)S(1)} collective-permute-done((bf16[320,640]{1,0:T(8,128)(2,1)S(1)}, bf16[320,640]{1,0:T(8,128)(2,1)S(1)}, u32[]{:S(2)}, u32[]{:S(2)}) %collective-permute-start) | collective-permute-done | bytes 409632 | tf_op jit(solution)/shard_map/ppermute | solution.py:25
  45.8 1.5 collective-permute-start.4
  47.3 2.7 %collective-permute-start.6 = (bf16[3,320,384]{2,1,0:T(8,128)(2,1)}, bf16[3,320,384]{2,1,0:T(8,128)(2,1)}, u32[]{:S(2)}, u32[]{:S(2)}) collective-permute-start(bf16[3,320,384]{2,1,0:T(8,128)(2,1)} %collective-permute-done.2.refs_9_), channel_id=1, source_target_pairs={{0,224},{32,0},{64,32},{96,64},{128,96},{160,128},{192,160},{224,1... | collective-permute-start | bytes 2211848 | tf_op jit(solution)/shard_map/ppermute | solution.py:25
  50.0 2.1 %copy-done.2 = bf16[384,5120]{1,0:T(8,128)(2,1)S(1)} copy-done((bf16[384,5120]{1,0:T(8,128)(2,1)S(1)}, bf16[384,5120]{1,0:T(8,128)(2,1)}, u32[]{:S(2)}) %copy-start.2) | copy-done | bytes 3932184
  53.8 11.6 %collective-permute-done.5.refs_10_ = bf16[3,320,384]{2,1,0:T(8,128)(2,1)} collective-permute-done((bf16[3,320,384]{2,1,0:T(8,128)(2,1)}, bf16[3,320,384]{2,1,0:T(8,128)(2,1)}, u32[]{:S(2)}, u32[]{:S(2)}) %collective-permute-start.5) | collective-permute-done | bytes 737312 | tf_op jit(solution)/shard_map/ppermute | solution.py:25
  65.5 1.9 %collective-permute-start.10 = (bf16[2,160,640]{2,1,0:T(8,128)(2,1)S(1)}, bf16[2,160,640]{2,1,0:T(8,128)(2,1)}, u32[]{:S(2)}, u32[]{:S(2)}) collective-permute-start(bf16[2,160,640]{2,1,0:T(8,128)(2,1)S(1)} %slice.32), channel_id=1, source_target_pairs={{0,12},{4,0},{8,4},{12,8},{1,13},{5,1},{9,5},{13,9},{2,14},{6,2},{... | collective-permute-start | bytes 1228808 | tf_op jit(solution)/shard_map/ppermute | solution.py:25
  68.7 1.5 collective-permute-start.8
  70.2 4.0 %collective-permute-done.10.refs_5_ = bf16[2,160,640]{2,1,0:T(8,128)(2,1)} collective-permute-done((bf16[2,160,640]{2,1,0:T(8,128)(2,1)S(1)}, bf16[2,160,640]{2,1,0:T(8,128)(2,1)}, u32[]{:S(2)}, u32[]{:S(2)}) %collective-permute-start.10) | collective-permute-done | bytes 409632 | tf_op jit(solution)/shard_map/ppermute | solution.py:25
  74.2 3.2 %collective-permute-done.9.refs_4_ = bf16[2,160,640]{2,1,0:T(8,128)(2,1)} collective-permute-done((bf16[2,160,640]{2,1,0:T(8,128)(2,1)S(1)}, bf16[2,160,640]{2,1,0:T(8,128)(2,1)}, u32[]{:S(2)}, u32[]{:S(2)}) %collective-permute-start.9) | collective-permute-done | bytes 409632 | tf_op jit(solution)/shard_map/ppermute | solution.py:25
  77.5 4.2 %all-to-all-start.1 = ((bf16[8,192,640]{2,1,0:T(8,128)(2,1)}), bf16[8,192,640]{2,1,0:T(8,128)(2,1)S(1)}, u32[]{:S(2)}, u32[]{:S(2)}) async-start(bf16[8,192,640]{2,1,0:T(8,128)(2,1)} %copy-done.1), calls=%async_computation.1 | async-start | bytes 3932160 | tf_op jit(solution)/shard_map/all_to_all | solution.py:20
  81.7 2.8 %collective-permute-done.7.refs_12_ = bf16[3,320,384]{2,1,0:T(8,128)(2,1)S(1)} collective-permute-done((bf16[3,320,384]{2,1,0:T(8,128)(2,1)}, bf16[3,320,384]{2,1,0:T(8,128)(2,1)S(1)}, u32[]{:S(2)}, u32[]{:S(2)}) %collective-permute-start.7) | collective-permute-done | bytes 737312 | tf_op jit(solution)/shard_map/ppermute | solution.py:25
  85.3 1.6 collective-permute-start.11
  86.9 1.8 slice.34
  90.4 10.1 %shard_map.114.refs_9_ = f32[640,1152]{1,0:T(8,128)} custom-call(s32[7]{0:T(128)} %bitcast.35, s32[1]{0:T(128)} %bitcast.core.refs_1_, bf16[2,320,640]{2,1,0:T(8,128)(2,1)} %copy-done.5, bf16[2,320,640]{2,1,0:T(8,128)(2,1)} %copy-done.7, bf16[2,160,640]{2,1,0:T(8,128)(2,1)} %collective-permute-done.9.refs_4_, ...), custom_call_target="tpu_custom_call" | custom-call | tf_op jit(solution)/shard_map/pallas_call | solution.py:114
  100.6 6.3 %shard_map.115 = (f32[320,1152]{1,0:T(8,128)}, bf16[320,1152]{1,0:T(8,128)(2,1)}) custom-call(s32[1]{0:T(128)} %slice.30.refs_0_, s32[1]{0:T(128)} %bitcast.core.refs_1_, bf16[2,320,640]{2,1,0:T(8,128)(2,1)} %copy-done.5, bf16[2,320,640]{2,1,0:T(8,128)(2,1)} %copy-done.7, bf16[2,160,640]{2,1,0:T(8,128)(2,1)} %collective-permute-done.9.refs_4_, ...), custom_call_target="tpu_custom_call" | custom-call | tf_op jit(solution)/shard_map/pallas_call | solution.py:114
  106.9 4.2 %collective-permute-start.13 = (bf16[320,1152]{1,0:T(8,128)(2,1)}, bf16[320,1152]{1,0:T(8,128)(2,1)S(1)}, u32[]{:S(2)}, u32[]{:S(2)}) collective-permute-start(bf16[320,1152]{1,0:T(8,128)(2,1)} %get-tuple-element.40), channel_id=1, source_target_pairs={{0,16},{16,0},{1,17},{17,1},{2,18},{18,2},{3,19},{19,3},{4,20},{20... | collective-permute-start | bytes 2211848 | tf_op jit(solution)/shard_map/ppermute | solution.py:25
  111.2 1.9 %collective-permute-done.13.other_ref = bf16[320,1152]{1,0:T(8,128)(2,1)S(1)} collective-permute-done((bf16[320,1152]{1,0:T(8,128)(2,1)}, bf16[320,1152]{1,0:T(8,128)(2,1)S(1)}, u32[]{:S(2)}, u32[]{:S(2)}) %collective-permute-start.13) | collective-permute-done | bytes 737312 | tf_op jit(solution)/shard_map/ppermute | solution.py:25
  113.2 1.4 copy-done.3
  114.5 1.4 shard_map.116
  116.4 17.5 %all_to_all.20 = bf16[16,20,384]{2,1,0:T(8,128)(2,1)S(1)} all-to-all(bf16[16,20,384]{2,1,0:T(8,128)(2,1)S(1)} %shard_map.116), channel_id=1, replica_groups=mesh['z'=8,'core'=2,'x'=4,'yhi'=2,'dp'=2] {'z','core'}, dimensions={0} | all-to-all | bytes 491520 | tf_op jit(solution)/shard_map/all_to_all | solution.py:20
  134.0 3.0 %collective-permute-start.14 = (bf16[320,384]{1,0:T(8,128)(2,1)S(1)}, bf16[320,384]{1,0:T(8,128)(2,1)S(1)}, u32[]{:S(2)}, u32[]{:S(2)}) collective-permute-start(bf16[320,384]{1,0:T(8,128)(2,1)S(1)} %reshape.69), channel_id=1, source_target_pairs={{0,2},{2,0},{1,3},{3,1},{4,6},{6,4},{5,7},{7,5},{8,10},{10,8},{9,1... | collective-permute-start | bytes 737288 | tf_op jit(solution)/shard_map/ppermute | solution.py:25
  137.0 6.5 %collective-permute-done.14 = bf16[320,384]{1,0:T(8,128)(2,1)S(1)} collective-permute-done((bf16[320,384]{1,0:T(8,128)(2,1)S(1)}, bf16[320,384]{1,0:T(8,128)(2,1)S(1)}, u32[]{:S(2)}, u32[]{:S(2)}) %collective-permute-start.14) | collective-permute-done | bytes 245792 | tf_op jit(solution)/shard_map/ppermute | solution.py:25
  143.6 2.7 %collective-permute-start.17 = (bf16[2,320,384]{2,1,0:T(8,128)(2,1)S(1)}, bf16[2,320,384]{2,1,0:T(8,128)(2,1)S(1)}, u32[]{:S(2)}, u32[]{:S(2)}) collective-permute-start(bf16[2,320,384]{2,1,0:T(8,128)(2,1)S(1)} %pad_maximum_fusion.1.both), channel_id=1, source_target_pairs={{0,12},{4,0},{8,4},{12,8},{1,13},{5,1},{9,5},{13,9},{2,14},{6,2},{... | collective-permute-start | bytes 1474568 | tf_op jit(solution)/shard_map/ppermute | solution.py:25
  146.5 10.8 %collective-permute-done.15.left = bf16[2,320,384]{2,1,0:T(8,128)(2,1)S(1)} collective-permute-done((bf16[2,320,384]{2,1,0:T(8,128)(2,1)S(1)}, bf16[2,320,384]{2,1,0:T(8,128)(2,1)S(1)}, u32[]{:S(2)}, u32[]{:S(2)}) %collective-permute-start.15) | collective-permute-done | bytes 491552 | tf_op jit(solution)/shard_map/ppermute | solution.py:25
  157.4 2.9 %collective-permute-start.18 = (bf16[2,160,384]{2,1,0:T(8,128)(2,1)S(1)}, bf16[2,160,384]{2,1,0:T(8,128)(2,1)S(1)}, u32[]{:S(2)}, u32[]{:S(2)}) collective-permute-start(bf16[2,160,384]{2,1,0:T(8,128)(2,1)S(1)} %slice.41), channel_id=1, source_target_pairs={{0,12},{4,0},{8,4},{12,8},{1,13},{5,1},{9,5},{13,9},{2,14},{6,2},{... | collective-permute-start | bytes 737288 | tf_op jit(solution)/shard_map/ppermute | solution.py:25
  160.6 3.0 %shard_map.117.acc = f32[320,640]{1,0:T(8,128)S(1)} custom-call(s32[3]{0:T(128)S(1)} %pad_add_fusion.where, bf16[2,320,384]{2,1,0:T(8,128)(2,1)S(1)} %pad_maximum_fusion.1.both, bf16[2,320,384]{2,1,0:T(8,128)(2,1)S(1)} %collective-permute-done.17.right, bf16[2,320,384]{2,1,0:T(8,128)(2,1)S(1)} %collective-permute-done.15.left, ...), custom_call_target="tpu_custom_call" | custom-call | tf_op jit(solution)/shard_map/pallas_call | solution.py:210
  164.8 2.9 %shard_map.118 = (bf16[320,640]{1,0:T(8,128)(2,1)}, f32[32,2,672]{2,1,0:T(2,128)S(1)}) custom-call(s32[3]{0:T(128)S(1)} %pad_add_fusion.where, bf16[2,160,384]{2,1,0:T(8,128)(2,1)S(1)} %collective-permute-done.16.top, bf16[2,160,384]{2,1,0:T(8,128)(2,1)S(1)} %collective-permute-done.18.low, bf16[8,192,640]{2,1,0:T(8,128)(2,1)S(1)} %all-to-all-done.1.half, ...), custom_call_target="tpu_custom_call" | custom-call | tf_op jit(solution)/shard_map/pallas_call | solution.py:223
  167.7 15.2 %all_to_all.21 = f32[32,2,672]{2,1,0:T(2,128)S(1)} all-to-all(f32[32,2,672]{2,1,0:T(2,128)S(1)} %get-tuple-element.45), channel_id=1, replica_groups=mesh['z'=8,'core'=2,'x'=4,'yhi'=2,'dp'=2] {'z','core','dp'}, dimensions={0} | all-to-all | bytes 344064 | tf_op jit(solution)/shard_map/all_to_all | solution.py:20
  (76 shorter events, 17.1 us)
Async XLA Ops:
  0.6 159.8 %copy-start = (f32[32,640]{1,0:T(8,128)S(1)}, f32[32,640]{1,0:T(8,128)}, u32[]{:S(2)}) copy-start(f32[32,640]{1,0:T(8,128)} %param.17) | copy-start | bytes 245764
  2.9 11.7 %copy-start.9 = (bf16[320,3,384]{2,0,1:T(8,128)(2,1)S(1)}, bf16[320,3,384]{2,0,1:T(8,128)(2,1)}, u32[]{:S(2)}) copy-start(bf16[320,3,384]{2,0,1:T(8,128)(2,1)} %param.13) | copy-start | bytes 2211844
  4.6 26.6 %all-to-all-start = ((bf16[16,20,640]{2,1,0:T(8,128)(2,1)}), bf16[16,20,640]{2,1,0:T(8,128)(2,1)S(1)}, u32[]{:S(2)}, u32[]{:S(2)}) async-start(bf16[16,20,640]{2,1,0:T(8,128)(2,1)} %copy.19), calls=%async_computation | async-start | bytes 983040 | tf_op jit(solution)/shard_map/all_to_all | solution.py:20
  14.6 30.0 %collective-permute-start.1 = (bf16[3,320,384]{2,1,0:T(8,128)(2,1)S(1)}, bf16[3,320,384]{2,1,0:T(8,128)(2,1)}, u32[]{:S(2)}, u32[]{:S(2)}) collective-permute-start(bf16[3,320,384]{2,1,0:T(8,128)(2,1)S(1)} %bitcast.30), channel_id=1, source_target_pairs={{0,32},{32,64},{64,96},{96,128},{128,160},{160,192},{192,224},{224... | collective-permute-start | bytes 2211848 | tf_op jit(solution)/shard_map/ppermute | solution.py:25
  16.1 28.5 %collective-permute-start.2 = (bf16[3,320,384]{2,1,0:T(8,128)(2,1)S(1)}, bf16[3,320,384]{2,1,0:T(8,128)(2,1)}, u32[]{:S(2)}, u32[]{:S(2)}) collective-permute-start(bf16[3,320,384]{2,1,0:T(8,128)(2,1)S(1)} %bitcast.31), channel_id=1, source_target_pairs={{0,224},{32,0},{64,32},{96,64},{128,96},{160,128},{192,160},{224,1... | collective-permute-start | bytes 2211848 | tf_op jit(solution)/shard_map/ppermute | solution.py:25
  31.3 12.2 %collective-permute-start = (bf16[320,640]{1,0:T(8,128)(2,1)S(1)}, bf16[320,640]{1,0:T(8,128)(2,1)S(1)}, u32[]{:S(2)}, u32[]{:S(2)}) collective-permute-start(bf16[320,640]{1,0:T(8,128)(2,1)S(1)} %reshape.68), channel_id=1, source_target_pairs={{0,2},{2,0},{1,3},{3,1},{4,6},{6,4},{5,7},{7,5},{8,10},{10,8},{9,1... | collective-permute-start | bytes 1228808 | tf_op jit(solution)/shard_map/ppermute | solution.py:25
  43.6 8.9 %copy-start.5 = (bf16[2,320,640]{2,1,0:T(8,128)(2,1)}, bf16[2,320,640]{2,1,0:T(8,128)(2,1)S(1)}, u32[]{:S(2)}) copy-start(bf16[2,320,640]{2,1,0:T(8,128)(2,1)S(1)} %pad_maximum_fusion.refs_2_) | copy-start | bytes 2457604
  44.6 20.8 %collective-permute-start.3 = (bf16[2,320,640]{2,1,0:T(8,128)(2,1)S(1)}, bf16[2,320,640]{2,1,0:T(8,128)(2,1)S(1)}, u32[]{:S(2)}, u32[]{:S(2)}) collective-permute-start(bf16[2,320,640]{2,1,0:T(8,128)(2,1)S(1)} %pad_maximum_fusion.refs_2_), channel_id=1, source_target_pairs={{0,4},{4,8},{8,12},{12,0},{1,5},{5,9},{9,13},{13,1},{2,6},{6,10},{... | collective-permute-start | bytes 2457608 | tf_op jit(solution)/shard_map/ppermute | solution.py:25
  45.8 19.6 %collective-permute-start.4 = (bf16[2,320,640]{2,1,0:T(8,128)(2,1)S(1)}, bf16[2,320,640]{2,1,0:T(8,128)(2,1)S(1)}, u32[]{:S(2)}, u32[]{:S(2)}) collective-permute-start(bf16[2,320,640]{2,1,0:T(8,128)(2,1)S(1)} %pad_maximum_fusion.refs_2_), channel_id=1, source_target_pairs={{0,12},{4,0},{8,4},{12,8},{1,13},{5,1},{9,5},{13,9},{2,14},{6,2},{... | collective-permute-start | bytes 2457608 | tf_op jit(solution)/shard_map/ppermute | solution.py:25
  47.3 18.1 %collective-permute-start.5 = (bf16[3,320,384]{2,1,0:T(8,128)(2,1)}, bf16[3,320,384]{2,1,0:T(8,128)(2,1)}, u32[]{:S(2)}, u32[]{:S(2)}) collective-permute-start(bf16[3,320,384]{2,1,0:T(8,128)(2,1)} %collective-permute-done.1.refs_8_), channel_id=1, source_target_pairs={{0,32},{32,64},{64,96},{96,128},{128,160},{160,192},{192,224},{224... | collective-permute-start | bytes 2211848 | tf_op jit(solution)/shard_map/ppermute | solution.py:25
  47.3 18.1 %collective-permute-start.6 = (bf16[3,320,384]{2,1,0:T(8,128)(2,1)}, bf16[3,320,384]{2,1,0:T(8,128)(2,1)}, u32[]{:S(2)}, u32[]{:S(2)}) collective-permute-start(bf16[3,320,384]{2,1,0:T(8,128)(2,1)} %collective-permute-done.2.refs_9_), channel_id=1, source_target_pairs={{0,224},{32,0},{64,32},{96,64},{128,96},{160,128},{192,160},{224,1... | collective-permute-start | bytes 2211848 | tf_op jit(solution)/shard_map/ppermute | solution.py:25
  65.4 12.1 %copy-start.6 = (bf16[2,320,640]{2,1,0:T(8,128)(2,1)}, bf16[2,320,640]{2,1,0:T(8,128)(2,1)S(1)}, u32[]{:S(2)}) copy-start(bf16[2,320,640]{2,1,0:T(8,128)(2,1)S(1)} %collective-permute-done.3.refs_6_) | copy-start | bytes 2457604
  65.4 12.1 %copy-start.7 = (bf16[2,320,640]{2,1,0:T(8,128)(2,1)}, bf16[2,320,640]{2,1,0:T(8,128)(2,1)S(1)}, u32[]{:S(2)}) copy-start(bf16[2,320,640]{2,1,0:T(8,128)(2,1)S(1)} %collective-permute-done.4.refs_3_) | copy-start | bytes 2457604
  65.5 8.8 %collective-permute-start.10 = (bf16[2,160,640]{2,1,0:T(8,128)(2,1)S(1)}, bf16[2,160,640]{2,1,0:T(8,128)(2,1)}, u32[]{:S(2)}, u32[]{:S(2)}) collective-permute-start(bf16[2,160,640]{2,1,0:T(8,128)(2,1)S(1)} %slice.32), channel_id=1, source_target_pairs={{0,12},{4,0},{8,4},{12,8},{1,13},{5,1},{9,5},{13,9},{2,14},{6,2},{... | collective-permute-start | bytes 1228808 | tf_op jit(solution)/shard_map/ppermute | solution.py:25
  67.4 22.4 %copy-start.11 = (s32[8]{0:T(128)S(1)}, s32[8]{0:T(128)}, u32[]{:S(2)}) copy-start(s32[8]{0:T(128)} %constant.52.clone) | copy-start | bytes 100
  67.4 10.1 %collective-permute-start.9 = (bf16[2,160,640]{2,1,0:T(8,128)(2,1)S(1)}, bf16[2,160,640]{2,1,0:T(8,128)(2,1)}, u32[]{:S(2)}, u32[]{:S(2)}) collective-permute-start(bf16[2,160,640]{2,1,0:T(8,128)(2,1)S(1)} %slice.31), channel_id=1, source_target_pairs={{0,4},{4,8},{8,12},{12,0},{1,5},{5,9},{9,13},{13,1},{2,6},{6,10},{... | collective-permute-start | bytes 1228808 | tf_op jit(solution)/shard_map/ppermute | solution.py:25
  67.5 17.0 %collective-permute-start.7 = (bf16[3,320,384]{2,1,0:T(8,128)(2,1)}, bf16[3,320,384]{2,1,0:T(8,128)(2,1)S(1)}, u32[]{:S(2)}, u32[]{:S(2)}) collective-permute-start(bf16[3,320,384]{2,1,0:T(8,128)(2,1)} %collective-permute-done.5.refs_10_), channel_id=1, source_target_pairs={{0,32},{32,64},{64,96},{96,128},{128,160},{160,192},{192,224},{224... | collective-permute-start | bytes 2211848 | tf_op jit(solution)/shard_map/ppermute | solution.py:25
  68.7 15.7 %collective-permute-start.8 = (bf16[3,320,384]{2,1,0:T(8,128)(2,1)}, bf16[3,320,384]{2,1,0:T(8,128)(2,1)}, u32[]{:S(2)}, u32[]{:S(2)}) collective-permute-start(bf16[3,320,384]{2,1,0:T(8,128)(2,1)} %collective-permute-done.6.refs_11_), channel_id=1, source_target_pairs={{0,224},{32,0},{64,32},{96,64},{128,96},{160,128},{192,160},{224,1... | collective-permute-start | bytes 2211848 | tf_op jit(solution)/shard_map/ppermute | solution.py:25
  77.5 38.5 %all-to-all-start.1 = ((bf16[8,192,640]{2,1,0:T(8,128)(2,1)}), bf16[8,192,640]{2,1,0:T(8,128)(2,1)S(1)}, u32[]{:S(2)}, u32[]{:S(2)}) async-start(bf16[8,192,640]{2,1,0:T(8,128)(2,1)} %copy-done.1), calls=%async_computation.1 | async-start | bytes 3932160 | tf_op jit(solution)/shard_map/all_to_all | solution.py:20
  84.4 6.0 %copy-start.8 = (bf16[3,320,384]{2,1,0:T(8,128)(2,1)}, bf16[3,320,384]{2,1,0:T(8,128)(2,1)S(1)}, u32[]{:S(2)}) copy-start(bf16[3,320,384]{2,1,0:T(8,128)(2,1)S(1)} %collective-permute-done.7.refs_12_) | copy-start | bytes 2211844
  85.3 15.3 %collective-permute-start.11 = (bf16[3,160,384]{2,1,0:T(8,128)(2,1)}, bf16[3,160,384]{2,1,0:T(8,128)(2,1)}, u32[]{:S(2)}, u32[]{:S(2)}) collective-permute-start(bf16[3,160,384]{2,1,0:T(8,128)(2,1)} %slice.33), channel_id=1, source_target_pairs={{0,32},{32,64},{64,96},{96,128},{128,160},{160,192},{192,224},{224... | collective-permute-start | bytes 1105928 | tf_op jit(solution)/shard_map/ppermute | solution.py:25
  88.6 11.9 %collective-permute-start.12 = (bf16[3,160,384]{2,1,0:T(8,128)(2,1)}, bf16[3,160,384]{2,1,0:T(8,128)(2,1)}, u32[]{:S(2)}, u32[]{:S(2)}) collective-permute-start(bf16[3,160,384]{2,1,0:T(8,128)(2,1)} %slice.34), channel_id=1, source_target_pairs={{0,224},{32,0},{64,32},{96,64},{128,96},{160,128},{192,160},{224,1... | collective-permute-start | bytes 1105928 | tf_op jit(solution)/shard_map/ppermute | solution.py:25
  106.9 6.2 %collective-permute-start.13 = (bf16[320,1152]{1,0:T(8,128)(2,1)}, bf16[320,1152]{1,0:T(8,128)(2,1)S(1)}, u32[]{:S(2)}, u32[]{:S(2)}) collective-permute-start(bf16[320,1152]{1,0:T(8,128)(2,1)} %get-tuple-element.40), channel_id=1, source_target_pairs={{0,16},{16,0},{1,17},{17,1},{2,18},{18,2},{3,19},{19,3},{4,20},{20... | collective-permute-start | bytes 2211848 | tf_op jit(solution)/shard_map/ppermute | solution.py:25
  115.9 30.4 %copy-start.12 = (f32[8,32]{1,0:T(8,128)S(1)}, f32[8,32]{1,0:T(8,128)}, u32[]{:S(2)}) copy-start(f32[8,32]{1,0:T(8,128)} %param.16) | copy-start | bytes 3076
  115.9 30.4 %copy-start.13 = (s32[2,1]{0,1:T(1,128)S(1)}, s32[2,1]{0,1:T(1,128)}, u32[]{:S(2)}) copy-start(s32[2,1]{0,1:T(1,128)} %param.15) | copy-start | bytes 28
  115.9 44.7 %collective-permute-start.19 = (bf16[8,192,640]{2,1,0:T(8,128)(2,1)S(1)}, bf16[8,192,640]{2,1,0:T(8,128)(2,1)}, u32[]{:S(2)}, u32[]{:S(2)}) collective-permute-start(bf16[8,192,640]{2,1,0:T(8,128)(2,1)S(1)} %all-to-all-done.1.half), channel_id=1, source_target_pairs={{0,16},{16,0},{1,17},{17,1},{2,18},{18,2},{3,19},{19,3},{4,20},{20... | collective-permute-start | bytes 5898248 | tf_op jit(solution)/shard_map/ppermute | solution.py:25
  134.0 9.5 %collective-permute-start.14 = (bf16[320,384]{1,0:T(8,128)(2,1)S(1)}, bf16[320,384]{1,0:T(8,128)(2,1)S(1)}, u32[]{:S(2)}, u32[]{:S(2)}) collective-permute-start(bf16[320,384]{1,0:T(8,128)(2,1)S(1)} %reshape.69), channel_id=1, source_target_pairs={{0,2},{2,0},{1,3},{3,1},{4,6},{6,4},{5,7},{7,5},{8,10},{10,8},{9,1... | collective-permute-start | bytes 737288 | tf_op jit(solution)/shard_map/ppermute | solution.py:25
  143.5 13.7 %collective-permute-start.15 = (bf16[2,320,384]{2,1,0:T(8,128)(2,1)S(1)}, bf16[2,320,384]{2,1,0:T(8,128)(2,1)S(1)}, u32[]{:S(2)}, u32[]{:S(2)}) collective-permute-start(bf16[2,320,384]{2,1,0:T(8,128)(2,1)S(1)} %pad_maximum_fusion.1.both), channel_id=1, source_target_pairs={{0,4},{4,8},{8,12},{12,0},{1,5},{5,9},{9,13},{13,1},{2,6},{6,10},{... | collective-permute-start | bytes 1474568 | tf_op jit(solution)/shard_map/ppermute | solution.py:25
  143.6 13.7 %collective-permute-start.17 = (bf16[2,320,384]{2,1,0:T(8,128)(2,1)S(1)}, bf16[2,320,384]{2,1,0:T(8,128)(2,1)S(1)}, u32[]{:S(2)}, u32[]{:S(2)}) collective-permute-start(bf16[2,320,384]{2,1,0:T(8,128)(2,1)S(1)} %pad_maximum_fusion.1.both), channel_id=1, source_target_pairs={{0,12},{4,0},{8,4},{12,8},{1,13},{5,1},{9,5},{13,9},{2,14},{6,2},{... | collective-permute-start | bytes 1474568 | tf_op jit(solution)/shard_map/ppermute | solution.py:25
  157.3 7.5 %collective-permute-start.16 = (bf16[2,160,384]{2,1,0:T(8,128)(2,1)S(1)}, bf16[2,160,384]{2,1,0:T(8,128)(2,1)S(1)}, u32[]{:S(2)}, u32[]{:S(2)}) collective-permute-start(bf16[2,160,384]{2,1,0:T(8,128)(2,1)S(1)} %slice.40), channel_id=1, source_target_pairs={{0,4},{4,8},{8,12},{12,0},{1,5},{5,9},{9,13},{13,1},{2,6},{6,10},{... | collective-permute-start | bytes 737288 | tf_op jit(solution)/shard_map/ppermute | solution.py:25
  157.4 7.4 %collective-permute-start.18 = (bf16[2,160,384]{2,1,0:T(8,128)(2,1)S(1)}, bf16[2,160,384]{2,1,0:T(8,128)(2,1)S(1)}, u32[]{:S(2)}, u32[]{:S(2)}) collective-permute-start(bf16[2,160,384]{2,1,0:T(8,128)(2,1)S(1)} %slice.41), channel_id=1, source_target_pairs={{0,12},{4,0},{8,4},{12,8},{1,13},{5,1},{9,5},{13,9},{2,14},{6,2},{... | collective-permute-start | bytes 737288 | tf_op jit(solution)/shard_map/ppermute | solution.py:25
  160.6 4.2 %copy-start.4 = (bf16[2,1,160,640]{3,2,1,0:T(8,128)(2,1)S(1)}, bf16[2,1,160,640]{3,2,1,0:T(8,128)(2,1)}, u32[]{:S(2)}) copy-start(bf16[2,1,160,640]{3,2,1,0:T(8,128)(2,1)} %param.18) | copy-start | bytes 1228804
  (4 other events, 5.5 us)

commit v9 on v8

--- a/solution.py
+++ b/solution.py
@@ -11,6 +11,9 @@
 HS = 128
 MASKED = -1e30
 QKV_VMEM = 58
+SMEM = pl.BlockSpec(memory_space=pltpu.SMEM)
+WHOLE = pl.BlockSpec(memory_space=pltpu.VMEM)
+ANYWHERE = pl.BlockSpec(memory_space=pl.ANY)
 FRAME = ("z", "core")
 MP = ("x", "yhi")
 SMALL = pltpu.CompilerParams(vmem_limit_bytes=10 * 1024 * 1024)
@@ -25,29 +28,30 @@
     return lax.ppermute(x, axis, [(i, (i + by) % n) for i in range(n)])
 
 
-def qkv_kernel(groups, first, last, slots, core, both, right, top, low, left, *refs):
+def fetch_features(slot, both, right, top, low, left, target, sem):
+    far, own = slot >> 1, slot & 1
+    for k, source in ((0, both), (1, right), (3, left)):
+
+        @pl.when(far == k)
+        def _():
+            pltpu.make_async_copy(source.at[own], target, sem).start()
+
+    @pl.when(far == 2)
+    def _():
+        half = target.shape[0] // 2
+        pltpu.make_async_copy(top.at[own], target.at[pl.ds(0, half)], sem).start()
+        pltpu.make_async_copy(low.at[own], target.at[pl.ds(half, half)], sem).start()
+
+
+def qkv_kernel(groups, slots, both, right, top, low, left, *refs):
     pieces = [w for group in groups for w in group]
     count = sum(pieces)
     shards, refs = refs[:count], refs[count:]
-    acc_in, refs = (None, refs) if first else (refs[0], refs[1:])
-    outs, (x_ref, w_ref, x_sem, w_sem) = refs[:-4], refs[-4:]
-    acc = outs[-1]
+    acc, x_ref, w_ref, x_sem, w_sem = refs
     rows, full = x_ref.shape[1], x_ref.shape[2] // 2
     copies, at = [], 0
     for j, n in enumerate(pieces):
-        far, own = slots[j] >> 1, slots[j] & 1
-        for k, source in ((0, both), (1, right), (3, left)):
-
-            @pl.when(far == k)
-            def _():
-                pltpu.make_async_copy(source.at[own], x_ref.at[j], x_sem.at[j]).start()
-
-        @pl.when(far == 2)
-        def _():
-            half = rows // 2
-            pltpu.make_async_copy(top.at[own], x_ref.at[j, pl.ds(0, half)], x_sem.at[j]).start()
-            pltpu.make_async_copy(low.at[own], x_ref.at[j, pl.ds(half, half)], x_sem.at[j]).start()
-
+        fetch_features(slots[j], both, right, top, low, left, x_ref.at[j], x_sem.at[j])
         copies.append([])
         row = j * full
         for source in shards[at : at + n]:
@@ -77,54 +81,76 @@
         part = jnp.dot(x, w, preferred_element_type=jnp.float32)
         if number:
             acc[...] += part
-        elif first:
+        else:
             acc[...] = part
-        else:
-            acc[...] = acc_in[...] + part
         j += len(group)
-    if last:
-        me = core[0]
-        outs[0][...] = acc[pl.ds(me * rows, rows)]
-        outs[1][...] = acc[pl.ds((1 - me) * rows, rows)].astype(jnp.bfloat16)
-
-
-def project(features, groups, slots, core, acc=None, last=False):
+
+
+def project(features, groups, slots):
     _, rows, width = features[0].shape
     counts = [[len(s) for s in group] for group in groups]
     shards = [w for group in groups for s in group for w in s]
     heads = shards[0].shape[-1]
-    smem = pl.BlockSpec(memory_space=pltpu.SMEM)
-    vmem = pl.BlockSpec(memory_space=pltpu.VMEM)
-    anywhere = pl.BlockSpec(memory_space=pl.ANY)
-    total = (2 * rows, 3 * heads)
-    if last:
-        out_shape = [
-            jax.ShapeDtypeStruct((rows, 3 * heads), jnp.float32),
-            jax.ShapeDtypeStruct((rows, 3 * heads), jnp.bfloat16),
-        ]
-    else:
-        out_shape = [jax.ShapeDtypeStruct(total, jnp.float32)]
-    pieces = [*features, *shards]
-    operands = pieces + ([] if acc is None else [acc])
+    operands = [*features, *shards]
     n = sum(len(c) for c in counts)
 
     def kernel(*refs):
-        qkv_kernel(counts, acc is None, last, *refs)
+        qkv_kernel(counts, *refs)
 
     return pl.pallas_call(
         kernel,
-        in_specs=[smem, smem] + [anywhere] * len(pieces) + ([] if acc is None else [vmem]),
-        out_specs=[vmem] * len(out_shape),
-        out_shape=out_shape,
-        scratch_shapes=([pltpu.VMEM(total, jnp.float32)] if last else [])
-        + [
+        in_specs=[SMEM] + [ANYWHERE] * len(operands),
+        out_specs=WHOLE,
+        out_shape=jax.ShapeDtypeStruct((2 * rows, 3 * heads), jnp.float32),
+        scratch_shapes=[
             pltpu.VMEM((n, rows, width), jnp.bfloat16),
             pltpu.VMEM((3, n * width // 2, heads), jnp.bfloat16),
             pltpu.SemaphoreType.DMA((n,)),
             pltpu.SemaphoreType.DMA((len(shards),)),
         ],
         compiler_params=pltpu.CompilerParams(vmem_limit_bytes=QKV_VMEM << 20),
-    )(slots, core, *operands)
+    )(slots, *operands)
+
+
+def last_kernel(slots, side, both, right, top, low, left, first, second, acc, out, *refs):
+    x_ref, w_ref, acc_ref, x_sem, w_sem = refs
+    rows, full = x_ref.shape[0], x_ref.shape[1] // 2
+    depth = first.shape[1]
+    at = pl.multiple_of(side[0] * rows, rows)
+    copies = [
+        pltpu.make_async_copy(acc.at[pl.ds(at, rows)], acc_ref, w_sem.at[0]),
+        pltpu.make_async_copy(first, w_ref.at[:, pl.ds(0, depth)], w_sem.at[1]),
+        pltpu.make_async_copy(second, w_ref.at[:, pl.ds(depth, depth)], w_sem.at[2]),
+    ]
+    fetch_features(slots[0], both, right, top, low, left, x_ref, x_sem.at[0])
+    for copy in copies:
+        copy.start()
+    pltpu.make_async_copy(both.at[0], x_ref, x_sem.at[0]).wait()
+    for copy in copies:
+        copy.wait()
+    x = jnp.where(side[0] == 0, x_ref[:, :full], x_ref[:, full:])
+    w = jnp.concatenate([w_ref[i] for i in range(3)], axis=1)
+    total = acc_ref[...] + jnp.dot(x, w, preferred_element_type=jnp.float32)
+    out[...] = total.astype(out.dtype)
+
+
+def project_last(features, shard, slots, acc, side, dtype):
+    _, rows, width = features[0].shape
+    total, heads = acc.shape[1], shard[0].shape[-1]
+    return pl.pallas_call(
+        last_kernel,
+        in_specs=[SMEM, SMEM] + [ANYWHERE] * (len(features) + 3),
+        out_specs=WHOLE,
+        out_shape=jax.ShapeDtypeStruct((rows, total), dtype),
+        scratch_shapes=[
+            pltpu.VMEM((rows, width), jnp.bfloat16),
+            pltpu.VMEM((3, width // 2, heads), jnp.bfloat16),
+            pltpu.VMEM((rows, total), jnp.float32),
+            pltpu.SemaphoreType.DMA((1,)),
+            pltpu.SemaphoreType.DMA((3,)),
+        ],
+        compiler_params=pltpu.CompilerParams(vmem_limit_bytes=QKV_VMEM << 20),
+    )(slots, side, *features, *shard, acc)
 
 
 def attend(q, k, v, bias):
@@ -294,8 +320,9 @@
     slots = (2 * (((shard >> 1) - x) & (mp // 2 - 1)) + ((shard & 1) ^ yhi)).astype(jnp.int32)
     features = (both, right, top, low, left)
     early = [[(own,), (up1,)], [(down1,), (up2,)], [(down2,), (up3,)], [(down3,)]]
-    (acc,) = project(features, early, slots[:7], core1)
-    kept, sent = project(features, [[(up4, down4)]], slots[7:], core1, acc, last=True)
+    acc = project(features, early, slots[:7])
+    sent = project_last(features, (up4, down4), slots[7:], acc, 1 - core1, jnp.bfloat16)
+    kept = project_last(features, (up4, down4), slots[7:], acc, core1, jnp.float32)
     attn = attention(kept, shift(sent, "core", 1), frames)
     attn, half = lax.optimization_barrier((attn, half))
     other_half = shift(half, "core", 1)

time: 185 us -> 186 us (level)
    pallas_call x2 -> x3, Pallas kernels: 16.4 us -> 18 us  [the longest x1 10.1 us: project(): pl.pallas_call(kernel, in_specs=[SMEM] + [ANYWHERE] * len(operands), out_...]
    unnamed x29 -> x33, local copies, waits for them, and re-layouts: 4.85 us -> 5.58 us
  transfers between devices with their start and end apart: 22 -> 22, of which waited for: 11 -> 10; matrix products, arithmetic and copies ran while one was open for 2% -> 2% of each run, Pallas kernels for 12% -> 12%
where the time goes in v9:
time: 186 us; the launch traced here: 185 us
  waiting for transfers between devices  64.1 us (34%)
  starting transfers between devices  45.9 us (25%)
  blocking collectives  33.1 us (18%)
  Pallas kernels  25.7 us (14%)
  local copies, waits for them, and re-layouts  11.6 us (6%)
  other arithmetic  2.2 us (1%)
    ppermute x20, waiting for transfers between devices, shift(): return lax.ppermute(x, axis, [(i, (i + by) % n) for i in range(n)])  50.2 us
    all_to_all x2, blocking collectives, exchange(): return lax.all_to_all(x, axis, split_axis=0, concat_axis=0, tiled=True)  33.1 us
    ppermute x20, starting transfers between devices, shift(): return lax.ppermute(x, axis, [(i, (i + by) % n) for i in range(n)])  31.7 us
    all_to_all x2, starting transfers between devices, exchange(): return lax.all_to_all(x, axis, split_axis=0, concat_axis=0, tiled=True)  14.2 us
    all_to_all x2, waiting for transfers between devices, exchange(): return lax.all_to_all(x, axis, split_axis=0, concat_axis=0, tiled=True)  13.9 us
    pallas_call x1, Pallas kernels, project(): pl.pallas_call(kernel, in_specs=[SMEM] + [ANYWHERE] * len(operands), out_...  10.1 us
    pallas_call x2, Pallas kernels, project_last(): pl.pallas_call(last_kernel, in_specs=[SMEM, SMEM] + [ANYWHERE] * (len(fea...  7.89 us
    unnamed x33, local copies, waits for them, and re-layouts  5.58 us
  transfers between devices with their start and end apart: 22, of which 10 were waited for; matrix products, arithmetic and copies ran while one was open for 2% of the time, Pallas kernels for 12%

profile of v9, /device:TPU:1, one launch (start us, length us, event | category | flops | bytes accessed | tf_op | source)
XLA Modules:
  0.0 184.7 jit_solution(14837329510241135733)
XLA Ops:
  4.6 10.0 %all-to-all-start = ((bf16[16,20,640]{2,1,0:T(8,128)(2,1)}), bf16[16,20,640]{2,1,0:T(8,128)(2,1)S(1)}, u32[]{:S(2)}, u32[]{:S(2)}) async-start(bf16[16,20,640]{2,1,0:T(8,128)(2,1)} %copy.19), calls=%async_computation | async-start | bytes 983040 | tf_op jit(solution)/shard_map/all_to_all | solution.py:23
  14.6 1.5 collective-permute-start.1
  17.4 13.8 %all-to-all-done = bf16[16,20,640]{2,1,0:T(8,128)(2,1)S(1)} async-done(((bf16[16,20,640]{2,1,0:T(8,128)(2,1)}), bf16[16,20,640]{2,1,0:T(8,128)(2,1)S(1)}, u32[]{:S(2)}, u32[]{:S(2)}) %all-to-all-start) | async-done | bytes 409632 | tf_op jit(solution)/shard_map/all_to_all | solution.py:23
  31.3 3.0 %collective-permute-start = (bf16[320,640]{1,0:T(8,128)(2,1)S(1)}, bf16[320,640]{1,0:T(8,128)(2,1)S(1)}, u32[]{:S(2)}, u32[]{:S(2)}) collective-permute-start(bf16[320,640]{1,0:T(8,128)(2,1)S(1)} %reshape.68), channel_id=1, source_target_pairs={{0,2},{2,0},{1,3},{3,1},{4,6},{6,4},{5,7},{7,5},{8,10},{10,8},{9,1... | collective-permute-start | bytes 1228808 | tf_op jit(solution)/shard_map/ppermute | solution.py:28
  34.4 9.1 %collective-permute-done = bf16[320,640]{1,0:T(8,128)(2,1)S(1)} collective-permute-done((bf16[320,640]{1,0:T(8,128)(2,1)S(1)}, bf16[320,640]{1,0:T(8,128)(2,1)S(1)}, u32[]{:S(2)}, u32[]{:S(2)}) %collective-permute-start) | collective-permute-done | bytes 409632 | tf_op jit(solution)/shard_map/ppermute | solution.py:28
  45.8 1.5 collective-permute-start.4
  47.3 2.7 %collective-permute-start.6 = (bf16[3,320,384]{2,1,0:T(8,128)(2,1)}, bf16[3,320,384]{2,1,0:T(8,128)(2,1)}, u32[]{:S(2)}, u32[]{:S(2)}) collective-permute-start(bf16[3,320,384]{2,1,0:T(8,128)(2,1)} %collective-permute-done.2.refs_8_), channel_id=1, source_target_pairs={{0,224},{32,0},{64,32},{96,64},{128,96},{160,128},{192,160},{224,1... | collective-permute-start | bytes 2211848 | tf_op jit(solution)/shard_map/ppermute | solution.py:28
  50.0 2.1 %copy-done.3 = bf16[384,5120]{1,0:T(8,128)(2,1)S(1)} copy-done((bf16[384,5120]{1,0:T(8,128)(2,1)S(1)}, bf16[384,5120]{1,0:T(8,128)(2,1)}, u32[]{:S(2)}) %copy-start.3) | copy-done | bytes 3932184
  53.8 11.6 %collective-permute-done.5.refs_9_ = bf16[3,320,384]{2,1,0:T(8,128)(2,1)} collective-permute-done((bf16[3,320,384]{2,1,0:T(8,128)(2,1)}, bf16[3,320,384]{2,1,0:T(8,128)(2,1)}, u32[]{:S(2)}, u32[]{:S(2)}) %collective-permute-start.5) | collective-permute-done | bytes 737312 | tf_op jit(solution)/shard_map/ppermute | solution.py:28
  65.5 1.9 %collective-permute-start.10 = (bf16[2,160,640]{2,1,0:T(8,128)(2,1)S(1)}, bf16[2,160,640]{2,1,0:T(8,128)(2,1)S(1)}, u32[]{:S(2)}, u32[]{:S(2)}) collective-permute-start(bf16[2,160,640]{2,1,0:T(8,128)(2,1)S(1)} %slice.33), channel_id=1, source_target_pairs={{0,12},{4,0},{8,4},{12,8},{1,13},{5,1},{9,5},{13,9},{2,14},{6,2},{... | collective-permute-start | bytes 1228808 | tf_op jit(solution)/shard_map/ppermute | solution.py:28
  68.7 1.5 collective-permute-start.8
  70.2 3.9 %collective-permute-done.10.refs_4_.low = bf16[2,160,640]{2,1,0:T(8,128)(2,1)S(1)} collective-permute-done((bf16[2,160,640]{2,1,0:T(8,128)(2,1)S(1)}, bf16[2,160,640]{2,1,0:T(8,128)(2,1)S(1)}, u32[]{:S(2)}, u32[]{:S(2)}) %collective-permute-start.10) | collective-permute-done | bytes 409632 | tf_op jit(solution)/shard_map/ppermute | solution.py:28
  74.1 3.3 %collective-permute-done.9.refs_3_.top = bf16[2,160,640]{2,1,0:T(8,128)(2,1)S(1)} collective-permute-done((bf16[2,160,640]{2,1,0:T(8,128)(2,1)S(1)}, bf16[2,160,640]{2,1,0:T(8,128)(2,1)S(1)}, u32[]{:S(2)}, u32[]{:S(2)}) %collective-permute-start.9) | collective-permute-done | bytes 409632 | tf_op jit(solution)/shard_map/ppermute | solution.py:28
  77.5 4.2 %all-to-all-start.1 = ((bf16[8,192,640]{2,1,0:T(8,128)(2,1)}), bf16[8,192,640]{2,1,0:T(8,128)(2,1)S(1)}, u32[]{:S(2)}, u32[]{:S(2)}) async-start(bf16[8,192,640]{2,1,0:T(8,128)(2,1)} %copy-done.1), calls=%async_computation.1 | async-start | bytes 3932160 | tf_op jit(solution)/shard_map/all_to_all | solution.py:23
  81.7 2.9 %collective-permute-done.7.refs_11_ = bf16[3,320,384]{2,1,0:T(8,128)(2,1)} collective-permute-done((bf16[3,320,384]{2,1,0:T(8,128)(2,1)}, bf16[3,320,384]{2,1,0:T(8,128)(2,1)}, u32[]{:S(2)}, u32[]{:S(2)}) %collective-permute-start.7) | collective-permute-done | bytes 737312 | tf_op jit(solution)/shard_map/ppermute | solution.py:28
  84.6 1.8 slice.34
  86.4 1.5 collective-permute-start.11
  88.9 1.4 collective-permute-start.12
  90.9 10.1 %shard_map.114.acc = f32[640,1152]{1,0:T(8,128)} custom-call(s32[7]{0:T(128)} %bitcast.35, bf16[2,320,640]{2,1,0:T(8,128)(2,1)} %copy-done.5, bf16[2,320,640]{2,1,0:T(8,128)(2,1)} %copy-done.7, bf16[2,160,640]{2,1,0:T(8,128)(2,1)} %copy-done.9, bf16[2,160,640]{2,1,0:T(8,128)(2,1)} %copy-done.8, bf16[2,320,640]{2,1,0:T(8,128)(2,1)} %copy-done.6, ...), custom_call_target="tpu_custom_call" | custom-call | tf_op jit(solution)/shard_map/pallas_call | solution.py:100
  101.8 3.8 %shard_map.116 = bf16[320,1152]{1,0:T(8,128)(2,1)} custom-call(s32[1]{0:T(128)} %slice.31.slots, s32[1]{0:T(128)S(6)} %sub.11.side, bf16[2,320,640]{2,1,0:T(8,128)(2,1)} %copy-done.5, bf16[2,320,640]{2,1,0:T(8,128)(2,1)} %copy-done.7, bf16[2,160,640]{2,1,0:T(8,128)(2,1)} %copy-done.9, bf16[2,160,640]{2,1,0:T(8,128)(2,1)} %copy-done.8, ...), custom_call_target="tpu_custom_call" | custom-call | tf_op jit(solution)/shard_map/pallas_call | solution.py:140
  105.6 4.1 %collective-permute-start.13 = (bf16[320,1152]{1,0:T(8,128)(2,1)}, bf16[320,1152]{1,0:T(8,128)(2,1)S(1)}, u32[]{:S(2)}, u32[]{:S(2)}) collective-permute-start(bf16[320,1152]{1,0:T(8,128)(2,1)} %shard_map.116), channel_id=1, source_target_pairs={{0,16},{16,0},{1,17},{17,1},{2,18},{18,2},{3,19},{19,3},{4,20},{20... | collective-permute-start | bytes 2211848 | tf_op jit(solution)/shard_map/ppermute | solution.py:28
  109.8 4.1 %shard_map.115.own_ref = f32[320,1152]{1,0:T(8,128)} custom-call(s32[1]{0:T(128)} %slice.31.slots, s32[1]{0:T(128)} %bitcast.core.side, bf16[2,320,640]{2,1,0:T(8,128)(2,1)} %copy-done.5, bf16[2,320,640]{2,1,0:T(8,128)(2,1)} %copy-done.7, bf16[2,160,640]{2,1,0:T(8,128)(2,1)} %copy-done.9, bf16[2,160,640]{2,1,0:T(8,128)(2,1)} %copy-done.8, ...), custom_call_target="tpu_custom_call" | custom-call | tf_op jit(solution)/shard_map/pallas_call | solution.py:140
  114.0 1.4 copy-done.2
  116.8 17.9 %all_to_all.20 = bf16[16,20,384]{2,1,0:T(8,128)(2,1)S(1)} all-to-all(bf16[16,20,384]{2,1,0:T(8,128)(2,1)S(1)} %shard_map.117), channel_id=1, replica_groups=mesh['z'=8,'core'=2,'x'=4,'yhi'=2,'dp'=2] {'z','core'}, dimensions={0} | all-to-all | bytes 491520 | tf_op jit(solution)/shard_map/all_to_all | solution.py:23
  134.8 3.0 %collective-permute-start.14 = (bf16[320,384]{1,0:T(8,128)(2,1)S(1)}, bf16[320,384]{1,0:T(8,128)(2,1)S(1)}, u32[]{:S(2)}, u32[]{:S(2)}) collective-permute-start(bf16[320,384]{1,0:T(8,128)(2,1)S(1)} %reshape.69), channel_id=1, source_target_pairs={{0,2},{2,0},{1,3},{3,1},{4,6},{6,4},{5,7},{7,5},{8,10},{10,8},{9,1... | collective-permute-start | bytes 737288 | tf_op jit(solution)/shard_map/ppermute | solution.py:28
  137.8 6.5 %collective-permute-done.14 = bf16[320,384]{1,0:T(8,128)(2,1)S(1)} collective-permute-done((bf16[320,384]{1,0:T(8,128)(2,1)S(1)}, bf16[320,384]{1,0:T(8,128)(2,1)S(1)}, u32[]{:S(2)}, u32[]{:S(2)}) %collective-permute-start.14) | collective-permute-done | bytes 245792 | tf_op jit(solution)/shard_map/ppermute | solution.py:28
  144.4 2.7 %collective-permute-start.17 = (bf16[2,320,384]{2,1,0:T(8,128)(2,1)S(1)}, bf16[2,320,384]{2,1,0:T(8,128)(2,1)S(1)}, u32[]{:S(2)}, u32[]{:S(2)}) collective-permute-start(bf16[2,320,384]{2,1,0:T(8,128)(2,1)S(1)} %pad_maximum_fusion.1.both), channel_id=1, source_target_pairs={{0,12},{4,0},{8,4},{12,8},{1,13},{5,1},{9,5},{13,9},{2,14},{6,2},{... | collective-permute-start | bytes 1474568 | tf_op jit(solution)/shard_map/ppermute | solution.py:28
  147.3 10.8 %collective-permute-done.15.left = bf16[2,320,384]{2,1,0:T(8,128)(2,1)S(1)} collective-permute-done((bf16[2,320,384]{2,1,0:T(8,128)(2,1)S(1)}, bf16[2,320,384]{2,1,0:T(8,128)(2,1)S(1)}, u32[]{:S(2)}, u32[]{:S(2)}) %collective-permute-start.15) | collective-permute-done | bytes 491552 | tf_op jit(solution)/shard_map/ppermute | solution.py:28
  158.2 2.9 %collective-permute-start.18 = (bf16[2,160,384]{2,1,0:T(8,128)(2,1)S(1)}, bf16[2,160,384]{2,1,0:T(8,128)(2,1)S(1)}, u32[]{:S(2)}, u32[]{:S(2)}) collective-permute-start(bf16[2,160,384]{2,1,0:T(8,128)(2,1)S(1)} %slice.42), channel_id=1, source_target_pairs={{0,12},{4,0},{8,4},{12,8},{1,13},{5,1},{9,5},{13,9},{2,14},{6,2},{... | collective-permute-start | bytes 737288 | tf_op jit(solution)/shard_map/ppermute | solution.py:28
  161.4 3.0 %shard_map.118.acc = f32[320,640]{1,0:T(8,128)S(1)} custom-call(s32[3]{0:T(128)S(1)} %pad_add_fusion.where, bf16[2,320,384]{2,1,0:T(8,128)(2,1)S(1)} %pad_maximum_fusion.1.both, bf16[2,320,384]{2,1,0:T(8,128)(2,1)S(1)} %collective-permute-done.17.right, bf16[2,320,384]{2,1,0:T(8,128)(2,1)S(1)} %collective-permute-done.15.left, ...), custom_call_target="tpu_custom_call" | custom-call | tf_op jit(solution)/shard_map/pallas_call | solution.py:236
  165.6 2.9 %shard_map.119 = (bf16[320,640]{1,0:T(8,128)(2,1)}, f32[32,2,672]{2,1,0:T(2,128)S(1)}) custom-call(s32[3]{0:T(128)S(1)} %pad_add_fusion.where, bf16[2,160,384]{2,1,0:T(8,128)(2,1)S(1)} %collective-permute-done.16.top, bf16[2,160,384]{2,1,0:T(8,128)(2,1)S(1)} %collective-permute-done.18.low, bf16[8,192,640]{2,1,0:T(8,128)(2,1)S(1)} %all-to-all-done.1.half, ...), custom_call_target="tpu_custom_call" | custom-call | tf_op jit(solution)/shard_map/pallas_call | solution.py:249
  168.5 15.2 %all_to_all.21 = f32[32,2,672]{2,1,0:T(2,128)S(1)} all-to-all(f32[32,2,672]{2,1,0:T(2,128)S(1)} %get-tuple-element.41), channel_id=1, replica_groups=mesh['z'=8,'core'=2,'x'=4,'yhi'=2,'dp'=2] {'z','core','dp'}, dimensions={0} | all-to-all | bytes 344064 | tf_op jit(solution)/shard_map/all_to_all | solution.py:23
  (81 shorter events, 17.8 us)
Async XLA Ops:
  0.6 160.6 %copy-start = (f32[32,640]{1,0:T(8,128)S(1)}, f32[32,640]{1,0:T(8,128)}, u32[]{:S(2)}) copy-start(f32[32,640]{1,0:T(8,128)} %param.17) | copy-start | bytes 245764
  2.9 11.7 %copy-start.11 = (bf16[320,3,384]{2,0,1:T(8,128)(2,1)S(1)}, bf16[320,3,384]{2,0,1:T(8,128)(2,1)}, u32[]{:S(2)}) copy-start(bf16[320,3,384]{2,0,1:T(8,128)(2,1)} %param.13) | copy-start | bytes 2211844
  4.6 26.6 %all-to-all-start = ((bf16[16,20,640]{2,1,0:T(8,128)(2,1)}), bf16[16,20,640]{2,1,0:T(8,128)(2,1)S(1)}, u32[]{:S(2)}, u32[]{:S(2)}) async-start(bf16[16,20,640]{2,1,0:T(8,128)(2,1)} %copy.19), calls=%async_computation | async-start | bytes 983040 | tf_op jit(solution)/shard_map/all_to_all | solution.py:23
  14.6 30.0 %collective-permute-start.1 = (bf16[3,320,384]{2,1,0:T(8,128)(2,1)S(1)}, bf16[3,320,384]{2,1,0:T(8,128)(2,1)}, u32[]{:S(2)}, u32[]{:S(2)}) collective-permute-start(bf16[3,320,384]{2,1,0:T(8,128)(2,1)S(1)} %bitcast.30), channel_id=1, source_target_pairs={{0,32},{32,64},{64,96},{96,128},{128,160},{160,192},{192,224},{224... | collective-permute-start | bytes 2211848 | tf_op jit(solution)/shard_map/ppermute | solution.py:28
  16.1 28.5 %collective-permute-start.2 = (bf16[3,320,384]{2,1,0:T(8,128)(2,1)S(1)}, bf16[3,320,384]{2,1,0:T(8,128)(2,1)}, u32[]{:S(2)}, u32[]{:S(2)}) collective-permute-start(bf16[3,320,384]{2,1,0:T(8,128)(2,1)S(1)} %bitcast.31), channel_id=1, source_target_pairs={{0,224},{32,0},{64,32},{96,64},{128,96},{160,128},{192,160},{224,1... | collective-permute-start | bytes 2211848 | tf_op jit(solution)/shard_map/ppermute | solution.py:28
  31.3 12.2 %collective-permute-start = (bf16[320,640]{1,0:T(8,128)(2,1)S(1)}, bf16[320,640]{1,0:T(8,128)(2,1)S(1)}, u32[]{:S(2)}, u32[]{:S(2)}) collective-permute-start(bf16[320,640]{1,0:T(8,128)(2,1)S(1)} %reshape.68), channel_id=1, source_target_pairs={{0,2},{2,0},{1,3},{3,1},{4,6},{6,4},{5,7},{7,5},{8,10},{10,8},{9,1... | collective-permute-start | bytes 1228808 | tf_op jit(solution)/shard_map/ppermute | solution.py:28
  43.6 8.9 %copy-start.5 = (bf16[2,320,640]{2,1,0:T(8,128)(2,1)}, bf16[2,320,640]{2,1,0:T(8,128)(2,1)S(1)}, u32[]{:S(2)}) copy-start(bf16[2,320,640]{2,1,0:T(8,128)(2,1)S(1)} %pad_maximum_fusion.refs_1_.both) | copy-start | bytes 2457604
  44.6 20.8 %collective-permute-start.3 = (bf16[2,320,640]{2,1,0:T(8,128)(2,1)S(1)}, bf16[2,320,640]{2,1,0:T(8,128)(2,1)S(1)}, u32[]{:S(2)}, u32[]{:S(2)}) collective-permute-start(bf16[2,320,640]{2,1,0:T(8,128)(2,1)S(1)} %pad_maximum_fusion.refs_1_.both), channel_id=1, source_target_pairs={{0,4},{4,8},{8,12},{12,0},{1,5},{5,9},{9,13},{13,1},{2,6},{6,10},{... | collective-permute-start | bytes 2457608 | tf_op jit(solution)/shard_map/ppermute | solution.py:28
  45.8 19.6 %collective-permute-start.4 = (bf16[2,320,640]{2,1,0:T(8,128)(2,1)S(1)}, bf16[2,320,640]{2,1,0:T(8,128)(2,1)S(1)}, u32[]{:S(2)}, u32[]{:S(2)}) collective-permute-start(bf16[2,320,640]{2,1,0:T(8,128)(2,1)S(1)} %pad_maximum_fusion.refs_1_.both), channel_id=1, source_target_pairs={{0,12},{4,0},{8,4},{12,8},{1,13},{5,1},{9,5},{13,9},{2,14},{6,2},{... | collective-permute-start | bytes 2457608 | tf_op jit(solution)/shard_map/ppermute | solution.py:28
  47.3 18.1 %collective-permute-start.5 = (bf16[3,320,384]{2,1,0:T(8,128)(2,1)}, bf16[3,320,384]{2,1,0:T(8,128)(2,1)}, u32[]{:S(2)}, u32[]{:S(2)}) collective-permute-start(bf16[3,320,384]{2,1,0:T(8,128)(2,1)} %collective-permute-done.1.refs_7_), channel_id=1, source_target_pairs={{0,32},{32,64},{64,96},{96,128},{128,160},{160,192},{192,224},{224... | collective-permute-start | bytes 2211848 | tf_op jit(solution)/shard_map/ppermute | solution.py:28
  47.3 18.1 %collective-permute-start.6 = (bf16[3,320,384]{2,1,0:T(8,128)(2,1)}, bf16[3,320,384]{2,1,0:T(8,128)(2,1)}, u32[]{:S(2)}, u32[]{:S(2)}) collective-permute-start(bf16[3,320,384]{2,1,0:T(8,128)(2,1)} %collective-permute-done.2.refs_8_), channel_id=1, source_target_pairs={{0,224},{32,0},{64,32},{96,64},{128,96},{160,128},{192,160},{224,1... | collective-permute-start | bytes 2211848 | tf_op jit(solution)/shard_map/ppermute | solution.py:28
  65.4 12.1 %copy-start.6 = (bf16[2,320,640]{2,1,0:T(8,128)(2,1)}, bf16[2,320,640]{2,1,0:T(8,128)(2,1)S(1)}, u32[]{:S(2)}) copy-start(bf16[2,320,640]{2,1,0:T(8,128)(2,1)S(1)} %collective-permute-done.3.refs_5_.left) | copy-start | bytes 2457604
  65.4 12.1 %copy-start.7 = (bf16[2,320,640]{2,1,0:T(8,128)(2,1)}, bf16[2,320,640]{2,1,0:T(8,128)(2,1)S(1)}, u32[]{:S(2)}) copy-start(bf16[2,320,640]{2,1,0:T(8,128)(2,1)S(1)} %collective-permute-done.4.refs_2_.right) | copy-start | bytes 2457604
  65.5 8.7 %collective-permute-start.10 = (bf16[2,160,640]{2,1,0:T(8,128)(2,1)S(1)}, bf16[2,160,640]{2,1,0:T(8,128)(2,1)S(1)}, u32[]{:S(2)}, u32[]{:S(2)}) collective-permute-start(bf16[2,160,640]{2,1,0:T(8,128)(2,1)S(1)} %slice.33), channel_id=1, source_target_pairs={{0,12},{4,0},{8,4},{12,8},{1,13},{5,1},{9,5},{13,9},{2,14},{6,2},{... | collective-permute-start | bytes 1228808 | tf_op jit(solution)/shard_map/ppermute | solution.py:28
  67.4 23.0 %copy-start.13 = (s32[8]{0:T(128)S(1)}, s32[8]{0:T(128)}, u32[]{:S(2)}) copy-start(s32[8]{0:T(128)} %constant.54.clone) | copy-start | bytes 100
  67.4 10.1 %collective-permute-start.9 = (bf16[2,160,640]{2,1,0:T(8,128)(2,1)S(1)}, bf16[2,160,640]{2,1,0:T(8,128)(2,1)S(1)}, u32[]{:S(2)}, u32[]{:S(2)}) collective-permute-start(bf16[2,160,640]{2,1,0:T(8,128)(2,1)S(1)} %slice.32), channel_id=1, source_target_pairs={{0,4},{4,8},{8,12},{12,0},{1,5},{5,9},{9,13},{13,1},{2,6},{6,10},{... | collective-permute-start | bytes 1228808 | tf_op jit(solution)/shard_map/ppermute | solution.py:28
  67.5 17.1 %collective-permute-start.7 = (bf16[3,320,384]{2,1,0:T(8,128)(2,1)}, bf16[3,320,384]{2,1,0:T(8,128)(2,1)}, u32[]{:S(2)}, u32[]{:S(2)}) collective-permute-start(bf16[3,320,384]{2,1,0:T(8,128)(2,1)} %collective-permute-done.5.refs_9_), channel_id=1, source_target_pairs={{0,32},{32,64},{64,96},{96,128},{128,160},{160,192},{192,224},{224... | collective-permute-start | bytes 2211848 | tf_op jit(solution)/shard_map/ppermute | solution.py:28
  68.7 15.8 %collective-permute-start.8 = (bf16[3,320,384]{2,1,0:T(8,128)(2,1)}, bf16[3,320,384]{2,1,0:T(8,128)(2,1)}, u32[]{:S(2)}, u32[]{:S(2)}) collective-permute-start(bf16[3,320,384]{2,1,0:T(8,128)(2,1)} %collective-permute-done.6.refs_10_), channel_id=1, source_target_pairs={{0,224},{32,0},{64,32},{96,64},{128,96},{160,128},{192,160},{224,1... | collective-permute-start | bytes 2211848 | tf_op jit(solution)/shard_map/ppermute | solution.py:28
  74.1 12.2 %copy-start.8 = (bf16[2,160,640]{2,1,0:T(8,128)(2,1)}, bf16[2,160,640]{2,1,0:T(8,128)(2,1)S(1)}, u32[]{:S(2)}) copy-start(bf16[2,160,640]{2,1,0:T(8,128)(2,1)S(1)} %collective-permute-done.10.refs_4_.low) | copy-start | bytes 1228804
  77.5 8.9 %copy-start.9 = (bf16[2,160,640]{2,1,0:T(8,128)(2,1)}, bf16[2,160,640]{2,1,0:T(8,128)(2,1)S(1)}, u32[]{:S(2)}) copy-start(bf16[2,160,640]{2,1,0:T(8,128)(2,1)S(1)} %collective-permute-done.9.refs_3_.top) | copy-start | bytes 1228804
  77.5 39.2 %all-to-all-start.1 = ((bf16[8,192,640]{2,1,0:T(8,128)(2,1)}), bf16[8,192,640]{2,1,0:T(8,128)(2,1)S(1)}, u32[]{:S(2)}, u32[]{:S(2)}) async-start(bf16[8,192,640]{2,1,0:T(8,128)(2,1)} %copy-done.1), calls=%async_computation.1 | async-start | bytes 3932160 | tf_op jit(solution)/shard_map/all_to_all | solution.py:23
  86.4 14.7 %collective-permute-start.11 = (bf16[3,160,384]{2,1,0:T(8,128)(2,1)}, bf16[3,160,384]{2,1,0:T(8,128)(2,1)}, u32[]{:S(2)}, u32[]{:S(2)}) collective-permute-start(bf16[3,160,384]{2,1,0:T(8,128)(2,1)} %slice.34), channel_id=1, source_target_pairs={{0,32},{32,64},{64,96},{96,128},{128,160},{160,192},{192,224},{224... | collective-permute-start | bytes 1105928 | tf_op jit(solution)/shard_map/ppermute | solution.py:28
  88.9 12.2 %collective-permute-start.12 = (bf16[3,160,384]{2,1,0:T(8,128)(2,1)S(1)}, bf16[3,160,384]{2,1,0:T(8,128)(2,1)S(1)}, u32[]{:S(2)}, u32[]{:S(2)}) collective-permute-start(bf16[3,160,384]{2,1,0:T(8,128)(2,1)S(1)} %slice.35), channel_id=1, source_target_pairs={{0,224},{32,0},{64,32},{96,64},{128,96},{160,128},{192,160},{224,1... | collective-permute-start | bytes 1105928 | tf_op jit(solution)/shard_map/ppermute | solution.py:28
  105.6 8.3 %collective-permute-start.13 = (bf16[320,1152]{1,0:T(8,128)(2,1)}, bf16[320,1152]{1,0:T(8,128)(2,1)S(1)}, u32[]{:S(2)}, u32[]{:S(2)}) collective-permute-start(bf16[320,1152]{1,0:T(8,128)(2,1)} %shard_map.116), channel_id=1, source_target_pairs={{0,16},{16,0},{1,17},{17,1},{2,18},{18,2},{3,19},{19,3},{4,20},{20... | collective-permute-start | bytes 2211848 | tf_op jit(solution)/shard_map/ppermute | solution.py:28
  116.7 30.4 %copy-start.14 = (f32[8,32]{1,0:T(8,128)S(1)}, f32[8,32]{1,0:T(8,128)}, u32[]{:S(2)}) copy-start(f32[8,32]{1,0:T(8,128)} %param.16) | copy-start | bytes 3076
  116.7 30.4 %copy-start.15 = (s32[2,1]{0,1:T(1,128)S(1)}, s32[2,1]{0,1:T(1,128)}, u32[]{:S(2)}) copy-start(s32[2,1]{0,1:T(1,128)} %param.15) | copy-start | bytes 28
  116.7 44.7 %collective-permute-start.19 = (bf16[8,192,640]{2,1,0:T(8,128)(2,1)S(1)}, bf16[8,192,640]{2,1,0:T(8,128)(2,1)}, u32[]{:S(2)}, u32[]{:S(2)}) collective-permute-start(bf16[8,192,640]{2,1,0:T(8,128)(2,1)S(1)} %all-to-all-done.1.half), channel_id=1, source_target_pairs={{0,16},{16,0},{1,17},{17,1},{2,18},{18,2},{3,19},{19,3},{4,20},{20... | collective-permute-start | bytes 5898248 | tf_op jit(solution)/shard_map/ppermute | solution.py:28
  134.8 9.5 %collective-permute-start.14 = (bf16[320,384]{1,0:T(8,128)(2,1)S(1)}, bf16[320,384]{1,0:T(8,128)(2,1)S(1)}, u32[]{:S(2)}, u32[]{:S(2)}) collective-permute-start(bf16[320,384]{1,0:T(8,128)(2,1)S(1)} %reshape.69), channel_id=1, source_target_pairs={{0,2},{2,0},{1,3},{3,1},{4,6},{6,4},{5,7},{7,5},{8,10},{10,8},{9,1... | collective-permute-start | bytes 737288 | tf_op jit(solution)/shard_map/ppermute | solution.py:28
  144.3 13.7 %collective-permute-start.15 = (bf16[2,320,384]{2,1,0:T(8,128)(2,1)S(1)}, bf16[2,320,384]{2,1,0:T(8,128)(2,1)S(1)}, u32[]{:S(2)}, u32[]{:S(2)}) collective-permute-start(bf16[2,320,384]{2,1,0:T(8,128)(2,1)S(1)} %pad_maximum_fusion.1.both), channel_id=1, source_target_pairs={{0,4},{4,8},{8,12},{12,0},{1,5},{5,9},{9,13},{13,1},{2,6},{6,10},{... | collective-permute-start | bytes 1474568 | tf_op jit(solution)/shard_map/ppermute | solution.py:28
  144.4 13.7 %collective-permute-start.17 = (bf16[2,320,384]{2,1,0:T(8,128)(2,1)S(1)}, bf16[2,320,384]{2,1,0:T(8,128)(2,1)S(1)}, u32[]{:S(2)}, u32[]{:S(2)}) collective-permute-start(bf16[2,320,384]{2,1,0:T(8,128)(2,1)S(1)} %pad_maximum_fusion.1.both), channel_id=1, source_target_pairs={{0,12},{4,0},{8,4},{12,8},{1,13},{5,1},{9,5},{13,9},{2,14},{6,2},{... | collective-permute-start | bytes 1474568 | tf_op jit(solution)/shard_map/ppermute | solution.py:28
  158.1 7.5 %collective-permute-start.16 = (bf16[2,160,384]{2,1,0:T(8,128)(2,1)S(1)}, bf16[2,160,384]{2,1,0:T(8,128)(2,1)S(1)}, u32[]{:S(2)}, u32[]{:S(2)}) collective-permute-start(bf16[2,160,384]{2,1,0:T(8,128)(2,1)S(1)} %slice.41), channel_id=1, source_target_pairs={{0,4},{4,8},{8,12},{12,0},{1,5},{5,9},{9,13},{13,1},{2,6},{6,10},{... | collective-permute-start | bytes 737288 | tf_op jit(solution)/shard_map/ppermute | solution.py:28
  158.2 7.4 %collective-permute-start.18 = (bf16[2,160,384]{2,1,0:T(8,128)(2,1)S(1)}, bf16[2,160,384]{2,1,0:T(8,128)(2,1)S(1)}, u32[]{:S(2)}, u32[]{:S(2)}) collective-permute-start(bf16[2,160,384]{2,1,0:T(8,128)(2,1)S(1)} %slice.42), channel_id=1, source_target_pairs={{0,12},{4,0},{8,4},{12,8},{1,13},{5,1},{9,5},{13,9},{2,14},{6,2},{... | collective-permute-start | bytes 737288 | tf_op jit(solution)/shard_map/ppermute | solution.py:28
  (6 other events, 10.3 us)

commit v10 on v9

--- a/solution.py
+++ b/solution.py
@@ -16,7 +16,7 @@
 ANYWHERE = pl.BlockSpec(memory_space=pl.ANY)
 FRAME = ("z", "core")
 MP = ("x", "yhi")
-SMALL = pltpu.CompilerParams(vmem_limit_bytes=10 * 1024 * 1024)
+SMALL = pltpu.CompilerParams(vmem_limit_bytes=12 << 20)
 
 
 def exchange(x, axis):
@@ -47,7 +47,7 @@
     pieces = [w for group in groups for w in group]
     count = sum(pieces)
     shards, refs = refs[:count], refs[count:]
-    acc, x_ref, w_ref, x_sem, w_sem = refs
+    acc, spare, x_ref, w_ref, x_sem, w_sem = refs
     rows, full = x_ref.shape[1], x_ref.shape[2] // 2
     copies, at = [], 0
     for j, n in enumerate(pieces):
@@ -62,6 +62,8 @@
             row += depth
             at += 1
 
+    n = len(pieces)
+    fetch_features(slots[n], both, right, top, low, left, spare, x_sem.at[n])
     j = 0
     for number, group in enumerate(groups):
         for i in range(j, j + len(group)):
@@ -84,6 +86,7 @@
         else:
             acc[...] = part
         j += len(group)
+    pltpu.make_async_copy(both.at[0], spare, x_sem.at[n]).wait()
 
 
 def project(features, groups, slots):
@@ -100,57 +103,45 @@
     return pl.pallas_call(
         kernel,
         in_specs=[SMEM] + [ANYWHERE] * len(operands),
-        out_specs=WHOLE,
-        out_shape=jax.ShapeDtypeStruct((2 * rows, 3 * heads), jnp.float32),
+        out_specs=[WHOLE, WHOLE],
+        out_shape=[
+            jax.ShapeDtypeStruct((2 * rows, 3 * heads), jnp.float32),
+            jax.ShapeDtypeStruct((rows, width), jnp.bfloat16),
+        ],
         scratch_shapes=[
             pltpu.VMEM((n, rows, width), jnp.bfloat16),
             pltpu.VMEM((3, n * width // 2, heads), jnp.bfloat16),
-            pltpu.SemaphoreType.DMA((n,)),
+            pltpu.SemaphoreType.DMA((n + 1,)),
             pltpu.SemaphoreType.DMA((len(shards),)),
         ],
         compiler_params=pltpu.CompilerParams(vmem_limit_bytes=QKV_VMEM << 20),
     )(slots, *operands)
 
 
-def last_kernel(slots, side, both, right, top, low, left, first, second, acc, out, *refs):
-    x_ref, w_ref, acc_ref, x_sem, w_sem = refs
+def last_kernel(core, x_ref, first, second, acc, kept, sent):
     rows, full = x_ref.shape[0], x_ref.shape[1] // 2
-    depth = first.shape[1]
-    at = pl.multiple_of(side[0] * rows, rows)
-    copies = [
-        pltpu.make_async_copy(acc.at[pl.ds(at, rows)], acc_ref, w_sem.at[0]),
-        pltpu.make_async_copy(first, w_ref.at[:, pl.ds(0, depth)], w_sem.at[1]),
-        pltpu.make_async_copy(second, w_ref.at[:, pl.ds(depth, depth)], w_sem.at[2]),
-    ]
-    fetch_features(slots[0], both, right, top, low, left, x_ref, x_sem.at[0])
-    for copy in copies:
-        copy.start()
-    pltpu.make_async_copy(both.at[0], x_ref, x_sem.at[0]).wait()
-    for copy in copies:
-        copy.wait()
-    x = jnp.where(side[0] == 0, x_ref[:, :full], x_ref[:, full:])
-    w = jnp.concatenate([w_ref[i] for i in range(3)], axis=1)
-    total = acc_ref[...] + jnp.dot(x, w, preferred_element_type=jnp.float32)
-    out[...] = total.astype(out.dtype)
-
-
-def project_last(features, shard, slots, acc, side, dtype):
-    _, rows, width = features[0].shape
-    total, heads = acc.shape[1], shard[0].shape[-1]
+    me = core[0]
+    w = jnp.concatenate(
+        [jnp.concatenate([first[i], second[i]], axis=0) for i in range(3)], axis=1
+    )
+    for side, out in ((me, kept), (1 - me, sent)):
+        x = jnp.where(side == 0, x_ref[:, :full], x_ref[:, full:])
+        part = jnp.dot(x, w, preferred_element_type=jnp.float32)
+        out[...] = (acc[pl.ds(pl.multiple_of(side * rows, rows), rows)] + part).astype(out.dtype)
+
+
+def project_last(core, x, first, second, acc):
+    rows, total = x.shape[0], acc.shape[1]
     return pl.pallas_call(
         last_kernel,
-        in_specs=[SMEM, SMEM] + [ANYWHERE] * (len(features) + 3),
-        out_specs=WHOLE,
-        out_shape=jax.ShapeDtypeStruct((rows, total), dtype),
-        scratch_shapes=[
-            pltpu.VMEM((rows, width), jnp.bfloat16),
-            pltpu.VMEM((3, width // 2, heads), jnp.bfloat16),
-            pltpu.VMEM((rows, total), jnp.float32),
-            pltpu.SemaphoreType.DMA((1,)),
-            pltpu.SemaphoreType.DMA((3,)),
+        in_specs=[SMEM] + [WHOLE] * 4,
+        out_specs=[WHOLE, WHOLE],
+        out_shape=[
+            jax.ShapeDtypeStruct((rows, total), jnp.float32),
+            jax.ShapeDtypeStruct((rows, total), jnp.bfloat16),
         ],
-        compiler_params=pltpu.CompilerParams(vmem_limit_bytes=QKV_VMEM << 20),
-    )(slots, side, *features, *shard, acc)
+        compiler_params=SMALL,
+    )(core, x, first, second, acc)
 
 
 def attend(q, k, v, bias):
@@ -320,9 +311,8 @@
     slots = (2 * (((shard >> 1) - x) & (mp // 2 - 1)) + ((shard & 1) ^ yhi)).astype(jnp.int32)
     features = (both, right, top, low, left)
     early = [[(own,), (up1,)], [(down1,), (up2,)], [(down2,), (up3,)], [(down3,)]]
-    acc = project(features, early, slots[:7])
-    sent = project_last(features, (up4, down4), slots[7:], acc, 1 - core1, jnp.bfloat16)
-    kept = project_last(features, (up4, down4), slots[7:], acc, core1, jnp.float32)
+    acc, spare = project(features, early, slots)
+    kept, sent = project_last(core1, spare, up4, down4, acc)
     attn = attention(kept, shift(sent, "core", 1), frames)
     attn, half = lax.optimization_barrier((attn, half))
     other_half = shift(half, "core", 1)

time: 186 us -> 183 us (0.984)
  Pallas kernels: 25.7 us -> 19.1 us
  starting transfers between devices: 45.9 us -> 49.1 us
  local copies, waits for them, and re-layouts: 11.6 us -> 14.2 us
  waiting for transfers between devices: 64.1 us -> 62 us
    pallas_call x2 -> x1, Pallas kernels: 7.89 us -> 1.05 us  [project_last(): pl.pallas_call(last_kernel, in_specs=[SMEM] + [WHOLE] * 4, out_specs=[WHO...]
    unnamed x33 -> x31, local copies, waits for them, and re-layouts: 5.58 us -> 8.02 us
    all_to_all x2, starting transfers between devices: 14.2 us -> 16.3 us  [exchange(): return lax.all_to_all(x, axis, split_axis=0, concat_axis=0, tiled=True)]
    ppermute x20, waiting for transfers between devices: 50.2 us -> 48.2 us  [shift(): return lax.ppermute(x, axis, [(i, (i + by) % n) for i in range(n)])]
  transfers between devices with their start and end apart: 22 -> 22, of which waited for: 10 -> 9; matrix products, arithmetic and copies ran while one was open for 2% -> 3% of each run, Pallas kernels for 12% -> 9%
where the time goes in v10:
time: 183 us
  waiting for transfers between devices  62 us (34%)
  starting transfers between devices  49.1 us (27%)
  blocking collectives  32.3 us (18%)
  Pallas kernels  19.1 us (10%)
  local copies, waits for them, and re-layouts  14.2 us (8%)
  other arithmetic  3.76 us (2%)
    ppermute x20, waiting for transfers between devices, shift(): return lax.ppermute(x, axis, [(i, (i + by) % n) for i in range(n)])  48.2 us
    ppermute x20, starting transfers between devices, shift(): return lax.ppermute(x, axis, [(i, (i + by) % n) for i in range(n)])  32.8 us
    all_to_all x2, blocking collectives, exchange(): return lax.all_to_all(x, axis, split_axis=0, concat_axis=0, tiled=True)  32.3 us
    all_to_all x2, starting transfers between devices, exchange(): return lax.all_to_all(x, axis, split_axis=0, concat_axis=0, tiled=True)  16.3 us
    all_to_all x2, waiting for transfers between devices, exchange(): return lax.all_to_all(x, axis, split_axis=0, concat_axis=0, tiled=True)  13.9 us
    pallas_call x1, Pallas kernels, project(): pl.pallas_call(kernel, in_specs=[SMEM] + [ANYWHERE] * len(operands), out_...  10.5 us
    unnamed x31, local copies, waits for them, and re-layouts  8.02 us
  transfers between devices with their start and end apart: 22, of which 9 were waited for; matrix products, arithmetic and copies ran while one was open for 3% of the time, Pallas kernels for 9%

profile of v10, /device:TPU:1, one launch (start us, length us, event | category | flops | bytes accessed | tf_op | source)
XLA Modules:
  0.0 182.7 jit_solution(4086990477434495015)
XLA Ops:
  4.6 10.0 %all-to-all-start = ((bf16[16,20,640]{2,1,0:T(8,128)(2,1)}), bf16[16,20,640]{2,1,0:T(8,128)(2,1)S(1)}, u32[]{:S(2)}, u32[]{:S(2)}) async-start(bf16[16,20,640]{2,1,0:T(8,128)(2,1)} %copy.19), calls=%async_computation | async-start | bytes 983040 | tf_op jit(solution)/shard_map/all_to_all | solution.py:23
  14.6 1.5 collective-permute-start.1
  16.1 1.3 collective-permute-start.2
  17.4 13.8 %all-to-all-done = bf16[16,20,640]{2,1,0:T(8,128)(2,1)S(1)} async-done(((bf16[16,20,640]{2,1,0:T(8,128)(2,1)}), bf16[16,20,640]{2,1,0:T(8,128)(2,1)S(1)}, u32[]{:S(2)}, u32[]{:S(2)}) %all-to-all-start) | async-done | bytes 409632 | tf_op jit(solution)/shard_map/all_to_all | solution.py:23
  31.3 3.0 %collective-permute-start = (bf16[320,640]{1,0:T(8,128)(2,1)S(1)}, bf16[320,640]{1,0:T(8,128)(2,1)}, u32[]{:S(2)}, u32[]{:S(2)}) collective-permute-start(bf16[320,640]{1,0:T(8,128)(2,1)S(1)} %reshape.68), channel_id=1, source_target_pairs={{0,2},{2,0},{1,3},{3,1},{4,6},{6,4},{5,7},{7,5},{8,10},{10,8},{9,1... | collective-permute-start | bytes 1228808 | tf_op jit(solution)/shard_map/ppermute | solution.py:28
  34.4 9.2 %collective-permute-done = bf16[320,640]{1,0:T(8,128)(2,1)} collective-permute-done((bf16[320,640]{1,0:T(8,128)(2,1)S(1)}, bf16[320,640]{1,0:T(8,128)(2,1)}, u32[]{:S(2)}, u32[]{:S(2)}) %collective-permute-start) | collective-permute-done | bytes 409632 | tf_op jit(solution)/shard_map/ppermute | solution.py:28
  46.9 1.5 collective-permute-start.4
  48.4 2.7 %collective-permute-start.6 = (bf16[3,320,384]{2,1,0:T(8,128)(2,1)}, bf16[3,320,384]{2,1,0:T(8,128)(2,1)}, u32[]{:S(2)}, u32[]{:S(2)}) collective-permute-start(bf16[3,320,384]{2,1,0:T(8,128)(2,1)} %collective-permute-done.2.refs_8_), channel_id=1, source_target_pairs={{0,224},{32,0},{64,32},{96,64},{128,96},{160,128},{192,160},{224,1... | collective-permute-start | bytes 2211848 | tf_op jit(solution)/shard_map/ppermute | solution.py:28
  51.1 2.1 %copy-done.2 = bf16[384,5120]{1,0:T(8,128)(2,1)S(1)} copy-done((bf16[384,5120]{1,0:T(8,128)(2,1)S(1)}, bf16[384,5120]{1,0:T(8,128)(2,1)}, u32[]{:S(2)}) %copy-start.2) | copy-done | bytes 3932184
  54.8 11.8 %collective-permute-done.5.refs_9_ = bf16[3,320,384]{2,1,0:T(8,128)(2,1)} collective-permute-done((bf16[3,320,384]{2,1,0:T(8,128)(2,1)}, bf16[3,320,384]{2,1,0:T(8,128)(2,1)}, u32[]{:S(2)}, u32[]{:S(2)}) %collective-permute-start.5) | collective-permute-done | bytes 737312 | tf_op jit(solution)/shard_map/ppermute | solution.py:28
  67.2 2.4 %collective-permute-start.10 = (bf16[2,160,640]{2,1,0:T(8,128)(2,1)S(1)}, bf16[2,160,640]{2,1,0:T(8,128)(2,1)}, u32[]{:S(2)}, u32[]{:S(2)}) collective-permute-start(bf16[2,160,640]{2,1,0:T(8,128)(2,1)S(1)} %slice.25), channel_id=1, source_target_pairs={{0,12},{4,0},{8,4},{12,8},{1,13},{5,1},{9,5},{13,9},{2,14},{6,2},{... | collective-permute-start | bytes 1228808 | tf_op jit(solution)/shard_map/ppermute | solution.py:28
  69.9 2.4 %collective-permute-start.8 = (bf16[3,320,384]{2,1,0:T(8,128)(2,1)}, bf16[3,320,384]{2,1,0:T(8,128)(2,1)}, u32[]{:S(2)}, u32[]{:S(2)}) collective-permute-start(bf16[3,320,384]{2,1,0:T(8,128)(2,1)} %collective-permute-done.6.refs_10_), channel_id=1, source_target_pairs={{0,224},{32,0},{64,32},{96,64},{128,96},{160,128},{192,160},{224,1... | collective-permute-start | bytes 2211848 | tf_op jit(solution)/shard_map/ppermute | solution.py:28
  72.3 4.6 %collective-permute-done.9.refs_3_ = bf16[2,160,640]{2,1,0:T(8,128)(2,1)S(1)} collective-permute-done((bf16[2,160,640]{2,1,0:T(8,128)(2,1)S(1)}, bf16[2,160,640]{2,1,0:T(8,128)(2,1)S(1)}, u32[]{:S(2)}, u32[]{:S(2)}) %collective-permute-start.9) | collective-permute-done | bytes 409632 | tf_op jit(solution)/shard_map/ppermute | solution.py:28
  77.7 6.4 %all-to-all-start.1 = ((bf16[8,192,640]{2,1,0:T(8,128)(2,1)}), bf16[8,192,640]{2,1,0:T(8,128)(2,1)S(1)}, u32[]{:S(2)}, u32[]{:S(2)}) async-start(bf16[8,192,640]{2,1,0:T(8,128)(2,1)} %copy-done.1), calls=%async_computation.1 | async-start | bytes 3932160 | tf_op jit(solution)/shard_map/all_to_all | solution.py:23
  84.0 2.5 %collective-permute-done.7.refs_11_ = bf16[3,320,384]{2,1,0:T(8,128)(2,1)} collective-permute-done((bf16[3,320,384]{2,1,0:T(8,128)(2,1)}, bf16[3,320,384]{2,1,0:T(8,128)(2,1)}, u32[]{:S(2)}, u32[]{:S(2)}) %collective-permute-start.7) | collective-permute-done | bytes 737312 | tf_op jit(solution)/shard_map/ppermute | solution.py:28
  86.5 1.8 slice.26
  89.1 1.8 slice.27
  90.8 1.9 %collective-permute-start.12 = (bf16[3,160,384]{2,1,0:T(8,128)(2,1)}, bf16[3,160,384]{2,1,0:T(8,128)(2,1)S(1)}, u32[]{:S(2)}, u32[]{:S(2)}) collective-permute-start(bf16[3,160,384]{2,1,0:T(8,128)(2,1)} %slice.27), channel_id=1, source_target_pairs={{0,224},{32,0},{64,32},{96,64},{128,96},{160,128},{192,160},{224,1... | collective-permute-start | bytes 1105928 | tf_op jit(solution)/shard_map/ppermute | solution.py:28
  93.3 10.5 %shard_map.114 = (f32[640,1152]{1,0:T(8,128)}, bf16[320,640]{1,0:T(8,128)(2,1)}) custom-call(s32[8]{0:T(128)} %xor_add_fusion.refs_0_, bf16[2,320,640]{2,1,0:T(8,128)(2,1)} %copy-done.6, bf16[2,320,640]{2,1,0:T(8,128)(2,1)} %copy-done.8, bf16[2,160,640]{2,1,0:T(8,128)(2,1)} %copy-done.11, bf16[2,160,640]{2,1,0:T(8,128)(2,1)} %collective-permute-done.10.refs_4_, ...), custom_call_target="tpu_custom_call" | custom-call | tf_op jit(solution)/shard_map/pallas_call | solution.py:103
  103.8 1.8 copy-done.3
  107.6 4.2 %collective-permute-start.13 = (bf16[320,1152]{1,0:T(8,128)(2,1)S(1)}, bf16[320,1152]{1,0:T(8,128)(2,1)S(1)}, u32[]{:S(2)}, u32[]{:S(2)}) collective-permute-start(bf16[320,1152]{1,0:T(8,128)(2,1)S(1)} %get-tuple-element.44), channel_id=1, source_target_pairs={{0,16},{16,0},{1,17},{17,1},{2,18},{18,2},{3,19},{19,3},{4,20},{20... | collective-permute-start | bytes 2211848 | tf_op jit(solution)/shard_map/ppermute | solution.py:28
  112.0 1.7 collective-permute-done.13.other_ref
  113.7 1.4 shard_map.116
  115.6 17.1 %all_to_all.20 = bf16[16,20,384]{2,1,0:T(8,128)(2,1)S(1)} all-to-all(bf16[16,20,384]{2,1,0:T(8,128)(2,1)S(1)} %shard_map.116), channel_id=1, replica_groups=mesh['z'=8,'core'=2,'x'=4,'yhi'=2,'dp'=2] {'z','core'}, dimensions={0} | all-to-all | bytes 491520 | tf_op jit(solution)/shard_map/all_to_all | solution.py:23
  132.7 3.0 %collective-permute-start.14 = (bf16[320,384]{1,0:T(8,128)(2,1)S(1)}, bf16[320,384]{1,0:T(8,128)(2,1)S(1)}, u32[]{:S(2)}, u32[]{:S(2)}) collective-permute-start(bf16[320,384]{1,0:T(8,128)(2,1)S(1)} %reshape.69), channel_id=1, source_target_pairs={{0,2},{2,0},{1,3},{3,1},{4,6},{6,4},{5,7},{7,5},{8,10},{10,8},{9,1... | collective-permute-start | bytes 737288 | tf_op jit(solution)/shard_map/ppermute | solution.py:28
  135.8 6.5 %collective-permute-done.14 = bf16[320,384]{1,0:T(8,128)(2,1)S(1)} collective-permute-done((bf16[320,384]{1,0:T(8,128)(2,1)S(1)}, bf16[320,384]{1,0:T(8,128)(2,1)S(1)}, u32[]{:S(2)}, u32[]{:S(2)}) %collective-permute-start.14) | collective-permute-done | bytes 245792 | tf_op jit(solution)/shard_map/ppermute | solution.py:28
  142.4 2.7 %collective-permute-start.17 = (bf16[2,320,384]{2,1,0:T(8,128)(2,1)S(1)}, bf16[2,320,384]{2,1,0:T(8,128)(2,1)S(1)}, u32[]{:S(2)}, u32[]{:S(2)}) collective-permute-start(bf16[2,320,384]{2,1,0:T(8,128)(2,1)S(1)} %pad_maximum_fusion.1.both), channel_id=1, source_target_pairs={{0,12},{4,0},{8,4},{12,8},{1,13},{5,1},{9,5},{13,9},{2,14},{6,2},{... | collective-permute-start | bytes 1474568 | tf_op jit(solution)/shard_map/ppermute | solution.py:28
  145.2 10.8 %collective-permute-done.15.left = bf16[2,320,384]{2,1,0:T(8,128)(2,1)S(1)} collective-permute-done((bf16[2,320,384]{2,1,0:T(8,128)(2,1)S(1)}, bf16[2,320,384]{2,1,0:T(8,128)(2,1)S(1)}, u32[]{:S(2)}, u32[]{:S(2)}) %collective-permute-start.15) | collective-permute-done | bytes 491552 | tf_op jit(solution)/shard_map/ppermute | solution.py:28
  156.2 2.9 %collective-permute-start.18 = (bf16[2,160,384]{2,1,0:T(8,128)(2,1)S(1)}, bf16[2,160,384]{2,1,0:T(8,128)(2,1)S(1)}, u32[]{:S(2)}, u32[]{:S(2)}) collective-permute-start(bf16[2,160,384]{2,1,0:T(8,128)(2,1)S(1)} %slice.33), channel_id=1, source_target_pairs={{0,12},{4,0},{8,4},{12,8},{1,13},{5,1},{9,5},{13,9},{2,14},{6,2},{... | collective-permute-start | bytes 737288 | tf_op jit(solution)/shard_map/ppermute | solution.py:28
  159.4 3.0 %shard_map.117.acc = f32[320,640]{1,0:T(8,128)S(1)} custom-call(s32[3]{0:T(128)S(1)} %pad_add_fusion.where, bf16[2,320,384]{2,1,0:T(8,128)(2,1)S(1)} %pad_maximum_fusion.1.both, bf16[2,320,384]{2,1,0:T(8,128)(2,1)S(1)} %collective-permute-done.17.right, bf16[2,320,384]{2,1,0:T(8,128)(2,1)S(1)} %collective-permute-done.15.left, ...), custom_call_target="tpu_custom_call" | custom-call | tf_op jit(solution)/shard_map/pallas_call | solution.py:227
  163.5 2.9 %shard_map.118 = (bf16[320,640]{1,0:T(8,128)(2,1)}, f32[32,2,672]{2,1,0:T(2,128)S(1)}) custom-call(s32[3]{0:T(128)S(1)} %pad_add_fusion.where, bf16[2,160,384]{2,1,0:T(8,128)(2,1)S(1)} %collective-permute-done.16.top, bf16[2,160,384]{2,1,0:T(8,128)(2,1)S(1)} %collective-permute-done.18.low, bf16[8,192,640]{2,1,0:T(8,128)(2,1)S(1)} %all-to-all-done.1.half, ...), custom_call_target="tpu_custom_call" | custom-call | tf_op jit(solution)/shard_map/pallas_call | solution.py:240
  166.5 15.2 %all_to_all.21 = f32[32,2,672]{2,1,0:T(2,128)S(1)} all-to-all(f32[32,2,672]{2,1,0:T(2,128)S(1)} %get-tuple-element.49), channel_id=1, replica_groups=mesh['z'=8,'core'=2,'x'=4,'yhi'=2,'dp'=2] {'z','core','dp'}, dimensions={0} | all-to-all | bytes 344064 | tf_op jit(solution)/shard_map/all_to_all | solution.py:23
  (77 shorter events, 17.7 us)
Async XLA Ops:
  0.6 158.6 %copy-start = (f32[32,640]{1,0:T(8,128)S(1)}, f32[32,640]{1,0:T(8,128)}, u32[]{:S(2)}) copy-start(f32[32,640]{1,0:T(8,128)} %param.17) | copy-start | bytes 245764
  2.9 11.7 %copy-start.9 = (bf16[320,3,384]{2,0,1:T(8,128)(2,1)S(1)}, bf16[320,3,384]{2,0,1:T(8,128)(2,1)}, u32[]{:S(2)}) copy-start(bf16[320,3,384]{2,0,1:T(8,128)(2,1)} %param.13) | copy-start | bytes 2211844
  4.6 26.6 %all-to-all-start = ((bf16[16,20,640]{2,1,0:T(8,128)(2,1)}), bf16[16,20,640]{2,1,0:T(8,128)(2,1)S(1)}, u32[]{:S(2)}, u32[]{:S(2)}) async-start(bf16[16,20,640]{2,1,0:T(8,128)(2,1)} %copy.19), calls=%async_computation | async-start | bytes 983040 | tf_op jit(solution)/shard_map/all_to_all | solution.py:23
  14.6 30.1 %collective-permute-start.1 = (bf16[3,320,384]{2,1,0:T(8,128)(2,1)S(1)}, bf16[3,320,384]{2,1,0:T(8,128)(2,1)S(1)}, u32[]{:S(2)}, u32[]{:S(2)}) collective-permute-start(bf16[3,320,384]{2,1,0:T(8,128)(2,1)S(1)} %bitcast.29), channel_id=1, source_target_pairs={{0,32},{32,64},{64,96},{96,128},{128,160},{160,192},{192,224},{224... | collective-permute-start | bytes 2211848 | tf_op jit(solution)/shard_map/ppermute | solution.py:28
  16.1 28.6 %collective-permute-start.2 = (bf16[3,320,384]{2,1,0:T(8,128)(2,1)S(1)}, bf16[3,320,384]{2,1,0:T(8,128)(2,1)}, u32[]{:S(2)}, u32[]{:S(2)}) collective-permute-start(bf16[3,320,384]{2,1,0:T(8,128)(2,1)S(1)} %bitcast.30), channel_id=1, source_target_pairs={{0,224},{32,0},{64,32},{96,64},{128,96},{160,128},{192,160},{224,1... | collective-permute-start | bytes 2211848 | tf_op jit(solution)/shard_map/ppermute | solution.py:28
  31.3 12.3 %collective-permute-start = (bf16[320,640]{1,0:T(8,128)(2,1)S(1)}, bf16[320,640]{1,0:T(8,128)(2,1)}, u32[]{:S(2)}, u32[]{:S(2)}) collective-permute-start(bf16[320,640]{1,0:T(8,128)(2,1)S(1)} %reshape.68), channel_id=1, source_target_pairs={{0,2},{2,0},{1,3},{3,1},{4,6},{6,4},{5,7},{7,5},{8,10},{10,8},{9,1... | collective-permute-start | bytes 1228808 | tf_op jit(solution)/shard_map/ppermute | solution.py:28
  44.7 8.8 %copy-start.6 = (bf16[2,320,640]{2,1,0:T(8,128)(2,1)}, bf16[2,320,640]{2,1,0:T(8,128)(2,1)S(1)}, u32[]{:S(2)}) copy-start(bf16[2,320,640]{2,1,0:T(8,128)(2,1)S(1)} %pad_maximum_fusion.refs_1_) | copy-start | bytes 2457604
  45.7 21.0 %collective-permute-start.3 = (bf16[2,320,640]{2,1,0:T(8,128)(2,1)S(1)}, bf16[2,320,640]{2,1,0:T(8,128)(2,1)S(1)}, u32[]{:S(2)}, u32[]{:S(2)}) collective-permute-start(bf16[2,320,640]{2,1,0:T(8,128)(2,1)S(1)} %pad_maximum_fusion.refs_1_), channel_id=1, source_target_pairs={{0,4},{4,8},{8,12},{12,0},{1,5},{5,9},{9,13},{13,1},{2,6},{6,10},{... | collective-permute-start | bytes 2457608 | tf_op jit(solution)/shard_map/ppermute | solution.py:28
  46.9 19.8 %collective-permute-start.4 = (bf16[2,320,640]{2,1,0:T(8,128)(2,1)S(1)}, bf16[2,320,640]{2,1,0:T(8,128)(2,1)S(1)}, u32[]{:S(2)}, u32[]{:S(2)}) collective-permute-start(bf16[2,320,640]{2,1,0:T(8,128)(2,1)S(1)} %pad_maximum_fusion.refs_1_), channel_id=1, source_target_pairs={{0,12},{4,0},{8,4},{12,8},{1,13},{5,1},{9,5},{13,9},{2,14},{6,2},{... | collective-permute-start | bytes 2457608 | tf_op jit(solution)/shard_map/ppermute | solution.py:28
  48.4 18.3 %collective-permute-start.5 = (bf16[3,320,384]{2,1,0:T(8,128)(2,1)}, bf16[3,320,384]{2,1,0:T(8,128)(2,1)}, u32[]{:S(2)}, u32[]{:S(2)}) collective-permute-start(bf16[3,320,384]{2,1,0:T(8,128)(2,1)} %copy-done.10), channel_id=1, source_target_pairs={{0,32},{32,64},{64,96},{96,128},{128,160},{160,192},{192,224},{224... | collective-permute-start | bytes 2211848 | tf_op jit(solution)/shard_map/ppermute | solution.py:28
  48.4 18.3 %collective-permute-start.6 = (bf16[3,320,384]{2,1,0:T(8,128)(2,1)}, bf16[3,320,384]{2,1,0:T(8,128)(2,1)}, u32[]{:S(2)}, u32[]{:S(2)}) collective-permute-start(bf16[3,320,384]{2,1,0:T(8,128)(2,1)} %collective-permute-done.2.refs_8_), channel_id=1, source_target_pairs={{0,224},{32,0},{64,32},{96,64},{128,96},{160,128},{192,160},{224,1... | collective-permute-start | bytes 2211848 | tf_op jit(solution)/shard_map/ppermute | solution.py:28
  51.1 2.1 %copy-start.2 = (bf16[384,5120]{1,0:T(8,128)(2,1)S(1)}, bf16[384,5120]{1,0:T(8,128)(2,1)}, u32[]{:S(2)}) copy-start(bf16[384,5120]{1,0:T(8,128)(2,1)} %w_ref) | copy-start | bytes 11796484
  66.7 11.0 %copy-start.7 = (bf16[2,320,640]{2,1,0:T(8,128)(2,1)}, bf16[2,320,640]{2,1,0:T(8,128)(2,1)S(1)}, u32[]{:S(2)}) copy-start(bf16[2,320,640]{2,1,0:T(8,128)(2,1)S(1)} %collective-permute-done.3.refs_5_) | copy-start | bytes 2457604
  66.7 11.0 %copy-start.8 = (bf16[2,320,640]{2,1,0:T(8,128)(2,1)}, bf16[2,320,640]{2,1,0:T(8,128)(2,1)S(1)}, u32[]{:S(2)}) copy-start(bf16[2,320,640]{2,1,0:T(8,128)(2,1)S(1)} %collective-permute-done.4.refs_2_) | copy-start | bytes 2457604
  66.8 10.1 %collective-permute-start.9 = (bf16[2,160,640]{2,1,0:T(8,128)(2,1)S(1)}, bf16[2,160,640]{2,1,0:T(8,128)(2,1)S(1)}, u32[]{:S(2)}, u32[]{:S(2)}) collective-permute-start(bf16[2,160,640]{2,1,0:T(8,128)(2,1)S(1)} %slice.24), channel_id=1, source_target_pairs={{0,4},{4,8},{8,12},{12,0},{1,5},{5,9},{9,13},{13,1},{2,6},{6,10},{... | collective-permute-start | bytes 1228808 | tf_op jit(solution)/shard_map/ppermute | solution.py:28
  67.2 25.5 %copy-start.12 = (s32[8]{0:T(128)S(1)}, s32[8]{0:T(128)}, u32[]{:S(2)}) copy-start(s32[8]{0:T(128)} %constant.52.clone) | copy-start | bytes 100
  67.2 10.4 %collective-permute-start.10 = (bf16[2,160,640]{2,1,0:T(8,128)(2,1)S(1)}, bf16[2,160,640]{2,1,0:T(8,128)(2,1)}, u32[]{:S(2)}, u32[]{:S(2)}) collective-permute-start(bf16[2,160,640]{2,1,0:T(8,128)(2,1)S(1)} %slice.25), channel_id=1, source_target_pairs={{0,12},{4,0},{8,4},{12,8},{1,13},{5,1},{9,5},{13,9},{2,14},{6,2},{... | collective-permute-start | bytes 1228808 | tf_op jit(solution)/shard_map/ppermute | solution.py:28
  69.7 16.8 %collective-permute-start.7 = (bf16[3,320,384]{2,1,0:T(8,128)(2,1)}, bf16[3,320,384]{2,1,0:T(8,128)(2,1)}, u32[]{:S(2)}, u32[]{:S(2)}) collective-permute-start(bf16[3,320,384]{2,1,0:T(8,128)(2,1)} %collective-permute-done.5.refs_9_), channel_id=1, source_target_pairs={{0,32},{32,64},{64,96},{96,128},{128,160},{160,192},{192,224},{224... | collective-permute-start | bytes 2211848 | tf_op jit(solution)/shard_map/ppermute | solution.py:28
  69.9 16.5 %collective-permute-start.8 = (bf16[3,320,384]{2,1,0:T(8,128)(2,1)}, bf16[3,320,384]{2,1,0:T(8,128)(2,1)}, u32[]{:S(2)}, u32[]{:S(2)}) collective-permute-start(bf16[3,320,384]{2,1,0:T(8,128)(2,1)} %collective-permute-done.6.refs_10_), channel_id=1, source_target_pairs={{0,224},{32,0},{64,32},{96,64},{128,96},{160,128},{192,160},{224,1... | collective-permute-start | bytes 2211848 | tf_op jit(solution)/shard_map/ppermute | solution.py:28
  77.7 37.4 %all-to-all-start.1 = ((bf16[8,192,640]{2,1,0:T(8,128)(2,1)}), bf16[8,192,640]{2,1,0:T(8,128)(2,1)S(1)}, u32[]{:S(2)}, u32[]{:S(2)}) async-start(bf16[8,192,640]{2,1,0:T(8,128)(2,1)} %copy-done.1), calls=%async_computation.1 | async-start | bytes 3932160 | tf_op jit(solution)/shard_map/all_to_all | solution.py:23
  88.3 15.5 %collective-permute-start.11 = (bf16[3,160,384]{2,1,0:T(8,128)(2,1)}, bf16[3,160,384]{2,1,0:T(8,128)(2,1)S(1)}, u32[]{:S(2)}, u32[]{:S(2)}) collective-permute-start(bf16[3,160,384]{2,1,0:T(8,128)(2,1)} %slice.26), channel_id=1, source_target_pairs={{0,32},{32,64},{64,96},{96,128},{128,160},{160,192},{192,224},{224... | collective-permute-start | bytes 1105928 | tf_op jit(solution)/shard_map/ppermute | solution.py:28
  90.8 12.9 %collective-permute-start.12 = (bf16[3,160,384]{2,1,0:T(8,128)(2,1)}, bf16[3,160,384]{2,1,0:T(8,128)(2,1)S(1)}, u32[]{:S(2)}, u32[]{:S(2)}) collective-permute-start(bf16[3,160,384]{2,1,0:T(8,128)(2,1)} %slice.27), channel_id=1, source_target_pairs={{0,224},{32,0},{64,32},{96,64},{128,96},{160,128},{192,160},{224,1... | collective-permute-start | bytes 1105928 | tf_op jit(solution)/shard_map/ppermute | solution.py:28
  107.6 6.1 %collective-permute-start.13 = (bf16[320,1152]{1,0:T(8,128)(2,1)S(1)}, bf16[320,1152]{1,0:T(8,128)(2,1)S(1)}, u32[]{:S(2)}, u32[]{:S(2)}) collective-permute-start(bf16[320,1152]{1,0:T(8,128)(2,1)S(1)} %get-tuple-element.44), channel_id=1, source_target_pairs={{0,16},{16,0},{1,17},{17,1},{2,18},{18,2},{3,19},{19,3},{4,20},{20... | collective-permute-start | bytes 2211848 | tf_op jit(solution)/shard_map/ppermute | solution.py:28
  115.1 30.0 %copy-start.13 = (f32[8,32]{1,0:T(8,128)S(1)}, f32[8,32]{1,0:T(8,128)}, u32[]{:S(2)}) copy-start(f32[8,32]{1,0:T(8,128)} %param.16) | copy-start | bytes 3076
  115.1 30.0 %copy-start.14 = (s32[2,1]{0,1:T(1,128)S(1)}, s32[2,1]{0,1:T(1,128)}, u32[]{:S(2)}) copy-start(s32[2,1]{0,1:T(1,128)} %param.15) | copy-start | bytes 28
  115.1 44.3 %collective-permute-start.19 = (bf16[8,192,640]{2,1,0:T(8,128)(2,1)S(1)}, bf16[8,192,640]{2,1,0:T(8,128)(2,1)}, u32[]{:S(2)}, u32[]{:S(2)}) collective-permute-start(bf16[8,192,640]{2,1,0:T(8,128)(2,1)S(1)} %all-to-all-done.1.half), channel_id=1, source_target_pairs={{0,16},{16,0},{1,17},{17,1},{2,18},{18,2},{3,19},{19,3},{4,20},{20... | collective-permute-start | bytes 5898248 | tf_op jit(solution)/shard_map/ppermute | solution.py:28
  132.7 9.5 %collective-permute-start.14 = (bf16[320,384]{1,0:T(8,128)(2,1)S(1)}, bf16[320,384]{1,0:T(8,128)(2,1)S(1)}, u32[]{:S(2)}, u32[]{:S(2)}) collective-permute-start(bf16[320,384]{1,0:T(8,128)(2,1)S(1)} %reshape.69), channel_id=1, source_target_pairs={{0,2},{2,0},{1,3},{3,1},{4,6},{6,4},{5,7},{7,5},{8,10},{10,8},{9,1... | collective-permute-start | bytes 737288 | tf_op jit(solution)/shard_map/ppermute | solution.py:28
  142.3 13.7 %collective-permute-start.15 = (bf16[2,320,384]{2,1,0:T(8,128)(2,1)S(1)}, bf16[2,320,384]{2,1,0:T(8,128)(2,1)S(1)}, u32[]{:S(2)}, u32[]{:S(2)}) collective-permute-start(bf16[2,320,384]{2,1,0:T(8,128)(2,1)S(1)} %pad_maximum_fusion.1.both), channel_id=1, source_target_pairs={{0,4},{4,8},{8,12},{12,0},{1,5},{5,9},{9,13},{13,1},{2,6},{6,10},{... | collective-permute-start | bytes 1474568 | tf_op jit(solution)/shard_map/ppermute | solution.py:28
  142.4 13.7 %collective-permute-start.17 = (bf16[2,320,384]{2,1,0:T(8,128)(2,1)S(1)}, bf16[2,320,384]{2,1,0:T(8,128)(2,1)S(1)}, u32[]{:S(2)}, u32[]{:S(2)}) collective-permute-start(bf16[2,320,384]{2,1,0:T(8,128)(2,1)S(1)} %pad_maximum_fusion.1.both), channel_id=1, source_target_pairs={{0,12},{4,0},{8,4},{12,8},{1,13},{5,1},{9,5},{13,9},{2,14},{6,2},{... | collective-permute-start | bytes 1474568 | tf_op jit(solution)/shard_map/ppermute | solution.py:28
  156.0 7.5 %collective-permute-start.16 = (bf16[2,160,384]{2,1,0:T(8,128)(2,1)S(1)}, bf16[2,160,384]{2,1,0:T(8,128)(2,1)S(1)}, u32[]{:S(2)}, u32[]{:S(2)}) collective-permute-start(bf16[2,160,384]{2,1,0:T(8,128)(2,1)S(1)} %slice.32), channel_id=1, source_target_pairs={{0,4},{4,8},{8,12},{12,0},{1,5},{5,9},{9,13},{13,1},{2,6},{6,10},{... | collective-permute-start | bytes 737288 | tf_op jit(solution)/shard_map/ppermute | solution.py:28
  156.2 7.4 %collective-permute-start.18 = (bf16[2,160,384]{2,1,0:T(8,128)(2,1)S(1)}, bf16[2,160,384]{2,1,0:T(8,128)(2,1)S(1)}, u32[]{:S(2)}, u32[]{:S(2)}) collective-permute-start(bf16[2,160,384]{2,1,0:T(8,128)(2,1)S(1)} %slice.33), channel_id=1, source_target_pairs={{0,12},{4,0},{8,4},{12,8},{1,13},{5,1},{9,5},{13,9},{2,14},{6,2},{... | collective-permute-start | bytes 737288 | tf_op jit(solution)/shard_map/ppermute | solution.py:28
  159.4 4.2 %copy-start.4 = (bf16[2,1,160,640]{3,2,1,0:T(8,128)(2,1)S(1)}, bf16[2,1,160,640]{3,2,1,0:T(8,128)(2,1)}, u32[]{:S(2)}) copy-start(bf16[2,1,160,640]{3,2,1,0:T(8,128)(2,1)} %param.18) | copy-start | bytes 1228804
  (5 other events, 5.9 us)

commit v11 on v10

--- a/solution.py
+++ b/solution.py
@@ -28,22 +28,24 @@
     return lax.ppermute(x, axis, [(i, (i + by) % n) for i in range(n)])
 
 
-def fetch_features(slot, both, right, top, low, left, target, sem):
-    far, own = slot >> 1, slot & 1
-    for k, source in ((0, both), (1, right), (3, left)):
-
-        @pl.when(far == k)
+def fetch_features(slot, pieces, target, sem):
+    half = target.shape[0] // 2
+    for own in range(2):
+        here, right, left, top, low = pieces[5 * own : 5 * own + 5]
+        for k, source in ((0, here), (1, right), (3, left)):
+
+            @pl.when(slot == 2 * k + own)
+            def _():
+                pltpu.make_async_copy(source, target, sem).start()
+
+        @pl.when(slot == 4 + own)
         def _():
-            pltpu.make_async_copy(source.at[own], target, sem).start()
-
-    @pl.when(far == 2)
-    def _():
-        half = target.shape[0] // 2
-        pltpu.make_async_copy(top.at[own], target.at[pl.ds(0, half)], sem).start()
-        pltpu.make_async_copy(low.at[own], target.at[pl.ds(half, half)], sem).start()
-
-
-def qkv_kernel(groups, slots, both, right, top, low, left, *refs):
+            pltpu.make_async_copy(top, target.at[pl.ds(0, half)], sem).start()
+            pltpu.make_async_copy(low, target.at[pl.ds(half, half)], sem).start()
+
+
+def qkv_kernel(groups, slots, *refs):
+    features, refs = refs[:10], refs[10:]
     pieces = [w for group in groups for w in group]
     count = sum(pieces)
     shards, refs = refs[:count], refs[count:]
@@ -51,7 +53,7 @@
     rows, full = x_ref.shape[1], x_ref.shape[2] // 2
     copies, at = [], 0
     for j, n in enumerate(pieces):
-        fetch_features(slots[j], both, right, top, low, left, x_ref.at[j], x_sem.at[j])
+        fetch_features(slots[j], features, x_ref.at[j], x_sem.at[j])
         copies.append([])
         row = j * full
         for source in shards[at : at + n]:
@@ -63,11 +65,11 @@
             at += 1
 
     n = len(pieces)
-    fetch_features(slots[n], both, right, top, low, left, spare, x_sem.at[n])
+    fetch_features(slots[n], features, spare, x_sem.at[n])
     j = 0
     for number, group in enumerate(groups):
         for i in range(j, j + len(group)):
-            pltpu.make_async_copy(both.at[0], x_ref.at[i], x_sem.at[i]).wait()
+            pltpu.make_async_copy(features[0], x_ref.at[i], x_sem.at[i]).wait()
             for copy in copies[i]:
                 copy.wait()
         xs = [x_ref[j + i] for i in range(len(group))]
@@ -86,11 +88,11 @@
         else:
             acc[...] = part
         j += len(group)
-    pltpu.make_async_copy(both.at[0], spare, x_sem.at[n]).wait()
+    pltpu.make_async_copy(features[0], spare, x_sem.at[n]).wait()
 
 
 def project(features, groups, slots):
-    _, rows, width = features[0].shape
+    rows, width = features[0].shape
     counts = [[len(s) for s in group] for group in groups]
     shards = [w for group in groups for s in group for w in s]
     heads = shards[0].shape[-1]
@@ -196,14 +198,16 @@
     return jnp.dot(x, jnp.concatenate(w, axis=0), preferred_element_type=jnp.float32)
 
 
-def near_kernel(where, both, right, left, half, other, acc):
-    acc[...] = out_product((both[0], both[1]), where, 0, half, other)
-    acc[...] += out_product((right[0], right[1]), where, 1, half, other)
-    acc[...] += out_product((left[0], left[1]), where, 3, half, other)
-
-
-def far_kernel(where, top, low, half, other, acc, xin, gate, cot, codevec, next_ref, terms):
-    far = tuple(jnp.concatenate([top[b], low[b]], axis=0) for b in range(2))
+def near_kernel(where, m0, m1, r0, r1, l0, l1, half, other, acc):
+    acc[...] = out_product((m0[...], m1[...]), where, 0, half, other)
+    acc[...] += out_product((r0[...], r1[...]), where, 1, half, other)
+    acc[...] += out_product((l0[...], l1[...]), where, 3, half, other)
+
+
+def far_kernel(
+    where, t0, w0, t1, w1, half, other, acc, xin, gate, cot, codevec, next_ref, terms
+):
+    far = tuple(jnp.concatenate([t[...], w[...]], axis=0) for t, w in ((t0, w0), (t1, w1)))
     mixed = acc[...] + out_product(far, where, 2, half, other)
     rows, width = mixed.shape
     clips = gate.shape[0]
@@ -222,11 +226,11 @@
 
 
 def near(where, *operands):
-    rows, width = operands[0].shape[1], operands[3].shape[2]
+    rows, width = operands[0].shape[0], operands[6].shape[2]
     smem, vmem = pl.BlockSpec(memory_space=pltpu.SMEM), pl.BlockSpec(memory_space=pltpu.VMEM)
     return pl.pallas_call(
         near_kernel,
-        in_specs=[smem] + [vmem] * 5,
+        in_specs=[smem] + [vmem] * 8,
         out_specs=vmem,
         out_shape=jax.ShapeDtypeStruct((rows, width), jnp.float32),
         compiler_params=SMALL,
@@ -234,16 +238,16 @@
 
 
 def finish(where, peers, *operands):
-    rows, width = operands[4].shape
-    clips = operands[6].shape[0]
+    rows, width = operands[6].shape
+    clips = operands[8].shape[0]
     smem, vmem = pl.BlockSpec(memory_space=pltpu.SMEM), pl.BlockSpec(memory_space=pltpu.VMEM)
     return pl.pallas_call(
         far_kernel,
-        in_specs=[smem] + [vmem] * 9,
+        in_specs=[smem] + [vmem] * 11,
         out_specs=[vmem, vmem],
         out_shape=[
             jax.ShapeDtypeStruct((rows, width), jnp.bfloat16),
-            jax.ShapeDtypeStruct((peers, clips, width + operands[8].shape[1]), jnp.float32),
+            jax.ShapeDtypeStruct((peers, clips, width + operands[10].shape[1]), jnp.float32),
         ],
         compiler_params=SMALL,
     )(where, *operands)
@@ -290,17 +294,27 @@
 
     own = w_qkv.transpose(1, 0, 2)
     up1, down1 = shift(own, "z", 1), shift(own, "z", -1)
-    both = jnp.stack([mine, shift(mine, "yhi", 1)])
-    both, w_out, up1, down1 = lax.optimization_barrier((both, w_out, up1, down1))
-    left, right = shift(both, "x", 1), shift(both, "x", -1)
+    middle = rows // 2
+
+    def sideways(block):
+        return shift(block, "x", -1), shift(block, "x", 1)
+
+    def onward(right, left):
+        return shift(left[:middle], "x", 1), shift(right[middle:], "x", -1)
+
+    other = shift(mine, "yhi", 1)
+    side = sideways(mine)
+    other, side, up1, down1 = lax.optimization_barrier((other, side, up1, down1))
     up2, down2 = shift(up1, "z", 1), shift(down1, "z", -1)
+    other_side, far = sideways(other), onward(*side)
+    other_side, far, up2, down2, w_out = lax.optimization_barrier(
+        (other_side, far, up2, down2, w_out)
+    )
+    up3, down3 = shift(up2, "z", 1), shift(down2, "z", -1)
+    other_far = onward(*other_side)
     blocks = column_blocks(w_out, core1, width)
-    left, right, up2, down2, blocks = lax.optimization_barrier((left, right, up2, down2, blocks))
-    middle = rows // 2
-    top, low = shift(left[:, :middle], "x", 1), shift(right[:, middle:], "x", -1)
-    up3, down3 = shift(up2, "z", 1), shift(down2, "z", -1)
-    top, low, blocks = lax.optimization_barrier((top, low, blocks))
-    up3, down3, top, low = lax.optimization_barrier((up3, down3, top, low))
+    other_far, blocks = lax.optimization_barrier((other_far, blocks))
+    up3, down3, other_far = lax.optimization_barrier((up3, down3, other_far))
     up4 = shift(up3[:, : depth // 2], "z", 1)
     down4 = shift(down3[:, depth // 2 :], "z", -1)
 
@@ -309,7 +323,7 @@
     x, yhi = lax.axis_index("x"), lax.axis_index("yhi")
     shard = (z + jnp.array([0, zs - 1, 1, zs - 2, 2, zs - 3, 3, zs - 4], jnp.int32)) & (zs - 1)
     slots = (2 * (((shard >> 1) - x) & (mp // 2 - 1)) + ((shard & 1) ^ yhi)).astype(jnp.int32)
-    features = (both, right, top, low, left)
+    features = (mine, *side, *far, other, *other_side, *other_far)
     early = [[(own,), (up1,)], [(down1,), (up2,)], [(down2,), (up3,)], [(down3,)]]
     acc, spare = project(features, early, slots)
     kept, sent = project_last(core1, spare, up4, down4, acc)
@@ -317,12 +331,15 @@
     attn, half = lax.optimization_barrier((attn, half))
     other_half = shift(half, "core", 1)
     attn = exchange(attn, FRAME).reshape(rows, heads)
-    attn_both = jnp.stack([attn, shift(attn, "yhi", 1)])
-    attn_left, attn_right = shift(attn_both, "x", 1), shift(attn_both, "x", -1)
-    attn_top = shift(attn_left[:, :middle], "x", 1)
-    attn_low = shift(attn_right[:, middle:], "x", -1)
+    peer = shift(attn, "yhi", 1)
+    side = sideways(attn)
+    peer, side = lax.optimization_barrier((peer, side))
+    peer_side, far = sideways(peer), onward(*side)
+    peer_far = onward(*peer_side)
     where = jnp.stack([core, x, yhi]).astype(jnp.int32)
-    acc = near(where, attn_both, attn_right, attn_left, half, other_half)
+    acc = near(
+        where, attn, peer, side[0], peer_side[0], side[1], peer_side[1], half, other_half
+    )
     onehot = (action_idx.reshape(clips)[:, None] == jnp.arange(codebook.shape[0])[None, :]).astype(
         jnp.float32
     )
@@ -330,7 +347,7 @@
     gate = jnp.dot(codevec, act_proj, precision=lax.Precision.HIGHEST)
     peers = frames * lax.axis_size("dp")
     next_state, terms = finish(
-        where, peers, attn_top, attn_low, half, other_half, acc, xin, gate,
+        where, peers, *far, *peer_far, half, other_half, acc, xin, gate,
         cotangent.reshape(rows, width), codevec,
     )
     terms = exchange(terms, FRAME + ("dp",))

time: 183 us -> 178 us (0.973)
  waiting for transfers between devices: 62 us -> 59 us
    ppermute x20 -> x28, starting transfers between devices: 32.8 us -> 36.1 us  [shift(): return lax.ppermute(x, axis, [(i, (i + by) % n) for i in range(n)])]
    ppermute x20 -> x28, waiting for transfers between devices: 48.2 us -> 45.2 us  [shift(): return lax.ppermute(x, axis, [(i, (i + by) % n) for i in range(n)])]
    all_to_all x2, starting transfers between devices: 16.3 us -> 13.6 us  [exchange(): return lax.all_to_all(x, axis, split_axis=0, concat_axis=0, tiled=True)]
    unnamed x31 -> x41, local copies, waits for them, and re-layouts: 8.02 us -> 7.87 us
  transfers between devices with their start and end apart: 22 -> 30, of which waited for: 9 -> 13; matrix products, arithmetic and copies ran while one was open for 3% -> 2% of each run, Pallas kernels for 9% -> 9%
where the time goes in v11:
time: 178 us; the launch traced here: 177 us
  waiting for transfers between devices  59 us (33%)
  starting transfers between devices  49.6 us (28%)
  blocking collectives  31.5 us (18%)
  Pallas kernels  19.1 us (11%)
  local copies, waits for them, and re-layouts  12.9 us (7%)
  other arithmetic  2.64 us (1%)
    ppermute x28, waiting for transfers between devices, shift(): return lax.ppermute(x, axis, [(i, (i + by) % n) for i in range(n)])  45.2 us
    ppermute x28, starting transfers between devices, shift(): return lax.ppermute(x, axis, [(i, (i + by) % n) for i in range(n)])  36.1 us
    all_to_all x2, blocking collectives, exchange(): return lax.all_to_all(x, axis, split_axis=0, concat_axis=0, tiled=True)  31.5 us
    all_to_all x2, waiting for transfers between devices, exchange(): return lax.all_to_all(x, axis, split_axis=0, concat_axis=0, tiled=True)  13.9 us
    all_to_all x2, starting transfers between devices, exchange(): return lax.all_to_all(x, axis, split_axis=0, concat_axis=0, tiled=True)  13.6 us
    pallas_call x1, Pallas kernels, project(): pl.pallas_call(kernel, in_specs=[SMEM] + [ANYWHERE] * len(operands), out_...  10.5 us
    unnamed x41, local copies, waits for them, and re-layouts  7.87 us
  transfers between devices with their start and end apart: 30, of which 13 were waited for; matrix products, arithmetic and copies ran while one was open for 2% of the time, Pallas kernels for 9%

profile of v11, /device:TPU:1, one launch (start us, length us, event | category | flops | bytes accessed | tf_op | source)
XLA Modules:
  0.0 177.2 jit_solution(6119049660995368118)
XLA Ops:
  4.6 10.0 %all-to-all-start = ((bf16[16,20,640]{2,1,0:T(8,128)(2,1)}), bf16[16,20,640]{2,1,0:T(8,128)(2,1)S(1)}, u32[]{:S(2)}, u32[]{:S(2)}) async-start(bf16[16,20,640]{2,1,0:T(8,128)(2,1)} %copy.18), calls=%async_computation | async-start | bytes 983040 | tf_op jit(solution)/shard_map/all_to_all | solution.py:23
  14.6 1.5 collective-permute-start.3
  17.4 13.8 %all-to-all-done = bf16[16,20,640]{2,1,0:T(8,128)(2,1)S(1)} async-done(((bf16[16,20,640]{2,1,0:T(8,128)(2,1)}), bf16[16,20,640]{2,1,0:T(8,128)(2,1)S(1)}, u32[]{:S(2)}, u32[]{:S(2)}) %all-to-all-start) | async-done | bytes 409632 | tf_op jit(solution)/shard_map/all_to_all | solution.py:23
  31.3 3.0 %collective-permute-start = (bf16[320,640]{1,0:T(8,128)(2,1)S(1)}, bf16[320,640]{1,0:T(8,128)(2,1)S(1)}, u32[]{:S(2)}, u32[]{:S(2)}) collective-permute-start(bf16[320,640]{1,0:T(8,128)(2,1)S(1)} %reshape.68.refs_1_), channel_id=1, source_target_pairs={{0,2},{2,0},{1,3},{3,1},{4,6},{6,4},{5,7},{7,5},{8,10},{10,8},{9,1... | collective-permute-start | bytes 1228808 | tf_op jit(solution)/shard_map/ppermute | solution.py:28
  34.3 2.5 %collective-permute-start.1 = (bf16[320,640]{1,0:T(8,128)(2,1)S(1)}, bf16[320,640]{1,0:T(8,128)(2,1)S(1)}, u32[]{:S(2)}, u32[]{:S(2)}) collective-permute-start(bf16[320,640]{1,0:T(8,128)(2,1)S(1)} %reshape.68.refs_1_), channel_id=1, source_target_pairs={{0,12},{4,0},{8,4},{12,8},{1,13},{5,1},{9,5},{13,9},{2,14},{6,2},{... | collective-permute-start | bytes 1228808 | tf_op jit(solution)/shard_map/ppermute | solution.py:28
  36.8 7.8 %collective-permute-done.3.refs_12_ = bf16[3,320,384]{2,1,0:T(8,128)(2,1)} collective-permute-done((bf16[3,320,384]{2,1,0:T(8,128)(2,1)S(1)}, bf16[3,320,384]{2,1,0:T(8,128)(2,1)}, u32[]{:S(2)}, u32[]{:S(2)}) %collective-permute-start.3) | collective-permute-done | bytes 737312 | tf_op jit(solution)/shard_map/ppermute | solution.py:28
  45.8 3.6 %collective-permute-done.2.refs_3_ = bf16[320,640]{1,0:T(8,128)(2,1)S(1)} collective-permute-done((bf16[320,640]{1,0:T(8,128)(2,1)S(1)}, bf16[320,640]{1,0:T(8,128)(2,1)S(1)}, u32[]{:S(2)}, u32[]{:S(2)}) %collective-permute-start.2) | collective-permute-done | bytes 409632 | tf_op jit(solution)/shard_map/ppermute | solution.py:28
  49.4 2.7 %collective-permute-start.10 = (bf16[3,320,384]{2,1,0:T(8,128)(2,1)}, bf16[3,320,384]{2,1,0:T(8,128)(2,1)}, u32[]{:S(2)}, u32[]{:S(2)}) collective-permute-start(bf16[3,320,384]{2,1,0:T(8,128)(2,1)} %collective-permute-done.4.refs_13_), channel_id=1, source_target_pairs={{0,224},{32,0},{64,32},{96,64},{128,96},{160,128},{192,160},{224,1... | collective-permute-start | bytes 2211848 | tf_op jit(solution)/shard_map/ppermute | solution.py:28
  52.2 2.7 %collective-permute-start.5 = (bf16[320,640]{1,0:T(8,128)(2,1)S(1)}, bf16[320,640]{1,0:T(8,128)(2,1)S(1)}, u32[]{:S(2)}, u32[]{:S(2)}) collective-permute-start(bf16[320,640]{1,0:T(8,128)(2,1)S(1)} %collective-permute-done.refs_6_), channel_id=1, source_target_pairs={{0,12},{4,0},{8,4},{12,8},{1,13},{5,1},{9,5},{13,9},{2,14},{6,2},{... | collective-permute-start | bytes 1228808 | tf_op jit(solution)/shard_map/ppermute | solution.py:28
  54.9 4.2 %collective-permute-done.7.refs_4_ = bf16[160,640]{1,0:T(8,128)(2,1)S(1)} collective-permute-done((bf16[160,640]{1,0:T(8,128)(2,1)S(1)}, bf16[160,640]{1,0:T(8,128)(2,1)S(1)}, u32[]{:S(2)}, u32[]{:S(2)}) %collective-permute-start.7) | collective-permute-done | bytes 204832 | tf_op jit(solution)/shard_map/ppermute | solution.py:28
  59.1 7.6 %collective-permute-done.8.refs_5_ = bf16[160,640]{1,0:T(8,128)(2,1)S(1)} collective-permute-done((bf16[160,640]{1,0:T(8,128)(2,1)S(1)}, bf16[160,640]{1,0:T(8,128)(2,1)S(1)}, u32[]{:S(2)}, u32[]{:S(2)}) %collective-permute-start.8) | collective-permute-done | bytes 204832 | tf_op jit(solution)/shard_map/ppermute | solution.py:28
  68.8 2.7 %collective-permute-start.14 = (bf16[160,640]{1,0:T(8,128)(2,1)S(1)}, bf16[160,640]{1,0:T(8,128)(2,1)}, u32[]{:S(2)}, u32[]{:S(2)}) collective-permute-start(bf16[160,640]{1,0:T(8,128)(2,1)S(1)} %slice.39), channel_id=1, source_target_pairs={{0,12},{4,0},{8,4},{12,8},{1,13},{5,1},{9,5},{13,9},{2,14},{6,2},{... | collective-permute-start | bytes 614408 | tf_op jit(solution)/shard_map/ppermute | solution.py:28
  71.5 2.7 %collective-permute-start.12 = (bf16[3,320,384]{2,1,0:T(8,128)(2,1)}, bf16[3,320,384]{2,1,0:T(8,128)(2,1)}, u32[]{:S(2)}, u32[]{:S(2)}) collective-permute-start(bf16[3,320,384]{2,1,0:T(8,128)(2,1)} %collective-permute-done.10.refs_15_), channel_id=1, source_target_pairs={{0,224},{32,0},{64,32},{96,64},{128,96},{160,128},{192,160},{224,1... | collective-permute-start | bytes 2211848 | tf_op jit(solution)/shard_map/ppermute | solution.py:28
  74.2 2.1 %copy-done.2 = bf16[384,5120]{1,0:T(8,128)(2,1)S(1)} copy-done((bf16[384,5120]{1,0:T(8,128)(2,1)S(1)}, bf16[384,5120]{1,0:T(8,128)(2,1)}, u32[]{:S(2)}) %copy-start.2) | copy-done | bytes 3932184
  78.7 3.6 %all-to-all-start.1 = ((bf16[8,192,640]{2,1,0:T(8,128)(2,1)}), bf16[8,192,640]{2,1,0:T(8,128)(2,1)S(1)}, u32[]{:S(2)}, u32[]{:S(2)}) async-start(bf16[8,192,640]{2,1,0:T(8,128)(2,1)} %copy-done.1), calls=%async_computation.1 | async-start | bytes 3932160 | tf_op jit(solution)/shard_map/all_to_all | solution.py:23
  82.3 6.6 %collective-permute-done.11.refs_16_ = bf16[3,320,384]{2,1,0:T(8,128)(2,1)S(1)} collective-permute-done((bf16[3,320,384]{2,1,0:T(8,128)(2,1)}, bf16[3,320,384]{2,1,0:T(8,128)(2,1)S(1)}, u32[]{:S(2)}, u32[]{:S(2)}) %collective-permute-start.11) | collective-permute-done | bytes 737312 | tf_op jit(solution)/shard_map/ppermute | solution.py:28
  90.5 1.8 %slice.41 = bf16[3,160,384]{2,1,0:T(8,128)(2,1)} slice(bf16[3,320,384]{2,1,0:T(8,128)(2,1)} %collective-permute-done.12.refs_17_), slice={[0:3], [160:320], [0:384]} | slice | bytes 737280 | tf_op jit(solution)/shard_map/slice | solution.py:319
  92.3 2.7 %collective-permute-start.16 = (bf16[3,160,384]{2,1,0:T(8,128)(2,1)}, bf16[3,160,384]{2,1,0:T(8,128)(2,1)S(1)}, u32[]{:S(2)}, u32[]{:S(2)}) collective-permute-start(bf16[3,160,384]{2,1,0:T(8,128)(2,1)} %slice.41), channel_id=1, source_target_pairs={{0,224},{32,0},{64,32},{96,64},{128,96},{160,128},{192,160},{224,1... | collective-permute-start | bytes 1105928 | tf_op jit(solution)/shard_map/ppermute | solution.py:28
  95.6 10.5 %shard_map.114 = (f32[640,1152]{1,0:T(8,128)}, bf16[320,640]{1,0:T(8,128)(2,1)}) custom-call(s32[8]{0:T(128)} %xor_add_fusion.refs_0_, bf16[320,640]{1,0:T(8,128)(2,1)} %copy-done.7, bf16[320,640]{1,0:T(8,128)(2,1)} %copy-done.8, bf16[320,640]{1,0:T(8,128)(2,1)} %copy-done.9, bf16[160,640]{1,0:T(8,128)(2,1)} %copy-done.14, bf16[160,640]{1,0:T(8,128)(2,1)} %copy-done.15, ...), custom_call_target="tpu_custom_call" | custom-call | tf_op jit(solution)/shard_map/pallas_call | solution.py:105
  106.2 1.8 %copy-done.3 = f32[640,1152]{1,0:T(8,128)S(1)} copy-done((f32[640,1152]{1,0:T(8,128)S(1)}, f32[640,1152]{1,0:T(8,128)}, u32[]{:S(2)}) %copy-start.3) | copy-done | bytes 2949144
  110.0 3.6 %collective-permute-start.17 = (bf16[320,1152]{1,0:T(8,128)(2,1)S(1)}, bf16[320,1152]{1,0:T(8,128)(2,1)S(1)}, u32[]{:S(2)}, u32[]{:S(2)}) collective-permute-start(bf16[320,1152]{1,0:T(8,128)(2,1)S(1)} %get-tuple-element.53), channel_id=1, source_target_pairs={{0,16},{16,0},{1,17},{17,1},{2,18},{18,2},{3,19},{19,3},{4,20},{20... | collective-permute-start | bytes 2211848 | tf_op jit(solution)/shard_map/ppermute | solution.py:28
  113.8 1.7 collective-permute-done.17.other_ref
  115.5 1.4 shard_map.116
  117.4 15.0 %all_to_all.20 = bf16[16,20,384]{2,1,0:T(8,128)(2,1)S(1)} all-to-all(bf16[16,20,384]{2,1,0:T(8,128)(2,1)S(1)} %shard_map.116), channel_id=1, replica_groups=mesh['z'=8,'core'=2,'x'=4,'yhi'=2,'dp'=2] {'z','core'}, dimensions={0} | all-to-all | bytes 491520 | tf_op jit(solution)/shard_map/all_to_all | solution.py:23
  134.2 7.5 %collective-permute-done.18.m1 = bf16[320,384]{1,0:T(8,128)(2,1)S(1)} collective-permute-done((bf16[320,384]{1,0:T(8,128)(2,1)S(1)}, bf16[320,384]{1,0:T(8,128)(2,1)S(1)}, u32[]{:S(2)}, u32[]{:S(2)}) %collective-permute-start.18) | collective-permute-done | bytes 245792 | tf_op jit(solution)/shard_map/ppermute | solution.py:28
  142.7 2.7 %collective-permute-start.25 = (bf16[320,384]{1,0:T(8,128)(2,1)S(1)}, bf16[320,384]{1,0:T(8,128)(2,1)S(1)}, u32[]{:S(2)}, u32[]{:S(2)}) collective-permute-start(bf16[320,384]{1,0:T(8,128)(2,1)S(1)} %collective-permute-done.18.m1), channel_id=1, source_target_pairs={{0,12},{4,0},{8,4},{12,8},{1,13},{5,1},{9,5},{13,9},{2,14},{6,2},{... | collective-permute-start | bytes 737288 | tf_op jit(solution)/shard_map/ppermute | solution.py:28
  145.7 2.7 %collective-permute-start.22 = (bf16[160,384]{1,0:T(8,128)(2,1)S(1)}, bf16[160,384]{1,0:T(8,128)(2,1)S(1)}, u32[]{:S(2)}, u32[]{:S(2)}) collective-permute-start(bf16[160,384]{1,0:T(8,128)(2,1)S(1)} %slice.43), channel_id=1, source_target_pairs={{0,12},{4,0},{8,4},{12,8},{1,13},{5,1},{9,5},{13,9},{2,14},{6,2},{... | collective-permute-start | bytes 368648 | tf_op jit(solution)/shard_map/ppermute | solution.py:28
  148.5 2.1 %collective-permute-done.23.l1 = bf16[320,384]{1,0:T(8,128)(2,1)S(1)} collective-permute-done((bf16[320,384]{1,0:T(8,128)(2,1)S(1)}, bf16[320,384]{1,0:T(8,128)(2,1)S(1)}, u32[]{:S(2)}, u32[]{:S(2)}) %collective-permute-start.23) | collective-permute-done | bytes 245792 | tf_op jit(solution)/shard_map/ppermute | solution.py:28
  150.7 2.7 %collective-permute-start.26 = (bf16[160,384]{1,0:T(8,128)(2,1)S(1)}, bf16[160,384]{1,0:T(8,128)(2,1)S(1)}, u32[]{:S(2)}, u32[]{:S(2)}) collective-permute-start(bf16[160,384]{1,0:T(8,128)(2,1)S(1)} %slice.49), channel_id=1, source_target_pairs={{0,12},{4,0},{8,4},{12,8},{1,13},{5,1},{9,5},{13,9},{2,14},{6,2},{... | collective-permute-start | bytes 368648 | tf_op jit(solution)/shard_map/ppermute | solution.py:28
  153.7 2.9 %shard_map.117.acc = f32[320,640]{1,0:T(8,128)S(1)} custom-call(s32[3]{0:T(128)S(1)} %pad_add_fusion.where, bf16[320,384]{1,0:T(8,128)(2,1)S(1)} %reshape.69.m0, bf16[320,384]{1,0:T(8,128)(2,1)S(1)} %collective-permute-done.18.m1, bf16[320,384]{1,0:T(8,128)(2,1)S(1)} %collective-permute-done.19.r0, bf16[320,384]{1,0:T(8,128)(2,1)S(1)} %collective-permute-done.25.r1, ...), custom_call_target="tpu_custom_call" | custom-call | tf_op jit(solution)/shard_map/pallas_call | solution.py:231
  156.7 2.9 %shard_map.118 = (bf16[320,640]{1,0:T(8,128)(2,1)}, f32[32,2,672]{2,1,0:T(2,128)S(1)}) custom-call(s32[3]{0:T(128)S(1)} %pad_add_fusion.where, bf16[160,384]{1,0:T(8,128)(2,1)S(1)} %collective-permute-done.21.t0, bf16[160,384]{1,0:T(8,128)(2,1)S(1)} %collective-permute-done.22.w0, bf16[160,384]{1,0:T(8,128)(2,1)S(1)} %collective-permute-done.24.t1, ...), custom_call_target="tpu_custom_call" | custom-call | tf_op jit(solution)/shard_map/pallas_call | solution.py:244
  159.6 16.5 %all_to_all.21 = f32[32,2,672]{2,1,0:T(2,128)S(1)} all-to-all(f32[32,2,672]{2,1,0:T(2,128)S(1)} %get-tuple-element.61), channel_id=1, replica_groups=mesh['z'=8,'core'=2,'x'=4,'yhi'=2,'dp'=2] {'z','core','dp'}, dimensions={0} | all-to-all | bytes 344064 | tf_op jit(solution)/shard_map/all_to_all | solution.py:23
  (103 shorter events, 20.5 us)
Async XLA Ops:
  0.6 152.8 %copy-start = (f32[32,640]{1,0:T(8,128)S(1)}, f32[32,640]{1,0:T(8,128)}, u32[]{:S(2)}) copy-start(f32[32,640]{1,0:T(8,128)} %param.17) | copy-start | bytes 245764
  4.6 26.6 %all-to-all-start = ((bf16[16,20,640]{2,1,0:T(8,128)(2,1)}), bf16[16,20,640]{2,1,0:T(8,128)(2,1)S(1)}, u32[]{:S(2)}, u32[]{:S(2)}) async-start(bf16[16,20,640]{2,1,0:T(8,128)(2,1)} %copy.18), calls=%async_computation | async-start | bytes 983040 | tf_op jit(solution)/shard_map/all_to_all | solution.py:23
  14.6 30.0 %collective-permute-start.3 = (bf16[3,320,384]{2,1,0:T(8,128)(2,1)S(1)}, bf16[3,320,384]{2,1,0:T(8,128)(2,1)}, u32[]{:S(2)}, u32[]{:S(2)}) collective-permute-start(bf16[3,320,384]{2,1,0:T(8,128)(2,1)S(1)} %bitcast.27), channel_id=1, source_target_pairs={{0,32},{32,64},{64,96},{96,128},{128,160},{160,192},{192,224},{224... | collective-permute-start | bytes 2211848 | tf_op jit(solution)/shard_map/ppermute | solution.py:28
  16.1 28.5 %collective-permute-start.4 = (bf16[3,320,384]{2,1,0:T(8,128)(2,1)S(1)}, bf16[3,320,384]{2,1,0:T(8,128)(2,1)}, u32[]{:S(2)}, u32[]{:S(2)}) collective-permute-start(bf16[3,320,384]{2,1,0:T(8,128)(2,1)S(1)} %bitcast.28), channel_id=1, source_target_pairs={{0,224},{32,0},{64,32},{96,64},{128,96},{160,128},{192,160},{224,1... | collective-permute-start | bytes 2211848 | tf_op jit(solution)/shard_map/ppermute | solution.py:28
  31.3 45.3 %copy-start.7 = (bf16[320,640]{1,0:T(8,128)(2,1)}, bf16[320,640]{1,0:T(8,128)(2,1)S(1)}, u32[]{:S(2)}) copy-start(bf16[320,640]{1,0:T(8,128)(2,1)S(1)} %reshape.68.refs_1_) | copy-start | bytes 1228804
  31.3 13.3 %collective-permute-start = (bf16[320,640]{1,0:T(8,128)(2,1)S(1)}, bf16[320,640]{1,0:T(8,128)(2,1)S(1)}, u32[]{:S(2)}, u32[]{:S(2)}) collective-permute-start(bf16[320,640]{1,0:T(8,128)(2,1)S(1)} %reshape.68.refs_1_), channel_id=1, source_target_pairs={{0,2},{2,0},{1,3},{3,1},{4,6},{6,4},{5,7},{7,5},{8,10},{10,8},{9,1... | collective-permute-start | bytes 1228808 | tf_op jit(solution)/shard_map/ppermute | solution.py:28
  34.3 11.4 %collective-permute-start.1 = (bf16[320,640]{1,0:T(8,128)(2,1)S(1)}, bf16[320,640]{1,0:T(8,128)(2,1)S(1)}, u32[]{:S(2)}, u32[]{:S(2)}) collective-permute-start(bf16[320,640]{1,0:T(8,128)(2,1)S(1)} %reshape.68.refs_1_), channel_id=1, source_target_pairs={{0,12},{4,0},{8,4},{12,8},{1,13},{5,1},{9,5},{13,9},{2,14},{6,2},{... | collective-permute-start | bytes 1228808 | tf_op jit(solution)/shard_map/ppermute | solution.py:28
  36.8 12.6 %collective-permute-start.2 = (bf16[320,640]{1,0:T(8,128)(2,1)S(1)}, bf16[320,640]{1,0:T(8,128)(2,1)S(1)}, u32[]{:S(2)}, u32[]{:S(2)}) collective-permute-start(bf16[320,640]{1,0:T(8,128)(2,1)S(1)} %reshape.68.refs_1_), channel_id=1, source_target_pairs={{0,4},{4,8},{8,12},{12,0},{1,5},{5,9},{9,13},{13,1},{2,6},{6,10},{... | collective-permute-start | bytes 1228808 | tf_op jit(solution)/shard_map/ppermute | solution.py:28
  49.4 19.2 %collective-permute-start.9 = (bf16[3,320,384]{2,1,0:T(8,128)(2,1)}, bf16[3,320,384]{2,1,0:T(8,128)(2,1)}, u32[]{:S(2)}, u32[]{:S(2)}) collective-permute-start(bf16[3,320,384]{2,1,0:T(8,128)(2,1)} %collective-permute-done.3.refs_12_), channel_id=1, source_target_pairs={{0,32},{32,64},{64,96},{96,128},{128,160},{160,192},{192,224},{224... | collective-permute-start | bytes 2211848 | tf_op jit(solution)/shard_map/ppermute | solution.py:28
  49.4 19.2 %collective-permute-start.10 = (bf16[3,320,384]{2,1,0:T(8,128)(2,1)}, bf16[3,320,384]{2,1,0:T(8,128)(2,1)}, u32[]{:S(2)}, u32[]{:S(2)}) collective-permute-start(bf16[3,320,384]{2,1,0:T(8,128)(2,1)} %collective-permute-done.4.refs_13_), channel_id=1, source_target_pairs={{0,224},{32,0},{64,32},{96,64},{128,96},{160,128},{192,160},{224,1... | collective-permute-start | bytes 2211848 | tf_op jit(solution)/shard_map/ppermute | solution.py:28
  52.1 7.0 %collective-permute-start.7 = (bf16[160,640]{1,0:T(8,128)(2,1)S(1)}, bf16[160,640]{1,0:T(8,128)(2,1)S(1)}, u32[]{:S(2)}, u32[]{:S(2)}) collective-permute-start(bf16[160,640]{1,0:T(8,128)(2,1)S(1)} %slice.36), channel_id=1, source_target_pairs={{0,4},{4,8},{8,12},{12,0},{1,5},{5,9},{9,13},{13,1},{2,6},{6,10},{... | collective-permute-start | bytes 614408 | tf_op jit(solution)/shard_map/ppermute | solution.py:28
  52.2 14.6 %collective-permute-start.5 = (bf16[320,640]{1,0:T(8,128)(2,1)S(1)}, bf16[320,640]{1,0:T(8,128)(2,1)S(1)}, u32[]{:S(2)}, u32[]{:S(2)}) collective-permute-start(bf16[320,640]{1,0:T(8,128)(2,1)S(1)} %collective-permute-done.refs_6_), channel_id=1, source_target_pairs={{0,12},{4,0},{8,4},{12,8},{1,13},{5,1},{9,5},{13,9},{2,14},{6,2},{... | collective-permute-start | bytes 1228808 | tf_op jit(solution)/shard_map/ppermute | solution.py:28
  54.9 13.0 %collective-permute-start.6 = (bf16[320,640]{1,0:T(8,128)(2,1)S(1)}, bf16[320,640]{1,0:T(8,128)(2,1)S(1)}, u32[]{:S(2)}, u32[]{:S(2)}) collective-permute-start(bf16[320,640]{1,0:T(8,128)(2,1)S(1)} %collective-permute-done.refs_6_), channel_id=1, source_target_pairs={{0,4},{4,8},{8,12},{12,0},{1,5},{5,9},{9,13},{13,1},{2,6},{6,10},{... | collective-permute-start | bytes 1228808 | tf_op jit(solution)/shard_map/ppermute | solution.py:28
  59.1 7.6 %collective-permute-start.8 = (bf16[160,640]{1,0:T(8,128)(2,1)S(1)}, bf16[160,640]{1,0:T(8,128)(2,1)S(1)}, u32[]{:S(2)}, u32[]{:S(2)}) collective-permute-start(bf16[160,640]{1,0:T(8,128)(2,1)S(1)} %slice.37), channel_id=1, source_target_pairs={{0,12},{4,0},{8,4},{12,8},{1,13},{5,1},{9,5},{13,9},{2,14},{6,2},{... | collective-permute-start | bytes 614408 | tf_op jit(solution)/shard_map/ppermute | solution.py:28
  68.6 9.4 %collective-permute-start.13 = (bf16[160,640]{1,0:T(8,128)(2,1)S(1)}, bf16[160,640]{1,0:T(8,128)(2,1)S(1)}, u32[]{:S(2)}, u32[]{:S(2)}) collective-permute-start(bf16[160,640]{1,0:T(8,128)(2,1)S(1)} %slice.38), channel_id=1, source_target_pairs={{0,4},{4,8},{8,12},{12,0},{1,5},{5,9},{9,13},{13,1},{2,6},{6,10},{... | collective-permute-start | bytes 614408 | tf_op jit(solution)/shard_map/ppermute | solution.py:28
  68.8 9.3 %collective-permute-start.14 = (bf16[160,640]{1,0:T(8,128)(2,1)S(1)}, bf16[160,640]{1,0:T(8,128)(2,1)}, u32[]{:S(2)}, u32[]{:S(2)}) collective-permute-start(bf16[160,640]{1,0:T(8,128)(2,1)S(1)} %slice.39), channel_id=1, source_target_pairs={{0,12},{4,0},{8,4},{12,8},{1,13},{5,1},{9,5},{13,9},{2,14},{6,2},{... | collective-permute-start | bytes 614408 | tf_op jit(solution)/shard_map/ppermute | solution.py:28
  71.5 17.4 %collective-permute-start.11 = (bf16[3,320,384]{2,1,0:T(8,128)(2,1)}, bf16[3,320,384]{2,1,0:T(8,128)(2,1)S(1)}, u32[]{:S(2)}, u32[]{:S(2)}) collective-permute-start(bf16[3,320,384]{2,1,0:T(8,128)(2,1)} %collective-permute-done.9.refs_14_), channel_id=1, source_target_pairs={{0,32},{32,64},{64,96},{96,128},{128,160},{160,192},{192,224},{224... | collective-permute-start | bytes 2211848 | tf_op jit(solution)/shard_map/ppermute | solution.py:28
  71.5 17.4 %collective-permute-start.12 = (bf16[3,320,384]{2,1,0:T(8,128)(2,1)}, bf16[3,320,384]{2,1,0:T(8,128)(2,1)}, u32[]{:S(2)}, u32[]{:S(2)}) collective-permute-start(bf16[3,320,384]{2,1,0:T(8,128)(2,1)} %collective-permute-done.10.refs_15_), channel_id=1, source_target_pairs={{0,224},{32,0},{64,32},{96,64},{128,96},{160,128},{192,160},{224,1... | collective-permute-start | bytes 2211848 | tf_op jit(solution)/shard_map/ppermute | solution.py:28
  78.7 38.2 %all-to-all-start.1 = ((bf16[8,192,640]{2,1,0:T(8,128)(2,1)}), bf16[8,192,640]{2,1,0:T(8,128)(2,1)S(1)}, u32[]{:S(2)}, u32[]{:S(2)}) async-start(bf16[8,192,640]{2,1,0:T(8,128)(2,1)} %copy-done.1), calls=%async_computation.1 | async-start | bytes 3932160 | tf_op jit(solution)/shard_map/all_to_all | solution.py:23
  90.5 15.6 %collective-permute-start.15 = (bf16[3,160,384]{2,1,0:T(8,128)(2,1)}, bf16[3,160,384]{2,1,0:T(8,128)(2,1)S(1)}, u32[]{:S(2)}, u32[]{:S(2)}) collective-permute-start(bf16[3,160,384]{2,1,0:T(8,128)(2,1)} %slice.40), channel_id=1, source_target_pairs={{0,32},{32,64},{64,96},{96,128},{128,160},{160,192},{192,224},{224... | collective-permute-start | bytes 1105928 | tf_op jit(solution)/shard_map/ppermute | solution.py:28
  92.3 13.8 %collective-permute-start.16 = (bf16[3,160,384]{2,1,0:T(8,128)(2,1)}, bf16[3,160,384]{2,1,0:T(8,128)(2,1)S(1)}, u32[]{:S(2)}, u32[]{:S(2)}) collective-permute-start(bf16[3,160,384]{2,1,0:T(8,128)(2,1)} %slice.41), channel_id=1, source_target_pairs={{0,224},{32,0},{64,32},{96,64},{128,96},{160,128},{192,160},{224,1... | collective-permute-start | bytes 1105928 | tf_op jit(solution)/shard_map/ppermute | solution.py:28
  110.0 5.5 %collective-permute-start.17 = (bf16[320,1152]{1,0:T(8,128)(2,1)S(1)}, bf16[320,1152]{1,0:T(8,128)(2,1)S(1)}, u32[]{:S(2)}, u32[]{:S(2)}) collective-permute-start(bf16[320,1152]{1,0:T(8,128)(2,1)S(1)} %get-tuple-element.53), channel_id=1, source_target_pairs={{0,16},{16,0},{1,17},{17,1},{2,18},{18,2},{3,19},{19,3},{4,20},{20... | collective-permute-start | bytes 2211848 | tf_op jit(solution)/shard_map/ppermute | solution.py:28
  116.9 36.8 %collective-permute-start.27 = (bf16[8,192,640]{2,1,0:T(8,128)(2,1)S(1)}, bf16[8,192,640]{2,1,0:T(8,128)(2,1)}, u32[]{:S(2)}, u32[]{:S(2)}) collective-permute-start(bf16[8,192,640]{2,1,0:T(8,128)(2,1)S(1)} %all-to-all-done.1.half), channel_id=1, source_target_pairs={{0,16},{16,0},{1,17},{17,1},{2,18},{18,2},{3,19},{19,3},{4,20},{20... | collective-permute-start | bytes 5898248 | tf_op jit(solution)/shard_map/ppermute | solution.py:28
  132.4 9.3 %collective-permute-start.18 = (bf16[320,384]{1,0:T(8,128)(2,1)S(1)}, bf16[320,384]{1,0:T(8,128)(2,1)S(1)}, u32[]{:S(2)}, u32[]{:S(2)}) collective-permute-start(bf16[320,384]{1,0:T(8,128)(2,1)S(1)} %reshape.69.m0), channel_id=1, source_target_pairs={{0,2},{2,0},{1,3},{3,1},{4,6},{6,4},{5,7},{7,5},{8,10},{10,8},{9,1... | collective-permute-start | bytes 737288 | tf_op jit(solution)/shard_map/ppermute | solution.py:28
  132.8 8.9 %collective-permute-start.19 = (bf16[320,384]{1,0:T(8,128)(2,1)S(1)}, bf16[320,384]{1,0:T(8,128)(2,1)S(1)}, u32[]{:S(2)}, u32[]{:S(2)}) collective-permute-start(bf16[320,384]{1,0:T(8,128)(2,1)S(1)} %reshape.69.m0), channel_id=1, source_target_pairs={{0,12},{4,0},{8,4},{12,8},{1,13},{5,1},{9,5},{13,9},{2,14},{6,2},{... | collective-permute-start | bytes 737288 | tf_op jit(solution)/shard_map/ppermute | solution.py:28
  134.0 8.7 %collective-permute-start.20 = (bf16[320,384]{1,0:T(8,128)(2,1)S(1)}, bf16[320,384]{1,0:T(8,128)(2,1)S(1)}, u32[]{:S(2)}, u32[]{:S(2)}) collective-permute-start(bf16[320,384]{1,0:T(8,128)(2,1)S(1)} %reshape.69.m0), channel_id=1, source_target_pairs={{0,4},{4,8},{8,12},{12,0},{1,5},{5,9},{9,13},{13,1},{2,6},{6,10},{... | collective-permute-start | bytes 737288 | tf_op jit(solution)/shard_map/ppermute | solution.py:28
  142.7 7.8 %collective-permute-start.23 = (bf16[320,384]{1,0:T(8,128)(2,1)S(1)}, bf16[320,384]{1,0:T(8,128)(2,1)S(1)}, u32[]{:S(2)}, u32[]{:S(2)}) collective-permute-start(bf16[320,384]{1,0:T(8,128)(2,1)S(1)} %collective-permute-done.18.m1), channel_id=1, source_target_pairs={{0,4},{4,8},{8,12},{12,0},{1,5},{5,9},{9,13},{13,1},{2,6},{6,10},{... | collective-permute-start | bytes 737288 | tf_op jit(solution)/shard_map/ppermute | solution.py:28
  142.7 7.9 %collective-permute-start.25 = (bf16[320,384]{1,0:T(8,128)(2,1)S(1)}, bf16[320,384]{1,0:T(8,128)(2,1)S(1)}, u32[]{:S(2)}, u32[]{:S(2)}) collective-permute-start(bf16[320,384]{1,0:T(8,128)(2,1)S(1)} %collective-permute-done.18.m1), channel_id=1, source_target_pairs={{0,12},{4,0},{8,4},{12,8},{1,13},{5,1},{9,5},{13,9},{2,14},{6,2},{... | collective-permute-start | bytes 737288 | tf_op jit(solution)/shard_map/ppermute | solution.py:28
  145.6 11.0 %collective-permute-start.21 = (bf16[160,384]{1,0:T(8,128)(2,1)S(1)}, bf16[160,384]{1,0:T(8,128)(2,1)S(1)}, u32[]{:S(2)}, u32[]{:S(2)}) collective-permute-start(bf16[160,384]{1,0:T(8,128)(2,1)S(1)} %slice.42), channel_id=1, source_target_pairs={{0,4},{4,8},{8,12},{12,0},{1,5},{5,9},{9,13},{13,1},{2,6},{6,10},{... | collective-permute-start | bytes 368648 | tf_op jit(solution)/shard_map/ppermute | solution.py:28
  145.7 10.9 %collective-permute-start.22 = (bf16[160,384]{1,0:T(8,128)(2,1)S(1)}, bf16[160,384]{1,0:T(8,128)(2,1)S(1)}, u32[]{:S(2)}, u32[]{:S(2)}) collective-permute-start(bf16[160,384]{1,0:T(8,128)(2,1)S(1)} %slice.43), channel_id=1, source_target_pairs={{0,12},{4,0},{8,4},{12,8},{1,13},{5,1},{9,5},{13,9},{2,14},{6,2},{... | collective-permute-start | bytes 368648 | tf_op jit(solution)/shard_map/ppermute | solution.py:28
  150.6 6.1 %collective-permute-start.24 = (bf16[160,384]{1,0:T(8,128)(2,1)S(1)}, bf16[160,384]{1,0:T(8,128)(2,1)S(1)}, u32[]{:S(2)}, u32[]{:S(2)}) collective-permute-start(bf16[160,384]{1,0:T(8,128)(2,1)S(1)} %slice.48), channel_id=1, source_target_pairs={{0,4},{4,8},{8,12},{12,0},{1,5},{5,9},{9,13},{13,1},{2,6},{6,10},{... | collective-permute-start | bytes 368648 | tf_op jit(solution)/shard_map/ppermute | solution.py:28
  150.7 6.0 %collective-permute-start.26 = (bf16[160,384]{1,0:T(8,128)(2,1)S(1)}, bf16[160,384]{1,0:T(8,128)(2,1)S(1)}, u32[]{:S(2)}, u32[]{:S(2)}) collective-permute-start(bf16[160,384]{1,0:T(8,128)(2,1)S(1)} %slice.49), channel_id=1, source_target_pairs={{0,12},{4,0},{8,4},{12,8},{1,13},{5,1},{9,5},{13,9},{2,14},{6,2},{... | collective-permute-start | bytes 368648 | tf_op jit(solution)/shard_map/ppermute | solution.py:28
  (18 other events, 225.0 us)

commit v12 on v11

--- a/solution.py
+++ b/solution.py
@@ -304,12 +304,10 @@
 
     other = shift(mine, "yhi", 1)
     side = sideways(mine)
-    other, side, up1, down1 = lax.optimization_barrier((other, side, up1, down1))
+    other, side = lax.optimization_barrier((other, side))
     up2, down2 = shift(up1, "z", 1), shift(down1, "z", -1)
     other_side, far = sideways(other), onward(*side)
-    other_side, far, up2, down2, w_out = lax.optimization_barrier(
-        (other_side, far, up2, down2, w_out)
-    )
+    other_side, far, w_out = lax.optimization_barrier((other_side, far, w_out))
     up3, down3 = shift(up2, "z", 1), shift(down2, "z", -1)
     other_far = onward(*other_side)
     blocks = column_blocks(w_out, core1, width)

time: 178 us -> 178 us (level)
  waiting for transfers between devices: 59 us -> 55.9 us
  starting transfers between devices: 49.6 us -> 52.2 us
    ppermute x28, waiting for transfers between devices: 45.2 us -> 42 us  [shift(): return lax.ppermute(x, axis, [(i, (i + by) % n) for i in range(n)])]
    ppermute x28, starting transfers between devices: 36.1 us -> 38.6 us  [shift(): return lax.ppermute(x, axis, [(i, (i + by) % n) for i in range(n)])]
  transfers between devices with their start and end apart: 30 -> 30, of which waited for: 13 -> 12; matrix products, arithmetic and copies ran while one was open for 2% -> 2% of each run, Pallas kernels for 9% -> 9%
where the time goes in v12:
time: 178 us; the launch traced here: 177 us
  waiting for transfers between devices  55.9 us (31%)
  starting transfers between devices  52.2 us (29%)
  blocking collectives  31.5 us (18%)
  Pallas kernels  19.1 us (11%)
  local copies, waits for them, and re-layouts  13.6 us (8%)
  other arithmetic  2.64 us (1%)
    ppermute x28, waiting for transfers between devices, shift(): return lax.ppermute(x, axis, [(i, (i + by) % n) for i in range(n)])  42 us
    ppermute x28, starting transfers between devices, shift(): return lax.ppermute(x, axis, [(i, (i + by) % n) for i in range(n)])  38.6 us
    all_to_all x2, blocking collectives, exchange(): return lax.all_to_all(x, axis, split_axis=0, concat_axis=0, tiled=True)  31.5 us
    all_to_all x2, waiting for transfers between devices, exchange(): return lax.all_to_all(x, axis, split_axis=0, concat_axis=0, tiled=True)  13.9 us
    all_to_all x2, starting transfers between devices, exchange(): return lax.all_to_all(x, axis, split_axis=0, concat_axis=0, tiled=True)  13.6 us
    pallas_call x1, Pallas kernels, project(): pl.pallas_call(kernel, in_specs=[SMEM] + [ANYWHERE] * len(operands), out_...  10.5 us
    unnamed x41, local copies, waits for them, and re-layouts  8.55 us
  transfers between devices with their start and end apart: 30, of which 12 were waited for; matrix products, arithmetic and copies ran while one was open for 2% of the time, Pallas kernels for 9%

profile of v12, /device:TPU:1, one launch (start us, length us, event | category | flops | bytes accessed | tf_op | source)
XLA Modules:
  0.0 177.3 jit_solution(5826499807789367758)
XLA Ops:
  4.6 10.0 %all-to-all-start = ((bf16[16,20,640]{2,1,0:T(8,128)(2,1)}), bf16[16,20,640]{2,1,0:T(8,128)(2,1)S(1)}, u32[]{:S(2)}, u32[]{:S(2)}) async-start(bf16[16,20,640]{2,1,0:T(8,128)(2,1)} %copy.18), calls=%async_computation | async-start | bytes 983040 | tf_op jit(solution)/shard_map/all_to_all | solution.py:23
  17.4 13.8 %all-to-all-done = bf16[16,20,640]{2,1,0:T(8,128)(2,1)S(1)} async-done(((bf16[16,20,640]{2,1,0:T(8,128)(2,1)}), bf16[16,20,640]{2,1,0:T(8,128)(2,1)S(1)}, u32[]{:S(2)}, u32[]{:S(2)}) %all-to-all-start) | async-done | bytes 409632 | tf_op jit(solution)/shard_map/all_to_all | solution.py:23
  31.3 3.0 %collective-permute-start = (bf16[320,640]{1,0:T(8,128)(2,1)S(1)}, bf16[320,640]{1,0:T(8,128)(2,1)S(1)}, u32[]{:S(2)}, u32[]{:S(2)}) collective-permute-start(bf16[320,640]{1,0:T(8,128)(2,1)S(1)} %reshape.68.refs_1_), channel_id=1, source_target_pairs={{0,2},{2,0},{1,3},{3,1},{4,6},{6,4},{5,7},{7,5},{8,10},{10,8},{9,1... | collective-permute-start | bytes 1228808 | tf_op jit(solution)/shard_map/ppermute | solution.py:28
  34.3 2.5 %collective-permute-start.1 = (bf16[320,640]{1,0:T(8,128)(2,1)S(1)}, bf16[320,640]{1,0:T(8,128)(2,1)S(1)}, u32[]{:S(2)}, u32[]{:S(2)}) collective-permute-start(bf16[320,640]{1,0:T(8,128)(2,1)S(1)} %reshape.68.refs_1_), channel_id=1, source_target_pairs={{0,12},{4,0},{8,4},{12,8},{1,13},{5,1},{9,5},{13,9},{2,14},{6,2},{... | collective-permute-start | bytes 1228808 | tf_op jit(solution)/shard_map/ppermute | solution.py:28
  36.8 7.8 %collective-permute-done.7.refs_12_ = bf16[3,320,384]{2,1,0:T(8,128)(2,1)} collective-permute-done((bf16[3,320,384]{2,1,0:T(8,128)(2,1)S(1)}, bf16[3,320,384]{2,1,0:T(8,128)(2,1)}, u32[]{:S(2)}, u32[]{:S(2)}) %collective-permute-start.7) | collective-permute-done | bytes 737312 | tf_op jit(solution)/shard_map/ppermute | solution.py:28
  44.6 2.7 %collective-permute-start.11 = (bf16[3,320,384]{2,1,0:T(8,128)(2,1)}, bf16[3,320,384]{2,1,0:T(8,128)(2,1)}, u32[]{:S(2)}, u32[]{:S(2)}) collective-permute-start(bf16[3,320,384]{2,1,0:T(8,128)(2,1)} %collective-permute-done.10.refs_13_), channel_id=1, source_target_pairs={{0,224},{32,0},{64,32},{96,64},{128,96},{160,128},{192,160},{224,1... | collective-permute-start | bytes 2211848 | tf_op jit(solution)/shard_map/ppermute | solution.py:28
  47.3 2.1 %collective-permute-done.2.refs_3_ = bf16[320,640]{1,0:T(8,128)(2,1)S(1)} collective-permute-done((bf16[320,640]{1,0:T(8,128)(2,1)S(1)}, bf16[320,640]{1,0:T(8,128)(2,1)S(1)}, u32[]{:S(2)}, u32[]{:S(2)}) %collective-permute-start.2) | collective-permute-done | bytes 409632 | tf_op jit(solution)/shard_map/ppermute | solution.py:28
  49.5 2.7 %collective-permute-start.3 = (bf16[320,640]{1,0:T(8,128)(2,1)S(1)}, bf16[320,640]{1,0:T(8,128)(2,1)S(1)}, u32[]{:S(2)}, u32[]{:S(2)}) collective-permute-start(bf16[320,640]{1,0:T(8,128)(2,1)S(1)} %collective-permute-done.refs_6_), channel_id=1, source_target_pairs={{0,12},{4,0},{8,4},{12,8},{1,13},{5,1},{9,5},{13,9},{2,14},{6,2},{... | collective-permute-start | bytes 1228808 | tf_op jit(solution)/shard_map/ppermute | solution.py:28
  52.2 4.9 %collective-permute-done.5.refs_4_ = bf16[160,640]{1,0:T(8,128)(2,1)S(1)} collective-permute-done((bf16[160,640]{1,0:T(8,128)(2,1)S(1)}, bf16[160,640]{1,0:T(8,128)(2,1)S(1)}, u32[]{:S(2)}, u32[]{:S(2)}) %collective-permute-start.5) | collective-permute-done | bytes 204832 | tf_op jit(solution)/shard_map/ppermute | solution.py:28
  57.1 7.6 %collective-permute-done.6.refs_5_ = bf16[160,640]{1,0:T(8,128)(2,1)S(1)} collective-permute-done((bf16[160,640]{1,0:T(8,128)(2,1)S(1)}, bf16[160,640]{1,0:T(8,128)(2,1)S(1)}, u32[]{:S(2)}, u32[]{:S(2)}) %collective-permute-start.6) | collective-permute-done | bytes 204832 | tf_op jit(solution)/shard_map/ppermute | solution.py:28
  65.9 3.1 %collective-permute-start.14 = (bf16[160,640]{1,0:T(8,128)(2,1)S(1)}, bf16[160,640]{1,0:T(8,128)(2,1)}, u32[]{:S(2)}, u32[]{:S(2)}) collective-permute-start(bf16[160,640]{1,0:T(8,128)(2,1)S(1)} %slice.39), channel_id=1, source_target_pairs={{0,12},{4,0},{8,4},{12,8},{1,13},{5,1},{9,5},{13,9},{2,14},{6,2},{... | collective-permute-start | bytes 614408 | tf_op jit(solution)/shard_map/ppermute | solution.py:28
  69.3 2.6 %collective-permute-start.12 = (bf16[3,320,384]{2,1,0:T(8,128)(2,1)}, bf16[3,320,384]{2,1,0:T(8,128)(2,1)}, u32[]{:S(2)}, u32[]{:S(2)}) collective-permute-start(bf16[3,320,384]{2,1,0:T(8,128)(2,1)} %collective-permute-done.11.refs_15_), channel_id=1, source_target_pairs={{0,224},{32,0},{64,32},{96,64},{128,96},{160,128},{192,160},{224,1... | collective-permute-start | bytes 2211848 | tf_op jit(solution)/shard_map/ppermute | solution.py:28
  72.0 2.1 %copy-done.2 = bf16[384,5120]{1,0:T(8,128)(2,1)S(1)} copy-done((bf16[384,5120]{1,0:T(8,128)(2,1)S(1)}, bf16[384,5120]{1,0:T(8,128)(2,1)}, u32[]{:S(2)}) %copy-start.2) | copy-done | bytes 3932184
  76.5 3.6 %all-to-all-start.1 = ((bf16[8,192,640]{2,1,0:T(8,128)(2,1)}), bf16[8,192,640]{2,1,0:T(8,128)(2,1)S(1)}, u32[]{:S(2)}, u32[]{:S(2)}) async-start(bf16[8,192,640]{2,1,0:T(8,128)(2,1)} %copy-done.1), calls=%async_computation.1 | async-start | bytes 3932160 | tf_op jit(solution)/shard_map/all_to_all | solution.py:23
  80.1 6.8 %collective-permute-done.9.refs_16_ = bf16[3,320,384]{2,1,0:T(8,128)(2,1)S(1)} collective-permute-done((bf16[3,320,384]{2,1,0:T(8,128)(2,1)}, bf16[3,320,384]{2,1,0:T(8,128)(2,1)S(1)}, u32[]{:S(2)}, u32[]{:S(2)}) %collective-permute-start.9) | collective-permute-done | bytes 737312 | tf_op jit(solution)/shard_map/ppermute | solution.py:28
  88.5 1.8 %slice.41 = bf16[3,160,384]{2,1,0:T(8,128)(2,1)} slice(bf16[3,320,384]{2,1,0:T(8,128)(2,1)} %collective-permute-done.12.refs_17_), slice={[0:3], [160:320], [0:384]} | slice | bytes 737280 | tf_op jit(solution)/shard_map/slice | solution.py:317
  90.3 2.7 %collective-permute-start.16 = (bf16[3,160,384]{2,1,0:T(8,128)(2,1)}, bf16[3,160,384]{2,1,0:T(8,128)(2,1)S(1)}, u32[]{:S(2)}, u32[]{:S(2)}) collective-permute-start(bf16[3,160,384]{2,1,0:T(8,128)(2,1)} %slice.41), channel_id=1, source_target_pairs={{0,224},{32,0},{64,32},{96,64},{128,96},{160,128},{192,160},{224,1... | collective-permute-start | bytes 1105928 | tf_op jit(solution)/shard_map/ppermute | solution.py:28
  93.6 10.5 %shard_map.114 = (f32[640,1152]{1,0:T(8,128)}, bf16[320,640]{1,0:T(8,128)(2,1)}) custom-call(s32[8]{0:T(128)} %xor_add_fusion.refs_0_, bf16[320,640]{1,0:T(8,128)(2,1)} %copy-done.7, bf16[320,640]{1,0:T(8,128)(2,1)} %copy-done.8, bf16[320,640]{1,0:T(8,128)(2,1)} %copy-done.9, bf16[160,640]{1,0:T(8,128)(2,1)} %copy-done.14, bf16[160,640]{1,0:T(8,128)(2,1)} %copy-done.15, ...), custom_call_target="tpu_custom_call" | custom-call | tf_op jit(solution)/shard_map/pallas_call | solution.py:105
  104.2 1.8 %copy-done.3 = f32[640,1152]{1,0:T(8,128)S(1)} copy-done((f32[640,1152]{1,0:T(8,128)S(1)}, f32[640,1152]{1,0:T(8,128)}, u32[]{:S(2)}) %copy-start.3) | copy-done | bytes 2949144
  108.1 3.4 %collective-permute-start.17 = (bf16[320,1152]{1,0:T(8,128)(2,1)S(1)}, bf16[320,1152]{1,0:T(8,128)(2,1)S(1)}, u32[]{:S(2)}, u32[]{:S(2)}) collective-permute-start(bf16[320,1152]{1,0:T(8,128)(2,1)S(1)} %get-tuple-element.45), channel_id=1, source_target_pairs={{0,16},{16,0},{1,17},{17,1},{2,18},{18,2},{3,19},{19,3},{4,20},{20... | collective-permute-start | bytes 2211848 | tf_op jit(solution)/shard_map/ppermute | solution.py:28
  111.6 1.7 collective-permute-done.17.other_ref
  115.1 15.0 %all_to_all.20 = bf16[16,20,384]{2,1,0:T(8,128)(2,1)S(1)} all-to-all(bf16[16,20,384]{2,1,0:T(8,128)(2,1)S(1)} %shard_map.116), channel_id=1, replica_groups=mesh['z'=8,'core'=2,'x'=4,'yhi'=2,'dp'=2] {'z','core'}, dimensions={0} | all-to-all | bytes 491520 | tf_op jit(solution)/shard_map/all_to_all | solution.py:23
  130.2 2.5 %collective-permute-start.18 = (bf16[320,384]{1,0:T(8,128)(2,1)S(1)}, bf16[320,384]{1,0:T(8,128)(2,1)S(1)}, u32[]{:S(2)}, u32[]{:S(2)}) collective-permute-start(bf16[320,384]{1,0:T(8,128)(2,1)S(1)} %reshape.69.m0), channel_id=1, source_target_pairs={{0,2},{2,0},{1,3},{3,1},{4,6},{6,4},{5,7},{7,5},{8,10},{10,8},{9,1... | collective-permute-start | bytes 737288 | tf_op jit(solution)/shard_map/ppermute | solution.py:28
  134.1 5.3 %collective-permute-done.18.m1 = bf16[320,384]{1,0:T(8,128)(2,1)S(1)} collective-permute-done((bf16[320,384]{1,0:T(8,128)(2,1)S(1)}, bf16[320,384]{1,0:T(8,128)(2,1)S(1)}, u32[]{:S(2)}, u32[]{:S(2)}) %collective-permute-start.18) | collective-permute-done | bytes 245792 | tf_op jit(solution)/shard_map/ppermute | solution.py:28
  140.4 2.5 %collective-permute-done.20.l0 = bf16[320,384]{1,0:T(8,128)(2,1)S(1)} collective-permute-done((bf16[320,384]{1,0:T(8,128)(2,1)S(1)}, bf16[320,384]{1,0:T(8,128)(2,1)S(1)}, u32[]{:S(2)}, u32[]{:S(2)}) %collective-permute-start.20) | collective-permute-done | bytes 245792 | tf_op jit(solution)/shard_map/ppermute | solution.py:28
  142.8 2.7 %collective-permute-start.25 = (bf16[320,384]{1,0:T(8,128)(2,1)S(1)}, bf16[320,384]{1,0:T(8,128)(2,1)S(1)}, u32[]{:S(2)}, u32[]{:S(2)}) collective-permute-start(bf16[320,384]{1,0:T(8,128)(2,1)S(1)} %collective-permute-done.18.m1), channel_id=1, source_target_pairs={{0,12},{4,0},{8,4},{12,8},{1,13},{5,1},{9,5},{13,9},{2,14},{6,2},{... | collective-permute-start | bytes 737288 | tf_op jit(solution)/shard_map/ppermute | solution.py:28
  145.8 2.7 %collective-permute-start.22 = (bf16[160,384]{1,0:T(8,128)(2,1)S(1)}, bf16[160,384]{1,0:T(8,128)(2,1)S(1)}, u32[]{:S(2)}, u32[]{:S(2)}) collective-permute-start(bf16[160,384]{1,0:T(8,128)(2,1)S(1)} %slice.43), channel_id=1, source_target_pairs={{0,12},{4,0},{8,4},{12,8},{1,13},{5,1},{9,5},{13,9},{2,14},{6,2},{... | collective-permute-start | bytes 368648 | tf_op jit(solution)/shard_map/ppermute | solution.py:28
  148.6 2.1 %collective-permute-done.23.l1 = bf16[320,384]{1,0:T(8,128)(2,1)S(1)} collective-permute-done((bf16[320,384]{1,0:T(8,128)(2,1)S(1)}, bf16[320,384]{1,0:T(8,128)(2,1)S(1)}, u32[]{:S(2)}, u32[]{:S(2)}) %collective-permute-start.23) | collective-permute-done | bytes 245792 | tf_op jit(solution)/shard_map/ppermute | solution.py:28
  150.8 2.7 %collective-permute-start.26 = (bf16[160,384]{1,0:T(8,128)(2,1)S(1)}, bf16[160,384]{1,0:T(8,128)(2,1)S(1)}, u32[]{:S(2)}, u32[]{:S(2)}) collective-permute-start(bf16[160,384]{1,0:T(8,128)(2,1)S(1)} %slice.49), channel_id=1, source_target_pairs={{0,12},{4,0},{8,4},{12,8},{1,13},{5,1},{9,5},{13,9},{2,14},{6,2},{... | collective-permute-start | bytes 368648 | tf_op jit(solution)/shard_map/ppermute | solution.py:28
  153.8 2.9 %shard_map.117.acc = f32[320,640]{1,0:T(8,128)S(1)} custom-call(s32[3]{0:T(128)S(1)} %pad_add_fusion.where, bf16[320,384]{1,0:T(8,128)(2,1)S(1)} %reshape.69.m0, bf16[320,384]{1,0:T(8,128)(2,1)S(1)} %collective-permute-done.18.m1, bf16[320,384]{1,0:T(8,128)(2,1)S(1)} %collective-permute-done.19.r0, bf16[320,384]{1,0:T(8,128)(2,1)S(1)} %collective-permute-done.25.r1, ...), custom_call_target="tpu_custom_call" | custom-call | tf_op jit(solution)/shard_map/pallas_call | solution.py:231
  156.8 2.9 %shard_map.118 = (bf16[320,640]{1,0:T(8,128)(2,1)}, f32[32,2,672]{2,1,0:T(2,128)S(1)}) custom-call(s32[3]{0:T(128)S(1)} %pad_add_fusion.where, bf16[160,384]{1,0:T(8,128)(2,1)S(1)} %collective-permute-done.21.t0, bf16[160,384]{1,0:T(8,128)(2,1)S(1)} %collective-permute-done.22.w0, bf16[160,384]{1,0:T(8,128)(2,1)S(1)} %collective-permute-done.24.t1, ...), custom_call_target="tpu_custom_call" | custom-call | tf_op jit(solution)/shard_map/pallas_call | solution.py:244
  159.7 16.5 %all_to_all.21 = f32[32,2,672]{2,1,0:T(2,128)S(1)} all-to-all(f32[32,2,672]{2,1,0:T(2,128)S(1)} %get-tuple-element.53), channel_id=1, replica_groups=mesh['z'=8,'core'=2,'x'=4,'yhi'=2,'dp'=2] {'z','core','dp'}, dimensions={0} | all-to-all | bytes 344064 | tf_op jit(solution)/shard_map/all_to_all | solution.py:23
  (103 shorter events, 21.2 us)
Async XLA Ops:
  0.6 152.9 %copy-start = (f32[32,640]{1,0:T(8,128)S(1)}, f32[32,640]{1,0:T(8,128)}, u32[]{:S(2)}) copy-start(f32[32,640]{1,0:T(8,128)} %param.17) | copy-start | bytes 245764
  4.6 26.6 %all-to-all-start = ((bf16[16,20,640]{2,1,0:T(8,128)(2,1)}), bf16[16,20,640]{2,1,0:T(8,128)(2,1)S(1)}, u32[]{:S(2)}, u32[]{:S(2)}) async-start(bf16[16,20,640]{2,1,0:T(8,128)(2,1)} %copy.18), calls=%async_computation | async-start | bytes 983040 | tf_op jit(solution)/shard_map/all_to_all | solution.py:23
  14.6 30.0 %collective-permute-start.7 = (bf16[3,320,384]{2,1,0:T(8,128)(2,1)S(1)}, bf16[3,320,384]{2,1,0:T(8,128)(2,1)}, u32[]{:S(2)}, u32[]{:S(2)}) collective-permute-start(bf16[3,320,384]{2,1,0:T(8,128)(2,1)S(1)} %bitcast.27), channel_id=1, source_target_pairs={{0,32},{32,64},{64,96},{96,128},{128,160},{160,192},{192,224},{224... | collective-permute-start | bytes 2211848 | tf_op jit(solution)/shard_map/ppermute | solution.py:28
  16.1 28.5 %collective-permute-start.10 = (bf16[3,320,384]{2,1,0:T(8,128)(2,1)S(1)}, bf16[3,320,384]{2,1,0:T(8,128)(2,1)}, u32[]{:S(2)}, u32[]{:S(2)}) collective-permute-start(bf16[3,320,384]{2,1,0:T(8,128)(2,1)S(1)} %bitcast.28), channel_id=1, source_target_pairs={{0,224},{32,0},{64,32},{96,64},{128,96},{160,128},{192,160},{224,1... | collective-permute-start | bytes 2211848 | tf_op jit(solution)/shard_map/ppermute | solution.py:28
  31.3 43.1 %copy-start.7 = (bf16[320,640]{1,0:T(8,128)(2,1)}, bf16[320,640]{1,0:T(8,128)(2,1)S(1)}, u32[]{:S(2)}) copy-start(bf16[320,640]{1,0:T(8,128)(2,1)S(1)} %reshape.68.refs_1_) | copy-start | bytes 1228804
  31.3 16.0 %collective-permute-start = (bf16[320,640]{1,0:T(8,128)(2,1)S(1)}, bf16[320,640]{1,0:T(8,128)(2,1)S(1)}, u32[]{:S(2)}, u32[]{:S(2)}) collective-permute-start(bf16[320,640]{1,0:T(8,128)(2,1)S(1)} %reshape.68.refs_1_), channel_id=1, source_target_pairs={{0,2},{2,0},{1,3},{3,1},{4,6},{6,4},{5,7},{7,5},{8,10},{10,8},{9,1... | collective-permute-start | bytes 1228808 | tf_op jit(solution)/shard_map/ppermute | solution.py:28
  34.3 13.0 %collective-permute-start.1 = (bf16[320,640]{1,0:T(8,128)(2,1)S(1)}, bf16[320,640]{1,0:T(8,128)(2,1)S(1)}, u32[]{:S(2)}, u32[]{:S(2)}) collective-permute-start(bf16[320,640]{1,0:T(8,128)(2,1)S(1)} %reshape.68.refs_1_), channel_id=1, source_target_pairs={{0,12},{4,0},{8,4},{12,8},{1,13},{5,1},{9,5},{13,9},{2,14},{6,2},{... | collective-permute-start | bytes 1228808 | tf_op jit(solution)/shard_map/ppermute | solution.py:28
  36.8 12.6 %collective-permute-start.2 = (bf16[320,640]{1,0:T(8,128)(2,1)S(1)}, bf16[320,640]{1,0:T(8,128)(2,1)S(1)}, u32[]{:S(2)}, u32[]{:S(2)}) collective-permute-start(bf16[320,640]{1,0:T(8,128)(2,1)S(1)} %reshape.68.refs_1_), channel_id=1, source_target_pairs={{0,4},{4,8},{8,12},{12,0},{1,5},{5,9},{9,13},{13,1},{2,6},{6,10},{... | collective-permute-start | bytes 1228808 | tf_op jit(solution)/shard_map/ppermute | solution.py:28
  44.6 24.4 %collective-permute-start.8 = (bf16[3,320,384]{2,1,0:T(8,128)(2,1)}, bf16[3,320,384]{2,1,0:T(8,128)(2,1)}, u32[]{:S(2)}, u32[]{:S(2)}) collective-permute-start(bf16[3,320,384]{2,1,0:T(8,128)(2,1)} %collective-permute-done.7.refs_12_), channel_id=1, source_target_pairs={{0,32},{32,64},{64,96},{96,128},{128,160},{160,192},{192,224},{224... | collective-permute-start | bytes 2211848 | tf_op jit(solution)/shard_map/ppermute | solution.py:28
  44.6 24.7 %collective-permute-start.11 = (bf16[3,320,384]{2,1,0:T(8,128)(2,1)}, bf16[3,320,384]{2,1,0:T(8,128)(2,1)}, u32[]{:S(2)}, u32[]{:S(2)}) collective-permute-start(bf16[3,320,384]{2,1,0:T(8,128)(2,1)} %collective-permute-done.10.refs_13_), channel_id=1, source_target_pairs={{0,224},{32,0},{64,32},{96,64},{128,96},{160,128},{192,160},{224,1... | collective-permute-start | bytes 2211848 | tf_op jit(solution)/shard_map/ppermute | solution.py:28
  49.4 7.7 %collective-permute-start.5 = (bf16[160,640]{1,0:T(8,128)(2,1)S(1)}, bf16[160,640]{1,0:T(8,128)(2,1)S(1)}, u32[]{:S(2)}, u32[]{:S(2)}) collective-permute-start(bf16[160,640]{1,0:T(8,128)(2,1)S(1)} %slice.36), channel_id=1, source_target_pairs={{0,4},{4,8},{8,12},{12,0},{1,5},{5,9},{9,13},{13,1},{2,6},{6,10},{... | collective-permute-start | bytes 614408 | tf_op jit(solution)/shard_map/ppermute | solution.py:28
  49.5 15.2 %collective-permute-start.3 = (bf16[320,640]{1,0:T(8,128)(2,1)S(1)}, bf16[320,640]{1,0:T(8,128)(2,1)S(1)}, u32[]{:S(2)}, u32[]{:S(2)}) collective-permute-start(bf16[320,640]{1,0:T(8,128)(2,1)S(1)} %collective-permute-done.refs_6_), channel_id=1, source_target_pairs={{0,12},{4,0},{8,4},{12,8},{1,13},{5,1},{9,5},{13,9},{2,14},{6,2},{... | collective-permute-start | bytes 1228808 | tf_op jit(solution)/shard_map/ppermute | solution.py:28
  52.2 13.6 %collective-permute-start.4 = (bf16[320,640]{1,0:T(8,128)(2,1)S(1)}, bf16[320,640]{1,0:T(8,128)(2,1)S(1)}, u32[]{:S(2)}, u32[]{:S(2)}) collective-permute-start(bf16[320,640]{1,0:T(8,128)(2,1)S(1)} %collective-permute-done.refs_6_), channel_id=1, source_target_pairs={{0,4},{4,8},{8,12},{12,0},{1,5},{5,9},{9,13},{13,1},{2,6},{6,10},{... | collective-permute-start | bytes 1228808 | tf_op jit(solution)/shard_map/ppermute | solution.py:28
  57.1 7.6 %collective-permute-start.6 = (bf16[160,640]{1,0:T(8,128)(2,1)S(1)}, bf16[160,640]{1,0:T(8,128)(2,1)S(1)}, u32[]{:S(2)}, u32[]{:S(2)}) collective-permute-start(bf16[160,640]{1,0:T(8,128)(2,1)S(1)} %slice.37), channel_id=1, source_target_pairs={{0,12},{4,0},{8,4},{12,8},{1,13},{5,1},{9,5},{13,9},{2,14},{6,2},{... | collective-permute-start | bytes 614408 | tf_op jit(solution)/shard_map/ppermute | solution.py:28
  65.8 10.0 %collective-permute-start.13 = (bf16[160,640]{1,0:T(8,128)(2,1)S(1)}, bf16[160,640]{1,0:T(8,128)(2,1)S(1)}, u32[]{:S(2)}, u32[]{:S(2)}) collective-permute-start(bf16[160,640]{1,0:T(8,128)(2,1)S(1)} %slice.38), channel_id=1, source_target_pairs={{0,4},{4,8},{8,12},{12,0},{1,5},{5,9},{9,13},{13,1},{2,6},{6,10},{... | collective-permute-start | bytes 614408 | tf_op jit(solution)/shard_map/ppermute | solution.py:28
  65.9 9.9 %collective-permute-start.14 = (bf16[160,640]{1,0:T(8,128)(2,1)S(1)}, bf16[160,640]{1,0:T(8,128)(2,1)}, u32[]{:S(2)}, u32[]{:S(2)}) collective-permute-start(bf16[160,640]{1,0:T(8,128)(2,1)S(1)} %slice.39), channel_id=1, source_target_pairs={{0,12},{4,0},{8,4},{12,8},{1,13},{5,1},{9,5},{13,9},{2,14},{6,2},{... | collective-permute-start | bytes 614408 | tf_op jit(solution)/shard_map/ppermute | solution.py:28
  69.0 17.8 %collective-permute-start.9 = (bf16[3,320,384]{2,1,0:T(8,128)(2,1)}, bf16[3,320,384]{2,1,0:T(8,128)(2,1)S(1)}, u32[]{:S(2)}, u32[]{:S(2)}) collective-permute-start(bf16[3,320,384]{2,1,0:T(8,128)(2,1)} %collective-permute-done.8.refs_14_), channel_id=1, source_target_pairs={{0,32},{32,64},{64,96},{96,128},{128,160},{160,192},{192,224},{224... | collective-permute-start | bytes 2211848 | tf_op jit(solution)/shard_map/ppermute | solution.py:28
  69.3 17.5 %collective-permute-start.12 = (bf16[3,320,384]{2,1,0:T(8,128)(2,1)}, bf16[3,320,384]{2,1,0:T(8,128)(2,1)}, u32[]{:S(2)}, u32[]{:S(2)}) collective-permute-start(bf16[3,320,384]{2,1,0:T(8,128)(2,1)} %collective-permute-done.11.refs_15_), channel_id=1, source_target_pairs={{0,224},{32,0},{64,32},{96,64},{128,96},{160,128},{192,160},{224,1... | collective-permute-start | bytes 2211848 | tf_op jit(solution)/shard_map/ppermute | solution.py:28
  76.5 38.2 %all-to-all-start.1 = ((bf16[8,192,640]{2,1,0:T(8,128)(2,1)}), bf16[8,192,640]{2,1,0:T(8,128)(2,1)S(1)}, u32[]{:S(2)}, u32[]{:S(2)}) async-start(bf16[8,192,640]{2,1,0:T(8,128)(2,1)} %copy-done.1), calls=%async_computation.1 | async-start | bytes 3932160 | tf_op jit(solution)/shard_map/all_to_all | solution.py:23
  88.5 15.6 %collective-permute-start.15 = (bf16[3,160,384]{2,1,0:T(8,128)(2,1)}, bf16[3,160,384]{2,1,0:T(8,128)(2,1)S(1)}, u32[]{:S(2)}, u32[]{:S(2)}) collective-permute-start(bf16[3,160,384]{2,1,0:T(8,128)(2,1)} %slice.40), channel_id=1, source_target_pairs={{0,32},{32,64},{64,96},{96,128},{128,160},{160,192},{192,224},{224... | collective-permute-start | bytes 1105928 | tf_op jit(solution)/shard_map/ppermute | solution.py:28
  90.3 13.8 %collective-permute-start.16 = (bf16[3,160,384]{2,1,0:T(8,128)(2,1)}, bf16[3,160,384]{2,1,0:T(8,128)(2,1)S(1)}, u32[]{:S(2)}, u32[]{:S(2)}) collective-permute-start(bf16[3,160,384]{2,1,0:T(8,128)(2,1)} %slice.41), channel_id=1, source_target_pairs={{0,224},{32,0},{64,32},{96,64},{128,96},{160,128},{192,160},{224,1... | collective-permute-start | bytes 1105928 | tf_op jit(solution)/shard_map/ppermute | solution.py:28
  108.1 5.2 %collective-permute-start.17 = (bf16[320,1152]{1,0:T(8,128)(2,1)S(1)}, bf16[320,1152]{1,0:T(8,128)(2,1)S(1)}, u32[]{:S(2)}, u32[]{:S(2)}) collective-permute-start(bf16[320,1152]{1,0:T(8,128)(2,1)S(1)} %get-tuple-element.45), channel_id=1, source_target_pairs={{0,16},{16,0},{1,17},{17,1},{2,18},{18,2},{3,19},{19,3},{4,20},{20... | collective-permute-start | bytes 2211848 | tf_op jit(solution)/shard_map/ppermute | solution.py:28
  114.7 39.1 %collective-permute-start.27 = (bf16[8,192,640]{2,1,0:T(8,128)(2,1)S(1)}, bf16[8,192,640]{2,1,0:T(8,128)(2,1)}, u32[]{:S(2)}, u32[]{:S(2)}) collective-permute-start(bf16[8,192,640]{2,1,0:T(8,128)(2,1)S(1)} %all-to-all-done.1.half), channel_id=1, source_target_pairs={{0,16},{16,0},{1,17},{17,1},{2,18},{18,2},{3,19},{19,3},{4,20},{20... | collective-permute-start | bytes 5898248 | tf_op jit(solution)/shard_map/ppermute | solution.py:28
  130.2 9.3 %collective-permute-start.18 = (bf16[320,384]{1,0:T(8,128)(2,1)S(1)}, bf16[320,384]{1,0:T(8,128)(2,1)S(1)}, u32[]{:S(2)}, u32[]{:S(2)}) collective-permute-start(bf16[320,384]{1,0:T(8,128)(2,1)S(1)} %reshape.69.m0), channel_id=1, source_target_pairs={{0,2},{2,0},{1,3},{3,1},{4,6},{6,4},{5,7},{7,5},{8,10},{10,8},{9,1... | collective-permute-start | bytes 737288 | tf_op jit(solution)/shard_map/ppermute | solution.py:28
  132.7 7.7 %collective-permute-start.19 = (bf16[320,384]{1,0:T(8,128)(2,1)S(1)}, bf16[320,384]{1,0:T(8,128)(2,1)S(1)}, u32[]{:S(2)}, u32[]{:S(2)}) collective-permute-start(bf16[320,384]{1,0:T(8,128)(2,1)S(1)} %reshape.69.m0), channel_id=1, source_target_pairs={{0,12},{4,0},{8,4},{12,8},{1,13},{5,1},{9,5},{13,9},{2,14},{6,2},{... | collective-permute-start | bytes 737288 | tf_op jit(solution)/shard_map/ppermute | solution.py:28
  134.1 8.7 %collective-permute-start.20 = (bf16[320,384]{1,0:T(8,128)(2,1)S(1)}, bf16[320,384]{1,0:T(8,128)(2,1)S(1)}, u32[]{:S(2)}, u32[]{:S(2)}) collective-permute-start(bf16[320,384]{1,0:T(8,128)(2,1)S(1)} %reshape.69.m0), channel_id=1, source_target_pairs={{0,4},{4,8},{8,12},{12,0},{1,5},{5,9},{9,13},{13,1},{2,6},{6,10},{... | collective-permute-start | bytes 737288 | tf_op jit(solution)/shard_map/ppermute | solution.py:28
  142.8 7.8 %collective-permute-start.23 = (bf16[320,384]{1,0:T(8,128)(2,1)S(1)}, bf16[320,384]{1,0:T(8,128)(2,1)S(1)}, u32[]{:S(2)}, u32[]{:S(2)}) collective-permute-start(bf16[320,384]{1,0:T(8,128)(2,1)S(1)} %collective-permute-done.18.m1), channel_id=1, source_target_pairs={{0,4},{4,8},{8,12},{12,0},{1,5},{5,9},{9,13},{13,1},{2,6},{6,10},{... | collective-permute-start | bytes 737288 | tf_op jit(solution)/shard_map/ppermute | solution.py:28
  142.8 7.9 %collective-permute-start.25 = (bf16[320,384]{1,0:T(8,128)(2,1)S(1)}, bf16[320,384]{1,0:T(8,128)(2,1)S(1)}, u32[]{:S(2)}, u32[]{:S(2)}) collective-permute-start(bf16[320,384]{1,0:T(8,128)(2,1)S(1)} %collective-permute-done.18.m1), channel_id=1, source_target_pairs={{0,12},{4,0},{8,4},{12,8},{1,13},{5,1},{9,5},{13,9},{2,14},{6,2},{... | collective-permute-start | bytes 737288 | tf_op jit(solution)/shard_map/ppermute | solution.py:28
  145.7 11.0 %collective-permute-start.21 = (bf16[160,384]{1,0:T(8,128)(2,1)S(1)}, bf16[160,384]{1,0:T(8,128)(2,1)S(1)}, u32[]{:S(2)}, u32[]{:S(2)}) collective-permute-start(bf16[160,384]{1,0:T(8,128)(2,1)S(1)} %slice.42), channel_id=1, source_target_pairs={{0,4},{4,8},{8,12},{12,0},{1,5},{5,9},{9,13},{13,1},{2,6},{6,10},{... | collective-permute-start | bytes 368648 | tf_op jit(solution)/shard_map/ppermute | solution.py:28
  145.8 10.9 %collective-permute-start.22 = (bf16[160,384]{1,0:T(8,128)(2,1)S(1)}, bf16[160,384]{1,0:T(8,128)(2,1)S(1)}, u32[]{:S(2)}, u32[]{:S(2)}) collective-permute-start(bf16[160,384]{1,0:T(8,128)(2,1)S(1)} %slice.43), channel_id=1, source_target_pairs={{0,12},{4,0},{8,4},{12,8},{1,13},{5,1},{9,5},{13,9},{2,14},{6,2},{... | collective-permute-start | bytes 368648 | tf_op jit(solution)/shard_map/ppermute | solution.py:28
  150.7 6.1 %collective-permute-start.24 = (bf16[160,384]{1,0:T(8,128)(2,1)S(1)}, bf16[160,384]{1,0:T(8,128)(2,1)S(1)}, u32[]{:S(2)}, u32[]{:S(2)}) collective-permute-start(bf16[160,384]{1,0:T(8,128)(2,1)S(1)} %slice.48), channel_id=1, source_target_pairs={{0,4},{4,8},{8,12},{12,0},{1,5},{5,9},{9,13},{13,1},{2,6},{6,10},{... | collective-permute-start | bytes 368648 | tf_op jit(solution)/shard_map/ppermute | solution.py:28
  150.8 6.0 %collective-permute-start.26 = (bf16[160,384]{1,0:T(8,128)(2,1)S(1)}, bf16[160,384]{1,0:T(8,128)(2,1)S(1)}, u32[]{:S(2)}, u32[]{:S(2)}) collective-permute-start(bf16[160,384]{1,0:T(8,128)(2,1)S(1)} %slice.49), channel_id=1, source_target_pairs={{0,12},{4,0},{8,4},{12,8},{1,13},{5,1},{9,5},{13,9},{2,14},{6,2},{... | collective-permute-start | bytes 368648 | tf_op jit(solution)/shard_map/ppermute | solution.py:28
  (18 other events, 219.2 us)

commit v13 on v12

--- a/solution.py
+++ b/solution.py
@@ -198,9 +198,12 @@
     return jnp.dot(x, jnp.concatenate(w, axis=0), preferred_element_type=jnp.float32)
 
 
-def near_kernel(where, m0, m1, r0, r1, l0, l1, half, other, acc):
+def own_kernel(where, m0, m1, half, other, acc):
     acc[...] = out_product((m0[...], m1[...]), where, 0, half, other)
-    acc[...] += out_product((r0[...], r1[...]), where, 1, half, other)
+
+
+def side_kernel(where, r0, r1, l0, l1, half, other, own, acc):
+    acc[...] = own[...] + out_product((r0[...], r1[...]), where, 1, half, other)
     acc[...] += out_product((l0[...], l1[...]), where, 3, half, other)
 
 
@@ -225,13 +228,11 @@
         terms[i, :, width:] = codevec[...]
 
 
-def near(where, *operands):
-    rows, width = operands[0].shape[0], operands[6].shape[2]
-    smem, vmem = pl.BlockSpec(memory_space=pltpu.SMEM), pl.BlockSpec(memory_space=pltpu.VMEM)
-    return pl.pallas_call(
-        near_kernel,
-        in_specs=[smem] + [vmem] * 8,
-        out_specs=vmem,
+def near(kernel, rows, width, where, *operands):
+    return pl.pallas_call(
+        kernel,
+        in_specs=[SMEM] + [WHOLE] * len(operands),
+        out_specs=WHOLE,
         out_shape=jax.ShapeDtypeStruct((rows, width), jnp.float32),
         compiler_params=SMALL,
     )(where, *operands)
@@ -305,9 +306,12 @@
     other = shift(mine, "yhi", 1)
     side = sideways(mine)
     other, side = lax.optimization_barrier((other, side))
+    x, yhi = lax.axis_index("x"), lax.axis_index("yhi")
+    shard = (z + jnp.array([0, zs - 1, 1, zs - 2, 2, zs - 3, 3, zs - 4], jnp.int32)) & (zs - 1)
+    slots = (2 * (((shard >> 1) - x) & (mp // 2 - 1)) + ((shard & 1) ^ yhi)).astype(jnp.int32)
     up2, down2 = shift(up1, "z", 1), shift(down1, "z", -1)
     other_side, far = sideways(other), onward(*side)
-    other_side, far, w_out = lax.optimization_barrier((other_side, far, w_out))
+    other_side, far, w_out, slots = lax.optimization_barrier((other_side, far, w_out, slots))
     up3, down3 = shift(up2, "z", 1), shift(down2, "z", -1)
     other_far = onward(*other_side)
     blocks = column_blocks(w_out, core1, width)
@@ -318,9 +322,6 @@
 
     half = exchange(blocks, MP)
 
-    x, yhi = lax.axis_index("x"), lax.axis_index("yhi")
-    shard = (z + jnp.array([0, zs - 1, 1, zs - 2, 2, zs - 3, 3, zs - 4], jnp.int32)) & (zs - 1)
-    slots = (2 * (((shard >> 1) - x) & (mp // 2 - 1)) + ((shard & 1) ^ yhi)).astype(jnp.int32)
     features = (mine, *side, *far, other, *other_side, *other_far)
     early = [[(own,), (up1,)], [(down1,), (up2,)], [(down2,), (up3,)], [(down3,)]]
     acc, spare = project(features, early, slots)
@@ -331,12 +332,16 @@
     attn = exchange(attn, FRAME).reshape(rows, heads)
     peer = shift(attn, "yhi", 1)
     side = sideways(attn)
-    peer, side = lax.optimization_barrier((peer, side))
-    peer_side, far = sideways(peer), onward(*side)
+    peer_side = sideways(peer)
+    _, side = lax.optimization_barrier((peer, side))
+    far = onward(*side)
+    where = jnp.stack([core, x, yhi]).astype(jnp.int32)
+    acc = near(own_kernel, rows, width, where, attn, peer, half, other_half)
+    peer_side, acc = lax.optimization_barrier((peer_side, acc))
     peer_far = onward(*peer_side)
-    where = jnp.stack([core, x, yhi]).astype(jnp.int32)
     acc = near(
-        where, attn, peer, side[0], peer_side[0], side[1], peer_side[1], half, other_half
+        side_kernel, rows, width, where,
+        side[0], peer_side[0], side[1], peer_side[1], half, other_half, acc,
     )
     onehot = (action_idx.reshape(clips)[:, None] == jnp.arange(codebook.shape[0])[None, :]).astype(
         jnp.float32

time: 178 us -> 173 us (0.972)
  local copies, waits for them, and re-layouts: 13.6 us -> 10.7 us
  waiting for transfers between devices: 55.9 us -> 54 us
  Pallas kernels: 19.1 us -> 20.9 us
    ppermute x28, waiting for transfers between devices: 42 us -> 40.1 us  [shift(): return lax.ppermute(x, axis, [(i, (i + by) % n) for i in range(n)])]
    pallas_call x1 -> x2, Pallas kernels: 2.93 us -> 4.7 us  [near(): pl.pallas_call(kernel, in_specs=[SMEM] + [WHOLE] * len(operands), out_spe...]
    unnamed x41 -> x37, local copies, waits for them, and re-layouts: 8.55 us -> 6.99 us
  transfers between devices with their start and end apart: 30 -> 30, of which waited for: 12 -> 11; matrix products, arithmetic and copies ran while one was open for 2% -> 1% of each run, Pallas kernels for 9% -> 10%
where the time goes in v13:
time: 173 us
  waiting for transfers between devices  54 us (31%)
  starting transfers between devices  50.8 us (29%)
  blocking collectives  31.5 us (18%)
  Pallas kernels  20.9 us (12%)
  local copies, waits for them, and re-layouts  10.7 us (6%)
  other arithmetic  2.57 us (1%)
    ppermute x28, waiting for transfers between devices, shift(): return lax.ppermute(x, axis, [(i, (i + by) % n) for i in range(n)])  40.1 us
    ppermute x28, starting transfers between devices, shift(): return lax.ppermute(x, axis, [(i, (i + by) % n) for i in range(n)])  37.2 us
    all_to_all x2, blocking collectives, exchange(): return lax.all_to_all(x, axis, split_axis=0, concat_axis=0, tiled=True)  31.5 us
    all_to_all x2, waiting for transfers between devices, exchange(): return lax.all_to_all(x, axis, split_axis=0, concat_axis=0, tiled=True)  13.9 us
    all_to_all x2, starting transfers between devices, exchange(): return lax.all_to_all(x, axis, split_axis=0, concat_axis=0, tiled=True)  13.6 us
    pallas_call x1, Pallas kernels, project(): pl.pallas_call(kernel, in_specs=[SMEM] + [ANYWHERE] * len(operands), out_...  10.5 us
    unnamed x37, local copies, waits for them, and re-layouts  6.99 us
    pallas_call x2, Pallas kernels, near(): pl.pallas_call(kernel, in_specs=[SMEM] + [WHOLE] * len(operands), out_spe...  4.7 us
  transfers between devices with their start and end apart: 30, of which 11 were waited for; matrix products, arithmetic and copies ran while one was open for 1% of the time, Pallas kernels for 10%

profile of v13, /device:TPU:1, one launch (start us, length us, event | category | flops | bytes accessed | tf_op | source)
XLA Modules:
  0.0 172.8 jit_solution(4044185386207861153)
XLA Ops:
  4.7 10.0 %all-to-all-start = ((bf16[16,20,640]{2,1,0:T(8,128)(2,1)}), bf16[16,20,640]{2,1,0:T(8,128)(2,1)S(1)}, u32[]{:S(2)}, u32[]{:S(2)}) async-start(bf16[16,20,640]{2,1,0:T(8,128)(2,1)} %copy.18), calls=%async_computation | async-start | bytes 983040 | tf_op jit(solution)/shard_map/all_to_all | solution.py:23
  14.6 1.5 collective-permute-start.7
  17.4 13.8 %all-to-all-done = bf16[16,20,640]{2,1,0:T(8,128)(2,1)S(1)} async-done(((bf16[16,20,640]{2,1,0:T(8,128)(2,1)}), bf16[16,20,640]{2,1,0:T(8,128)(2,1)S(1)}, u32[]{:S(2)}, u32[]{:S(2)}) %all-to-all-start) | async-done | bytes 409632 | tf_op jit(solution)/shard_map/all_to_all | solution.py:23
  31.4 3.0 %collective-permute-start = (bf16[320,640]{1,0:T(8,128)(2,1)S(1)}, bf16[320,640]{1,0:T(8,128)(2,1)}, u32[]{:S(2)}, u32[]{:S(2)}) collective-permute-start(bf16[320,640]{1,0:T(8,128)(2,1)S(1)} %reshape.68.refs_1_), channel_id=1, source_target_pairs={{0,2},{2,0},{1,3},{3,1},{4,6},{6,4},{5,7},{7,5},{8,10},{10,8},{9,1... | collective-permute-start | bytes 1228808 | tf_op jit(solution)/shard_map/ppermute | solution.py:28
  34.4 2.5 %collective-permute-start.1 = (bf16[320,640]{1,0:T(8,128)(2,1)S(1)}, bf16[320,640]{1,0:T(8,128)(2,1)S(1)}, u32[]{:S(2)}, u32[]{:S(2)}) collective-permute-start(bf16[320,640]{1,0:T(8,128)(2,1)S(1)} %reshape.68.refs_1_), channel_id=1, source_target_pairs={{0,12},{4,0},{8,4},{12,8},{1,13},{5,1},{9,5},{13,9},{2,14},{6,2},{... | collective-permute-start | bytes 1228808 | tf_op jit(solution)/shard_map/ppermute | solution.py:28
  36.9 7.8 %collective-permute-done.7.refs_12_ = bf16[3,320,384]{2,1,0:T(8,128)(2,1)} collective-permute-done((bf16[3,320,384]{2,1,0:T(8,128)(2,1)S(1)}, bf16[3,320,384]{2,1,0:T(8,128)(2,1)}, u32[]{:S(2)}, u32[]{:S(2)}) %collective-permute-start.7) | collective-permute-done | bytes 737312 | tf_op jit(solution)/shard_map/ppermute | solution.py:28
  44.7 2.7 %collective-permute-start.11 = (bf16[3,320,384]{2,1,0:T(8,128)(2,1)}, bf16[3,320,384]{2,1,0:T(8,128)(2,1)}, u32[]{:S(2)}, u32[]{:S(2)}) collective-permute-start(bf16[3,320,384]{2,1,0:T(8,128)(2,1)} %collective-permute-done.10.refs_13_), channel_id=1, source_target_pairs={{0,224},{32,0},{64,32},{96,64},{128,96},{160,128},{192,160},{224,1... | collective-permute-start | bytes 2211848 | tf_op jit(solution)/shard_map/ppermute | solution.py:28
  47.3 2.1 %collective-permute-done.2.refs_3_ = bf16[320,640]{1,0:T(8,128)(2,1)S(1)} collective-permute-done((bf16[320,640]{1,0:T(8,128)(2,1)S(1)}, bf16[320,640]{1,0:T(8,128)(2,1)S(1)}, u32[]{:S(2)}, u32[]{:S(2)}) %collective-permute-start.2) | collective-permute-done | bytes 409632 | tf_op jit(solution)/shard_map/ppermute | solution.py:28
  49.5 2.7 %collective-permute-start.3 = (bf16[320,640]{1,0:T(8,128)(2,1)}, bf16[320,640]{1,0:T(8,128)(2,1)S(1)}, u32[]{:S(2)}, u32[]{:S(2)}) collective-permute-start(bf16[320,640]{1,0:T(8,128)(2,1)} %collective-permute-done.refs_6_), channel_id=1, source_target_pairs={{0,12},{4,0},{8,4},{12,8},{1,13},{5,1},{9,5},{13,9},{2,14},{6,2},{... | collective-permute-start | bytes 1228808 | tf_op jit(solution)/shard_map/ppermute | solution.py:28
  52.2 4.9 %collective-permute-done.5.refs_4_ = bf16[160,640]{1,0:T(8,128)(2,1)S(1)} collective-permute-done((bf16[160,640]{1,0:T(8,128)(2,1)S(1)}, bf16[160,640]{1,0:T(8,128)(2,1)S(1)}, u32[]{:S(2)}, u32[]{:S(2)}) %collective-permute-start.5) | collective-permute-done | bytes 204832 | tf_op jit(solution)/shard_map/ppermute | solution.py:28
  57.6 7.3 %collective-permute-done.6.refs_5_ = bf16[160,640]{1,0:T(8,128)(2,1)S(1)} collective-permute-done((bf16[160,640]{1,0:T(8,128)(2,1)S(1)}, bf16[160,640]{1,0:T(8,128)(2,1)S(1)}, u32[]{:S(2)}, u32[]{:S(2)}) %collective-permute-start.6) | collective-permute-done | bytes 204832 | tf_op jit(solution)/shard_map/ppermute | solution.py:28
  65.9 3.3 %collective-permute-start.14 = (bf16[160,640]{1,0:T(8,128)(2,1)S(1)}, bf16[160,640]{1,0:T(8,128)(2,1)}, u32[]{:S(2)}, u32[]{:S(2)}) collective-permute-start(bf16[160,640]{1,0:T(8,128)(2,1)S(1)} %slice.39), channel_id=1, source_target_pairs={{0,12},{4,0},{8,4},{12,8},{1,13},{5,1},{9,5},{13,9},{2,14},{6,2},{... | collective-permute-start | bytes 614408 | tf_op jit(solution)/shard_map/ppermute | solution.py:28
  69.6 2.7 %collective-permute-start.12 = (bf16[3,320,384]{2,1,0:T(8,128)(2,1)}, bf16[3,320,384]{2,1,0:T(8,128)(2,1)}, u32[]{:S(2)}, u32[]{:S(2)}) collective-permute-start(bf16[3,320,384]{2,1,0:T(8,128)(2,1)} %collective-permute-done.11.refs_15_), channel_id=1, source_target_pairs={{0,224},{32,0},{64,32},{96,64},{128,96},{160,128},{192,160},{224,1... | collective-permute-start | bytes 2211848 | tf_op jit(solution)/shard_map/ppermute | solution.py:28
  72.2 2.1 %copy-done.2 = bf16[384,5120]{1,0:T(8,128)(2,1)S(1)} copy-done((bf16[384,5120]{1,0:T(8,128)(2,1)S(1)}, bf16[384,5120]{1,0:T(8,128)(2,1)}, u32[]{:S(2)}) %copy-start.2) | copy-done | bytes 3932184
  76.0 3.6 %all-to-all-start.1 = ((bf16[8,192,640]{2,1,0:T(8,128)(2,1)}), bf16[8,192,640]{2,1,0:T(8,128)(2,1)S(1)}, u32[]{:S(2)}, u32[]{:S(2)}) async-start(bf16[8,192,640]{2,1,0:T(8,128)(2,1)} %copy-done.1), calls=%async_computation.1 | async-start | bytes 3932160 | tf_op jit(solution)/shard_map/all_to_all | solution.py:23
  79.7 7.5 %collective-permute-done.9.refs_16_ = bf16[3,320,384]{2,1,0:T(8,128)(2,1)S(1)} collective-permute-done((bf16[3,320,384]{2,1,0:T(8,128)(2,1)}, bf16[3,320,384]{2,1,0:T(8,128)(2,1)S(1)}, u32[]{:S(2)}, u32[]{:S(2)}) %collective-permute-start.9) | collective-permute-done | bytes 737312 | tf_op jit(solution)/shard_map/ppermute | solution.py:28
  88.4 2.6 %collective-permute-start.16 = (bf16[3,160,384]{2,1,0:T(8,128)(2,1)S(1)}, bf16[3,160,384]{2,1,0:T(8,128)(2,1)S(1)}, u32[]{:S(2)}, u32[]{:S(2)}) collective-permute-start(bf16[3,160,384]{2,1,0:T(8,128)(2,1)S(1)} %slice.41), channel_id=1, source_target_pairs={{0,224},{32,0},{64,32},{96,64},{128,96},{160,128},{192,160},{224,1... | collective-permute-start | bytes 1105928 | tf_op jit(solution)/shard_map/ppermute | solution.py:28
  91.0 10.5 %shard_map.114 = (f32[640,1152]{1,0:T(8,128)}, bf16[320,640]{1,0:T(8,128)(2,1)}) custom-call(s32[8]{0:T(128)} %xor_add_fusion.refs_0_, bf16[320,640]{1,0:T(8,128)(2,1)} %copy-done.7, bf16[320,640]{1,0:T(8,128)(2,1)} %copy-done.8, bf16[320,640]{1,0:T(8,128)(2,1)} %copy-done.9, bf16[160,640]{1,0:T(8,128)(2,1)} %copy-done.13, bf16[160,640]{1,0:T(8,128)(2,1)} %copy-done.14, ...), custom_call_target="tpu_custom_call" | custom-call | tf_op jit(solution)/shard_map/pallas_call | solution.py:105
  101.6 1.8 %copy-done.3 = f32[640,1152]{1,0:T(8,128)S(1)} copy-done((f32[640,1152]{1,0:T(8,128)S(1)}, f32[640,1152]{1,0:T(8,128)}, u32[]{:S(2)}) %copy-start.3) | copy-done | bytes 2949144
  105.5 3.4 %collective-permute-start.17 = (bf16[320,1152]{1,0:T(8,128)(2,1)S(1)}, bf16[320,1152]{1,0:T(8,128)(2,1)S(1)}, u32[]{:S(2)}, u32[]{:S(2)}) collective-permute-start(bf16[320,1152]{1,0:T(8,128)(2,1)S(1)} %get-tuple-element.49), channel_id=1, source_target_pairs={{0,16},{16,0},{1,17},{17,1},{2,18},{18,2},{3,19},{19,3},{4,20},{20... | collective-permute-start | bytes 2211848 | tf_op jit(solution)/shard_map/ppermute | solution.py:28
  109.0 1.7 collective-permute-done.17.other_ref
  112.6 15.4 %all_to_all.20 = bf16[16,20,384]{2,1,0:T(8,128)(2,1)S(1)} all-to-all(bf16[16,20,384]{2,1,0:T(8,128)(2,1)S(1)} %shard_map.116), channel_id=1, replica_groups=mesh['z'=8,'core'=2,'x'=4,'yhi'=2,'dp'=2] {'z','core'}, dimensions={0} | all-to-all | bytes 491520 | tf_op jit(solution)/shard_map/all_to_all | solution.py:23
  128.0 2.1 %collective-permute-start.18 = (bf16[320,384]{1,0:T(8,128)(2,1)S(1)}, bf16[320,384]{1,0:T(8,128)(2,1)S(1)}, u32[]{:S(2)}, u32[]{:S(2)}) collective-permute-start(bf16[320,384]{1,0:T(8,128)(2,1)S(1)} %reshape.69.m0), channel_id=1, source_target_pairs={{0,2},{2,0},{1,3},{3,1},{4,6},{6,4},{5,7},{7,5},{8,10},{10,8},{9,1... | collective-permute-start | bytes 737288 | tf_op jit(solution)/shard_map/ppermute | solution.py:28
  131.6 5.9 %collective-permute-done.18.m1 = bf16[320,384]{1,0:T(8,128)(2,1)S(1)} collective-permute-done((bf16[320,384]{1,0:T(8,128)(2,1)S(1)}, bf16[320,384]{1,0:T(8,128)(2,1)S(1)}, u32[]{:S(2)}, u32[]{:S(2)}) %collective-permute-start.18) | collective-permute-done | bytes 245792 | tf_op jit(solution)/shard_map/ppermute | solution.py:28
  137.5 1.5 collective-permute-start.23
  140.3 2.7 %collective-permute-start.22 = (bf16[160,384]{1,0:T(8,128)(2,1)S(1)}, bf16[160,384]{1,0:T(8,128)(2,1)S(1)}, u32[]{:S(2)}, u32[]{:S(2)}) collective-permute-start(bf16[160,384]{1,0:T(8,128)(2,1)S(1)} %slice.43), channel_id=1, source_target_pairs={{0,12},{4,0},{8,4},{12,8},{1,13},{5,1},{9,5},{13,9},{2,14},{6,2},{... | collective-permute-start | bytes 368648 | tf_op jit(solution)/shard_map/ppermute | solution.py:28
  143.1 2.1 %shard_map.117.own = f32[320,640]{1,0:T(8,128)S(1)} custom-call(s32[3]{0:T(128)S(1)} %pad_add_fusion.where, bf16[320,384]{1,0:T(8,128)(2,1)S(1)} %reshape.69.m0, bf16[320,384]{1,0:T(8,128)(2,1)S(1)} %collective-permute-done.18.m1, bf16[8,192,640]{2,1,0:T(8,128)(2,1)S(1)} %all-to-all-done.1.half, bf16[8,192,640]{2,1,0:T(8,128)(2,1)} %collective-permute-done.25.other), custom_call_target="tpu_custom_call" | custom-call | tf_op jit(solution)/shard_map/pallas_call | solution.py:232
  145.2 1.8 %collective-permute-done.24.l1 = bf16[320,384]{1,0:T(8,128)(2,1)S(1)} collective-permute-done((bf16[320,384]{1,0:T(8,128)(2,1)S(1)}, bf16[320,384]{1,0:T(8,128)(2,1)S(1)}, u32[]{:S(2)}, u32[]{:S(2)}) %collective-permute-start.24) | collective-permute-done | bytes 245792 | tf_op jit(solution)/shard_map/ppermute | solution.py:28
  147.1 2.7 %collective-permute-start.27 = (bf16[160,384]{1,0:T(8,128)(2,1)S(1)}, bf16[160,384]{1,0:T(8,128)(2,1)S(1)}, u32[]{:S(2)}, u32[]{:S(2)}) collective-permute-start(bf16[160,384]{1,0:T(8,128)(2,1)S(1)} %slice.45), channel_id=1, source_target_pairs={{0,12},{4,0},{8,4},{12,8},{1,13},{5,1},{9,5},{13,9},{2,14},{6,2},{... | collective-permute-start | bytes 368648 | tf_op jit(solution)/shard_map/ppermute | solution.py:28
  150.0 2.6 %shard_map.118.acc = f32[320,640]{1,0:T(8,128)S(1)} custom-call(s32[3]{0:T(128)S(1)} %pad_add_fusion.where, bf16[320,384]{1,0:T(8,128)(2,1)S(1)} %collective-permute-done.19.r0, bf16[320,384]{1,0:T(8,128)(2,1)S(1)} %collective-permute-done.23.r1, bf16[320,384]{1,0:T(8,128)(2,1)S(1)} %collective-permute-done.20.l0, ...), custom_call_target="tpu_custom_call" | custom-call | tf_op jit(solution)/shard_map/pallas_call | solution.py:232
  152.7 2.9 %shard_map.119 = (bf16[320,640]{1,0:T(8,128)(2,1)}, f32[32,2,672]{2,1,0:T(2,128)S(1)}) custom-call(s32[3]{0:T(128)S(1)} %pad_add_fusion.where, bf16[160,384]{1,0:T(8,128)(2,1)S(1)} %collective-permute-done.21.t0, bf16[160,384]{1,0:T(8,128)(2,1)S(1)} %collective-permute-done.22.w0, bf16[160,384]{1,0:T(8,128)(2,1)S(1)} %collective-permute-done.26.t1, ...), custom_call_target="tpu_custom_call" | custom-call | tf_op jit(solution)/shard_map/pallas_call | solution.py:245
  155.6 16.2 %all_to_all.21 = f32[32,2,672]{2,1,0:T(2,128)S(1)} all-to-all(f32[32,2,672]{2,1,0:T(2,128)S(1)} %get-tuple-element.59), channel_id=1, replica_groups=mesh['z'=8,'core'=2,'x'=4,'yhi'=2,'dp'=2] {'z','core','dp'}, dimensions={0} | all-to-all | bytes 344064 | tf_op jit(solution)/shard_map/all_to_all | solution.py:23
  (100 shorter events, 18.5 us)
Async XLA Ops:
  0.6 149.2 %copy-start = (f32[32,640]{1,0:T(8,128)S(1)}, f32[32,640]{1,0:T(8,128)}, u32[]{:S(2)}) copy-start(f32[32,640]{1,0:T(8,128)} %param.17) | copy-start | bytes 245764
  3.8 53.3 %copy-start.15 = (s32[8]{0:T(128)S(1)}, s32[8]{0:T(128)}, u32[]{:S(2)}) copy-start(s32[8]{0:T(128)} %constant.52.clone) | copy-start | bytes 100
  4.7 26.6 %all-to-all-start = ((bf16[16,20,640]{2,1,0:T(8,128)(2,1)}), bf16[16,20,640]{2,1,0:T(8,128)(2,1)S(1)}, u32[]{:S(2)}, u32[]{:S(2)}) async-start(bf16[16,20,640]{2,1,0:T(8,128)(2,1)} %copy.18), calls=%async_computation | async-start | bytes 983040 | tf_op jit(solution)/shard_map/all_to_all | solution.py:23
  14.6 30.0 %collective-permute-start.7 = (bf16[3,320,384]{2,1,0:T(8,128)(2,1)S(1)}, bf16[3,320,384]{2,1,0:T(8,128)(2,1)}, u32[]{:S(2)}, u32[]{:S(2)}) collective-permute-start(bf16[3,320,384]{2,1,0:T(8,128)(2,1)S(1)} %bitcast.27), channel_id=1, source_target_pairs={{0,32},{32,64},{64,96},{96,128},{128,160},{160,192},{192,224},{224... | collective-permute-start | bytes 2211848 | tf_op jit(solution)/shard_map/ppermute | solution.py:28
  16.1 28.5 %collective-permute-start.10 = (bf16[3,320,384]{2,1,0:T(8,128)(2,1)S(1)}, bf16[3,320,384]{2,1,0:T(8,128)(2,1)}, u32[]{:S(2)}, u32[]{:S(2)}) collective-permute-start(bf16[3,320,384]{2,1,0:T(8,128)(2,1)S(1)} %bitcast.28), channel_id=1, source_target_pairs={{0,224},{32,0},{64,32},{96,64},{128,96},{160,128},{192,160},{224,1... | collective-permute-start | bytes 2211848 | tf_op jit(solution)/shard_map/ppermute | solution.py:28
  31.4 16.0 %collective-permute-start = (bf16[320,640]{1,0:T(8,128)(2,1)S(1)}, bf16[320,640]{1,0:T(8,128)(2,1)}, u32[]{:S(2)}, u32[]{:S(2)}) collective-permute-start(bf16[320,640]{1,0:T(8,128)(2,1)S(1)} %reshape.68.refs_1_), channel_id=1, source_target_pairs={{0,2},{2,0},{1,3},{3,1},{4,6},{6,4},{5,7},{7,5},{8,10},{10,8},{9,1... | collective-permute-start | bytes 1228808 | tf_op jit(solution)/shard_map/ppermute | solution.py:28
  34.4 13.0 %collective-permute-start.1 = (bf16[320,640]{1,0:T(8,128)(2,1)S(1)}, bf16[320,640]{1,0:T(8,128)(2,1)S(1)}, u32[]{:S(2)}, u32[]{:S(2)}) collective-permute-start(bf16[320,640]{1,0:T(8,128)(2,1)S(1)} %reshape.68.refs_1_), channel_id=1, source_target_pairs={{0,12},{4,0},{8,4},{12,8},{1,13},{5,1},{9,5},{13,9},{2,14},{6,2},{... | collective-permute-start | bytes 1228808 | tf_op jit(solution)/shard_map/ppermute | solution.py:28
  36.9 12.6 %collective-permute-start.2 = (bf16[320,640]{1,0:T(8,128)(2,1)S(1)}, bf16[320,640]{1,0:T(8,128)(2,1)S(1)}, u32[]{:S(2)}, u32[]{:S(2)}) collective-permute-start(bf16[320,640]{1,0:T(8,128)(2,1)S(1)} %reshape.68.refs_1_), channel_id=1, source_target_pairs={{0,4},{4,8},{8,12},{12,0},{1,5},{5,9},{9,13},{13,1},{2,6},{6,10},{... | collective-permute-start | bytes 1228808 | tf_op jit(solution)/shard_map/ppermute | solution.py:28
  44.6 24.6 %collective-permute-start.8 = (bf16[3,320,384]{2,1,0:T(8,128)(2,1)}, bf16[3,320,384]{2,1,0:T(8,128)(2,1)}, u32[]{:S(2)}, u32[]{:S(2)}) collective-permute-start(bf16[3,320,384]{2,1,0:T(8,128)(2,1)} %collective-permute-done.7.refs_12_), channel_id=1, source_target_pairs={{0,32},{32,64},{64,96},{96,128},{128,160},{160,192},{192,224},{224... | collective-permute-start | bytes 2211848 | tf_op jit(solution)/shard_map/ppermute | solution.py:28
  44.7 24.9 %collective-permute-start.11 = (bf16[3,320,384]{2,1,0:T(8,128)(2,1)}, bf16[3,320,384]{2,1,0:T(8,128)(2,1)}, u32[]{:S(2)}, u32[]{:S(2)}) collective-permute-start(bf16[3,320,384]{2,1,0:T(8,128)(2,1)} %collective-permute-done.10.refs_13_), channel_id=1, source_target_pairs={{0,224},{32,0},{64,32},{96,64},{128,96},{160,128},{192,160},{224,1... | collective-permute-start | bytes 2211848 | tf_op jit(solution)/shard_map/ppermute | solution.py:28
  49.4 7.7 %collective-permute-start.5 = (bf16[160,640]{1,0:T(8,128)(2,1)S(1)}, bf16[160,640]{1,0:T(8,128)(2,1)S(1)}, u32[]{:S(2)}, u32[]{:S(2)}) collective-permute-start(bf16[160,640]{1,0:T(8,128)(2,1)S(1)} %slice.36), channel_id=1, source_target_pairs={{0,4},{4,8},{8,12},{12,0},{1,5},{5,9},{9,13},{13,1},{2,6},{6,10},{... | collective-permute-start | bytes 614408 | tf_op jit(solution)/shard_map/ppermute | solution.py:28
  49.5 15.4 %collective-permute-start.3 = (bf16[320,640]{1,0:T(8,128)(2,1)}, bf16[320,640]{1,0:T(8,128)(2,1)S(1)}, u32[]{:S(2)}, u32[]{:S(2)}) collective-permute-start(bf16[320,640]{1,0:T(8,128)(2,1)} %collective-permute-done.refs_6_), channel_id=1, source_target_pairs={{0,12},{4,0},{8,4},{12,8},{1,13},{5,1},{9,5},{13,9},{2,14},{6,2},{... | collective-permute-start | bytes 1228808 | tf_op jit(solution)/shard_map/ppermute | solution.py:28
  52.2 13.6 %collective-permute-start.4 = (bf16[320,640]{1,0:T(8,128)(2,1)}, bf16[320,640]{1,0:T(8,128)(2,1)S(1)}, u32[]{:S(2)}, u32[]{:S(2)}) collective-permute-start(bf16[320,640]{1,0:T(8,128)(2,1)} %collective-permute-done.refs_6_), channel_id=1, source_target_pairs={{0,4},{4,8},{8,12},{12,0},{1,5},{5,9},{9,13},{13,1},{2,6},{6,10},{... | collective-permute-start | bytes 1228808 | tf_op jit(solution)/shard_map/ppermute | solution.py:28
  57.1 7.8 %collective-permute-start.6 = (bf16[160,640]{1,0:T(8,128)(2,1)S(1)}, bf16[160,640]{1,0:T(8,128)(2,1)S(1)}, u32[]{:S(2)}, u32[]{:S(2)}) collective-permute-start(bf16[160,640]{1,0:T(8,128)(2,1)S(1)} %slice.37), channel_id=1, source_target_pairs={{0,12},{4,0},{8,4},{12,8},{1,13},{5,1},{9,5},{13,9},{2,14},{6,2},{... | collective-permute-start | bytes 614408 | tf_op jit(solution)/shard_map/ppermute | solution.py:28
  65.8 10.2 %collective-permute-start.13 = (bf16[160,640]{1,0:T(8,128)(2,1)S(1)}, bf16[160,640]{1,0:T(8,128)(2,1)}, u32[]{:S(2)}, u32[]{:S(2)}) collective-permute-start(bf16[160,640]{1,0:T(8,128)(2,1)S(1)} %slice.38), channel_id=1, source_target_pairs={{0,4},{4,8},{8,12},{12,0},{1,5},{5,9},{9,13},{13,1},{2,6},{6,10},{... | collective-permute-start | bytes 614408 | tf_op jit(solution)/shard_map/ppermute | solution.py:28
  65.9 10.1 %collective-permute-start.14 = (bf16[160,640]{1,0:T(8,128)(2,1)S(1)}, bf16[160,640]{1,0:T(8,128)(2,1)}, u32[]{:S(2)}, u32[]{:S(2)}) collective-permute-start(bf16[160,640]{1,0:T(8,128)(2,1)S(1)} %slice.39), channel_id=1, source_target_pairs={{0,12},{4,0},{8,4},{12,8},{1,13},{5,1},{9,5},{13,9},{2,14},{6,2},{... | collective-permute-start | bytes 614408 | tf_op jit(solution)/shard_map/ppermute | solution.py:28
  69.3 17.8 %collective-permute-start.9 = (bf16[3,320,384]{2,1,0:T(8,128)(2,1)}, bf16[3,320,384]{2,1,0:T(8,128)(2,1)S(1)}, u32[]{:S(2)}, u32[]{:S(2)}) collective-permute-start(bf16[3,320,384]{2,1,0:T(8,128)(2,1)} %collective-permute-done.8.refs_14_), channel_id=1, source_target_pairs={{0,32},{32,64},{64,96},{96,128},{128,160},{160,192},{192,224},{224... | collective-permute-start | bytes 2211848 | tf_op jit(solution)/shard_map/ppermute | solution.py:28
  69.6 17.6 %collective-permute-start.12 = (bf16[3,320,384]{2,1,0:T(8,128)(2,1)}, bf16[3,320,384]{2,1,0:T(8,128)(2,1)}, u32[]{:S(2)}, u32[]{:S(2)}) collective-permute-start(bf16[3,320,384]{2,1,0:T(8,128)(2,1)} %collective-permute-done.11.refs_15_), channel_id=1, source_target_pairs={{0,224},{32,0},{64,32},{96,64},{128,96},{160,128},{192,160},{224,1... | collective-permute-start | bytes 2211848 | tf_op jit(solution)/shard_map/ppermute | solution.py:28
  76.0 36.0 %all-to-all-start.1 = ((bf16[8,192,640]{2,1,0:T(8,128)(2,1)}), bf16[8,192,640]{2,1,0:T(8,128)(2,1)S(1)}, u32[]{:S(2)}, u32[]{:S(2)}) async-start(bf16[8,192,640]{2,1,0:T(8,128)(2,1)} %copy-done.1), calls=%async_computation.1 | async-start | bytes 3932160 | tf_op jit(solution)/shard_map/all_to_all | solution.py:23
  87.2 14.4 %collective-permute-start.15 = (bf16[3,160,384]{2,1,0:T(8,128)(2,1)S(1)}, bf16[3,160,384]{2,1,0:T(8,128)(2,1)S(1)}, u32[]{:S(2)}, u32[]{:S(2)}) collective-permute-start(bf16[3,160,384]{2,1,0:T(8,128)(2,1)S(1)} %slice.40), channel_id=1, source_target_pairs={{0,32},{32,64},{64,96},{96,128},{128,160},{160,192},{192,224},{224... | collective-permute-start | bytes 1105928 | tf_op jit(solution)/shard_map/ppermute | solution.py:28
  88.4 13.2 %collective-permute-start.16 = (bf16[3,160,384]{2,1,0:T(8,128)(2,1)S(1)}, bf16[3,160,384]{2,1,0:T(8,128)(2,1)S(1)}, u32[]{:S(2)}, u32[]{:S(2)}) collective-permute-start(bf16[3,160,384]{2,1,0:T(8,128)(2,1)S(1)} %slice.41), channel_id=1, source_target_pairs={{0,224},{32,0},{64,32},{96,64},{128,96},{160,128},{192,160},{224,1... | collective-permute-start | bytes 1105928 | tf_op jit(solution)/shard_map/ppermute | solution.py:28
  105.5 5.2 %collective-permute-start.17 = (bf16[320,1152]{1,0:T(8,128)(2,1)S(1)}, bf16[320,1152]{1,0:T(8,128)(2,1)S(1)}, u32[]{:S(2)}, u32[]{:S(2)}) collective-permute-start(bf16[320,1152]{1,0:T(8,128)(2,1)S(1)} %get-tuple-element.49), channel_id=1, source_target_pairs={{0,16},{16,0},{1,17},{17,1},{2,18},{18,2},{3,19},{19,3},{4,20},{20... | collective-permute-start | bytes 2211848 | tf_op jit(solution)/shard_map/ppermute | solution.py:28
  112.1 31.0 %collective-permute-start.25 = (bf16[8,192,640]{2,1,0:T(8,128)(2,1)S(1)}, bf16[8,192,640]{2,1,0:T(8,128)(2,1)}, u32[]{:S(2)}, u32[]{:S(2)}) collective-permute-start(bf16[8,192,640]{2,1,0:T(8,128)(2,1)S(1)} %all-to-all-done.1.half), channel_id=1, source_target_pairs={{0,16},{16,0},{1,17},{17,1},{2,18},{18,2},{3,19},{19,3},{4,20},{20... | collective-permute-start | bytes 5898248 | tf_op jit(solution)/shard_map/ppermute | solution.py:28
  128.0 9.5 %collective-permute-start.18 = (bf16[320,384]{1,0:T(8,128)(2,1)S(1)}, bf16[320,384]{1,0:T(8,128)(2,1)S(1)}, u32[]{:S(2)}, u32[]{:S(2)}) collective-permute-start(bf16[320,384]{1,0:T(8,128)(2,1)S(1)} %reshape.69.m0), channel_id=1, source_target_pairs={{0,2},{2,0},{1,3},{3,1},{4,6},{6,4},{5,7},{7,5},{8,10},{10,8},{9,1... | collective-permute-start | bytes 737288 | tf_op jit(solution)/shard_map/ppermute | solution.py:28
  130.1 9.2 %collective-permute-start.19 = (bf16[320,384]{1,0:T(8,128)(2,1)S(1)}, bf16[320,384]{1,0:T(8,128)(2,1)S(1)}, u32[]{:S(2)}, u32[]{:S(2)}) collective-permute-start(bf16[320,384]{1,0:T(8,128)(2,1)S(1)} %reshape.69.m0), channel_id=1, source_target_pairs={{0,12},{4,0},{8,4},{12,8},{1,13},{5,1},{9,5},{13,9},{2,14},{6,2},{... | collective-permute-start | bytes 737288 | tf_op jit(solution)/shard_map/ppermute | solution.py:28
  131.5 8.7 %collective-permute-start.20 = (bf16[320,384]{1,0:T(8,128)(2,1)S(1)}, bf16[320,384]{1,0:T(8,128)(2,1)S(1)}, u32[]{:S(2)}, u32[]{:S(2)}) collective-permute-start(bf16[320,384]{1,0:T(8,128)(2,1)S(1)} %reshape.69.m0), channel_id=1, source_target_pairs={{0,4},{4,8},{8,12},{12,0},{1,5},{5,9},{9,13},{13,1},{2,6},{6,10},{... | collective-permute-start | bytes 737288 | tf_op jit(solution)/shard_map/ppermute | solution.py:28
  137.5 7.7 %collective-permute-start.23 = (bf16[320,384]{1,0:T(8,128)(2,1)S(1)}, bf16[320,384]{1,0:T(8,128)(2,1)S(1)}, u32[]{:S(2)}, u32[]{:S(2)}) collective-permute-start(bf16[320,384]{1,0:T(8,128)(2,1)S(1)} %collective-permute-done.18.m1), channel_id=1, source_target_pairs={{0,12},{4,0},{8,4},{12,8},{1,13},{5,1},{9,5},{13,9},{2,14},{6,2},{... | collective-permute-start | bytes 737288 | tf_op jit(solution)/shard_map/ppermute | solution.py:28
  139.0 8.0 %collective-permute-start.24 = (bf16[320,384]{1,0:T(8,128)(2,1)S(1)}, bf16[320,384]{1,0:T(8,128)(2,1)S(1)}, u32[]{:S(2)}, u32[]{:S(2)}) collective-permute-start(bf16[320,384]{1,0:T(8,128)(2,1)S(1)} %collective-permute-done.18.m1), channel_id=1, source_target_pairs={{0,4},{4,8},{8,12},{12,0},{1,5},{5,9},{9,13},{13,1},{2,6},{6,10},{... | collective-permute-start | bytes 737288 | tf_op jit(solution)/shard_map/ppermute | solution.py:28
  140.2 12.4 %collective-permute-start.21 = (bf16[160,384]{1,0:T(8,128)(2,1)S(1)}, bf16[160,384]{1,0:T(8,128)(2,1)S(1)}, u32[]{:S(2)}, u32[]{:S(2)}) collective-permute-start(bf16[160,384]{1,0:T(8,128)(2,1)S(1)} %slice.42), channel_id=1, source_target_pairs={{0,4},{4,8},{8,12},{12,0},{1,5},{5,9},{9,13},{13,1},{2,6},{6,10},{... | collective-permute-start | bytes 368648 | tf_op jit(solution)/shard_map/ppermute | solution.py:28
  140.3 12.3 %collective-permute-start.22 = (bf16[160,384]{1,0:T(8,128)(2,1)S(1)}, bf16[160,384]{1,0:T(8,128)(2,1)S(1)}, u32[]{:S(2)}, u32[]{:S(2)}) collective-permute-start(bf16[160,384]{1,0:T(8,128)(2,1)S(1)} %slice.43), channel_id=1, source_target_pairs={{0,12},{4,0},{8,4},{12,8},{1,13},{5,1},{9,5},{13,9},{2,14},{6,2},{... | collective-permute-start | bytes 368648 | tf_op jit(solution)/shard_map/ppermute | solution.py:28
  147.0 5.6 %collective-permute-start.26 = (bf16[160,384]{1,0:T(8,128)(2,1)S(1)}, bf16[160,384]{1,0:T(8,128)(2,1)S(1)}, u32[]{:S(2)}, u32[]{:S(2)}) collective-permute-start(bf16[160,384]{1,0:T(8,128)(2,1)S(1)} %slice.44), channel_id=1, source_target_pairs={{0,4},{4,8},{8,12},{12,0},{1,5},{5,9},{9,13},{13,1},{2,6},{6,10},{... | collective-permute-start | bytes 368648 | tf_op jit(solution)/shard_map/ppermute | solution.py:28
  147.1 5.5 %collective-permute-start.27 = (bf16[160,384]{1,0:T(8,128)(2,1)S(1)}, bf16[160,384]{1,0:T(8,128)(2,1)S(1)}, u32[]{:S(2)}, u32[]{:S(2)}) collective-permute-start(bf16[160,384]{1,0:T(8,128)(2,1)S(1)} %slice.45), channel_id=1, source_target_pairs={{0,12},{4,0},{8,4},{12,8},{1,13},{5,1},{9,5},{13,9},{2,14},{6,2},{... | collective-permute-start | bytes 368648 | tf_op jit(solution)/shard_map/ppermute | solution.py:28
  (16 other events, 202.7 us)

commit v14 on v13

--- a/solution.py
+++ b/solution.py
@@ -316,7 +316,6 @@
     other_far = onward(*other_side)
     blocks = column_blocks(w_out, core1, width)
     other_far, blocks = lax.optimization_barrier((other_far, blocks))
-    up3, down3, other_far = lax.optimization_barrier((up3, down3, other_far))
     up4 = shift(up3[:, : depth // 2], "z", 1)
     down4 = shift(down3[:, depth // 2 :], "z", -1)
 

time: 173 us -> 173 us (level)
  no operation moved by 1% of the time
where the time goes in v14:
time: 173 us; the launch traced here: 172 us
  waiting for transfers between devices  53.3 us (31%)
  starting transfers between devices  51.3 us (30%)
  blocking collectives  31.2 us (18%)
  Pallas kernels  20.9 us (12%)
  local copies, waits for them, and re-layouts  10.7 us (6%)
  other arithmetic  2.57 us (1%)
    ppermute x28, waiting for transfers between devices, shift(): return lax.ppermute(x, axis, [(i, (i + by) % n) for i in range(n)])  39.5 us
    ppermute x28, starting transfers between devices, shift(): return lax.ppermute(x, axis, [(i, (i + by) % n) for i in range(n)])  37.7 us
    all_to_all x2, blocking collectives, exchange(): return lax.all_to_all(x, axis, split_axis=0, concat_axis=0, tiled=True)  31.2 us
    all_to_all x2, waiting for transfers between devices, exchange(): return lax.all_to_all(x, axis, split_axis=0, concat_axis=0, tiled=True)  13.9 us
    all_to_all x2, starting transfers between devices, exchange(): return lax.all_to_all(x, axis, split_axis=0, concat_axis=0, tiled=True)  13.6 us
    pallas_call x1, Pallas kernels, project(): pl.pallas_call(kernel, in_specs=[SMEM] + [ANYWHERE] * len(operands), out_...  10.5 us
    unnamed x37, local copies, waits for them, and re-layouts  6.99 us
    pallas_call x2, Pallas kernels, near(): pl.pallas_call(kernel, in_specs=[SMEM] + [WHOLE] * len(operands), out_spe...  4.69 us
  transfers between devices with their start and end apart: 30, of which 11 were waited for; matrix products, arithmetic and copies ran while one was open for 1% of the time, Pallas kernels for 10%

profile of v14, /device:TPU:1, one launch (start us, length us, event | category | flops | bytes accessed | tf_op | source)
XLA Modules:
  0.0 172.3 jit_solution(17808241816620770455)
XLA Ops:
  4.7 10.0 %all-to-all-start = ((bf16[16,20,640]{2,1,0:T(8,128)(2,1)}), bf16[16,20,640]{2,1,0:T(8,128)(2,1)S(1)}, u32[]{:S(2)}, u32[]{:S(2)}) async-start(bf16[16,20,640]{2,1,0:T(8,128)(2,1)} %copy.18), calls=%async_computation | async-start | bytes 983040 | tf_op jit(solution)/shard_map/all_to_all | solution.py:23
  14.6 1.5 collective-permute-start.9
  17.4 13.8 %all-to-all-done = bf16[16,20,640]{2,1,0:T(8,128)(2,1)S(1)} async-done(((bf16[16,20,640]{2,1,0:T(8,128)(2,1)}), bf16[16,20,640]{2,1,0:T(8,128)(2,1)S(1)}, u32[]{:S(2)}, u32[]{:S(2)}) %all-to-all-start) | async-done | bytes 409632 | tf_op jit(solution)/shard_map/all_to_all | solution.py:23
  31.4 3.0 %collective-permute-start = (bf16[320,640]{1,0:T(8,128)(2,1)S(1)}, bf16[320,640]{1,0:T(8,128)(2,1)}, u32[]{:S(2)}, u32[]{:S(2)}) collective-permute-start(bf16[320,640]{1,0:T(8,128)(2,1)S(1)} %reshape.68.refs_1_), channel_id=1, source_target_pairs={{0,2},{2,0},{1,3},{3,1},{4,6},{6,4},{5,7},{7,5},{8,10},{10,8},{9,1... | collective-permute-start | bytes 1228808 | tf_op jit(solution)/shard_map/ppermute | solution.py:28
  34.4 2.5 %collective-permute-start.1 = (bf16[320,640]{1,0:T(8,128)(2,1)S(1)}, bf16[320,640]{1,0:T(8,128)(2,1)S(1)}, u32[]{:S(2)}, u32[]{:S(2)}) collective-permute-start(bf16[320,640]{1,0:T(8,128)(2,1)S(1)} %reshape.68.refs_1_), channel_id=1, source_target_pairs={{0,12},{4,0},{8,4},{12,8},{1,13},{5,1},{9,5},{13,9},{2,14},{6,2},{... | collective-permute-start | bytes 1228808 | tf_op jit(solution)/shard_map/ppermute | solution.py:28
  36.9 7.8 %collective-permute-done.9.refs_12_ = bf16[3,320,384]{2,1,0:T(8,128)(2,1)} collective-permute-done((bf16[3,320,384]{2,1,0:T(8,128)(2,1)S(1)}, bf16[3,320,384]{2,1,0:T(8,128)(2,1)}, u32[]{:S(2)}, u32[]{:S(2)}) %collective-permute-start.9) | collective-permute-done | bytes 737312 | tf_op jit(solution)/shard_map/ppermute | solution.py:28
  44.7 2.7 %collective-permute-start.12 = (bf16[3,320,384]{2,1,0:T(8,128)(2,1)}, bf16[3,320,384]{2,1,0:T(8,128)(2,1)}, u32[]{:S(2)}, u32[]{:S(2)}) collective-permute-start(bf16[3,320,384]{2,1,0:T(8,128)(2,1)} %collective-permute-done.10.refs_13_), channel_id=1, source_target_pairs={{0,224},{32,0},{64,32},{96,64},{128,96},{160,128},{192,160},{224,1... | collective-permute-start | bytes 2211848 | tf_op jit(solution)/shard_map/ppermute | solution.py:28
  47.3 2.1 %collective-permute-done.2.refs_3_ = bf16[320,640]{1,0:T(8,128)(2,1)S(1)} collective-permute-done((bf16[320,640]{1,0:T(8,128)(2,1)S(1)}, bf16[320,640]{1,0:T(8,128)(2,1)S(1)}, u32[]{:S(2)}, u32[]{:S(2)}) %collective-permute-start.2) | collective-permute-done | bytes 409632 | tf_op jit(solution)/shard_map/ppermute | solution.py:28
  49.5 2.7 %collective-permute-start.3 = (bf16[320,640]{1,0:T(8,128)(2,1)}, bf16[320,640]{1,0:T(8,128)(2,1)S(1)}, u32[]{:S(2)}, u32[]{:S(2)}) collective-permute-start(bf16[320,640]{1,0:T(8,128)(2,1)} %collective-permute-done.refs_6_), channel_id=1, source_target_pairs={{0,12},{4,0},{8,4},{12,8},{1,13},{5,1},{9,5},{13,9},{2,14},{6,2},{... | collective-permute-start | bytes 1228808 | tf_op jit(solution)/shard_map/ppermute | solution.py:28
  52.2 4.9 %collective-permute-done.5.refs_4_ = bf16[160,640]{1,0:T(8,128)(2,1)S(1)} collective-permute-done((bf16[160,640]{1,0:T(8,128)(2,1)S(1)}, bf16[160,640]{1,0:T(8,128)(2,1)S(1)}, u32[]{:S(2)}, u32[]{:S(2)}) %collective-permute-start.5) | collective-permute-done | bytes 204832 | tf_op jit(solution)/shard_map/ppermute | solution.py:28
  57.6 7.3 %collective-permute-done.6.refs_5_ = bf16[160,640]{1,0:T(8,128)(2,1)S(1)} collective-permute-done((bf16[160,640]{1,0:T(8,128)(2,1)S(1)}, bf16[160,640]{1,0:T(8,128)(2,1)S(1)}, u32[]{:S(2)}, u32[]{:S(2)}) %collective-permute-start.6) | collective-permute-done | bytes 204832 | tf_op jit(solution)/shard_map/ppermute | solution.py:28
  65.9 3.3 %collective-permute-start.8 = (bf16[160,640]{1,0:T(8,128)(2,1)S(1)}, bf16[160,640]{1,0:T(8,128)(2,1)}, u32[]{:S(2)}, u32[]{:S(2)}) collective-permute-start(bf16[160,640]{1,0:T(8,128)(2,1)S(1)} %slice.39), channel_id=1, source_target_pairs={{0,12},{4,0},{8,4},{12,8},{1,13},{5,1},{9,5},{13,9},{2,14},{6,2},{... | collective-permute-start | bytes 614408 | tf_op jit(solution)/shard_map/ppermute | solution.py:28
  69.6 2.7 %collective-permute-start.14 = (bf16[3,320,384]{2,1,0:T(8,128)(2,1)}, bf16[3,320,384]{2,1,0:T(8,128)(2,1)}, u32[]{:S(2)}, u32[]{:S(2)}) collective-permute-start(bf16[3,320,384]{2,1,0:T(8,128)(2,1)} %collective-permute-done.12.refs_15_), channel_id=1, source_target_pairs={{0,224},{32,0},{64,32},{96,64},{128,96},{160,128},{192,160},{224,1... | collective-permute-start | bytes 2211848 | tf_op jit(solution)/shard_map/ppermute | solution.py:28
  72.2 2.1 %copy-done.2 = bf16[384,5120]{1,0:T(8,128)(2,1)S(1)} copy-done((bf16[384,5120]{1,0:T(8,128)(2,1)S(1)}, bf16[384,5120]{1,0:T(8,128)(2,1)}, u32[]{:S(2)}) %copy-start.2) | copy-done | bytes 3932184
  76.0 3.6 %all-to-all-start.1 = ((bf16[8,192,640]{2,1,0:T(8,128)(2,1)}), bf16[8,192,640]{2,1,0:T(8,128)(2,1)S(1)}, u32[]{:S(2)}, u32[]{:S(2)}) async-start(bf16[8,192,640]{2,1,0:T(8,128)(2,1)} %copy-done.1), calls=%async_computation.1 | async-start | bytes 3932160 | tf_op jit(solution)/shard_map/all_to_all | solution.py:23
  79.7 7.5 %collective-permute-done.13.refs_16_ = bf16[3,320,384]{2,1,0:T(8,128)(2,1)S(1)} collective-permute-done((bf16[3,320,384]{2,1,0:T(8,128)(2,1)}, bf16[3,320,384]{2,1,0:T(8,128)(2,1)S(1)}, u32[]{:S(2)}, u32[]{:S(2)}) %collective-permute-start.13) | collective-permute-done | bytes 737312 | tf_op jit(solution)/shard_map/ppermute | solution.py:28
  88.4 2.6 %collective-permute-start.16 = (bf16[3,160,384]{2,1,0:T(8,128)(2,1)S(1)}, bf16[3,160,384]{2,1,0:T(8,128)(2,1)S(1)}, u32[]{:S(2)}, u32[]{:S(2)}) collective-permute-start(bf16[3,160,384]{2,1,0:T(8,128)(2,1)S(1)} %slice.49), channel_id=1, source_target_pairs={{0,224},{32,0},{64,32},{96,64},{128,96},{160,128},{192,160},{224,1... | collective-permute-start | bytes 1105928 | tf_op jit(solution)/shard_map/ppermute | solution.py:28
  91.0 10.5 %shard_map.114 = (f32[640,1152]{1,0:T(8,128)}, bf16[320,640]{1,0:T(8,128)(2,1)}) custom-call(s32[8]{0:T(128)} %xor_add_fusion.refs_0_, bf16[320,640]{1,0:T(8,128)(2,1)} %copy-done.7, bf16[320,640]{1,0:T(8,128)(2,1)} %copy-done.8, bf16[320,640]{1,0:T(8,128)(2,1)} %copy-done.9, bf16[160,640]{1,0:T(8,128)(2,1)} %copy-done.13, bf16[160,640]{1,0:T(8,128)(2,1)} %copy-done.14, ...), custom_call_target="tpu_custom_call" | custom-call | tf_op jit(solution)/shard_map/pallas_call | solution.py:105
  101.6 1.8 %copy-done.3 = f32[640,1152]{1,0:T(8,128)S(1)} copy-done((f32[640,1152]{1,0:T(8,128)S(1)}, f32[640,1152]{1,0:T(8,128)}, u32[]{:S(2)}) %copy-start.3) | copy-done | bytes 2949144
  105.5 3.4 %collective-permute-start.17 = (bf16[320,1152]{1,0:T(8,128)(2,1)S(1)}, bf16[320,1152]{1,0:T(8,128)(2,1)S(1)}, u32[]{:S(2)}, u32[]{:S(2)}) collective-permute-start(bf16[320,1152]{1,0:T(8,128)(2,1)S(1)} %get-tuple-element.41), channel_id=1, source_target_pairs={{0,16},{16,0},{1,17},{17,1},{2,18},{18,2},{3,19},{19,3},{4,20},{20... | collective-permute-start | bytes 2211848 | tf_op jit(solution)/shard_map/ppermute | solution.py:28
  109.0 1.7 collective-permute-done.17.other_ref
  112.6 15.0 %all_to_all.20 = bf16[16,20,384]{2,1,0:T(8,128)(2,1)S(1)} all-to-all(bf16[16,20,384]{2,1,0:T(8,128)(2,1)S(1)} %shard_map.116), channel_id=1, replica_groups=mesh['z'=8,'core'=2,'x'=4,'yhi'=2,'dp'=2] {'z','core'}, dimensions={0} | all-to-all | bytes 491520 | tf_op jit(solution)/shard_map/all_to_all | solution.py:23
  127.6 2.5 %collective-permute-start.18 = (bf16[320,384]{1,0:T(8,128)(2,1)S(1)}, bf16[320,384]{1,0:T(8,128)(2,1)S(1)}, u32[]{:S(2)}, u32[]{:S(2)}) collective-permute-start(bf16[320,384]{1,0:T(8,128)(2,1)S(1)} %reshape.69.m0), channel_id=1, source_target_pairs={{0,2},{2,0},{1,3},{3,1},{4,6},{6,4},{5,7},{7,5},{8,10},{10,8},{9,1... | collective-permute-start | bytes 737288 | tf_op jit(solution)/shard_map/ppermute | solution.py:28
  131.6 5.3 %collective-permute-done.18.m1 = bf16[320,384]{1,0:T(8,128)(2,1)S(1)} collective-permute-done((bf16[320,384]{1,0:T(8,128)(2,1)S(1)}, bf16[320,384]{1,0:T(8,128)(2,1)S(1)}, u32[]{:S(2)}, u32[]{:S(2)}) %collective-permute-start.18) | collective-permute-done | bytes 245792 | tf_op jit(solution)/shard_map/ppermute | solution.py:28
  136.9 1.5 collective-permute-start.23
  138.7 1.5 collective-permute-done.20.l0
  140.3 2.7 %collective-permute-start.22 = (bf16[160,384]{1,0:T(8,128)(2,1)S(1)}, bf16[160,384]{1,0:T(8,128)(2,1)S(1)}, u32[]{:S(2)}, u32[]{:S(2)}) collective-permute-start(bf16[160,384]{1,0:T(8,128)(2,1)S(1)} %slice.43), channel_id=1, source_target_pairs={{0,12},{4,0},{8,4},{12,8},{1,13},{5,1},{9,5},{13,9},{2,14},{6,2},{... | collective-permute-start | bytes 368648 | tf_op jit(solution)/shard_map/ppermute | solution.py:28
  143.1 2.1 %shard_map.117.own = f32[320,640]{1,0:T(8,128)S(1)} custom-call(s32[3]{0:T(128)S(1)} %pad_add_fusion.where, bf16[320,384]{1,0:T(8,128)(2,1)S(1)} %reshape.69.m0, bf16[320,384]{1,0:T(8,128)(2,1)S(1)} %collective-permute-done.18.m1, bf16[8,192,640]{2,1,0:T(8,128)(2,1)S(1)} %all-to-all-done.1.half, bf16[8,192,640]{2,1,0:T(8,128)(2,1)} %collective-permute-done.25.other), custom_call_target="tpu_custom_call" | custom-call | tf_op jit(solution)/shard_map/pallas_call | solution.py:232
  146.6 2.7 %collective-permute-start.27 = (bf16[160,384]{1,0:T(8,128)(2,1)S(1)}, bf16[160,384]{1,0:T(8,128)(2,1)S(1)}, u32[]{:S(2)}, u32[]{:S(2)}) collective-permute-start(bf16[160,384]{1,0:T(8,128)(2,1)S(1)} %slice.45), channel_id=1, source_target_pairs={{0,12},{4,0},{8,4},{12,8},{1,13},{5,1},{9,5},{13,9},{2,14},{6,2},{... | collective-permute-start | bytes 368648 | tf_op jit(solution)/shard_map/ppermute | solution.py:28
  149.5 2.6 %shard_map.118.acc = f32[320,640]{1,0:T(8,128)S(1)} custom-call(s32[3]{0:T(128)S(1)} %pad_add_fusion.where, bf16[320,384]{1,0:T(8,128)(2,1)S(1)} %collective-permute-done.19.r0, bf16[320,384]{1,0:T(8,128)(2,1)S(1)} %collective-permute-done.23.r1, bf16[320,384]{1,0:T(8,128)(2,1)S(1)} %collective-permute-done.20.l0, ...), custom_call_target="tpu_custom_call" | custom-call | tf_op jit(solution)/shard_map/pallas_call | solution.py:232
  152.1 2.9 %shard_map.119 = (bf16[320,640]{1,0:T(8,128)(2,1)}, f32[32,2,672]{2,1,0:T(2,128)S(1)}) custom-call(s32[3]{0:T(128)S(1)} %pad_add_fusion.where, bf16[160,384]{1,0:T(8,128)(2,1)S(1)} %collective-permute-done.21.t0, bf16[160,384]{1,0:T(8,128)(2,1)S(1)} %collective-permute-done.22.w0, bf16[160,384]{1,0:T(8,128)(2,1)S(1)} %collective-permute-done.26.t1, ...), custom_call_target="tpu_custom_call" | custom-call | tf_op jit(solution)/shard_map/pallas_call | solution.py:245
  155.1 16.2 %all_to_all.21 = f32[32,2,672]{2,1,0:T(2,128)S(1)} all-to-all(f32[32,2,672]{2,1,0:T(2,128)S(1)} %get-tuple-element.51), channel_id=1, replica_groups=mesh['z'=8,'core'=2,'x'=4,'yhi'=2,'dp'=2] {'z','core','dp'}, dimensions={0} | all-to-all | bytes 344064 | tf_op jit(solution)/shard_map/all_to_all | solution.py:23
  (100 shorter events, 18.7 us)
Async XLA Ops:
  0.6 148.7 %copy-start = (f32[32,640]{1,0:T(8,128)S(1)}, f32[32,640]{1,0:T(8,128)}, u32[]{:S(2)}) copy-start(f32[32,640]{1,0:T(8,128)} %param.17) | copy-start | bytes 245764
  3.8 53.3 %copy-start.15 = (s32[8]{0:T(128)S(1)}, s32[8]{0:T(128)}, u32[]{:S(2)}) copy-start(s32[8]{0:T(128)} %constant.52.clone) | copy-start | bytes 100
  4.7 26.6 %all-to-all-start = ((bf16[16,20,640]{2,1,0:T(8,128)(2,1)}), bf16[16,20,640]{2,1,0:T(8,128)(2,1)S(1)}, u32[]{:S(2)}, u32[]{:S(2)}) async-start(bf16[16,20,640]{2,1,0:T(8,128)(2,1)} %copy.18), calls=%async_computation | async-start | bytes 983040 | tf_op jit(solution)/shard_map/all_to_all | solution.py:23
  14.6 30.0 %collective-permute-start.9 = (bf16[3,320,384]{2,1,0:T(8,128)(2,1)S(1)}, bf16[3,320,384]{2,1,0:T(8,128)(2,1)}, u32[]{:S(2)}, u32[]{:S(2)}) collective-permute-start(bf16[3,320,384]{2,1,0:T(8,128)(2,1)S(1)} %bitcast.27), channel_id=1, source_target_pairs={{0,32},{32,64},{64,96},{96,128},{128,160},{160,192},{192,224},{224... | collective-permute-start | bytes 2211848 | tf_op jit(solution)/shard_map/ppermute | solution.py:28
  16.1 28.5 %collective-permute-start.10 = (bf16[3,320,384]{2,1,0:T(8,128)(2,1)S(1)}, bf16[3,320,384]{2,1,0:T(8,128)(2,1)}, u32[]{:S(2)}, u32[]{:S(2)}) collective-permute-start(bf16[3,320,384]{2,1,0:T(8,128)(2,1)S(1)} %bitcast.28), channel_id=1, source_target_pairs={{0,224},{32,0},{64,32},{96,64},{128,96},{160,128},{192,160},{224,1... | collective-permute-start | bytes 2211848 | tf_op jit(solution)/shard_map/ppermute | solution.py:28
  31.4 16.0 %collective-permute-start = (bf16[320,640]{1,0:T(8,128)(2,1)S(1)}, bf16[320,640]{1,0:T(8,128)(2,1)}, u32[]{:S(2)}, u32[]{:S(2)}) collective-permute-start(bf16[320,640]{1,0:T(8,128)(2,1)S(1)} %reshape.68.refs_1_), channel_id=1, source_target_pairs={{0,2},{2,0},{1,3},{3,1},{4,6},{6,4},{5,7},{7,5},{8,10},{10,8},{9,1... | collective-permute-start | bytes 1228808 | tf_op jit(solution)/shard_map/ppermute | solution.py:28
  34.4 13.0 %collective-permute-start.1 = (bf16[320,640]{1,0:T(8,128)(2,1)S(1)}, bf16[320,640]{1,0:T(8,128)(2,1)S(1)}, u32[]{:S(2)}, u32[]{:S(2)}) collective-permute-start(bf16[320,640]{1,0:T(8,128)(2,1)S(1)} %reshape.68.refs_1_), channel_id=1, source_target_pairs={{0,12},{4,0},{8,4},{12,8},{1,13},{5,1},{9,5},{13,9},{2,14},{6,2},{... | collective-permute-start | bytes 1228808 | tf_op jit(solution)/shard_map/ppermute | solution.py:28
  36.9 12.6 %collective-permute-start.2 = (bf16[320,640]{1,0:T(8,128)(2,1)S(1)}, bf16[320,640]{1,0:T(8,128)(2,1)S(1)}, u32[]{:S(2)}, u32[]{:S(2)}) collective-permute-start(bf16[320,640]{1,0:T(8,128)(2,1)S(1)} %reshape.68.refs_1_), channel_id=1, source_target_pairs={{0,4},{4,8},{8,12},{12,0},{1,5},{5,9},{9,13},{13,1},{2,6},{6,10},{... | collective-permute-start | bytes 1228808 | tf_op jit(solution)/shard_map/ppermute | solution.py:28
  44.6 24.6 %collective-permute-start.11 = (bf16[3,320,384]{2,1,0:T(8,128)(2,1)}, bf16[3,320,384]{2,1,0:T(8,128)(2,1)}, u32[]{:S(2)}, u32[]{:S(2)}) collective-permute-start(bf16[3,320,384]{2,1,0:T(8,128)(2,1)} %collective-permute-done.9.refs_12_), channel_id=1, source_target_pairs={{0,32},{32,64},{64,96},{96,128},{128,160},{160,192},{192,224},{224... | collective-permute-start | bytes 2211848 | tf_op jit(solution)/shard_map/ppermute | solution.py:28
  44.7 24.9 %collective-permute-start.12 = (bf16[3,320,384]{2,1,0:T(8,128)(2,1)}, bf16[3,320,384]{2,1,0:T(8,128)(2,1)}, u32[]{:S(2)}, u32[]{:S(2)}) collective-permute-start(bf16[3,320,384]{2,1,0:T(8,128)(2,1)} %collective-permute-done.10.refs_13_), channel_id=1, source_target_pairs={{0,224},{32,0},{64,32},{96,64},{128,96},{160,128},{192,160},{224,1... | collective-permute-start | bytes 2211848 | tf_op jit(solution)/shard_map/ppermute | solution.py:28
  49.4 7.7 %collective-permute-start.5 = (bf16[160,640]{1,0:T(8,128)(2,1)S(1)}, bf16[160,640]{1,0:T(8,128)(2,1)S(1)}, u32[]{:S(2)}, u32[]{:S(2)}) collective-permute-start(bf16[160,640]{1,0:T(8,128)(2,1)S(1)} %slice.36), channel_id=1, source_target_pairs={{0,4},{4,8},{8,12},{12,0},{1,5},{5,9},{9,13},{13,1},{2,6},{6,10},{... | collective-permute-start | bytes 614408 | tf_op jit(solution)/shard_map/ppermute | solution.py:28
  49.5 15.4 %collective-permute-start.3 = (bf16[320,640]{1,0:T(8,128)(2,1)}, bf16[320,640]{1,0:T(8,128)(2,1)S(1)}, u32[]{:S(2)}, u32[]{:S(2)}) collective-permute-start(bf16[320,640]{1,0:T(8,128)(2,1)} %collective-permute-done.refs_6_), channel_id=1, source_target_pairs={{0,12},{4,0},{8,4},{12,8},{1,13},{5,1},{9,5},{13,9},{2,14},{6,2},{... | collective-permute-start | bytes 1228808 | tf_op jit(solution)/shard_map/ppermute | solution.py:28
  52.2 13.6 %collective-permute-start.4 = (bf16[320,640]{1,0:T(8,128)(2,1)}, bf16[320,640]{1,0:T(8,128)(2,1)S(1)}, u32[]{:S(2)}, u32[]{:S(2)}) collective-permute-start(bf16[320,640]{1,0:T(8,128)(2,1)} %collective-permute-done.refs_6_), channel_id=1, source_target_pairs={{0,4},{4,8},{8,12},{12,0},{1,5},{5,9},{9,13},{13,1},{2,6},{6,10},{... | collective-permute-start | bytes 1228808 | tf_op jit(solution)/shard_map/ppermute | solution.py:28
  57.1 7.8 %collective-permute-start.6 = (bf16[160,640]{1,0:T(8,128)(2,1)S(1)}, bf16[160,640]{1,0:T(8,128)(2,1)S(1)}, u32[]{:S(2)}, u32[]{:S(2)}) collective-permute-start(bf16[160,640]{1,0:T(8,128)(2,1)S(1)} %slice.37), channel_id=1, source_target_pairs={{0,12},{4,0},{8,4},{12,8},{1,13},{5,1},{9,5},{13,9},{2,14},{6,2},{... | collective-permute-start | bytes 614408 | tf_op jit(solution)/shard_map/ppermute | solution.py:28
  65.8 10.2 %collective-permute-start.7 = (bf16[160,640]{1,0:T(8,128)(2,1)S(1)}, bf16[160,640]{1,0:T(8,128)(2,1)}, u32[]{:S(2)}, u32[]{:S(2)}) collective-permute-start(bf16[160,640]{1,0:T(8,128)(2,1)S(1)} %slice.38), channel_id=1, source_target_pairs={{0,4},{4,8},{8,12},{12,0},{1,5},{5,9},{9,13},{13,1},{2,6},{6,10},{... | collective-permute-start | bytes 614408 | tf_op jit(solution)/shard_map/ppermute | solution.py:28
  65.9 10.1 %collective-permute-start.8 = (bf16[160,640]{1,0:T(8,128)(2,1)S(1)}, bf16[160,640]{1,0:T(8,128)(2,1)}, u32[]{:S(2)}, u32[]{:S(2)}) collective-permute-start(bf16[160,640]{1,0:T(8,128)(2,1)S(1)} %slice.39), channel_id=1, source_target_pairs={{0,12},{4,0},{8,4},{12,8},{1,13},{5,1},{9,5},{13,9},{2,14},{6,2},{... | collective-permute-start | bytes 614408 | tf_op jit(solution)/shard_map/ppermute | solution.py:28
  69.3 17.8 %collective-permute-start.13 = (bf16[3,320,384]{2,1,0:T(8,128)(2,1)}, bf16[3,320,384]{2,1,0:T(8,128)(2,1)S(1)}, u32[]{:S(2)}, u32[]{:S(2)}) collective-permute-start(bf16[3,320,384]{2,1,0:T(8,128)(2,1)} %collective-permute-done.11.refs_14_), channel_id=1, source_target_pairs={{0,32},{32,64},{64,96},{96,128},{128,160},{160,192},{192,224},{224... | collective-permute-start | bytes 2211848 | tf_op jit(solution)/shard_map/ppermute | solution.py:28
  69.6 17.7 %collective-permute-start.14 = (bf16[3,320,384]{2,1,0:T(8,128)(2,1)}, bf16[3,320,384]{2,1,0:T(8,128)(2,1)}, u32[]{:S(2)}, u32[]{:S(2)}) collective-permute-start(bf16[3,320,384]{2,1,0:T(8,128)(2,1)} %collective-permute-done.12.refs_15_), channel_id=1, source_target_pairs={{0,224},{32,0},{64,32},{96,64},{128,96},{160,128},{192,160},{224,1... | collective-permute-start | bytes 2211848 | tf_op jit(solution)/shard_map/ppermute | solution.py:28
  76.0 36.0 %all-to-all-start.1 = ((bf16[8,192,640]{2,1,0:T(8,128)(2,1)}), bf16[8,192,640]{2,1,0:T(8,128)(2,1)S(1)}, u32[]{:S(2)}, u32[]{:S(2)}) async-start(bf16[8,192,640]{2,1,0:T(8,128)(2,1)} %copy-done.1), calls=%async_computation.1 | async-start | bytes 3932160 | tf_op jit(solution)/shard_map/all_to_all | solution.py:23
  87.2 14.4 %collective-permute-start.15 = (bf16[3,160,384]{2,1,0:T(8,128)(2,1)S(1)}, bf16[3,160,384]{2,1,0:T(8,128)(2,1)S(1)}, u32[]{:S(2)}, u32[]{:S(2)}) collective-permute-start(bf16[3,160,384]{2,1,0:T(8,128)(2,1)S(1)} %slice.48), channel_id=1, source_target_pairs={{0,32},{32,64},{64,96},{96,128},{128,160},{160,192},{192,224},{224... | collective-permute-start | bytes 1105928 | tf_op jit(solution)/shard_map/ppermute | solution.py:28
  88.4 13.2 %collective-permute-start.16 = (bf16[3,160,384]{2,1,0:T(8,128)(2,1)S(1)}, bf16[3,160,384]{2,1,0:T(8,128)(2,1)S(1)}, u32[]{:S(2)}, u32[]{:S(2)}) collective-permute-start(bf16[3,160,384]{2,1,0:T(8,128)(2,1)S(1)} %slice.49), channel_id=1, source_target_pairs={{0,224},{32,0},{64,32},{96,64},{128,96},{160,128},{192,160},{224,1... | collective-permute-start | bytes 1105928 | tf_op jit(solution)/shard_map/ppermute | solution.py:28
  105.5 5.2 %collective-permute-start.17 = (bf16[320,1152]{1,0:T(8,128)(2,1)S(1)}, bf16[320,1152]{1,0:T(8,128)(2,1)S(1)}, u32[]{:S(2)}, u32[]{:S(2)}) collective-permute-start(bf16[320,1152]{1,0:T(8,128)(2,1)S(1)} %get-tuple-element.41), channel_id=1, source_target_pairs={{0,16},{16,0},{1,17},{17,1},{2,18},{18,2},{3,19},{19,3},{4,20},{20... | collective-permute-start | bytes 2211848 | tf_op jit(solution)/shard_map/ppermute | solution.py:28
  112.1 31.0 %collective-permute-start.25 = (bf16[8,192,640]{2,1,0:T(8,128)(2,1)S(1)}, bf16[8,192,640]{2,1,0:T(8,128)(2,1)}, u32[]{:S(2)}, u32[]{:S(2)}) collective-permute-start(bf16[8,192,640]{2,1,0:T(8,128)(2,1)S(1)} %all-to-all-done.1.half), channel_id=1, source_target_pairs={{0,16},{16,0},{1,17},{17,1},{2,18},{18,2},{3,19},{19,3},{4,20},{20... | collective-permute-start | bytes 5898248 | tf_op jit(solution)/shard_map/ppermute | solution.py:28
  127.6 9.3 %collective-permute-start.18 = (bf16[320,384]{1,0:T(8,128)(2,1)S(1)}, bf16[320,384]{1,0:T(8,128)(2,1)S(1)}, u32[]{:S(2)}, u32[]{:S(2)}) collective-permute-start(bf16[320,384]{1,0:T(8,128)(2,1)S(1)} %reshape.69.m0), channel_id=1, source_target_pairs={{0,2},{2,0},{1,3},{3,1},{4,6},{6,4},{5,7},{7,5},{8,10},{10,8},{9,1... | collective-permute-start | bytes 737288 | tf_op jit(solution)/shard_map/ppermute | solution.py:28
  130.1 8.6 %collective-permute-start.19 = (bf16[320,384]{1,0:T(8,128)(2,1)S(1)}, bf16[320,384]{1,0:T(8,128)(2,1)S(1)}, u32[]{:S(2)}, u32[]{:S(2)}) collective-permute-start(bf16[320,384]{1,0:T(8,128)(2,1)S(1)} %reshape.69.m0), channel_id=1, source_target_pairs={{0,12},{4,0},{8,4},{12,8},{1,13},{5,1},{9,5},{13,9},{2,14},{6,2},{... | collective-permute-start | bytes 737288 | tf_op jit(solution)/shard_map/ppermute | solution.py:28
  131.5 8.7 %collective-permute-start.20 = (bf16[320,384]{1,0:T(8,128)(2,1)S(1)}, bf16[320,384]{1,0:T(8,128)(2,1)S(1)}, u32[]{:S(2)}, u32[]{:S(2)}) collective-permute-start(bf16[320,384]{1,0:T(8,128)(2,1)S(1)} %reshape.69.m0), channel_id=1, source_target_pairs={{0,4},{4,8},{8,12},{12,0},{1,5},{5,9},{9,13},{13,1},{2,6},{6,10},{... | collective-permute-start | bytes 737288 | tf_op jit(solution)/shard_map/ppermute | solution.py:28
  136.9 8.3 %collective-permute-start.23 = (bf16[320,384]{1,0:T(8,128)(2,1)S(1)}, bf16[320,384]{1,0:T(8,128)(2,1)S(1)}, u32[]{:S(2)}, u32[]{:S(2)}) collective-permute-start(bf16[320,384]{1,0:T(8,128)(2,1)S(1)} %collective-permute-done.18.m1), channel_id=1, source_target_pairs={{0,12},{4,0},{8,4},{12,8},{1,13},{5,1},{9,5},{13,9},{2,14},{6,2},{... | collective-permute-start | bytes 737288 | tf_op jit(solution)/shard_map/ppermute | solution.py:28
  138.4 8.0 %collective-permute-start.24 = (bf16[320,384]{1,0:T(8,128)(2,1)S(1)}, bf16[320,384]{1,0:T(8,128)(2,1)S(1)}, u32[]{:S(2)}, u32[]{:S(2)}) collective-permute-start(bf16[320,384]{1,0:T(8,128)(2,1)S(1)} %collective-permute-done.18.m1), channel_id=1, source_target_pairs={{0,4},{4,8},{8,12},{12,0},{1,5},{5,9},{9,13},{13,1},{2,6},{6,10},{... | collective-permute-start | bytes 737288 | tf_op jit(solution)/shard_map/ppermute | solution.py:28
  140.2 11.8 %collective-permute-start.21 = (bf16[160,384]{1,0:T(8,128)(2,1)S(1)}, bf16[160,384]{1,0:T(8,128)(2,1)S(1)}, u32[]{:S(2)}, u32[]{:S(2)}) collective-permute-start(bf16[160,384]{1,0:T(8,128)(2,1)S(1)} %slice.42), channel_id=1, source_target_pairs={{0,4},{4,8},{8,12},{12,0},{1,5},{5,9},{9,13},{13,1},{2,6},{6,10},{... | collective-permute-start | bytes 368648 | tf_op jit(solution)/shard_map/ppermute | solution.py:28
  140.3 11.7 %collective-permute-start.22 = (bf16[160,384]{1,0:T(8,128)(2,1)S(1)}, bf16[160,384]{1,0:T(8,128)(2,1)S(1)}, u32[]{:S(2)}, u32[]{:S(2)}) collective-permute-start(bf16[160,384]{1,0:T(8,128)(2,1)S(1)} %slice.43), channel_id=1, source_target_pairs={{0,12},{4,0},{8,4},{12,8},{1,13},{5,1},{9,5},{13,9},{2,14},{6,2},{... | collective-permute-start | bytes 368648 | tf_op jit(solution)/shard_map/ppermute | solution.py:28
  146.5 5.6 %collective-permute-start.26 = (bf16[160,384]{1,0:T(8,128)(2,1)S(1)}, bf16[160,384]{1,0:T(8,128)(2,1)S(1)}, u32[]{:S(2)}, u32[]{:S(2)}) collective-permute-start(bf16[160,384]{1,0:T(8,128)(2,1)S(1)} %slice.44), channel_id=1, source_target_pairs={{0,4},{4,8},{8,12},{12,0},{1,5},{5,9},{9,13},{13,1},{2,6},{6,10},{... | collective-permute-start | bytes 368648 | tf_op jit(solution)/shard_map/ppermute | solution.py:28
  146.6 5.5 %collective-permute-start.27 = (bf16[160,384]{1,0:T(8,128)(2,1)S(1)}, bf16[160,384]{1,0:T(8,128)(2,1)S(1)}, u32[]{:S(2)}, u32[]{:S(2)}) collective-permute-start(bf16[160,384]{1,0:T(8,128)(2,1)S(1)} %slice.45), channel_id=1, source_target_pairs={{0,12},{4,0},{8,4},{12,8},{1,13},{5,1},{9,5},{13,9},{2,14},{6,2},{... | collective-permute-start | bytes 368648 | tf_op jit(solution)/shard_map/ppermute | solution.py:28
  (16 other events, 201.6 us)

commit v15 on v14

--- a/solution.py
+++ b/solution.py
@@ -305,12 +305,13 @@
 
     other = shift(mine, "yhi", 1)
     side = sideways(mine)
-    other, side = lax.optimization_barrier((other, side))
+    other_side = sideways(other)
+    _, side = lax.optimization_barrier((other, side))
     x, yhi = lax.axis_index("x"), lax.axis_index("yhi")
     shard = (z + jnp.array([0, zs - 1, 1, zs - 2, 2, zs - 3, 3, zs - 4], jnp.int32)) & (zs - 1)
     slots = (2 * (((shard >> 1) - x) & (mp // 2 - 1)) + ((shard & 1) ^ yhi)).astype(jnp.int32)
     up2, down2 = shift(up1, "z", 1), shift(down1, "z", -1)
-    other_side, far = sideways(other), onward(*side)
+    far = onward(*side)
     other_side, far, w_out, slots = lax.optimization_barrier((other_side, far, w_out, slots))
     up3, down3 = shift(up2, "z", 1), shift(down2, "z", -1)
     other_far = onward(*other_side)

time: 173 us -> 173 us (level)
  no operation moved by 1% of the time
where the time goes in v15:
time: 173 us; the launch traced here: 172 us
  waiting for transfers between devices  53.3 us (31%)
  starting transfers between devices  51.3 us (30%)
  blocking collectives  31.2 us (18%)
  Pallas kernels  20.9 us (12%)
  local copies, waits for them, and re-layouts  10.7 us (6%)
  other arithmetic  2.57 us (1%)
    ppermute x28, waiting for transfers between devices, shift(): return lax.ppermute(x, axis, [(i, (i + by) % n) for i in range(n)])  39.5 us
    ppermute x28, starting transfers between devices, shift(): return lax.ppermute(x, axis, [(i, (i + by) % n) for i in range(n)])  37.7 us
    all_to_all x2, blocking collectives, exchange(): return lax.all_to_all(x, axis, split_axis=0, concat_axis=0, tiled=True)  31.2 us
    all_to_all x2, waiting for transfers between devices, exchange(): return lax.all_to_all(x, axis, split_axis=0, concat_axis=0, tiled=True)  13.9 us
    all_to_all x2, starting transfers between devices, exchange(): return lax.all_to_all(x, axis, split_axis=0, concat_axis=0, tiled=True)  13.6 us
    pallas_call x1, Pallas kernels, project(): pl.pallas_call(kernel, in_specs=[SMEM] + [ANYWHERE] * len(operands), out_...  10.5 us
    unnamed x37, local copies, waits for them, and re-layouts  6.99 us
    pallas_call x2, Pallas kernels, near(): pl.pallas_call(kernel, in_specs=[SMEM] + [WHOLE] * len(operands), out_spe...  4.69 us
  transfers between devices with their start and end apart: 30, of which 11 were waited for; matrix products, arithmetic and copies ran while one was open for 1% of the time, Pallas kernels for 10%

profile of v15, /device:TPU:1, one launch (start us, length us, event | category | flops | bytes accessed | tf_op | source)
XLA Modules:
  0.0 172.3 jit_solution(17808241816620770455)
XLA Ops:
  4.7 10.0 %all-to-all-start = ((bf16[16,20,640]{2,1,0:T(8,128)(2,1)}), bf16[16,20,640]{2,1,0:T(8,128)(2,1)S(1)}, u32[]{:S(2)}, u32[]{:S(2)}) async-start(bf16[16,20,640]{2,1,0:T(8,128)(2,1)} %copy.18), calls=%async_computation | async-start | bytes 983040 | tf_op jit(solution)/shard_map/all_to_all | solution.py:23
  14.6 1.5 collective-permute-start.9
  17.4 13.8 %all-to-all-done = bf16[16,20,640]{2,1,0:T(8,128)(2,1)S(1)} async-done(((bf16[16,20,640]{2,1,0:T(8,128)(2,1)}), bf16[16,20,640]{2,1,0:T(8,128)(2,1)S(1)}, u32[]{:S(2)}, u32[]{:S(2)}) %all-to-all-start) | async-done | bytes 409632 | tf_op jit(solution)/shard_map/all_to_all | solution.py:23
  31.4 3.0 %collective-permute-start = (bf16[320,640]{1,0:T(8,128)(2,1)S(1)}, bf16[320,640]{1,0:T(8,128)(2,1)}, u32[]{:S(2)}, u32[]{:S(2)}) collective-permute-start(bf16[320,640]{1,0:T(8,128)(2,1)S(1)} %reshape.68.refs_1_), channel_id=1, source_target_pairs={{0,2},{2,0},{1,3},{3,1},{4,6},{6,4},{5,7},{7,5},{8,10},{10,8},{9,1... | collective-permute-start | bytes 1228808 | tf_op jit(solution)/shard_map/ppermute | solution.py:28
  34.4 2.5 %collective-permute-start.3 = (bf16[320,640]{1,0:T(8,128)(2,1)S(1)}, bf16[320,640]{1,0:T(8,128)(2,1)S(1)}, u32[]{:S(2)}, u32[]{:S(2)}) collective-permute-start(bf16[320,640]{1,0:T(8,128)(2,1)S(1)} %reshape.68.refs_1_), channel_id=1, source_target_pairs={{0,12},{4,0},{8,4},{12,8},{1,13},{5,1},{9,5},{13,9},{2,14},{6,2},{... | collective-permute-start | bytes 1228808 | tf_op jit(solution)/shard_map/ppermute | solution.py:28
  36.9 7.8 %collective-permute-done.9.refs_12_ = bf16[3,320,384]{2,1,0:T(8,128)(2,1)} collective-permute-done((bf16[3,320,384]{2,1,0:T(8,128)(2,1)S(1)}, bf16[3,320,384]{2,1,0:T(8,128)(2,1)}, u32[]{:S(2)}, u32[]{:S(2)}) %collective-permute-start.9) | collective-permute-done | bytes 737312 | tf_op jit(solution)/shard_map/ppermute | solution.py:28
  44.7 2.7 %collective-permute-start.12 = (bf16[3,320,384]{2,1,0:T(8,128)(2,1)}, bf16[3,320,384]{2,1,0:T(8,128)(2,1)}, u32[]{:S(2)}, u32[]{:S(2)}) collective-permute-start(bf16[3,320,384]{2,1,0:T(8,128)(2,1)} %collective-permute-done.10.refs_13_), channel_id=1, source_target_pairs={{0,224},{32,0},{64,32},{96,64},{128,96},{160,128},{192,160},{224,1... | collective-permute-start | bytes 2211848 | tf_op jit(solution)/shard_map/ppermute | solution.py:28
  47.3 2.1 %collective-permute-done.4.refs_3_ = bf16[320,640]{1,0:T(8,128)(2,1)S(1)} collective-permute-done((bf16[320,640]{1,0:T(8,128)(2,1)S(1)}, bf16[320,640]{1,0:T(8,128)(2,1)S(1)}, u32[]{:S(2)}, u32[]{:S(2)}) %collective-permute-start.4) | collective-permute-done | bytes 409632 | tf_op jit(solution)/shard_map/ppermute | solution.py:28
  49.5 2.7 %collective-permute-start.1 = (bf16[320,640]{1,0:T(8,128)(2,1)}, bf16[320,640]{1,0:T(8,128)(2,1)S(1)}, u32[]{:S(2)}, u32[]{:S(2)}) collective-permute-start(bf16[320,640]{1,0:T(8,128)(2,1)} %collective-permute-done.refs_6_), channel_id=1, source_target_pairs={{0,12},{4,0},{8,4},{12,8},{1,13},{5,1},{9,5},{13,9},{2,14},{6,2},{... | collective-permute-start | bytes 1228808 | tf_op jit(solution)/shard_map/ppermute | solution.py:28
  52.2 4.9 %collective-permute-done.5.refs_4_ = bf16[160,640]{1,0:T(8,128)(2,1)S(1)} collective-permute-done((bf16[160,640]{1,0:T(8,128)(2,1)S(1)}, bf16[160,640]{1,0:T(8,128)(2,1)S(1)}, u32[]{:S(2)}, u32[]{:S(2)}) %collective-permute-start.5) | collective-permute-done | bytes 204832 | tf_op jit(solution)/shard_map/ppermute | solution.py:28
  57.6 7.3 %collective-permute-done.6.refs_5_ = bf16[160,640]{1,0:T(8,128)(2,1)S(1)} collective-permute-done((bf16[160,640]{1,0:T(8,128)(2,1)S(1)}, bf16[160,640]{1,0:T(8,128)(2,1)S(1)}, u32[]{:S(2)}, u32[]{:S(2)}) %collective-permute-start.6) | collective-permute-done | bytes 204832 | tf_op jit(solution)/shard_map/ppermute | solution.py:28
  65.9 3.3 %collective-permute-start.8 = (bf16[160,640]{1,0:T(8,128)(2,1)S(1)}, bf16[160,640]{1,0:T(8,128)(2,1)}, u32[]{:S(2)}, u32[]{:S(2)}) collective-permute-start(bf16[160,640]{1,0:T(8,128)(2,1)S(1)} %slice.39), channel_id=1, source_target_pairs={{0,12},{4,0},{8,4},{12,8},{1,13},{5,1},{9,5},{13,9},{2,14},{6,2},{... | collective-permute-start | bytes 614408 | tf_op jit(solution)/shard_map/ppermute | solution.py:28
  69.6 2.7 %collective-permute-start.14 = (bf16[3,320,384]{2,1,0:T(8,128)(2,1)}, bf16[3,320,384]{2,1,0:T(8,128)(2,1)}, u32[]{:S(2)}, u32[]{:S(2)}) collective-permute-start(bf16[3,320,384]{2,1,0:T(8,128)(2,1)} %collective-permute-done.12.refs_15_), channel_id=1, source_target_pairs={{0,224},{32,0},{64,32},{96,64},{128,96},{160,128},{192,160},{224,1... | collective-permute-start | bytes 2211848 | tf_op jit(solution)/shard_map/ppermute | solution.py:28
  72.2 2.1 %copy-done.2 = bf16[384,5120]{1,0:T(8,128)(2,1)S(1)} copy-done((bf16[384,5120]{1,0:T(8,128)(2,1)S(1)}, bf16[384,5120]{1,0:T(8,128)(2,1)}, u32[]{:S(2)}) %copy-start.2) | copy-done | bytes 3932184
  76.0 3.6 %all-to-all-start.1 = ((bf16[8,192,640]{2,1,0:T(8,128)(2,1)}), bf16[8,192,640]{2,1,0:T(8,128)(2,1)S(1)}, u32[]{:S(2)}, u32[]{:S(2)}) async-start(bf16[8,192,640]{2,1,0:T(8,128)(2,1)} %copy-done.1), calls=%async_computation.1 | async-start | bytes 3932160 | tf_op jit(solution)/shard_map/all_to_all | solution.py:23
  79.7 7.5 %collective-permute-done.13.refs_16_ = bf16[3,320,384]{2,1,0:T(8,128)(2,1)S(1)} collective-permute-done((bf16[3,320,384]{2,1,0:T(8,128)(2,1)}, bf16[3,320,384]{2,1,0:T(8,128)(2,1)S(1)}, u32[]{:S(2)}, u32[]{:S(2)}) %collective-permute-start.13) | collective-permute-done | bytes 737312 | tf_op jit(solution)/shard_map/ppermute | solution.py:28
  88.4 2.6 %collective-permute-start.16 = (bf16[3,160,384]{2,1,0:T(8,128)(2,1)S(1)}, bf16[3,160,384]{2,1,0:T(8,128)(2,1)S(1)}, u32[]{:S(2)}, u32[]{:S(2)}) collective-permute-start(bf16[3,160,384]{2,1,0:T(8,128)(2,1)S(1)} %slice.49), channel_id=1, source_target_pairs={{0,224},{32,0},{64,32},{96,64},{128,96},{160,128},{192,160},{224,1... | collective-permute-start | bytes 1105928 | tf_op jit(solution)/shard_map/ppermute | solution.py:28
  91.0 10.5 %shard_map.114 = (f32[640,1152]{1,0:T(8,128)}, bf16[320,640]{1,0:T(8,128)(2,1)}) custom-call(s32[8]{0:T(128)} %xor_add_fusion.refs_0_, bf16[320,640]{1,0:T(8,128)(2,1)} %copy-done.7, bf16[320,640]{1,0:T(8,128)(2,1)} %copy-done.8, bf16[320,640]{1,0:T(8,128)(2,1)} %copy-done.9, bf16[160,640]{1,0:T(8,128)(2,1)} %copy-done.13, bf16[160,640]{1,0:T(8,128)(2,1)} %copy-done.14, ...), custom_call_target="tpu_custom_call" | custom-call | tf_op jit(solution)/shard_map/pallas_call | solution.py:105
  101.6 1.8 %copy-done.3 = f32[640,1152]{1,0:T(8,128)S(1)} copy-done((f32[640,1152]{1,0:T(8,128)S(1)}, f32[640,1152]{1,0:T(8,128)}, u32[]{:S(2)}) %copy-start.3) | copy-done | bytes 2949144
  105.5 3.4 %collective-permute-start.17 = (bf16[320,1152]{1,0:T(8,128)(2,1)S(1)}, bf16[320,1152]{1,0:T(8,128)(2,1)S(1)}, u32[]{:S(2)}, u32[]{:S(2)}) collective-permute-start(bf16[320,1152]{1,0:T(8,128)(2,1)S(1)} %get-tuple-element.39), channel_id=1, source_target_pairs={{0,16},{16,0},{1,17},{17,1},{2,18},{18,2},{3,19},{19,3},{4,20},{20... | collective-permute-start | bytes 2211848 | tf_op jit(solution)/shard_map/ppermute | solution.py:28
  109.0 1.7 collective-permute-done.17.other_ref
  112.6 15.0 %all_to_all.20 = bf16[16,20,384]{2,1,0:T(8,128)(2,1)S(1)} all-to-all(bf16[16,20,384]{2,1,0:T(8,128)(2,1)S(1)} %shard_map.116), channel_id=1, replica_groups=mesh['z'=8,'core'=2,'x'=4,'yhi'=2,'dp'=2] {'z','core'}, dimensions={0} | all-to-all | bytes 491520 | tf_op jit(solution)/shard_map/all_to_all | solution.py:23
  127.6 2.5 %collective-permute-start.18 = (bf16[320,384]{1,0:T(8,128)(2,1)S(1)}, bf16[320,384]{1,0:T(8,128)(2,1)S(1)}, u32[]{:S(2)}, u32[]{:S(2)}) collective-permute-start(bf16[320,384]{1,0:T(8,128)(2,1)S(1)} %reshape.69.m0), channel_id=1, source_target_pairs={{0,2},{2,0},{1,3},{3,1},{4,6},{6,4},{5,7},{7,5},{8,10},{10,8},{9,1... | collective-permute-start | bytes 737288 | tf_op jit(solution)/shard_map/ppermute | solution.py:28
  131.6 5.3 %collective-permute-done.18.m1 = bf16[320,384]{1,0:T(8,128)(2,1)S(1)} collective-permute-done((bf16[320,384]{1,0:T(8,128)(2,1)S(1)}, bf16[320,384]{1,0:T(8,128)(2,1)S(1)}, u32[]{:S(2)}, u32[]{:S(2)}) %collective-permute-start.18) | collective-permute-done | bytes 245792 | tf_op jit(solution)/shard_map/ppermute | solution.py:28
  136.9 1.5 collective-permute-start.23
  138.7 1.5 collective-permute-done.20.l0
  140.3 2.7 %collective-permute-start.22 = (bf16[160,384]{1,0:T(8,128)(2,1)S(1)}, bf16[160,384]{1,0:T(8,128)(2,1)S(1)}, u32[]{:S(2)}, u32[]{:S(2)}) collective-permute-start(bf16[160,384]{1,0:T(8,128)(2,1)S(1)} %slice.43), channel_id=1, source_target_pairs={{0,12},{4,0},{8,4},{12,8},{1,13},{5,1},{9,5},{13,9},{2,14},{6,2},{... | collective-permute-start | bytes 368648 | tf_op jit(solution)/shard_map/ppermute | solution.py:28
  143.1 2.1 %shard_map.117.own = f32[320,640]{1,0:T(8,128)S(1)} custom-call(s32[3]{0:T(128)S(1)} %pad_add_fusion.where, bf16[320,384]{1,0:T(8,128)(2,1)S(1)} %reshape.69.m0, bf16[320,384]{1,0:T(8,128)(2,1)S(1)} %collective-permute-done.18.m1, bf16[8,192,640]{2,1,0:T(8,128)(2,1)S(1)} %all-to-all-done.1.half, bf16[8,192,640]{2,1,0:T(8,128)(2,1)} %collective-permute-done.25.other), custom_call_target="tpu_custom_call" | custom-call | tf_op jit(solution)/shard_map/pallas_call | solution.py:232
  146.6 2.7 %collective-permute-start.27 = (bf16[160,384]{1,0:T(8,128)(2,1)S(1)}, bf16[160,384]{1,0:T(8,128)(2,1)S(1)}, u32[]{:S(2)}, u32[]{:S(2)}) collective-permute-start(bf16[160,384]{1,0:T(8,128)(2,1)S(1)} %slice.45), channel_id=1, source_target_pairs={{0,12},{4,0},{8,4},{12,8},{1,13},{5,1},{9,5},{13,9},{2,14},{6,2},{... | collective-permute-start | bytes 368648 | tf_op jit(solution)/shard_map/ppermute | solution.py:28
  149.5 2.6 %shard_map.118.acc = f32[320,640]{1,0:T(8,128)S(1)} custom-call(s32[3]{0:T(128)S(1)} %pad_add_fusion.where, bf16[320,384]{1,0:T(8,128)(2,1)S(1)} %collective-permute-done.19.r0, bf16[320,384]{1,0:T(8,128)(2,1)S(1)} %collective-permute-done.23.r1, bf16[320,384]{1,0:T(8,128)(2,1)S(1)} %collective-permute-done.20.l0, ...), custom_call_target="tpu_custom_call" | custom-call | tf_op jit(solution)/shard_map/pallas_call | solution.py:232
  152.1 2.9 %shard_map.119 = (bf16[320,640]{1,0:T(8,128)(2,1)}, f32[32,2,672]{2,1,0:T(2,128)S(1)}) custom-call(s32[3]{0:T(128)S(1)} %pad_add_fusion.where, bf16[160,384]{1,0:T(8,128)(2,1)S(1)} %collective-permute-done.21.t0, bf16[160,384]{1,0:T(8,128)(2,1)S(1)} %collective-permute-done.22.w0, bf16[160,384]{1,0:T(8,128)(2,1)S(1)} %collective-permute-done.26.t1, ...), custom_call_target="tpu_custom_call" | custom-call | tf_op jit(solution)/shard_map/pallas_call | solution.py:245
  155.1 16.2 %all_to_all.21 = f32[32,2,672]{2,1,0:T(2,128)S(1)} all-to-all(f32[32,2,672]{2,1,0:T(2,128)S(1)} %get-tuple-element.49), channel_id=1, replica_groups=mesh['z'=8,'core'=2,'x'=4,'yhi'=2,'dp'=2] {'z','core','dp'}, dimensions={0} | all-to-all | bytes 344064 | tf_op jit(solution)/shard_map/all_to_all | solution.py:23
  (100 shorter events, 18.7 us)
Async XLA Ops:
  0.6 148.7 %copy-start = (f32[32,640]{1,0:T(8,128)S(1)}, f32[32,640]{1,0:T(8,128)}, u32[]{:S(2)}) copy-start(f32[32,640]{1,0:T(8,128)} %param.17) | copy-start | bytes 245764
  3.8 53.3 %copy-start.15 = (s32[8]{0:T(128)S(1)}, s32[8]{0:T(128)}, u32[]{:S(2)}) copy-start(s32[8]{0:T(128)} %constant.52.clone) | copy-start | bytes 100
  4.7 26.6 %all-to-all-start = ((bf16[16,20,640]{2,1,0:T(8,128)(2,1)}), bf16[16,20,640]{2,1,0:T(8,128)(2,1)S(1)}, u32[]{:S(2)}, u32[]{:S(2)}) async-start(bf16[16,20,640]{2,1,0:T(8,128)(2,1)} %copy.18), calls=%async_computation | async-start | bytes 983040 | tf_op jit(solution)/shard_map/all_to_all | solution.py:23
  14.6 30.0 %collective-permute-start.9 = (bf16[3,320,384]{2,1,0:T(8,128)(2,1)S(1)}, bf16[3,320,384]{2,1,0:T(8,128)(2,1)}, u32[]{:S(2)}, u32[]{:S(2)}) collective-permute-start(bf16[3,320,384]{2,1,0:T(8,128)(2,1)S(1)} %bitcast.27), channel_id=1, source_target_pairs={{0,32},{32,64},{64,96},{96,128},{128,160},{160,192},{192,224},{224... | collective-permute-start | bytes 2211848 | tf_op jit(solution)/shard_map/ppermute | solution.py:28
  16.1 28.5 %collective-permute-start.10 = (bf16[3,320,384]{2,1,0:T(8,128)(2,1)S(1)}, bf16[3,320,384]{2,1,0:T(8,128)(2,1)}, u32[]{:S(2)}, u32[]{:S(2)}) collective-permute-start(bf16[3,320,384]{2,1,0:T(8,128)(2,1)S(1)} %bitcast.28), channel_id=1, source_target_pairs={{0,224},{32,0},{64,32},{96,64},{128,96},{160,128},{192,160},{224,1... | collective-permute-start | bytes 2211848 | tf_op jit(solution)/shard_map/ppermute | solution.py:28
  31.4 16.0 %collective-permute-start = (bf16[320,640]{1,0:T(8,128)(2,1)S(1)}, bf16[320,640]{1,0:T(8,128)(2,1)}, u32[]{:S(2)}, u32[]{:S(2)}) collective-permute-start(bf16[320,640]{1,0:T(8,128)(2,1)S(1)} %reshape.68.refs_1_), channel_id=1, source_target_pairs={{0,2},{2,0},{1,3},{3,1},{4,6},{6,4},{5,7},{7,5},{8,10},{10,8},{9,1... | collective-permute-start | bytes 1228808 | tf_op jit(solution)/shard_map/ppermute | solution.py:28
  34.4 13.0 %collective-permute-start.3 = (bf16[320,640]{1,0:T(8,128)(2,1)S(1)}, bf16[320,640]{1,0:T(8,128)(2,1)S(1)}, u32[]{:S(2)}, u32[]{:S(2)}) collective-permute-start(bf16[320,640]{1,0:T(8,128)(2,1)S(1)} %reshape.68.refs_1_), channel_id=1, source_target_pairs={{0,12},{4,0},{8,4},{12,8},{1,13},{5,1},{9,5},{13,9},{2,14},{6,2},{... | collective-permute-start | bytes 1228808 | tf_op jit(solution)/shard_map/ppermute | solution.py:28
  36.9 12.6 %collective-permute-start.4 = (bf16[320,640]{1,0:T(8,128)(2,1)S(1)}, bf16[320,640]{1,0:T(8,128)(2,1)S(1)}, u32[]{:S(2)}, u32[]{:S(2)}) collective-permute-start(bf16[320,640]{1,0:T(8,128)(2,1)S(1)} %reshape.68.refs_1_), channel_id=1, source_target_pairs={{0,4},{4,8},{8,12},{12,0},{1,5},{5,9},{9,13},{13,1},{2,6},{6,10},{... | collective-permute-start | bytes 1228808 | tf_op jit(solution)/shard_map/ppermute | solution.py:28
  44.6 24.6 %collective-permute-start.11 = (bf16[3,320,384]{2,1,0:T(8,128)(2,1)}, bf16[3,320,384]{2,1,0:T(8,128)(2,1)}, u32[]{:S(2)}, u32[]{:S(2)}) collective-permute-start(bf16[3,320,384]{2,1,0:T(8,128)(2,1)} %collective-permute-done.9.refs_12_), channel_id=1, source_target_pairs={{0,32},{32,64},{64,96},{96,128},{128,160},{160,192},{192,224},{224... | collective-permute-start | bytes 2211848 | tf_op jit(solution)/shard_map/ppermute | solution.py:28
  44.7 24.9 %collective-permute-start.12 = (bf16[3,320,384]{2,1,0:T(8,128)(2,1)}, bf16[3,320,384]{2,1,0:T(8,128)(2,1)}, u32[]{:S(2)}, u32[]{:S(2)}) collective-permute-start(bf16[3,320,384]{2,1,0:T(8,128)(2,1)} %collective-permute-done.10.refs_13_), channel_id=1, source_target_pairs={{0,224},{32,0},{64,32},{96,64},{128,96},{160,128},{192,160},{224,1... | collective-permute-start | bytes 2211848 | tf_op jit(solution)/shard_map/ppermute | solution.py:28
  49.4 7.7 %collective-permute-start.5 = (bf16[160,640]{1,0:T(8,128)(2,1)S(1)}, bf16[160,640]{1,0:T(8,128)(2,1)S(1)}, u32[]{:S(2)}, u32[]{:S(2)}) collective-permute-start(bf16[160,640]{1,0:T(8,128)(2,1)S(1)} %slice.36), channel_id=1, source_target_pairs={{0,4},{4,8},{8,12},{12,0},{1,5},{5,9},{9,13},{13,1},{2,6},{6,10},{... | collective-permute-start | bytes 614408 | tf_op jit(solution)/shard_map/ppermute | solution.py:28
  49.5 15.4 %collective-permute-start.1 = (bf16[320,640]{1,0:T(8,128)(2,1)}, bf16[320,640]{1,0:T(8,128)(2,1)S(1)}, u32[]{:S(2)}, u32[]{:S(2)}) collective-permute-start(bf16[320,640]{1,0:T(8,128)(2,1)} %collective-permute-done.refs_6_), channel_id=1, source_target_pairs={{0,12},{4,0},{8,4},{12,8},{1,13},{5,1},{9,5},{13,9},{2,14},{6,2},{... | collective-permute-start | bytes 1228808 | tf_op jit(solution)/shard_map/ppermute | solution.py:28
  52.2 13.6 %collective-permute-start.2 = (bf16[320,640]{1,0:T(8,128)(2,1)}, bf16[320,640]{1,0:T(8,128)(2,1)S(1)}, u32[]{:S(2)}, u32[]{:S(2)}) collective-permute-start(bf16[320,640]{1,0:T(8,128)(2,1)} %collective-permute-done.refs_6_), channel_id=1, source_target_pairs={{0,4},{4,8},{8,12},{12,0},{1,5},{5,9},{9,13},{13,1},{2,6},{6,10},{... | collective-permute-start | bytes 1228808 | tf_op jit(solution)/shard_map/ppermute | solution.py:28
  57.1 7.8 %collective-permute-start.6 = (bf16[160,640]{1,0:T(8,128)(2,1)S(1)}, bf16[160,640]{1,0:T(8,128)(2,1)S(1)}, u32[]{:S(2)}, u32[]{:S(2)}) collective-permute-start(bf16[160,640]{1,0:T(8,128)(2,1)S(1)} %slice.37), channel_id=1, source_target_pairs={{0,12},{4,0},{8,4},{12,8},{1,13},{5,1},{9,5},{13,9},{2,14},{6,2},{... | collective-permute-start | bytes 614408 | tf_op jit(solution)/shard_map/ppermute | solution.py:28
  65.8 10.2 %collective-permute-start.7 = (bf16[160,640]{1,0:T(8,128)(2,1)S(1)}, bf16[160,640]{1,0:T(8,128)(2,1)}, u32[]{:S(2)}, u32[]{:S(2)}) collective-permute-start(bf16[160,640]{1,0:T(8,128)(2,1)S(1)} %slice.38), channel_id=1, source_target_pairs={{0,4},{4,8},{8,12},{12,0},{1,5},{5,9},{9,13},{13,1},{2,6},{6,10},{... | collective-permute-start | bytes 614408 | tf_op jit(solution)/shard_map/ppermute | solution.py:28
  65.9 10.1 %collective-permute-start.8 = (bf16[160,640]{1,0:T(8,128)(2,1)S(1)}, bf16[160,640]{1,0:T(8,128)(2,1)}, u32[]{:S(2)}, u32[]{:S(2)}) collective-permute-start(bf16[160,640]{1,0:T(8,128)(2,1)S(1)} %slice.39), channel_id=1, source_target_pairs={{0,12},{4,0},{8,4},{12,8},{1,13},{5,1},{9,5},{13,9},{2,14},{6,2},{... | collective-permute-start | bytes 614408 | tf_op jit(solution)/shard_map/ppermute | solution.py:28
  69.3 17.8 %collective-permute-start.13 = (bf16[3,320,384]{2,1,0:T(8,128)(2,1)}, bf16[3,320,384]{2,1,0:T(8,128)(2,1)S(1)}, u32[]{:S(2)}, u32[]{:S(2)}) collective-permute-start(bf16[3,320,384]{2,1,0:T(8,128)(2,1)} %collective-permute-done.11.refs_14_), channel_id=1, source_target_pairs={{0,32},{32,64},{64,96},{96,128},{128,160},{160,192},{192,224},{224... | collective-permute-start | bytes 2211848 | tf_op jit(solution)/shard_map/ppermute | solution.py:28
  69.6 17.7 %collective-permute-start.14 = (bf16[3,320,384]{2,1,0:T(8,128)(2,1)}, bf16[3,320,384]{2,1,0:T(8,128)(2,1)}, u32[]{:S(2)}, u32[]{:S(2)}) collective-permute-start(bf16[3,320,384]{2,1,0:T(8,128)(2,1)} %collective-permute-done.12.refs_15_), channel_id=1, source_target_pairs={{0,224},{32,0},{64,32},{96,64},{128,96},{160,128},{192,160},{224,1... | collective-permute-start | bytes 2211848 | tf_op jit(solution)/shard_map/ppermute | solution.py:28
  76.0 36.0 %all-to-all-start.1 = ((bf16[8,192,640]{2,1,0:T(8,128)(2,1)}), bf16[8,192,640]{2,1,0:T(8,128)(2,1)S(1)}, u32[]{:S(2)}, u32[]{:S(2)}) async-start(bf16[8,192,640]{2,1,0:T(8,128)(2,1)} %copy-done.1), calls=%async_computation.1 | async-start | bytes 3932160 | tf_op jit(solution)/shard_map/all_to_all | solution.py:23
  87.2 14.4 %collective-permute-start.15 = (bf16[3,160,384]{2,1,0:T(8,128)(2,1)S(1)}, bf16[3,160,384]{2,1,0:T(8,128)(2,1)S(1)}, u32[]{:S(2)}, u32[]{:S(2)}) collective-permute-start(bf16[3,160,384]{2,1,0:T(8,128)(2,1)S(1)} %slice.48), channel_id=1, source_target_pairs={{0,32},{32,64},{64,96},{96,128},{128,160},{160,192},{192,224},{224... | collective-permute-start | bytes 1105928 | tf_op jit(solution)/shard_map/ppermute | solution.py:28
  88.4 13.2 %collective-permute-start.16 = (bf16[3,160,384]{2,1,0:T(8,128)(2,1)S(1)}, bf16[3,160,384]{2,1,0:T(8,128)(2,1)S(1)}, u32[]{:S(2)}, u32[]{:S(2)}) collective-permute-start(bf16[3,160,384]{2,1,0:T(8,128)(2,1)S(1)} %slice.49), channel_id=1, source_target_pairs={{0,224},{32,0},{64,32},{96,64},{128,96},{160,128},{192,160},{224,1... | collective-permute-start | bytes 1105928 | tf_op jit(solution)/shard_map/ppermute | solution.py:28
  105.5 5.2 %collective-permute-start.17 = (bf16[320,1152]{1,0:T(8,128)(2,1)S(1)}, bf16[320,1152]{1,0:T(8,128)(2,1)S(1)}, u32[]{:S(2)}, u32[]{:S(2)}) collective-permute-start(bf16[320,1152]{1,0:T(8,128)(2,1)S(1)} %get-tuple-element.39), channel_id=1, source_target_pairs={{0,16},{16,0},{1,17},{17,1},{2,18},{18,2},{3,19},{19,3},{4,20},{20... | collective-permute-start | bytes 2211848 | tf_op jit(solution)/shard_map/ppermute | solution.py:28
  112.1 31.0 %collective-permute-start.25 = (bf16[8,192,640]{2,1,0:T(8,128)(2,1)S(1)}, bf16[8,192,640]{2,1,0:T(8,128)(2,1)}, u32[]{:S(2)}, u32[]{:S(2)}) collective-permute-start(bf16[8,192,640]{2,1,0:T(8,128)(2,1)S(1)} %all-to-all-done.1.half), channel_id=1, source_target_pairs={{0,16},{16,0},{1,17},{17,1},{2,18},{18,2},{3,19},{19,3},{4,20},{20... | collective-permute-start | bytes 5898248 | tf_op jit(solution)/shard_map/ppermute | solution.py:28
  127.6 9.3 %collective-permute-start.18 = (bf16[320,384]{1,0:T(8,128)(2,1)S(1)}, bf16[320,384]{1,0:T(8,128)(2,1)S(1)}, u32[]{:S(2)}, u32[]{:S(2)}) collective-permute-start(bf16[320,384]{1,0:T(8,128)(2,1)S(1)} %reshape.69.m0), channel_id=1, source_target_pairs={{0,2},{2,0},{1,3},{3,1},{4,6},{6,4},{5,7},{7,5},{8,10},{10,8},{9,1... | collective-permute-start | bytes 737288 | tf_op jit(solution)/shard_map/ppermute | solution.py:28
  130.1 8.6 %collective-permute-start.19 = (bf16[320,384]{1,0:T(8,128)(2,1)S(1)}, bf16[320,384]{1,0:T(8,128)(2,1)S(1)}, u32[]{:S(2)}, u32[]{:S(2)}) collective-permute-start(bf16[320,384]{1,0:T(8,128)(2,1)S(1)} %reshape.69.m0), channel_id=1, source_target_pairs={{0,12},{4,0},{8,4},{12,8},{1,13},{5,1},{9,5},{13,9},{2,14},{6,2},{... | collective-permute-start | bytes 737288 | tf_op jit(solution)/shard_map/ppermute | solution.py:28
  131.5 8.7 %collective-permute-start.20 = (bf16[320,384]{1,0:T(8,128)(2,1)S(1)}, bf16[320,384]{1,0:T(8,128)(2,1)S(1)}, u32[]{:S(2)}, u32[]{:S(2)}) collective-permute-start(bf16[320,384]{1,0:T(8,128)(2,1)S(1)} %reshape.69.m0), channel_id=1, source_target_pairs={{0,4},{4,8},{8,12},{12,0},{1,5},{5,9},{9,13},{13,1},{2,6},{6,10},{... | collective-permute-start | bytes 737288 | tf_op jit(solution)/shard_map/ppermute | solution.py:28
  136.9 8.3 %collective-permute-start.23 = (bf16[320,384]{1,0:T(8,128)(2,1)S(1)}, bf16[320,384]{1,0:T(8,128)(2,1)S(1)}, u32[]{:S(2)}, u32[]{:S(2)}) collective-permute-start(bf16[320,384]{1,0:T(8,128)(2,1)S(1)} %collective-permute-done.18.m1), channel_id=1, source_target_pairs={{0,12},{4,0},{8,4},{12,8},{1,13},{5,1},{9,5},{13,9},{2,14},{6,2},{... | collective-permute-start | bytes 737288 | tf_op jit(solution)/shard_map/ppermute | solution.py:28
  138.4 8.0 %collective-permute-start.24 = (bf16[320,384]{1,0:T(8,128)(2,1)S(1)}, bf16[320,384]{1,0:T(8,128)(2,1)S(1)}, u32[]{:S(2)}, u32[]{:S(2)}) collective-permute-start(bf16[320,384]{1,0:T(8,128)(2,1)S(1)} %collective-permute-done.18.m1), channel_id=1, source_target_pairs={{0,4},{4,8},{8,12},{12,0},{1,5},{5,9},{9,13},{13,1},{2,6},{6,10},{... | collective-permute-start | bytes 737288 | tf_op jit(solution)/shard_map/ppermute | solution.py:28
  140.2 11.8 %collective-permute-start.21 = (bf16[160,384]{1,0:T(8,128)(2,1)S(1)}, bf16[160,384]{1,0:T(8,128)(2,1)S(1)}, u32[]{:S(2)}, u32[]{:S(2)}) collective-permute-start(bf16[160,384]{1,0:T(8,128)(2,1)S(1)} %slice.42), channel_id=1, source_target_pairs={{0,4},{4,8},{8,12},{12,0},{1,5},{5,9},{9,13},{13,1},{2,6},{6,10},{... | collective-permute-start | bytes 368648 | tf_op jit(solution)/shard_map/ppermute | solution.py:28
  140.3 11.7 %collective-permute-start.22 = (bf16[160,384]{1,0:T(8,128)(2,1)S(1)}, bf16[160,384]{1,0:T(8,128)(2,1)S(1)}, u32[]{:S(2)}, u32[]{:S(2)}) collective-permute-start(bf16[160,384]{1,0:T(8,128)(2,1)S(1)} %slice.43), channel_id=1, source_target_pairs={{0,12},{4,0},{8,4},{12,8},{1,13},{5,1},{9,5},{13,9},{2,14},{6,2},{... | collective-permute-start | bytes 368648 | tf_op jit(solution)/shard_map/ppermute | solution.py:28
  146.5 5.6 %collective-permute-start.26 = (bf16[160,384]{1,0:T(8,128)(2,1)S(1)}, bf16[160,384]{1,0:T(8,128)(2,1)S(1)}, u32[]{:S(2)}, u32[]{:S(2)}) collective-permute-start(bf16[160,384]{1,0:T(8,128)(2,1)S(1)} %slice.44), channel_id=1, source_target_pairs={{0,4},{4,8},{8,12},{12,0},{1,5},{5,9},{9,13},{13,1},{2,6},{6,10},{... | collective-permute-start | bytes 368648 | tf_op jit(solution)/shard_map/ppermute | solution.py:28
  146.6 5.5 %collective-permute-start.27 = (bf16[160,384]{1,0:T(8,128)(2,1)S(1)}, bf16[160,384]{1,0:T(8,128)(2,1)S(1)}, u32[]{:S(2)}, u32[]{:S(2)}) collective-permute-start(bf16[160,384]{1,0:T(8,128)(2,1)S(1)} %slice.45), channel_id=1, source_target_pairs={{0,12},{4,0},{8,4},{12,8},{1,13},{5,1},{9,5},{13,9},{2,14},{6,2},{... | collective-permute-start | bytes 368648 | tf_op jit(solution)/shard_map/ppermute | solution.py:28
  (16 other events, 201.6 us)
